TPU v7x, 128 devices: a whole 4x4x4 slice. The times are simulated.
128 devices in a mesh: facet: 16 (over x, y), sub: 8 (over z, core).
Axes of the slice: x: 4, y: 4, z: 4, core: 2. Of those that a mesh axis runs over, the one named last changes fastest.
Arguments:
- model_image: float32 [16, 128, 8192], P('facet'), may hold values from -6 to 6
- step_sizes: float32 [2], replicated, may hold values from 0.3 to 1
- facet_offsets: int32 [2, 16], replicated, may hold values from 0 to 57344
- col_offsets: int32 [8], P('sub'), may hold values from 0 to 65280
- row_offsets: int32 [8, 16], P('sub'), may hold values from 0 to 65280
- counts: int32 [8, 16], P('sub'), may hold values from 1024 to 4096, as said below
- vis_uv: int32 [2, 8, 16, 4096], P(None, 'sub', 'facet'), may hold values from 32 to 2015
- vis_obs: bfloat16 [2, 8, 16, 4096], P(None, 'sub', 'facet'), may hold values from -6 to 6
- vis_weight: bfloat16 [8, 16, 4096], P('sub', 'facet'), may hold values from 0.25 to 4
Outputs:
- updated_image: float32 [16, 128, 8192], P('facet')
- residual_vis: float32 [2, 8, 16, 4096], P(None, 'sub', 'facet')
Inputs may be any that keep to these rules, and one draw needn't show every extreme that they name: The visibilities of a subgrid fill its first counts slots; every draw has a subgrid with exactly 4096 visibilities and one with exactly 1024.
All inputs are finite; a program needn't handle non-finite values.
Results may differ from a plain program's by a relative error of at most 0.017.
Values may be sent and summed in bfloat16 or wider, within the bound.
No kernel may reach another device: no remote copies, remote signals or barrier semaphores. Data moves between devices by JAX's collectives and lax.ppermute only.
A program may use at most 64 MiB of HBM per device.

v0:
```python
import math

import jax
import jax.numpy as jnp
from jax import lax
from jax.sharding import PartitionSpec as P

NIMG = 65536
FW = 8192
FROWS = 128
SGW = 256
VCAP = 4096
VMIN = 1024
VB = 512
OS = 8
KSUP = 4
ITERS = 2


two_pi = 2.0 * math.pi


def laid_out(blocks, dim):
    blocks = jnp.moveaxis(blocks, 0, dim)
    lengths = blocks.shape
    return blocks.reshape(*lengths[:dim], lengths[dim] * lengths[dim + 1], *lengths[dim + 2 :])


def from_everyone(value, axis):
    copies = jnp.broadcast_to(value, (lax.axis_size(axis), *value.shape))
    return lax.all_to_all(copies, axis, split_axis=0, concat_axis=0, tiled=True)


def gather_directly(value, axis, dim):
    return laid_out(from_everyone(value, axis), dim)


def passed_along(value, axis, by):
    peers = lax.axis_size(axis)
    return lax.ppermute(value, axis, [(i, (i + by) % peers) for i in range(peers)])


def in_blocks(value, dim, peers):
    before, after = (value.shape[:dim], value.shape[dim + 1 :])
    return jnp.moveaxis(value.reshape(*before, peers, -1, *after), dim, 0)


def sum_at_owner(value, axis, dim):
    blocks = in_blocks(value, dim, lax.axis_size(axis))
    arrived = lax.all_to_all(blocks, axis, split_axis=0, concat_axis=0, tiled=True)
    return arrived.astype(jnp.float32).sum(axis=0)


def padded_to(lines, peers):
    spare = -lines.shape[0] % peers
    if not spare:
        return lines
    return jnp.concatenate([lines, jnp.zeros((spare, *lines.shape[1:]), lines.dtype)])


def sum_in_two_steps(value, axis):
    lines = value.reshape(-1, *value.shape[1:][-1:])
    padded = padded_to(lines, lax.axis_size(axis))
    own = lax.psum_scatter(padded, axis, scatter_dimension=0, tiled=True)
    whole = lax.all_gather(own, axis, axis=0, tiled=True)
    return whole[: len(lines)].reshape(value.shape)


def phase_index(frequency, pixels):
    pixel_low = pixels % 256
    pixel_high = pixels // 256
    return (frequency * pixel_low + frequency * pixel_high % (NIMG // 256) * 256) % NIMG


def row_table(frequency_start, pixel_start):
    frequency = frequency_start + jnp.arange(SGW, dtype=jnp.int32)
    pixels = pixel_start + jnp.arange(FROWS, dtype=jnp.int32)
    angles = phase_index(frequency[:, None], pixels[None, :]).astype(jnp.float32) * (two_pi / NIMG)
    return jnp.concatenate([jnp.cos(angles), jnp.sin(angles)], axis=1).astype(jnp.bfloat16)


def column_table(frequency_start, pixel_start):
    frequency = frequency_start + jnp.arange(SGW, dtype=jnp.int32)
    pixels = pixel_start + jnp.arange(FW, dtype=jnp.int32)
    angles = phase_index(frequency[None, :], pixels[:, None]).astype(jnp.float32) * (two_pi / NIMG)
    return jnp.concatenate([jnp.cos(angles), -jnp.sin(angles)], axis=1).astype(jnp.bfloat16)


def expand_section(section_rows):
    real_half = section_rows[:, :SGW]
    imag_half = section_rows[:, SGW:]
    lower_rows = jnp.concatenate([imag_half, -real_half], axis=1)
    return jnp.concatenate([section_rows, lower_rows], axis=0)


def fold_back(back_rows):
    real_part = back_rows[..., :FROWS, :SGW] - back_rows[..., FROWS:, SGW:]
    imag_part = back_rows[..., :FROWS, SGW:] + back_rows[..., FROWS:, :SGW]
    return jnp.concatenate([real_part, imag_part], axis=-1)


def kernel_rows(position):
    offset = (jnp.arange(SGW, dtype=jnp.int32) * OS + OS // 2)[None, :] - position[:, None]
    distance = offset.astype(jnp.float32) / OS
    inside = jnp.abs(offset) <= KSUP * OS
    return jnp.where(inside, jnp.exp(-0.5 * distance * distance), 0.0).astype(jnp.bfloat16)


def block_pass(grid_bf, row_positions, column_positions, observed, weight, is_live):
    row_kernel = kernel_rows(row_positions)
    column_kernel = kernel_rows(column_positions)
    sampled = jnp.dot(row_kernel, grid_bf, preferred_element_type=jnp.float32)
    column_float = column_kernel.astype(jnp.float32)
    predicted_real = jnp.sum(sampled[:, :SGW] * column_float, axis=1)
    predicted_imag = jnp.sum(sampled[:, SGW:] * column_float, axis=1)
    weight_float = weight.astype(jnp.float32)
    residual_real = jnp.where(
        is_live, weight_float * (observed[0].astype(jnp.float32) - predicted_real), 0.0
    )
    residual_imag = jnp.where(
        is_live, weight_float * (observed[1].astype(jnp.float32) - predicted_imag), 0.0
    )
    weighted = jnp.concatenate(
        [residual_real[:, None] * column_float, residual_imag[:, None] * column_float], axis=1
    ).astype(jnp.bfloat16)
    block_grid = lax.dot_general(
        row_kernel, weighted, (((0,), (0,)), ((), ())), preferred_element_type=jnp.float32
    )
    return (block_grid, jnp.stack([residual_real, residual_imag]))


def sweep_blocks(grid_bf, positions, observed, weight, live_total, blocks):
    length = positions.shape[1]

    def one_block(block_index, running):
        grid_sum, residual = running
        first_row = (block_index * VB).astype(jnp.int32)
        position_part = lax.dynamic_slice_in_dim(positions, first_row, VB, 1)
        observed_part = lax.dynamic_slice_in_dim(observed, first_row, VB, 1)
        weight_part = lax.dynamic_slice_in_dim(weight, first_row, VB, 0)
        is_live = first_row + jnp.arange(VB, dtype=jnp.int32) < live_total
        block_grid, values = block_pass(
            grid_bf, position_part[0], position_part[1], observed_part, weight_part, is_live
        )
        residual = lax.dynamic_update_slice(residual, values, (jnp.int32(0), first_row))
        return (grid_sum + block_grid, residual)

    starting = (jnp.zeros((SGW, 2 * SGW), jnp.float32), jnp.zeros((2, length), jnp.float32))
    return lax.fori_loop(0, blocks, one_block, starting)


def kept_count(mine, theirs):
    even_split = VB * ((mine + theirs + 2 * VB - 1) // (2 * VB))
    return jnp.where(mine > theirs, jnp.minimum(mine, even_split), mine)


def local(
    model_image,
    step_sizes,
    facet_offsets,
    col_offsets,
    row_offsets,
    counts,
    vis_uv,
    vis_obs,
    vis_weight,
):
    facet_count = lax.axis_size("facet")
    norm_factor = 1.0 / math.sqrt(facet_count * FROWS * FW)
    spare_slots = (VCAP - VMIN) // 2
    my_facet = lax.axis_index("facet")
    half_way = facet_count // 2
    partner = (my_facet + half_way) % facet_count
    columns_factor = column_table(col_offsets[0], facet_offsets[1, my_facet])
    my_rows = row_offsets[0]
    facet_rows = jax.vmap(lambda offset: row_table(my_rows[my_facet], offset))(facet_offsets[0])
    own_count = counts[0, my_facet]
    positions = vis_uv[:, 0, 0]
    observed = vis_obs[:, 0, 0]
    weight = vis_weight[0, 0]
    model_now = model_image[0]
    residual = jnp.zeros((2, VCAP), jnp.float32)
    for cycle_index in range(ITERS):
        section_rows = jnp.dot(
            model_now.astype(jnp.bfloat16), columns_factor, preferred_element_type=jnp.float32
        ).astype(jnp.bfloat16)
        expanded_pieces = jax.vmap(expand_section)(gather_directly(section_rows[None], "facet", 0))
        summed = lax.dot_general(
            facet_rows,
            expanded_pieces,
            (((0, 2), (0, 1)), ((), ())),
            preferred_element_type=jnp.float32,
        )
        grid_bf = (norm_factor * summed).astype(jnp.bfloat16)
        other_count = counts[0, partner]
        keep_count = kept_count(own_count, other_count)
        other_keep = kept_count(other_count, own_count)
        padded_positions = jnp.pad(positions, ((0, 0), (0, spare_slots)))
        padded_observed = jnp.pad(observed, ((0, 0), (0, spare_slots)))
        padded_weight = jnp.pad(weight, ((0, spare_slots),))
        tail_positions = lax.dynamic_slice_in_dim(padded_positions, keep_count, spare_slots, 1)
        tail_observed = lax.dynamic_slice_in_dim(padded_observed, keep_count, spare_slots, 1)
        tail_weight = lax.dynamic_slice_in_dim(padded_weight, keep_count, spare_slots, 0)
        their_grid, their_positions, their_observed, their_weight = passed_along(
            (grid_bf, tail_positions, tail_observed, tail_weight), "facet", half_way
        )
        mine_grid, mine_residual = sweep_blocks(
            grid_bf, positions, observed, weight, keep_count, (keep_count + VB - 1) // VB
        )
        given_count = other_count - other_keep
        helper_grid, helper_residual = sweep_blocks(
            their_grid,
            their_positions,
            their_observed,
            their_weight,
            given_count,
            (given_count + VB - 1) // VB,
        )
        back_grid, back_residual = (
            passed_along(helper_grid.astype(jnp.bfloat16), "facet", half_way).astype(
                helper_grid.dtype
            ),
            passed_along(helper_residual.astype(jnp.bfloat16), "facet", half_way).astype(
                helper_residual.dtype
            ),
        )
        gridded = mine_grid + back_grid
        placed = lax.dynamic_update_slice(
            jnp.zeros((2, VCAP + spare_slots), jnp.float32),
            back_residual,
            (jnp.int32(0), keep_count),
        )
        residual = mine_residual + placed[:, :VCAP]
        gridded_bf = gridded.astype(jnp.bfloat16)
        back_block = lax.dot_general(
            facet_rows, gridded_bf, (((1,), (0,)), ((), ())), preferred_element_type=jnp.float32
        )
        adjoint_rows = sum_at_owner(fold_back(back_block).astype(jnp.bfloat16), "facet", 0)[
            0
        ].astype(jnp.bfloat16)
        partial_gradient = lax.dot_general(
            adjoint_rows,
            columns_factor,
            (((1,), (1,)), ((), ())),
            preferred_element_type=jnp.float32,
        )
        gradient = sum_in_two_steps(partial_gradient.astype(jnp.bfloat16), "sub").astype(
            jnp.float32
        )
        model_now = model_now + step_sizes[cycle_index] * (norm_factor * gradient)
    return (model_now[None], residual.reshape(2, 1, 1, VCAP))


def solution(mesh):
    in_specs = (
        P("facet", None, None),
        P(),
        P(),
        P("sub"),
        P("sub", None),
        P("sub", None),
        P(None, "sub", "facet", None),
        P(None, "sub", "facet", None),
        P("sub", "facet", None),
    )
    out_specs = (P("facet", None, None), P(None, "sub", "facet", None))
    return jax.shard_map(local, mesh=mesh, in_specs=in_specs, out_specs=out_specs, check_vma=False)
```

profile of v0, /device:TPU:1, one launch (start us, length us, event | category | flops | bytes accessed | tf_op | source)
XLA Modules:
  0.0 402.6 jit_solution(11274146628595070569)
XLA Ops:
  7.2 1.3 constant_dynamic-slice_fusion.7
  9.8 43.5 %cosine_convert_fusion = (bf16[8192,256]{1,0:T(8,128)(2,1)}, bf16[8192,256]{1,0:T(8,128)(2,1)}) fusion(s32[8192]{0:T(1024)S(1)} %get-tuple-element.717, s32[8192]{0:T(1024)S(1)} %get-tuple-element.718, s32[256]{0:T(256)S(1)} %iota_add_fusion.2), kind=kLoop, calls=%fused_computation.216 | loop fusion | flops 65011712 | bytes 8455168 | tf_op jit(solution)/shard_map/convert.26
  53.3 4.8 %fusion.195 = bf16[128,512]{0,1:T(8,128)(2,1)S(1)} fusion(bf16[8192,256]{1,0:T(8,128)(2,1)} %get-tuple-element.707, bf16[8192,256]{1,0:T(8,128)(2,1)} %get-tuple-element.706, f32[1,128,8192]{2,1,0:T(8,128)S(1)} %copy-done), kind=kOutput, calls=%fused_computation.271 | convolution fusion | flops 1090519040 | bytes 12713984 | tf_op jit(solution)/shard_map/dot_general | solution.py:184
  58.3 1.6 broadcast_in_dim.112
  59.9 7.6 %all-to-all-start = ((bf16[16,1,128,512]{3,2,1,0:T(8,128)(2,1)}), bf16[16,1,128,512]{3,2,1,0:T(8,128)(2,1)}, u32[]{:S(2)}, u32[]{:S(2)}) async-start(bf16[16,1,128,512]{3,2,1,0:T(8,128)(2,1)} %broadcast_in_dim.112), calls=%async_computation | async-start | bytes 4194304 | tf_op jit(solution)/shard_map/all_to_all | solution.py:31
  72.3 2.9 collective-permute-start
  75.9 9.6 %cosine_convert_fusion.1 = (bf16[16,256,128]{2,1,0:T(8,128)(2,1)S(1)}, bf16[16,256,128]{2,1,0:T(8,128)(2,1)S(1)}) fusion(s32[16,128]{1,0:T(8,128)S(1)} %get-tuple-element.713, s32[16,128]{1,0:T(8,128)S(1)} %get-tuple-element.712, s32[256]{0:T(256)S(1)} %iota_add_fusion.3), kind=kLoop, calls=%fused_computation.262 | loop fusion | flops 15728640 | bytes 2114560 | tf_op jit(solution)/shard_map/convert.28
  85.5 9.8 %all-to-all-done = bf16[16,1,128,512]{3,2,1,0:T(8,128)(2,1)} async-done(((bf16[16,1,128,512]{3,2,1,0:T(8,128)(2,1)}), bf16[16,1,128,512]{3,2,1,0:T(8,128)(2,1)}, u32[]{:S(2)}, u32[]{:S(2)}) %all-to-all-start) | async-done | bytes 2097184 | tf_op jit(solution)/shard_map/all_to_all | solution.py:31
  95.3 1.7 fusion.224
  97.0 2.8 fusion.188
  100.8 2.3 collective-permute-start.2
  107.4 2.3 collective-permute-start.4
  109.8 6.0 %while.60 = (s32[]{:T(128)}, f32[256,512]{1,0:T(8,128)S(1)}, s32[]{:T(128)}, s32[2,4096]{1,0:T(2,128)S(1)}, s32[]{:T(128)}, /*index=5*/bf16[4096]{0:T(1024)(128)...) while((s32[]{:T(128)}, f32[256,512]{1,0:T(8,128)S(1)}, ...), condition=%wide.region_3.4_spmd, body=%wide.region_0.3_spmd.sunk | while | flops 275649536 | bytes 4505811 | solution.py:149
  115.9 1.3 fusion.201
  118.0 35.7 %all_to_all.20 = bf16[16,1,128,512]{3,2,1,0:T(8,128)(2,1)} all-to-all(bf16[16,1,128,512]{3,2,1,0:T(8,128)(2,1)S(1)} %maximum_bitcast_fusion), channel_id=1, replica_groups=mesh['facet'=16,'sub'=8] {'facet'}, dimensions={0} | all-to-all | bytes 4194304 | tf_op jit(solution)/shard_map/all_to_all | solution.py:50
  153.8 1.9 reduce_sum.132
  155.7 7.6 %convolution_convert_fusion.1 = bf16[128,8192]{1,0:T(8,128)(2,1)} fusion(bf16[128,512]{1,0:T(8,128)(2,1)S(1)} %reduce_sum.132, bf16[8192,256]{1,0:T(8,128)(2,1)} %get-tuple-element.707, bf16[8192,256]{1,0:T(8,128)(2,1)} %get-tuple-element.706), kind=kOutput, calls=%fused_computation.207 | convolution fusion | flops 1091567616 | bytes 10616832 | tf_op jit(solution)/shard_map/dot_general | solution.py:241
  163.4 34.4 %reduce-scatter.3.cloned.1.call-done = bf16[16,8192]{1,0:T(8,128)(2,1)} async-done(((bf16[128,8192]{1,0:T(8,128)(2,1)}), bf16[16,8192]{1,0:T(8,128)(2,1)}) %reduce-scatter.3.cloned.1.call-update) | async-done | bytes 262160 | tf_op jit(solution)/shard_map/reduce_scatter | solution.py:64
  199.1 28.0 %all-gather.3.cloned.1.call-done = bf16[128,8192]{1,0:T(8,128)(2,1)} async-done(((bf16[16,8192]{1,0:T(8,128)(2,1)}), bf16[128,8192]{1,0:T(8,128)(2,1)}) %all-gather.3.cloned.1.call-update) | async-done | bytes 2097168 | tf_op jit(solution)/shard_map/all_gather | solution.py:65
  227.2 6.5 %fusion.191 = bf16[128,512]{1,0:T(8,128)(2,1)S(1)} fusion(bf16[128,8192]{1,0:T(8,128)(2,1)} %all-gather.3.cloned.1.call-done, f32[1,128,8192]{2,1,0:T(8,128)} %param.17, f32[]{:T(128)} %bitcast.35, bf16[8192,256]{1,0:T(8,128)(2,1)} %get-tuple-element.707, bf16[8192,256]{1,0:T(8,128)(2,1)} %get-tuple-element.706), kind=kOutput, calls=%fused_computation.269 | convolution fusion | flops 1094778880 | bytes 14811140 | tf_op jit(solution)/shard_map/dot_general | solution.py:184
  233.9 33.5 %all_to_all.21 = bf16[16,1,128,512]{3,2,1,0:T(8,128)(2,1)S(1)} all-to-all(bf16[16,1,128,512]{3,2,1,0:T(8,128)(2,1)S(1)} %broadcast_in_dim.113), channel_id=1, replica_groups=mesh['facet'=16,'sub'=8] {'facet'}, dimensions={0} | all-to-all | bytes 4194304 | tf_op jit(solution)/shard_map/all_to_all | solution.py:31
  268.7 1.2 collective-permute-start.5
  270.0 6.0 %collective-permute-done.5 = bf16[256,512]{1,0:T(8,128)(2,1)S(1)} collective-permute-done((bf16[256,512]{1,0:T(8,128)(2,1)S(1)}, bf16[256,512]{1,0:T(8,128)(2,1)S(1)}, u32[]{:S(2)}, u32[]{:S(2)}) %collective-permute-start.5) | collective-permute-done | bytes 262176 | tf_op jit(solution)/shard_map/ppermute | solution.py:40
  276.1 1.6 collective-permute-start.6
  277.8 6.1 %while.62 = (s32[]{:T(128)}, f32[256,512]{1,0:T(8,128)S(1)}, f32[2,4096]{1,0:T(2,128)S(1)}, s32[]{:T(128)}, s32[2,4096]{1,0:T(2,128)S(1)}, /*index=5*/s32[]{:T(1...) while((s32[]{:T(128)}, f32[256,512]{1,0:T(8,128)S(1)}, ...), condition=%wide.region_13.14_spmd, body=%wide.region_10.13_spmd.sunk | while | flops 275650560 | bytes 4514015 | solution.py:149
  284.0 1.3 fusion.204
  286.1 37.8 %all_to_all.22 = bf16[16,1,128,512]{3,2,1,0:T(8,128)(2,1)S(1)} all-to-all(bf16[16,1,128,512]{3,2,1,0:T(8,128)(2,1)S(1)} %maximum_bitcast_fusion.1), channel_id=1, replica_groups=mesh['facet'=16,'sub'=8] {'facet'}, dimensions={0} | all-to-all | bytes 4194304 | tf_op jit(solution)/shard_map/all_to_all | solution.py:50
  324.2 7.8 %convolution_convert_fusion = bf16[128,8192]{1,0:T(8,128)(2,1)} fusion(bf16[128,512]{1,0:T(8,128)(2,1)S(1)} %reduce_sum.133, bf16[8192,256]{1,0:T(8,128)(2,1)} %get-tuple-element.707, bf16[8192,256]{1,0:T(8,128)(2,1)} %get-tuple-element.706), kind=kOutput, calls=%fused_computation.206 | convolution fusion | flops 1091567616 | bytes 10616832 | tf_op jit(solution)/shard_map/dot_general | solution.py:241
  332.0 29.2 %reduce-scatter.5.cloned.1.call-done = bf16[16,8192]{1,0:T(8,128)(2,1)} async-done(((bf16[128,8192]{1,0:T(8,128)(2,1)}), bf16[16,8192]{1,0:T(8,128)(2,1)}) %reduce-scatter.5.cloned.1.call-update) | async-done | bytes 262160 | tf_op jit(solution)/shard_map/reduce_scatter | solution.py:64
  361.3 2.7 collective-permute-start.7
  366.5 23.8 %all-gather.5.cloned.1.call-done = bf16[128,8192]{1,0:T(8,128)(2,1)} async-done(((bf16[16,8192]{1,0:T(8,128)(2,1)}), bf16[128,8192]{1,0:T(8,128)(2,1)}) %all-gather.5.cloned.1.call-update) | async-done | bytes 2097168 | tf_op jit(solution)/shard_map/all_gather | solution.py:65
  390.4 5.7 %add_bitcast_fusion = f32[1,128,8192]{2,1,0:T(8,128)} fusion(bf16[128,8192]{1,0:T(8,128)(2,1)} %all-gather.5.cloned.1.call-done, bf16[128,8192]{1,0:T(8,128)(2,1)S(1)} %copy-done.1, f32[1,128,8192]{2,1,0:T(8,128)} %param.17, f32[]{:T(128)} %bitcast.42, f32[]{:T(128)} %bitcast.35), kind=kLoop, calls=%fused_computation.231 | loop fusion | flops 6291456 | bytes 12582920 | tf_op jit(solution)/shard_map/broadcast_in_dim | solution.py:251
  (122 shorter events, 22.1 us)
Async XLA Ops:
  9.8 43.5 %copy-start = (f32[1,128,8192]{2,1,0:T(8,128)S(1)}, f32[1,128,8192]{2,1,0:T(8,128)}, u32[]{:S(2)}) copy-start(f32[1,128,8192]{2,1,0:T(8,128)} %param.17) | copy-start | bytes 12582916
  58.1 9.5 %copy-start.6 = (s32[1,16]{1,0:T(1,128)S(1)}, s32[1,16]{1,0:T(1,128)}, u32[]{:S(2)}) copy-start(s32[1,16]{1,0:T(1,128)} %param.22) | copy-start | bytes 196
  58.1 9.5 %copy-start.7 = (s32[1,16]{1,0:T(1,128)S(1)}, s32[1,16]{1,0:T(1,128)}, u32[]{:S(2)}) copy-start(s32[1,16]{1,0:T(1,128)} %param.21) | copy-start | bytes 196
  58.1 14.0 %copy-start.3 = (s32[2,1,1,4096]{3,2,1,0:T(1,128)S(1)}, s32[2,1,1,4096]{3,2,1,0:T(1,128)}, u32[]{:S(2)}) copy-start(s32[2,1,1,4096]{3,2,1,0:T(1,128)} %param.23) | copy-start | bytes 98308
  58.1 17.7 %copy-start.8 = (s32[2,16]{1,0:T(2,128)S(1)}, s32[2,16]{1,0:T(2,128)}, u32[]{:S(2)}) copy-start(s32[2,16]{1,0:T(2,128)} %param.19) | copy-start | bytes 388
  59.9 35.5 %all-to-all-start = ((bf16[16,1,128,512]{3,2,1,0:T(8,128)(2,1)}), bf16[16,1,128,512]{3,2,1,0:T(8,128)(2,1)}, u32[]{:S(2)}, u32[]{:S(2)}) async-start(bf16[16,1,128,512]{3,2,1,0:T(8,128)(2,1)} %broadcast_in_dim.112), calls=%async_computation | async-start | bytes 4194304 | tf_op jit(solution)/shard_map/all_to_all | solution.py:31
  67.5 130.2 %reduce-scatter.3.cloned.1.call-start = ((), (), s32[]{:S(2)}) async-start(), calls=%async_computation.6 | async-start | bytes 2359296 | tf_op jit(solution)/shard_map/reduce_scatter | solution.py:64
  72.3 35.0 %collective-permute-start = (s32[2,1536]{1,0:T(2,128)S(1)}, s32[2,1536]{1,0:T(2,128)S(1)}, u32[]{:S(2)}, u32[]{:S(2)}) collective-permute-start(s32[2,1536]{1,0:T(2,128)S(1)} %pad_dynamic-slice_fusion), channel_id=1, source_target_pairs={{0,64},{8,72},{16,80},{24,88},{32,96},{40,104},{48,112},{56,120},{... | collective-permute-start | bytes 36872 | tf_op jit(solution)/shard_map/ppermute | solution.py:40
  97.0 3.7 copy-start.2
  97.0 6.1 %copy-start.4 = (bf16[1,1,4096]{2,1,0:T(2,128)(2,1)S(1)}, bf16[1,1,4096]{2,1,0:T(2,128)(2,1)}, u32[]{:S(2)}) copy-start(bf16[1,1,4096]{2,1,0:T(2,128)(2,1)} %param.25) | copy-start | bytes 24580
  99.9 7.4 %collective-permute-start.3 = (bf16[256,512]{1,0:T(8,128)(2,1)S(1)}, bf16[256,512]{1,0:T(8,128)(2,1)S(1)}, u32[]{:S(2)}, u32[]{:S(2)}) collective-permute-start(bf16[256,512]{1,0:T(8,128)(2,1)S(1)} %fusion.188), channel_id=1, source_target_pairs={{0,64},{8,72},{16,80},{24,88},{32,96},{40,104},{48,112},{56,120},{... | collective-permute-start | bytes 786440 | tf_op jit(solution)/shard_map/ppermute | solution.py:40
  100.8 6.5 %collective-permute-start.2 = (bf16[2,1536]{1,0:T(2,128)(2,1)S(1)}, bf16[2,1536]{1,0:T(2,128)(2,1)S(1)}, u32[]{:S(2)}, u32[]{:S(2)}) collective-permute-start(bf16[2,1536]{1,0:T(2,128)(2,1)S(1)} %pad_dynamic-slice_fusion.1), channel_id=1, source_target_pairs={{0,64},{8,72},{16,80},{24,88},{32,96},{40,104},{48,112},{56,120},{... | collective-permute-start | bytes 18440 | tf_op jit(solution)/shard_map/ppermute | solution.py:40
  103.3 4.0 collective-permute-start.1
  107.4 8.4 %collective-permute-start.4 = (bf16[256,512]{1,0:T(8,128)(2,1)S(1)}, bf16[256,512]{1,0:T(8,128)(2,1)S(1)}, u32[]{:S(2)}, u32[]{:S(2)}) collective-permute-start(bf16[256,512]{1,0:T(8,128)(2,1)S(1)} %convert_element_type.383), channel_id=1, source_target_pairs={{0,64},{8,72},{16,80},{24,88},{32,96},{40,104},{48,112},{56,120},{... | collective-permute-start | bytes 786440 | tf_op jit(solution)/shard_map/ppermute | solution.py:40
  155.7 42.2 %copy-start.5 = (f32[2]{0:T(128)S(1)}, f32[2]{0:T(128)}, u32[]{:S(2)}) copy-start(f32[2]{0:T(128)} %param.18) | copy-start | bytes 28
  163.3 63.8 %all-gather.3.cloned.1.call-start = ((), (), s32[]{:S(2)}) async-start(), calls=%async_computation.7 | async-start | bytes 2359296 | tf_op jit(solution)/shard_map/all_gather | solution.py:65
  197.8 163.5 %reduce-scatter.5.cloned.1.call-start = ((), (), s32[]{:S(2)}) async-start(), calls=%async_computation.8 | async-start | bytes 2359296 | tf_op jit(solution)/shard_map/reduce_scatter | solution.py:64
  268.7 7.2 %collective-permute-start.5 = (bf16[256,512]{1,0:T(8,128)(2,1)S(1)}, bf16[256,512]{1,0:T(8,128)(2,1)S(1)}, u32[]{:S(2)}, u32[]{:S(2)}) collective-permute-start(bf16[256,512]{1,0:T(8,128)(2,1)S(1)} %fusion.185), channel_id=1, source_target_pairs={{0,64},{8,72},{16,80},{24,88},{32,96},{40,104},{48,112},{56,120},{... | collective-permute-start | bytes 786440 | tf_op jit(solution)/shard_map/ppermute | solution.py:40
  276.1 7.8 %collective-permute-start.6 = (bf16[256,512]{1,0:T(8,128)(2,1)S(1)}, bf16[256,512]{1,0:T(8,128)(2,1)S(1)}, u32[]{:S(2)}, u32[]{:S(2)}) collective-permute-start(bf16[256,512]{1,0:T(8,128)(2,1)S(1)} %convert_element_type.391), channel_id=1, source_target_pairs={{0,64},{8,72},{16,80},{24,88},{32,96},{40,104},{48,112},{56,120},{... | collective-permute-start | bytes 786440 | tf_op jit(solution)/shard_map/ppermute | solution.py:40
  324.2 66.2 %copy-start.1 = (bf16[128,8192]{1,0:T(8,128)(2,1)S(1)}, bf16[128,8192]{1,0:T(8,128)(2,1)}, u32[]{:S(2)}) copy-start(bf16[128,8192]{1,0:T(8,128)(2,1)} %all-gather.3.cloned.1.call-done) | copy-start | bytes 6291460
  332.0 58.4 %all-gather.5.cloned.1.call-start = ((), (), s32[]{:S(2)}) async-start(), calls=%async_computation.9 | async-start | bytes 2359296 | tf_op jit(solution)/shard_map/all_gather | solution.py:65
  361.3 4.1 %collective-permute-start.7 = (bf16[2,1536]{1,0:T(2,128)(2,1)S(1)}, bf16[2,1536]{1,0:T(2,128)(2,1)S(1)}, u32[]{:S(2)}, u32[]{:S(2)}) collective-permute-start(bf16[2,1536]{1,0:T(2,128)(2,1)S(1)} %get-tuple-element.589), channel_id=1, source_target_pairs={{0,64},{8,72},{16,80},{24,88},{32,96},{40,104},{48,112},{56,120},{... | collective-permute-start | bytes 18440 | tf_op jit(solution)/shard_map/ppermute | solution.py:40
Sparse Core Ops, SparseCore 0:
  163.4 34.2 reduce-scatter.2
  199.5 27.6 all-gather.2
  332.1 29.0 reduce-scatter.4
  362.8 27.4 all-gather.4
where the time goes:
time: 403 us
  waiting for transfers between devices  132 us (33%)
  blocking collectives  107 us (27%)
  other arithmetic  71.1 us (18%)
  matrix products  39.2 us (10%)
  between operations  23.3 us (6%)
  starting transfers between devices  22.5 us (6%)
  local copies, waits for them, and re-layouts  6.68 us (2%)
    all_to_all x2, blocking collectives, sum_at_owner(): lax.all_to_all(blocks, axis, split_axis=0, concat_axis=0, tiled=True)  73.5 us
    reduce_scatter x2, waiting for transfers between devices, sum_in_two_steps(): own = lax.psum_scatter(padded, axis, scatter_dimension=0, tiled=True)  63.6 us
    another operation x8, other arithmetic  55 us
    all_gather x2, waiting for transfers between devices, sum_in_two_steps(): whole = lax.all_gather(own, axis, axis=0, tiled=True)  51.9 us
    all_to_all x1, blocking collectives, from_everyone(): return lax.all_to_all(copies, axis, split_axis=0, concat_axis=0, tiled=True)  33.5 us
    dot_general x2, matrix products, local(): lax.dot_general(adjoint_rows, columns_factor, (((1,), (1,)), ((), ())), p...  15.4 us
    ppermute x8, starting transfers between devices, passed_along(): lax.ppermute(value, axis, [(i, (i + by) % peers) for i in range(peers)])  14.7 us
    dot_general x2, matrix products, local(): jnp.dot(model_now.astype(jnp.bfloat16), columns_factor, preferred_element...  11.3 us
  transfers between devices with their start and end apart: 13, of which 7 were waited for; matrix products, arithmetic and copies ran while one was open for 7% of the time, Pallas kernels for 0%

commit v1 on v0

v1 whole, which is shorter than its diff:
```python
import math

import jax
import jax.numpy as jnp
from jax import lax
from jax.experimental import pallas as pl
from jax.experimental.pallas import tpu as pltpu
from jax.sharding import PartitionSpec as P

NIMG = 65536
FW = 8192
FROWS = 128
SGW = 256
VCAP = 4096
OS = 8
KSUP = 4
ITERS = 2
FACETS = 16
NCOL = 8
NROWSG = 16
SLICE = SGW // FACETS

STEP1 = 256
HIGH1 = FW // STEP1
STEP5 = 512
HIGH5 = FW // STEP5
PAIR5 = 2
VBLOCK = 1024

BF = jnp.bfloat16
F32 = jnp.float32
I32 = jnp.int32
NORM = 1.0 / math.sqrt(FACETS * FROWS * FW)
UNIT = 2.0 * math.pi / NIMG
PARAMS = pltpu.CompilerParams(vmem_limit_bytes=56 << 20)
SMEM_SPEC = pl.BlockSpec(memory_space=pltpu.SMEM)
VMEM_SPEC = pl.BlockSpec(memory_space=pltpu.VMEM)


def cos_sin(index):
    quadrant = (index + NIMG // 8) >> 14
    angle = (index - (quadrant << 14)).astype(F32) * UNIT
    square = angle * angle
    sine = angle * (1.0 + square * (-1.0 / 6 + square * (1.0 / 120 + square * (-1.0 / 5040 + square / 362880))))
    cosine = 1.0 + square * (-0.5 + square * (1.0 / 24 + square * (-1.0 / 720 + square / 40320)))
    swapped = (quadrant & 1) != 0
    c = jnp.where(swapped, sine, cosine)
    s = jnp.where(swapped, cosine, sine)
    c = jnp.where(((quadrant + 1) & 2) != 0, -c, c)
    s = jnp.where((quadrant & 2) != 0, -s, s)
    return c, s


def phase(frequency, pixel):
    return cos_sin((frequency * pixel) & (NIMG - 1))


def iota(shape, dim):
    return lax.broadcasted_iota(I32, shape, dim)


def section_kernel(scalars, model_ref, out_ref, table_ref, pc_ref, ps_ref):
    column_start = scalars[0]
    pixel_start = scalars[1]
    freq = column_start + iota((STEP1, SGW), 1)
    c, s = phase(freq, iota((STEP1, SGW), 0))
    table_ref[:, :SGW] = c.astype(BF)
    table_ref[:, SGW:] = (-s).astype(BF)
    freq = column_start + iota((HIGH1, SGW), 1)
    c, s = phase(freq, pixel_start + STEP1 * iota((HIGH1, SGW), 0))
    pc_ref[...] = c
    ps_ref[...] = s
    acc_re = jnp.zeros((FROWS, SGW), F32)
    acc_im = jnp.zeros((FROWS, SGW), F32)
    for high in range(HIGH1):
        block = model_ref[:, high * STEP1 : (high + 1) * STEP1].astype(BF)
        product = jnp.dot(block, table_ref[...], preferred_element_type=F32)
        re = product[:, :SGW]
        im = product[:, SGW:]
        pc = pc_ref[high : high + 1, :]
        ps = ps_ref[high : high + 1, :]
        acc_re = acc_re + (re * pc + im * ps)
        acc_im = acc_im + (im * pc - re * ps)
    re = acc_re.T.astype(BF)
    im = acc_im.T.astype(BF)
    out_ref[:, :SLICE, :] = re.reshape(FACETS, SLICE, FROWS)
    out_ref[:, SLICE:, :] = im.reshape(FACETS, SLICE, FROWS)


def section(scalars, model):
    return pl.pallas_call(
        section_kernel,
        out_shape=jax.ShapeDtypeStruct((FACETS, 2 * SLICE, FROWS), BF),
        in_specs=[SMEM_SPEC, VMEM_SPEC],
        out_specs=VMEM_SPEC,
        scratch_shapes=[
            pltpu.VMEM((STEP1, 2 * SGW), BF),
            pltpu.VMEM((HIGH1, SGW), F32),
            pltpu.VMEM((HIGH1, SGW), F32),
        ],
        compiler_params=PARAMS,
        name="section",
    )(scalars, model)


def fill_row_phases(facet_starts, row_starts_ref, c2_ref, s2_ref, c1_ref, s1_ref):
    rows = row_starts_ref[...]
    freq = rows + iota((NROWSG, SGW), 1)
    for f in range(FACETS):
        c, s = phase(freq, facet_starts[f])
        c2_ref[f] = c
        s2_ref[f] = s
    c, s = phase(jnp.broadcast_to(rows, (NROWSG, FROWS)), iota((NROWSG, FROWS), 1))
    c1_ref[...] = c
    s1_ref[...] = s


ROW_SCRATCH = [
    pltpu.VMEM((FACETS, NROWSG, SGW), F32),
    pltpu.VMEM((FACETS, NROWSG, SGW), F32),
    pltpu.VMEM((NROWSG, FROWS), F32),
    pltpu.VMEM((NROWSG, FROWS), F32),
]


def grid_kernel(facet_starts, row_starts_ref, in_ref, out_ref, w_ref, c2_ref, s2_ref, c1_ref, s1_ref):
    fill_row_phases(facet_starts, row_starts_ref, c2_ref, s2_ref, c1_ref, s1_ref)
    c, s = phase(iota((FROWS, SGW), 0), iota((FROWS, SGW), 1))
    w_ref[:FROWS, :SGW] = c.astype(BF)
    w_ref[:FROWS, SGW:] = (-s).astype(BF)
    w_ref[FROWS:, :SGW] = s.astype(BF)
    w_ref[FROWS:, SGW:] = c.astype(BF)

    def one(r, carry):
        c1 = c1_ref[pl.ds(r, 1), :]
        s1 = s1_ref[pl.ds(r, 1), :]
        re = in_ref[:, :SLICE, :].reshape(FACETS * SLICE, FROWS).astype(F32)
        im = in_ref[:, SLICE:, :].reshape(FACETS * SLICE, FROWS).astype(F32)
        turned = jnp.concatenate([re * c1 + im * s1, im * c1 - re * s1], axis=1).astype(BF)
        product = jnp.dot(turned, w_ref[...], preferred_element_type=F32)
        acc_re = jnp.zeros((SLICE, SGW), F32)
        acc_im = jnp.zeros((SLICE, SGW), F32)
        for f in range(FACETS):
            re = product[f * SLICE : (f + 1) * SLICE, :SGW]
            im = product[f * SLICE : (f + 1) * SLICE, SGW:]
            c2 = c2_ref[f, pl.ds(r, 1), :]
            s2 = s2_ref[f, pl.ds(r, 1), :]
            acc_re = acc_re + (re * c2 + im * s2)
            acc_im = acc_im + (im * c2 - re * s2)
        out_ref[r, :SLICE, :] = (NORM * acc_re).astype(BF)
        out_ref[r, SLICE:, :] = (NORM * acc_im).astype(BF)
        return carry

    lax.fori_loop(0, NROWSG, one, 0, unroll=4)


def grids(facet_starts, row_starts, sections):
    return pl.pallas_call(
        grid_kernel,
        out_shape=jax.ShapeDtypeStruct((NROWSG, 2 * SLICE, SGW), BF),
        in_specs=[SMEM_SPEC, VMEM_SPEC, VMEM_SPEC],
        out_specs=VMEM_SPEC,
        scratch_shapes=[pltpu.VMEM((2 * FROWS, 2 * SGW), BF)] + ROW_SCRATCH,
        compiler_params=PARAMS,
        name="grids",
    )(facet_starts, row_starts, sections)


def adjoint_kernel(facet_starts, row_starts_ref, in_ref, out_ref, w_ref, c2_ref, s2_ref, c1_ref, s1_ref):
    fill_row_phases(facet_starts, row_starts_ref, c2_ref, s2_ref, c1_ref, s1_ref)
    c, s = phase(iota((SGW, FROWS), 0), iota((SGW, FROWS), 1))
    w_ref[:SGW, :FROWS] = c.astype(BF)
    w_ref[:SGW, FROWS:] = s.astype(BF)
    w_ref[SGW:, :FROWS] = (-s).astype(BF)
    w_ref[SGW:, FROWS:] = c.astype(BF)

    def one(f, carry):
        lines_re = []
        lines_im = []
        for r in range(NROWSG):
            re = in_ref[r, :SLICE, :].astype(F32)
            im = in_ref[r, SLICE:, :].astype(F32)
            c2 = c2_ref[f, pl.ds(r, 1), :]
            s2 = s2_ref[f, pl.ds(r, 1), :]
            lines_re.append((re * c2 - im * s2).astype(BF))
            lines_im.append((im * c2 + re * s2).astype(BF))
        turned = jnp.concatenate(
            [jnp.concatenate(lines_re, axis=0), jnp.concatenate(lines_im, axis=0)], axis=1
        )
        product = jnp.dot(turned, w_ref[...], preferred_element_type=F32)
        acc_re = jnp.zeros((SLICE, FROWS), F32)
        acc_im = jnp.zeros((SLICE, FROWS), F32)
        for r in range(NROWSG):
            re = product[r * SLICE : (r + 1) * SLICE, :FROWS]
            im = product[r * SLICE : (r + 1) * SLICE, FROWS:]
            c1 = c1_ref[r : r + 1, :]
            s1 = s1_ref[r : r + 1, :]
            acc_re = acc_re + (re * c1 - im * s1)
            acc_im = acc_im + (im * c1 + re * s1)
        out_ref[f, :SLICE, :] = acc_re.astype(BF)
        out_ref[f, SLICE:, :] = acc_im.astype(BF)
        return carry

    lax.fori_loop(0, FACETS, one, 0, unroll=4)


def adjoint(facet_starts, row_starts, gridded):
    return pl.pallas_call(
        adjoint_kernel,
        out_shape=jax.ShapeDtypeStruct((FACETS, 2 * SLICE, FROWS), BF),
        in_specs=[SMEM_SPEC, VMEM_SPEC, VMEM_SPEC],
        out_specs=VMEM_SPEC,
        scratch_shapes=[pltpu.VMEM((2 * SGW, 2 * FROWS), BF)] + ROW_SCRATCH,
        compiler_params=PARAMS,
        name="adjoint",
    )(facet_starts, row_starts, gridded)


def kernel_columns(position):
    cells = iota((SGW, position.shape[1]), 0) * OS + OS // 2
    offset = cells - position
    distance = offset.astype(F32) * (1.0 / OS)
    inside = jnp.abs(offset) <= KSUP * OS
    return jnp.where(inside, jnp.exp(-0.5 * distance * distance), 0.0).astype(BF)


def visibility_kernel(count_ref, uv_ref, obs_ref, weight_ref, in_ref, gridded_ref, res_ref, acc_ref):
    count = count_ref[0]
    grid_re = in_ref[:, :SLICE, :].reshape(SGW, SGW)
    grid_im = in_ref[:, SLICE:, :].reshape(SGW, SGW)
    for block in range(VCAP // VBLOCK):
        cut = slice(block * VBLOCK, (block + 1) * VBLOCK)
        ku = kernel_columns(uv_ref[0:1, cut])
        kv = kernel_columns(uv_ref[1:2, cut])
        kvf = kv.astype(F32)
        live = block * VBLOCK + iota((1, VBLOCK), 1) < count
        weight = weight_ref[0:1, cut].astype(F32)
        for part, grid in ((0, grid_re), (1, grid_im)):
            sampled = jnp.dot(grid, ku, preferred_element_type=F32)
            predicted = jnp.sum(sampled * kvf, axis=0, keepdims=True)
            observed = obs_ref[part : part + 1, cut].astype(F32)
            residual = jnp.where(live, weight * (observed - predicted), 0.0)
            res_ref[part : part + 1, cut] = residual
            weighted = (residual * kvf).astype(BF)
            total = lax.dot_general(
                weighted, ku, (((1,), (1,)), ((), ())), preferred_element_type=F32
            )
            if block:
                total = total + acc_ref[part]
            if block + 1 < VCAP // VBLOCK:
                acc_ref[part] = total
            else:
                lines = total.astype(BF).reshape(FACETS, SLICE, SGW)
                gridded_ref[:, part * SLICE : (part + 1) * SLICE, :] = lines


def visibilities(count, uv, obs, weight, grid):
    return pl.pallas_call(
        visibility_kernel,
        out_shape=(
            jax.ShapeDtypeStruct((FACETS, 2 * SLICE, SGW), BF),
            jax.ShapeDtypeStruct((2, VCAP), F32),
        ),
        in_specs=[SMEM_SPEC] + [VMEM_SPEC] * 4,
        out_specs=(VMEM_SPEC, VMEM_SPEC),
        scratch_shapes=[pltpu.VMEM((2, SGW, SGW), F32)],
        compiler_params=PARAMS,
        name="visibilities",
    )(count, uv, obs, weight, grid)


def update_kernel(step_ref, adj_ref, tc_ref, ts_ref, pc_ref, ps_ref, model_ref, out_ref, re_ref, im_ref, turned_ref):
    columns = NCOL * SGW

    @pl.when(pl.program_id(0) == 0)
    def _():
        re = adj_ref[:, :SLICE, :].reshape(columns, FROWS).astype(F32)
        im = adj_ref[:, SLICE:, :].reshape(columns, FROWS).astype(F32)
        re_ref[...] = re.T
        im_ref[...] = im.T

    re = re_ref[...]
    im = im_ref[...]
    for p in range(PAIR5):
        pc = pc_ref[pl.ds(pl.program_id(0) * PAIR5 + p, 1), :]
        ps = ps_ref[pl.ds(pl.program_id(0) * PAIR5 + p, 1), :]
        turned_ref[p * FROWS : (p + 1) * FROWS, :columns] = (re * pc - im * ps).astype(BF)
        turned_ref[p * FROWS : (p + 1) * FROWS, columns:] = (im * pc + re * ps).astype(BF)
    gradient = jnp.dot(turned_ref[:, :columns], tc_ref[...], preferred_element_type=F32)
    gradient = gradient + jnp.dot(turned_ref[:, columns:], ts_ref[...], preferred_element_type=F32)
    step = step_ref[0] * NORM
    for p in range(PAIR5):
        cut = slice(p * STEP5, (p + 1) * STEP5)
        out_ref[:, cut] = model_ref[:, cut] + step * gradient[p * FROWS : (p + 1) * FROWS]


def update(step, adj, tables, model):
    columns = NCOL * SGW
    wide = pl.BlockSpec((FROWS, PAIR5 * STEP5), lambda i: (0, i))
    return pl.pallas_call(
        update_kernel,
        grid=(HIGH5 // PAIR5,),
        out_shape=jax.ShapeDtypeStruct((FROWS, FW), F32),
        in_specs=[SMEM_SPEC] + [VMEM_SPEC] * 5 + [wide],
        out_specs=wide,
        scratch_shapes=[
            pltpu.VMEM((FROWS, columns), F32),
            pltpu.VMEM((FROWS, columns), F32),
            pltpu.VMEM((PAIR5 * FROWS, 2 * columns), BF),
        ],
        compiler_params=PARAMS,
        name="update",
    )(step, adj, *tables, model)


def update_tables(column_starts, pixel_start):
    first = column_starts[None, :, None] + SLICE * jnp.arange(FACETS, dtype=I32)[:, None, None]
    freq = (first + jnp.arange(SLICE, dtype=I32)).reshape(-1)
    c, s = phase(freq[:, None], jnp.arange(STEP5, dtype=I32)[None, :])
    pc, ps = phase(freq[None, :], pixel_start + STEP5 * jnp.arange(HIGH5, dtype=I32)[:, None])
    return c.astype(BF), (-s).astype(BF), pc, ps


def exchange(value):
    return lax.all_to_all(value, "facet", split_axis=0, concat_axis=0, tiled=True)


def to_facets(value):
    copies = jnp.broadcast_to(value[:, None], (FACETS, NCOL, *value.shape[1:]))
    copies = copies.reshape(FACETS * NCOL, *value.shape[1:])
    return lax.all_to_all(copies, ("facet", "sub"), split_axis=0, concat_axis=0, tiled=True)


def local(
    model_image,
    step_sizes,
    facet_offsets,
    col_offsets,
    row_offsets,
    counts,
    vis_uv,
    vis_obs,
    vis_weight,
):
    my_facet = lax.axis_index("facet")
    column_starts = lax.all_gather(col_offsets, "sub", axis=0, tiled=True)
    pixel_start = facet_offsets[1, my_facet]
    scalars = jnp.stack([col_offsets[0], pixel_start])
    facet_starts = facet_offsets[0]
    row_starts = row_offsets.reshape(NROWSG, 1)
    count = lax.dynamic_slice_in_dim(counts[0], my_facet, 1, 0)
    uv = vis_uv.reshape(2, VCAP)
    obs = vis_obs.reshape(2, VCAP)
    weight = vis_weight.reshape(1, VCAP)
    tables = update_tables(column_starts, pixel_start)
    model = model_image[0]
    for cycle in range(ITERS):
        grid = exchange(grids(facet_starts, row_starts, exchange(section(scalars, model))))
        gridded, residual = visibilities(count, uv, obs, weight, grid)
        adj = to_facets(adjoint(facet_starts, row_starts, exchange(gridded)))
        model = update(lax.dynamic_slice_in_dim(step_sizes, cycle, 1, 0), adj, tables, model)
    return model[None], residual.reshape(2, 1, 1, VCAP)


def solution(mesh):
    in_specs = (
        P("facet", None, None),
        P(),
        P(),
        P("sub"),
        P("sub", None),
        P("sub", None),
        P(None, "sub", "facet", None),
        P(None, "sub", "facet", None),
        P("sub", "facet", None),
    )
    out_specs = (P("facet", None, None), P(None, "sub", "facet", None))
    return jax.shard_map(local, mesh=mesh, in_specs=in_specs, out_specs=out_specs, check_vma=False)
```

time: 403 us -> 221 us (0.55)
  waiting for transfers between devices: 132 us -> 43.1 us
  Pallas kernels: 0 us -> 72.9 us
  blocking collectives: 107 us -> 43.6 us
  other arithmetic: 71.1 us -> 10.4 us
  matrix products: 39.2 us -> 0 us
  between operations: 23.3 us -> 1.46 us
  starting transfers between devices: 22.5 us -> 34.1 us
  local copies, waits for them, and re-layouts: 6.68 us -> 14.6 us
    all_to_all x3, blocking collectives: 107 us -> 34 us  [exchange(): lax.all_to_all(value, 'facet', split_axis=0, concat_axis=0, tiled=True)]
    pallas_call x0 -> x10, Pallas kernels: none -> 72.9 us  [the longest x2 29.7 us: update(): pl.pallas_call(update_kernel, grid=(HIGH5 // PAIR5,), out_shape=jax.Shape...]
    reduce_scatter x2 -> x0, waiting for transfers between devices: 63.6 us -> none  [sum_in_two_steps(): own = lax.psum_scatter(padded, axis, scatter_dimension=0, tiled=True)]
    another operation x8 -> x1, other arithmetic: 55 us -> 1.18 us  [local(): scalars = jnp.stack([col_offsets[0], pixel_start])]
    all_gather x2 -> x0, waiting for transfers between devices: 51.9 us -> none  [sum_in_two_steps(): whole = lax.all_gather(own, axis, axis=0, tiled=True)]
    dot_general x20 -> x0, matrix products: 39.2 us -> none  [the longest x2 15.4 us: local(): lax.dot_general(adjoint_rows, columns_factor, (((1,), (1,)), ((), ())), p...]
    all_to_all x1 -> x5, waiting for transfers between devices: 9.83 us -> 43.1 us  [the longest x2 30.7 us: to_facets(): lax.all_to_all(copies, ('facet', 'sub'), split_axis=0, concat_axis=0, til...]
    all_to_all x1 -> x5, starting transfers between devices: 7.64 us -> 34.1 us  [the longest x3 17.8 us: exchange(): lax.all_to_all(value, 'facet', split_axis=0, concat_axis=0, tiled=True)]
  transfers between devices with their start and end apart: 13 -> 5, of which waited for: 7 -> 4; matrix products, arithmetic and copies ran while one was open for 7% -> 6% of each run, Pallas kernels for 0% -> 0%
where the time goes in v1:
time: 221 us; the launch traced here: 220 us
  Pallas kernels  72.9 us (33%)
  blocking collectives  43.6 us (20%)
  waiting for transfers between devices  43.1 us (20%)
  starting transfers between devices  34.1 us (15%)
  local copies, waits for them, and re-layouts  14.6 us (7%)
  other arithmetic  10.4 us (5%)
    all_to_all x3, blocking collectives, exchange(): lax.all_to_all(value, 'facet', split_axis=0, concat_axis=0, tiled=True)  34 us
    all_to_all x2, waiting for transfers between devices, to_facets(): lax.all_to_all(copies, ('facet', 'sub'), split_axis=0, concat_axis=0, til...  30.7 us
    pallas_call x2, Pallas kernels, update(): pl.pallas_call(update_kernel, grid=(HIGH5 // PAIR5,), out_shape=jax.Shape...  29.7 us
    all_to_all x3, starting transfers between devices, exchange(): lax.all_to_all(value, 'facet', split_axis=0, concat_axis=0, tiled=True)  17.8 us
    all_to_all x2, starting transfers between devices, to_facets(): lax.all_to_all(copies, ('facet', 'sub'), split_axis=0, concat_axis=0, til...  16.4 us
    pallas_call x2, Pallas kernels, visibilities(): pl.pallas_call(visibility_kernel, out_shape=(jax.ShapeDtypeStruct((FACETS...  15.1 us
    all_to_all x3, waiting for transfers between devices, exchange(): lax.all_to_all(value, 'facet', split_axis=0, concat_axis=0, tiled=True)  12.4 us
    pallas_call x2, Pallas kernels, section(): pl.pallas_call(section_kernel, out_shape=jax.ShapeDtypeStruct((FACETS, 2...  10.1 us
  transfers between devices with their start and end apart: 5, of which 4 were waited for; matrix products, arithmetic and copies ran while one was open for 6% of the time, Pallas kernels for 0%

profile of v1, /device:TPU:1, one launch (start us, length us, event | category | flops | bytes accessed | tf_op | source)
XLA Modules:
  0.0 220.1 jit_solution(11819150945401513132)
XLA Ops:
  1.4 1.3 constant_dynamic-slice_fusion
  2.7 1.2 pad_add_fusion.scalars
  3.9 5.0 %section.2 = bf16[16,32,128]{2,1,0:T(8,128)(2,1)} custom-call(s32[2]{0:T(128)} %pad_add_fusion.scalars, f32[128,8192]{1,0:T(8,128)} %bitcast.17), custom_call_target="tpu_custom_call" | custom-call | tf_op jit(solution)/shard_map/section/pallas_call | solution.py:91
  8.9 7.6 %all-to-all-start = ((bf16[16,32,128]{2,1,0:T(8,128)(2,1)}), bf16[16,32,128]{2,1,0:T(8,128)(2,1)S(1)}, u32[]{:S(2)}, u32[]{:S(2)}) async-start(bf16[16,32,128]{2,1,0:T(8,128)(2,1)} %section.2), calls=%async_computation | async-start | bytes 262144 | tf_op jit(solution)/shard_map/all_to_all | solution.py:325
  17.1 0.8 dynamic-update-slice
  18.5 9.5 %all-reduce = s32[8]{0:T(128)S(1)} all-reduce(s32[8]{0:T(128)S(1)} %dynamic-update-slice), channel_id=1, replica_groups=mesh['facet'=16,'sub'=8] {'sub'}, use_global_device_ids=true, to_apply=%add | all-reduce | flops 8 | bytes 64
  30.5 4.4 %grids.2 = bf16[16,32,256]{2,1,0:T(8,128)(2,1)} custom-call(s32[16]{0:T(128)} %slice_bitcast_fusion.facet_starts, s32[16,1]{1,0:T(8,128)} %copy.14.row_starts_ref, bf16[16,32,128]{2,1,0:T(8,128)(2,1)} %copy-done.5), custom_call_target="tpu_custom_call" | custom-call | tf_op jit(solution)/shard_map/grids/pallas_call | solution.py:158
  34.9 6.6 %all-to-all-start.1 = ((bf16[16,32,256]{2,1,0:T(8,128)(2,1)}), bf16[16,32,256]{2,1,0:T(8,128)(2,1)S(1)}, u32[]{:S(2)}, u32[]{:S(2)}) async-start(bf16[16,32,256]{2,1,0:T(8,128)(2,1)} %grids.2), calls=%async_computation.1 | async-start | bytes 524288 | tf_op jit(solution)/shard_map/all_to_all | solution.py:325
  42.4 6.7 %all-to-all-done.1.in_ref = bf16[16,32,256]{2,1,0:T(8,128)(2,1)S(1)} async-done(((bf16[16,32,256]{2,1,0:T(8,128)(2,1)}), bf16[16,32,256]{2,1,0:T(8,128)(2,1)S(1)}, u32[]{:S(2)}, u32[]{:S(2)}) %all-to-all-start.1) | async-done | bytes 262176 | tf_op jit(solution)/shard_map/all_to_all | solution.py:325
  49.8 7.6 %visibilities.2 = (bf16[16,32,256]{2,1,0:T(8,128)(2,1)}, f32[2,4096]{1,0:T(2,128)}) custom-call(s32[1]{0:T(128)} %bitcast.2.count_ref, s32[2,4096]{1,0:T(2,128)} %bitcast.20, bf16[2,4096]{1,0:T(2,128)(2,1)} %bitcast.22, bf16[1,4096]{1,0:T(2,128)(2,1)} %bitcast.24, bf16[16,32,256]{2,1,0:T(8,128)(2,1)} %copy-done.3), custom_call_target="tpu_custom_call" | custom-call | tf_op jit(solution)/shard_map/visibilities/pallas_call | solution.py:258
  57.3 3.5 %all-to-all-start.2 = ((bf16[16,32,256]{2,1,0:T(8,128)(2,1)}), bf16[16,32,256]{2,1,0:T(8,128)(2,1)S(1)}, u32[]{:S(2)}, u32[]{:S(2)}) async-start(bf16[16,32,256]{2,1,0:T(8,128)(2,1)} %get-tuple-element.5), calls=%async_computation.2 | async-start | bytes 524288 | tf_op jit(solution)/shard_map/all_to_all | solution.py:325
  60.9 0.9 negate_select_fusion.2
  62.4 5.8 %all-to-all-done.2.in_ref = bf16[16,32,256]{2,1,0:T(8,128)(2,1)S(1)} async-done(((bf16[16,32,256]{2,1,0:T(8,128)(2,1)}), bf16[16,32,256]{2,1,0:T(8,128)(2,1)S(1)}, u32[]{:S(2)}, u32[]{:S(2)}) %all-to-all-start.2) | async-done | bytes 262176 | tf_op jit(solution)/shard_map/all_to_all | solution.py:325
  68.9 4.6 %adjoint.2 = bf16[16,32,128]{2,1,0:T(8,128)(2,1)} custom-call(s32[16]{0:T(128)} %slice_bitcast_fusion.facet_starts, s32[16,1]{1,0:T(8,128)} %copy.14.row_starts_ref, bf16[16,32,256]{2,1,0:T(8,128)(2,1)} %copy-done.4), custom_call_target="tpu_custom_call" | custom-call | tf_op jit(solution)/shard_map/adjoint/pallas_call | solution.py:208
  73.5 2.0 broadcast_in_dim.6
  75.5 8.4 %all-to-all-start.3 = ((bf16[128,32,128]{2,1,0:T(8,128)(2,1)}), bf16[128,32,128]{2,1,0:T(8,128)(2,1)S(1)}, u32[]{:S(2)}, u32[]{:S(2)}) async-start(bf16[128,32,128]{2,1,0:T(8,128)(2,1)} %bitcast.7), calls=%async_computation.3 | async-start | bytes 2097152 | tf_op jit(solution)/shard_map/all_to_all | solution.py:331
  83.9 7.5 %fusion.2 = (bf16[2048,512]{1,0:T(8,128)(2,1)}, bf16[2048,512]{1,0:T(8,128)(2,1)}) fusion(s32[2048]{0:T(1024)S(1)} %add.166), kind=kLoop, calls=%fused_computation.4 | loop fusion | flops 44040192 | bytes 4202496 | tf_op jit(solution)/shard_map/convert_element_type | solution.py:321
  91.4 11.9 %all-to-all-done.3.adj_ref = bf16[128,32,128]{2,1,0:T(8,128)(2,1)S(1)} async-done(((bf16[128,32,128]{2,1,0:T(8,128)(2,1)}), bf16[128,32,128]{2,1,0:T(8,128)(2,1)S(1)}, u32[]{:S(2)}, u32[]{:S(2)}) %all-to-all-start.3) | async-done | bytes 1048608 | tf_op jit(solution)/shard_map/all_to_all | solution.py:331
  103.3 1.0 copy-done.2
  104.3 14.9 %update.2.model_ref = f32[128,8192]{1,0:T(8,128)} custom-call(f32[1]{0:T(128)} %get-tuple-element.14.step_ref, bf16[128,32,128]{2,1,0:T(8,128)(2,1)} %copy-done.2, bf16[2048,512]{1,0:T(8,128)(2,1)} %get-tuple-element.13.tc_ref, bf16[2048,512]{1,0:T(8,128)(2,1)} %get-tuple-element.12.ts_ref, f32[16,2048]{1,0:T(8,128)} %get-tuple-element.11.pc_ref, ...), custom_call_target="tpu_custom_call" | custom-call | tf_op jit(solution)/shard_map/update/pallas_call | solution.py:300
  119.2 5.0 %section.3 = bf16[16,32,128]{2,1,0:T(8,128)(2,1)} custom-call(s32[2]{0:T(128)} %pad_add_fusion.scalars, f32[128,8192]{1,0:T(8,128)} %update.2.model_ref), custom_call_target="tpu_custom_call" | custom-call | tf_op jit(solution)/shard_map/section/pallas_call | solution.py:91
  124.2 10.8 %all_to_all.40.in_ref = bf16[16,32,128]{2,1,0:T(8,128)(2,1)} all-to-all(bf16[16,32,128]{2,1,0:T(8,128)(2,1)} %section.3), channel_id=1, replica_groups=mesh['facet'=16,'sub'=8] {'facet'}, dimensions={0} | all-to-all | bytes 262144 | tf_op jit(solution)/shard_map/all_to_all | solution.py:325
  135.1 4.4 %grids.3 = bf16[16,32,256]{2,1,0:T(8,128)(2,1)} custom-call(s32[16]{0:T(128)} %slice_bitcast_fusion.facet_starts, s32[16,1]{1,0:T(8,128)} %copy.14.row_starts_ref, bf16[16,32,128]{2,1,0:T(8,128)(2,1)} %all_to_all.40.in_ref), custom_call_target="tpu_custom_call" | custom-call | tf_op jit(solution)/shard_map/grids/pallas_call | solution.py:158
  139.5 11.6 %all_to_all.41.in_ref = bf16[16,32,256]{2,1,0:T(8,128)(2,1)} all-to-all(bf16[16,32,256]{2,1,0:T(8,128)(2,1)} %grids.3), channel_id=1, replica_groups=mesh['facet'=16,'sub'=8] {'facet'}, dimensions={0} | all-to-all | bytes 524288 | tf_op jit(solution)/shard_map/all_to_all | solution.py:325
  151.0 7.5 %visibilities.3 = (bf16[16,32,256]{2,1,0:T(8,128)(2,1)}, f32[2,4096]{1,0:T(2,128)}) custom-call(s32[1]{0:T(128)} %bitcast.2.count_ref, s32[2,4096]{1,0:T(2,128)} %bitcast.21, bf16[2,4096]{1,0:T(2,128)(2,1)} %bitcast.23, bf16[1,4096]{1,0:T(2,128)(2,1)} %bitcast.25, bf16[16,32,256]{2,1,0:T(8,128)(2,1)} %all_to_all.41.in_ref), custom_call_target="tpu_custom_call" | custom-call | tf_op jit(solution)/shard_map/visibilities/pallas_call | solution.py:258
  158.6 11.6 %all_to_all.42.in_ref = bf16[16,32,256]{2,1,0:T(8,128)(2,1)} all-to-all(bf16[16,32,256]{2,1,0:T(8,128)(2,1)} %get-tuple-element.6), channel_id=1, replica_groups=mesh['facet'=16,'sub'=8] {'facet'}, dimensions={0} | all-to-all | bytes 524288 | tf_op jit(solution)/shard_map/all_to_all | solution.py:325
  170.2 4.6 %adjoint.3 = bf16[16,32,128]{2,1,0:T(8,128)(2,1)} custom-call(s32[16]{0:T(128)} %slice_bitcast_fusion.facet_starts, s32[16,1]{1,0:T(8,128)} %copy.14.row_starts_ref, bf16[16,32,256]{2,1,0:T(8,128)(2,1)} %all_to_all.42.in_ref), custom_call_target="tpu_custom_call" | custom-call | tf_op jit(solution)/shard_map/adjoint/pallas_call | solution.py:208
  174.8 2.0 broadcast_in_dim.7
  176.9 8.0 %all-to-all-start.7 = ((bf16[128,32,128]{2,1,0:T(8,128)(2,1)}), bf16[128,32,128]{2,1,0:T(8,128)(2,1)S(1)}, u32[]{:S(2)}, u32[]{:S(2)}) async-start(bf16[128,32,128]{2,1,0:T(8,128)(2,1)} %bitcast.10), calls=%async_computation.7 | async-start | bytes 2097152 | tf_op jit(solution)/shard_map/all_to_all | solution.py:331
  185.5 18.8 %all-to-all-done.7.adj_ref = bf16[128,32,128]{2,1,0:T(8,128)(2,1)S(1)} async-done(((bf16[128,32,128]{2,1,0:T(8,128)(2,1)}), bf16[128,32,128]{2,1,0:T(8,128)(2,1)S(1)}, u32[]{:S(2)}, u32[]{:S(2)}) %all-to-all-start.7) | async-done | bytes 1048608 | tf_op jit(solution)/shard_map/all_to_all | solution.py:331
  204.3 1.0 copy-done.1
  205.3 14.8 %update.3 = f32[128,8192]{1,0:T(8,128)} custom-call(f32[1]{0:T(128)} %get-tuple-element.15.step_ref, bf16[128,32,128]{2,1,0:T(8,128)(2,1)} %copy-done.1, bf16[2048,512]{1,0:T(8,128)(2,1)} %get-tuple-element.13.tc_ref, bf16[2048,512]{1,0:T(8,128)(2,1)} %get-tuple-element.12.ts_ref, f32[16,2048]{1,0:T(8,128)} %get-tuple-element.11.pc_ref, ...), custom_call_target="tpu_custom_call" | custom-call | tf_op jit(solution)/shard_map/update/pallas_call | solution.py:300
  (36 shorter events, 7.2 us)
Async XLA Ops:
  0.6 17.3 %copy-start = (s32[1,16]{1,0:T(1,128)S(1)}, s32[1,16]{1,0:T(1,128)}, u32[]{:S(2)}) copy-start(s32[1,16]{1,0:T(1,128)} %param.14) | copy-start | bytes 196
  0.6 15.9 %copy-start.11 = (u32[128]{0:T(128)S(1)}, u32[128]{0:T(128)}, u32[]{:S(2)}) copy-start(u32[128]{0:T(128)} %constant.17) | copy-start | bytes 1540
  0.7 28.7 %copy-start.10 = (s32[2,16]{1,0:T(2,128)S(1)}, s32[2,16]{1,0:T(2,128)}, u32[]{:S(2)}) copy-start(s32[2,16]{1,0:T(2,128)} %param.11) | copy-start | bytes 388
  0.7 27.3 %copy-start.9 = (s32[1,16]{1,0:T(1,128)S(1)}, s32[1,16]{1,0:T(1,128)}, u32[]{:S(2)}) copy-start(s32[1,16]{1,0:T(1,128)} %param.13) | copy-start | bytes 196
  0.7 28.0 %copy-start.6 = (s32[2,1,1,4096]{3,2,1,0:T(1,128)S(1)}, s32[2,1,1,4096]{3,2,1,0:T(1,128)}, u32[]{:S(2)}) copy-start(s32[2,1,1,4096]{3,2,1,0:T(1,128)} %param.15) | copy-start | bytes 98308
  0.7 61.1 %copy-start.8 = (f32[2]{0:T(128)S(1)}, f32[2]{0:T(128)}, u32[]{:S(2)}) copy-start(f32[2]{0:T(128)} %param.10) | copy-start | bytes 28
  8.9 21.0 %all-to-all-start = ((bf16[16,32,128]{2,1,0:T(8,128)(2,1)}), bf16[16,32,128]{2,1,0:T(8,128)(2,1)S(1)}, u32[]{:S(2)}, u32[]{:S(2)}) async-start(bf16[16,32,128]{2,1,0:T(8,128)(2,1)} %section.2), calls=%async_computation | async-start | bytes 262144 | tf_op jit(solution)/shard_map/all_to_all | solution.py:325
  29.9 0.6 copy-start.5
  34.9 14.1 %all-to-all-start.1 = ((bf16[16,32,256]{2,1,0:T(8,128)(2,1)}), bf16[16,32,256]{2,1,0:T(8,128)(2,1)S(1)}, u32[]{:S(2)}, u32[]{:S(2)}) async-start(bf16[16,32,256]{2,1,0:T(8,128)(2,1)} %grids.2), calls=%async_computation.1 | async-start | bytes 524288 | tf_op jit(solution)/shard_map/all_to_all | solution.py:325
  49.1 0.7 copy-start.3
  57.3 10.9 %all-to-all-start.2 = ((bf16[16,32,256]{2,1,0:T(8,128)(2,1)}), bf16[16,32,256]{2,1,0:T(8,128)(2,1)S(1)}, u32[]{:S(2)}, u32[]{:S(2)}) async-start(bf16[16,32,256]{2,1,0:T(8,128)(2,1)} %get-tuple-element.5), calls=%async_computation.2 | async-start | bytes 524288 | tf_op jit(solution)/shard_map/all_to_all | solution.py:325
  68.2 0.7 copy-start.4
  75.5 27.8 %all-to-all-start.3 = ((bf16[128,32,128]{2,1,0:T(8,128)(2,1)}), bf16[128,32,128]{2,1,0:T(8,128)(2,1)S(1)}, u32[]{:S(2)}, u32[]{:S(2)}) async-start(bf16[128,32,128]{2,1,0:T(8,128)(2,1)} %bitcast.7), calls=%async_computation.3 | async-start | bytes 2097152 | tf_op jit(solution)/shard_map/all_to_all | solution.py:331
  103.3 1.0 copy-start.2
  158.6 26.3 %copy-start.7 = (f32[2,4096]{1,0:T(2,128)S(1)}, f32[2,4096]{1,0:T(2,128)}, u32[]{:S(2)}) copy-start(f32[2,4096]{1,0:T(2,128)} %get-tuple-element.7) | copy-start | bytes 98308
  176.9 27.4 %all-to-all-start.7 = ((bf16[128,32,128]{2,1,0:T(8,128)(2,1)}), bf16[128,32,128]{2,1,0:T(8,128)(2,1)S(1)}, u32[]{:S(2)}, u32[]{:S(2)}) async-start(bf16[128,32,128]{2,1,0:T(8,128)(2,1)} %bitcast.10), calls=%async_computation.7 | async-start | bytes 2097152 | tf_op jit(solution)/shard_map/all_to_all | solution.py:331
  204.3 1.0 copy-start.1

commit v2 on v1

v2 whole, which is shorter than its diff:
```python
import math

import jax
import jax.numpy as jnp
from jax import lax
from jax.experimental import pallas as pl
from jax.experimental.pallas import tpu as pltpu
from jax.sharding import PartitionSpec as P

NIMG = 65536
FW = 8192
FROWS = 128
SGW = 256
VCAP = 4096
OS = 8
KSUP = 4
FACETS = 16
NCOL = 8
NROWSG = 16
SLICE = SGW // FACETS
COLUMNS = NCOL * SGW

STEP1 = 256
HIGH1 = FW // STEP1
PARTS1 = 4
STEP5 = 512
HIGH5 = FW // STEP5
PAIR5 = 2
VBLOCK = 1024
CHUNK = 4

BF = jnp.bfloat16
F32 = jnp.float32
I32 = jnp.int32
NORM = 1.0 / math.sqrt(FACETS * FROWS * FW)
PARAMS = pltpu.CompilerParams(vmem_limit_bytes=56 << 20)
SMEM_SPEC = pl.BlockSpec(memory_space=pltpu.SMEM)
VMEM_SPEC = pl.BlockSpec(memory_space=pltpu.VMEM)


def cos_sin(index, bits=16):
    quadrant = (index + (1 << (bits - 3))) >> (bits - 2)
    angle = (index - (quadrant << (bits - 2))).astype(F32) * (2.0 * math.pi / (1 << bits))
    square = angle * angle
    sine = angle * (1.0 + square * (-1.0 / 6 + square * (1.0 / 120 + square * (-1.0 / 5040 + square / 362880))))
    cosine = 1.0 + square * (-0.5 + square * (1.0 / 24 + square * (-1.0 / 720 + square / 40320)))
    swapped = (quadrant & 1) != 0
    c = jnp.where(swapped, sine, cosine)
    s = jnp.where(swapped, cosine, sine)
    c = jnp.where(((quadrant + 1) & 2) != 0, -c, c)
    s = jnp.where((quadrant & 2) != 0, -s, s)
    return c, s


def phase(frequency, pixel):
    return cos_sin((frequency * pixel) & (NIMG - 1))


def iota(shape, dim):
    return lax.broadcasted_iota(I32, shape, dim)


def column_of(ref, count, lanes):
    row = iota((count, lanes), 0)
    value = jnp.zeros((count, lanes), I32)
    for i in range(count):
        value = jnp.where(row == i, ref[i], value)
    return value


def section_kernel(column_ref, offsets_ref, model_ref, out_ref, table_ref, pc_ref, ps_ref, re_ref, im_ref):
    part = pl.program_id(0)
    highs = HIGH1 // PARTS1

    @pl.when(part == 0)
    def _():
        column_start = column_ref[0]
        pixel_start = offsets_ref[1, lax.axis_index("facet")]
        freq = column_start + iota((STEP1, SGW), 1)
        c, s = phase(freq, iota((STEP1, SGW), 0))
        table_ref[:, :SGW] = c.astype(BF)
        table_ref[:, SGW:] = (-s).astype(BF)
        freq = column_start + iota((HIGH1, SGW), 1)
        c, s = phase(freq, pixel_start + STEP1 * iota((HIGH1, SGW), 0))
        pc_ref[...] = c
        ps_ref[...] = s
        re_ref[...] = jnp.zeros((FROWS, SGW), F32)
        im_ref[...] = jnp.zeros((FROWS, SGW), F32)

    acc_re = re_ref[...]
    acc_im = im_ref[...]
    for high in range(highs):
        block = model_ref[:, high * STEP1 : (high + 1) * STEP1].astype(BF)
        product = jnp.dot(block, table_ref[...], preferred_element_type=F32)
        re = product[:, :SGW]
        im = product[:, SGW:]
        pc = pc_ref[pl.ds(part * highs + high, 1), :]
        ps = ps_ref[pl.ds(part * highs + high, 1), :]
        acc_re = acc_re + (re * pc + im * ps)
        acc_im = acc_im + (im * pc - re * ps)
    re_ref[...] = acc_re
    im_ref[...] = acc_im

    @pl.when(part == PARTS1 - 1)
    def _():
        re = re_ref[...].T.astype(BF)
        im = im_ref[...].T.astype(BF)
        out_ref[:, :SLICE, :] = re.reshape(FACETS, SLICE, FROWS)
        out_ref[:, SLICE:, :] = im.reshape(FACETS, SLICE, FROWS)


def section(column_start, offsets, model):
    return pl.pallas_call(
        section_kernel,
        grid=(PARTS1,),
        out_shape=jax.ShapeDtypeStruct((FACETS, 2 * SLICE, FROWS), BF),
        in_specs=[SMEM_SPEC, SMEM_SPEC, pl.BlockSpec((FROWS, FW // PARTS1), lambda i: (0, i))],
        out_specs=VMEM_SPEC,
        scratch_shapes=[
            pltpu.VMEM((STEP1, 2 * SGW), BF),
            pltpu.VMEM((HIGH1, SGW), F32),
            pltpu.VMEM((HIGH1, SGW), F32),
            pltpu.VMEM((FROWS, SGW), F32),
            pltpu.VMEM((FROWS, SGW), F32),
        ],
        compiler_params=PARAMS,
        name="section",
    )(column_start, offsets, model)


def row_table_kernel(offsets_ref, rows_ref, table_ref, c_ref, s_ref):
    f = pl.program_id(0)
    pixel = offsets_ref[0, f] + iota((FROWS, SGW), 0)
    c, s = phase(iota((FROWS, SGW), 1), pixel)
    table_ref[:FROWS, :SGW] = c.astype(BF)
    table_ref[:FROWS, SGW:] = (-s).astype(BF)
    table_ref[FROWS:, :SGW] = s.astype(BF)
    table_ref[FROWS:, SGW:] = c.astype(BF)
    row = iota((NROWSG, FROWS), 0)
    freq = jnp.zeros((NROWSG, FROWS), I32)
    for r in range(NROWSG):
        freq = jnp.where(row == r, rows_ref[0, r], freq)
    c, s = phase(freq, offsets_ref[0, f] + iota((NROWSG, FROWS), 1))
    c_ref[0] = c
    s_ref[0] = s


def row_tables(offsets, rows):
    small = pl.BlockSpec((1, NROWSG, FROWS), lambda f: (f, 0, 0))
    return pl.pallas_call(
        row_table_kernel,
        grid=(FACETS,),
        out_shape=(
            jax.ShapeDtypeStruct((FACETS * 2 * FROWS, 2 * SGW), BF),
            jax.ShapeDtypeStruct((FACETS, NROWSG, FROWS), F32),
            jax.ShapeDtypeStruct((FACETS, NROWSG, FROWS), F32),
        ),
        in_specs=[SMEM_SPEC, SMEM_SPEC],
        out_specs=(pl.BlockSpec((2 * FROWS, 2 * SGW), lambda f: (f, 0)), small, small),
        compiler_params=PARAMS,
        name="row_tables",
    )(offsets, rows)


def grid_kernel(in_ref, c_ref, s_ref, table_ref, out_ref, turned_ref, acc_ref):
    part = pl.program_id(0)
    for k in range(CHUNK):
        f = part * CHUNK + k
        re = in_ref[f, :SLICE, :].astype(F32)
        im = in_ref[f, SLICE:, :].astype(F32)
        left = k * 2 * FROWS
        for r in range(NROWSG):
            c = c_ref[f, r : r + 1, :]
            s = s_ref[f, r : r + 1, :]
            lines = slice(r * SLICE, (r + 1) * SLICE)
            turned_ref[lines, left : left + FROWS] = (re * c + im * s).astype(BF)
            turned_ref[lines, left + FROWS : left + 2 * FROWS] = (im * c - re * s).astype(BF)
    product = jnp.dot(turned_ref[...], table_ref[...], preferred_element_type=F32)
    last = FACETS // CHUNK - 1

    @pl.when(part == 0)
    def _():
        acc_ref[...] = product

    @pl.when((part > 0) & (part < last))
    def _():
        acc_ref[...] += product

    @pl.when(part == last)
    def _():
        total = (NORM * (acc_ref[...] + product)).astype(BF)
        out_ref[:, :SLICE, :] = total[:, :SGW].reshape(NROWSG, SLICE, SGW)
        out_ref[:, SLICE:, :] = total[:, SGW:].reshape(NROWSG, SLICE, SGW)


def grids(sections, tables):
    table, c, s = tables
    return pl.pallas_call(
        grid_kernel,
        grid=(FACETS // CHUNK,),
        out_shape=jax.ShapeDtypeStruct((NROWSG, 2 * SLICE, SGW), BF),
        in_specs=[VMEM_SPEC] * 3 + [pl.BlockSpec((CHUNK * 2 * FROWS, 2 * SGW), lambda i: (i, 0))],
        out_specs=VMEM_SPEC,
        scratch_shapes=[
            pltpu.VMEM((NROWSG * SLICE, CHUNK * 2 * FROWS), BF),
            pltpu.VMEM((NROWSG * SLICE, 2 * SGW), F32),
        ],
        compiler_params=PARAMS,
        name="grids",
    )(sections, c, s, table)


def adjoint_kernel(in_ref, c_ref, s_ref, table_ref, out_ref, lines_ref):
    part = pl.program_id(0)

    @pl.when(part == 0)
    def _():
        lines_ref[:, :SGW] = in_ref[:, :SLICE, :].reshape(NROWSG * SLICE, SGW)
        lines_ref[:, SGW:] = in_ref[:, SLICE:, :].reshape(NROWSG * SLICE, SGW)

    for k in range(CHUNK):
        f = part * CHUNK + k
        table = table_ref[k * 2 * FROWS : (k + 1) * 2 * FROWS, :]
        product = lax.dot_general(
            lines_ref[...], table, (((1,), (1,)), ((), ())), preferred_element_type=F32
        )
        acc_re = jnp.zeros((SLICE, FROWS), F32)
        acc_im = jnp.zeros((SLICE, FROWS), F32)
        for r in range(NROWSG):
            re = product[r * SLICE : (r + 1) * SLICE, :FROWS]
            im = product[r * SLICE : (r + 1) * SLICE, FROWS:]
            c = c_ref[f, r : r + 1, :]
            s = s_ref[f, r : r + 1, :]
            acc_re = acc_re + (re * c - im * s)
            acc_im = acc_im + (im * c + re * s)
        both = jnp.concatenate([acc_re, acc_im], axis=1).astype(BF)
        for copy in range(NCOL):
            out_ref[k, copy] = both


def adjoint(gridded, tables):
    table, c, s = tables
    return pl.pallas_call(
        adjoint_kernel,
        grid=(FACETS // CHUNK,),
        out_shape=jax.ShapeDtypeStruct((FACETS, NCOL, SLICE, 2 * FROWS), BF),
        in_specs=[VMEM_SPEC] * 3 + [pl.BlockSpec((CHUNK * 2 * FROWS, 2 * SGW), lambda i: (i, 0))],
        out_specs=pl.BlockSpec((CHUNK, NCOL, SLICE, 2 * FROWS), lambda i: (i, 0, 0, 0)),
        scratch_shapes=[pltpu.VMEM((NROWSG * SLICE, 2 * SGW), BF)],
        compiler_params=PARAMS,
        name="adjoint",
    )(gridded, c, s, table)


def kernel_columns(position):
    cells = iota((SGW, position.shape[1]), 0) * OS + OS // 2
    offset = cells - position
    distance = offset.astype(F32) * (1.0 / OS)
    inside = jnp.abs(offset) <= KSUP * OS
    return jnp.where(inside, jnp.exp(-0.5 * distance * distance), 0.0).astype(BF)


def vis_table_kernel(uv_ref, ku_ref, kv_ref):
    ku_ref[...] = kernel_columns(uv_ref[0:1, :])
    kv_ref[...] = kernel_columns(uv_ref[1:2, :])


def vis_tables(uv):
    wide = pl.BlockSpec((SGW, VBLOCK), lambda i: (0, i))
    shape = jax.ShapeDtypeStruct((SGW, VCAP), BF)
    return pl.pallas_call(
        vis_table_kernel,
        grid=(VCAP // VBLOCK,),
        out_shape=(shape, shape),
        in_specs=[pl.BlockSpec((2, VBLOCK), lambda i: (0, i))],
        out_specs=(wide, wide),
        compiler_params=PARAMS,
        name="vis_tables",
    )(uv)


def visibility_kernel(counts_ref, obs_ref, weight_ref, in_ref, ku_ref, kv_ref, gridded_ref, res_ref, acc_ref):
    part = pl.program_id(0)
    last = VCAP // VBLOCK - 1
    count = counts_ref[0, lax.axis_index("facet")]
    ku = ku_ref[...]
    kv = kv_ref[...].astype(F32)
    live = part * VBLOCK + iota((1, VBLOCK), 1) < count
    weight = weight_ref[...].astype(F32)
    totals = []
    for half in range(2):
        grid = in_ref[:, half * SLICE : (half + 1) * SLICE, :].reshape(SGW, SGW)
        sampled = jnp.dot(grid, ku, preferred_element_type=F32)
        predicted = jnp.sum(sampled * kv, axis=0, keepdims=True)
        observed = obs_ref[half : half + 1, :].astype(F32)
        residual = jnp.where(live, weight * (observed - predicted), 0.0)
        res_ref[half : half + 1, :] = residual
        weighted = (residual * kv).astype(BF)
        totals.append(
            lax.dot_general(weighted, ku, (((1,), (1,)), ((), ())), preferred_element_type=F32)
        )

    @pl.when(part == 0)
    def _():
        acc_ref[0] = totals[0]
        acc_ref[1] = totals[1]

    @pl.when((part > 0) & (part < last))
    def _():
        acc_ref[0] += totals[0]
        acc_ref[1] += totals[1]

    @pl.when(part == last)
    def _():
        for half in range(2):
            lines = (acc_ref[half] + totals[half]).astype(BF).reshape(FACETS, SLICE, SGW)
            gridded_ref[:, half * SLICE : (half + 1) * SLICE, :] = lines


def visibilities(counts, obs, weight, grid, tables):
    wide = pl.BlockSpec((SGW, VBLOCK), lambda i: (0, i))
    pair = pl.BlockSpec((2, VBLOCK), lambda i: (0, i))
    return pl.pallas_call(
        visibility_kernel,
        grid=(VCAP // VBLOCK,),
        out_shape=(
            jax.ShapeDtypeStruct((FACETS, 2 * SLICE, SGW), BF),
            jax.ShapeDtypeStruct((2, VCAP), F32),
        ),
        in_specs=[SMEM_SPEC, pair, pl.BlockSpec((1, VBLOCK), lambda i: (0, i)), VMEM_SPEC, wide, wide],
        out_specs=(VMEM_SPEC, pair),
        scratch_shapes=[pltpu.VMEM((2, SGW, SGW), F32)],
        compiler_params=PARAMS,
        name="visibilities",
    )(counts, obs, weight, grid, *tables)


def dirichlet(distance, pixel_start):
    distance = ((distance & (NIMG - 1)) ^ (NIMG // 2)) - NIMG // 2
    top = cos_sin((distance * (NIMG // (NIMG // FW * 2))) & (NIMG - 1))[1]
    bottom = cos_sin(distance, 17)[1]
    ratio = jnp.where(distance == 0, float(FW), top / jnp.where(distance == 0, 1.0, bottom))
    c, s = cos_sin((distance * (2 * pixel_start + FW - 1)) & (2 * NIMG - 1), 17)
    return c * ratio, s * ratio


def gram_kernel(step_ref, starts_ref, column_ref, offsets_ref, adj_ref, first_ref, out_ref, flip_ref, v_ref):
    wide = 2 * SGW
    pixel_start = offsets_ref[1, lax.axis_index("facet")]
    own = column_ref[0]
    row = iota((NCOL, wide), 0)
    starts = jnp.zeros((NCOL, wide), I32)
    for c in range(NCOL):
        starts = jnp.where(row == c, starts_ref[c], starts)
    lane = iota((NCOL, wide), 1)
    v_ref[0], v_ref[1] = dirichlet(starts - own + (lane - (SGW - 1)), pixel_start)
    v_ref[2], v_ref[3] = dirichlet(starts + own + (2 * (SGW - 1) - lane), pixel_start)
    anti = (iota((SGW, SGW), 0) + iota((SGW, SGW), 1)) == SGW - 1
    flip_ref[...] = jnp.where(anti, 1.0, 0.0).astype(BF)
    totals = [None] * 4
    for c in range(NCOL):
        lines = adj_ref[:, c].reshape(SGW, 2 * FROWS)
        turned = jnp.dot(flip_ref[...], lines, preferred_element_type=F32).astype(BF)
        for k in range(4):
            spread = jnp.broadcast_to(v_ref[k, c : c + 1, :], (SGW, wide))
            band = pltpu.roll(spread, SGW + 1, 1, stride=1, stride_axis=0)[:, :SGW].astype(BF)
            term = jnp.dot(band, lines if k < 2 else turned, preferred_element_type=F32)
            totals[k] = term if c == 0 else totals[k] + term
    scale = step_ref[0] * (0.5 * NORM)
    p1, p2, p3, p4 = totals
    re = p1[:, :FROWS] - p2[:, FROWS:] + p3[:, :FROWS] - p4[:, FROWS:]
    im = p2[:, :FROWS] + p1[:, FROWS:] - p4[:, :FROWS] - p3[:, FROWS:]
    first = first_ref[...].astype(F32)
    out_ref[:, :SLICE, :] = (first[:, :SLICE] + (scale * re).reshape(FACETS, SLICE, FROWS)).astype(BF)
    out_ref[:, SLICE:, :] = (first[:, SLICE:] + (scale * im).reshape(FACETS, SLICE, FROWS)).astype(BF)


def gram(steps, column_starts, column_start, offsets, adj, first):
    return pl.pallas_call(
        gram_kernel,
        out_shape=jax.ShapeDtypeStruct((FACETS, 2 * SLICE, FROWS), BF),
        in_specs=[SMEM_SPEC] * 4 + [VMEM_SPEC] * 2,
        out_specs=VMEM_SPEC,
        scratch_shapes=[
            pltpu.VMEM((SGW, SGW), BF),
            pltpu.VMEM((4, NCOL, 2 * SGW), F32),
        ],
        compiler_params=PARAMS,
        name="gram",
    )(steps, column_starts, column_start, offsets, adj.reshape(FACETS, NCOL, SLICE, 2 * FROWS), first)


def update_kernel(step_ref, adj0_ref, adj1_ref, tc_ref, ts_ref, pc_ref, ps_ref, model_ref, out_ref, both_ref, turned_ref):
    part = pl.program_id(0)

    @pl.when(part == 0)
    def _():
        first = step_ref[0] * NORM
        second = step_ref[1] * NORM
        for j in range(FACETS):
            lines0 = adj0_ref[j * NCOL : (j + 1) * NCOL].reshape(NCOL * SLICE, 2 * FROWS).astype(F32)
            lines1 = adj1_ref[j * NCOL : (j + 1) * NCOL].reshape(NCOL * SLICE, 2 * FROWS).astype(F32)
            both = first * lines0 + second * lines1
            both_ref[:, j * NCOL * SLICE : (j + 1) * NCOL * SLICE] = both.T

    re = both_ref[:FROWS, :]
    im = both_ref[FROWS:, :]
    for p in range(PAIR5):
        pc = pc_ref[pl.ds(part * PAIR5 + p, 1), :]
        ps = ps_ref[pl.ds(part * PAIR5 + p, 1), :]
        turned_ref[p * FROWS : (p + 1) * FROWS, :COLUMNS] = (re * pc - im * ps).astype(BF)
        turned_ref[p * FROWS : (p + 1) * FROWS, COLUMNS:] = (im * pc + re * ps).astype(BF)
    gradient = jnp.dot(turned_ref[:, :COLUMNS], tc_ref[...], preferred_element_type=F32)
    gradient = gradient + jnp.dot(turned_ref[:, COLUMNS:], ts_ref[...], preferred_element_type=F32)
    for p in range(PAIR5):
        cut = slice(p * STEP5, (p + 1) * STEP5)
        out_ref[:, cut] = model_ref[:, cut] + gradient[p * FROWS : (p + 1) * FROWS]


def update(steps, adj0, adj1, tables, model):
    wide = pl.BlockSpec((FROWS, PAIR5 * STEP5), lambda i: (0, i))
    return pl.pallas_call(
        update_kernel,
        grid=(HIGH5 // PAIR5,),
        out_shape=jax.ShapeDtypeStruct((FROWS, FW), F32),
        in_specs=[SMEM_SPEC] + [VMEM_SPEC] * 6 + [wide],
        out_specs=wide,
        scratch_shapes=[
            pltpu.VMEM((2 * FROWS, COLUMNS), F32),
            pltpu.VMEM((PAIR5 * FROWS, 2 * COLUMNS), BF),
        ],
        compiler_params=PARAMS,
        name="update",
    )(steps, adj0, adj1, *tables, model)


def update_tables(column_starts, pixel_start):
    first = column_starts[None, :, None] + SLICE * jnp.arange(FACETS, dtype=I32)[:, None, None]
    freq = (first + jnp.arange(SLICE, dtype=I32)).reshape(-1)
    c, s = phase(freq[:, None], jnp.arange(STEP5, dtype=I32)[None, :])
    pc, ps = phase(freq[None, :], pixel_start + STEP5 * jnp.arange(HIGH5, dtype=I32)[:, None])
    return c.astype(BF), (-s).astype(BF), pc, ps


def exchange(value):
    return lax.all_to_all(value, "facet", split_axis=0, concat_axis=0, tiled=True)


def to_facets(value):
    copies = value.reshape(FACETS * NCOL, *value.shape[2:])
    return lax.all_to_all(copies, ("facet", "sub"), split_axis=0, concat_axis=0, tiled=True)


def local(
    model_image,
    step_sizes,
    facet_offsets,
    col_offsets,
    row_offsets,
    counts,
    vis_uv,
    vis_obs,
    vis_weight,
):
    lines = jnp.broadcast_to(col_offsets[:, None], (8, 128))
    column_starts = lax.optimization_barrier(lax.all_gather(lines, "sub", axis=0, tiled=True))[::8, 0]
    uv = vis_uv.reshape(2, VCAP)
    obs = vis_obs.reshape(2, VCAP)
    weight = vis_weight.reshape(1, VCAP)
    model = model_image[0]
    first = section(col_offsets, facet_offsets, model)
    rows = row_tables(facet_offsets, row_offsets)
    kernels = vis_tables(uv)
    grid = exchange(grids(exchange(first), rows))
    gridded, residual = visibilities(counts, obs, weight, grid, kernels)
    adj0 = to_facets(adjoint(exchange(gridded), rows))
    tables = update_tables(column_starts, facet_offsets[1, lax.axis_index("facet")])
    second = gram(step_sizes, column_starts, col_offsets, facet_offsets, adj0, first)
    grid = exchange(grids(exchange(second), rows))
    gridded, residual = visibilities(counts, obs, weight, grid, kernels)
    adj1 = to_facets(adjoint(exchange(gridded), rows))
    model = update(step_sizes, adj0, adj1, tables, model)
    return model[None], residual.reshape(2, 1, 1, VCAP)


def solution(mesh):
    in_specs = (
        P("facet", None, None),
        P(),
        P(),
        P("sub"),
        P("sub", None),
        P("sub", None),
        P(None, "sub", "facet", None),
        P(None, "sub", "facet", None),
        P("sub", "facet", None),
    )
    out_specs = (P("facet", None, None), P(None, "sub", "facet", None))
    return jax.shard_map(local, mesh=mesh, in_specs=in_specs, out_specs=out_specs, check_vma=False)
```

time: 221 us -> 199 us (0.900)
  blocking collectives: 43.6 us -> 23.4 us
  starting transfers between devices: 34.1 us -> 44.7 us
  local copies, waits for them, and re-layouts: 14.6 us -> 8.81 us
  waiting for transfers between devices: 43.1 us -> 37.4 us
    all_to_all x3 -> x1, blocking collectives: 34 us -> 12.4 us  [exchange(): lax.all_to_all(value, 'facet', split_axis=0, concat_axis=0, tiled=True)]
    pallas_call x2 -> x1, Pallas kernels: 29.7 us -> 14.8 us  [update(): pl.pallas_call(update_kernel, grid=(HIGH5 // PAIR5,), out_shape=jax.Shape...]
    all_to_all x2, waiting for transfers between devices: 30.7 us -> 16.8 us  [to_facets(): lax.all_to_all(copies, ('facet', 'sub'), split_axis=0, concat_axis=0, til...]
    pallas_call x8 -> x10, Pallas kernels: 43.2 us -> 56.2 us  [the longest x2 13.3 us: visibilities(): pl.pallas_call(visibility_kernel, grid=(VCAP // VBLOCK,), out_shape=(jax....]
    all_to_all x3 -> x5, waiting for transfers between devices: 12.4 us -> 20.6 us  [exchange(): lax.all_to_all(value, 'facet', split_axis=0, concat_axis=0, tiled=True)]
    all_to_all x3 -> x5, starting transfers between devices: 17.8 us -> 25.6 us  [exchange(): lax.all_to_all(value, 'facet', split_axis=0, concat_axis=0, tiled=True)]
    broadcast_in_dim x2 -> x0, local copies, waits for them, and re-layouts: 4.07 us -> none  [to_facets(): copies = jnp.broadcast_to(value[:, None], (FACETS, NCOL, *value.shape[1:]))]
    all_to_all x2, starting transfers between devices: 16.4 us -> 19.2 us  [to_facets(): lax.all_to_all(copies, ('facet', 'sub'), split_axis=0, concat_axis=0, til...]
  transfers between devices with their start and end apart: 5 -> 7, of which waited for: 4 -> 6; matrix products, arithmetic and copies ran while one was open for 6% -> 7% of each run, Pallas kernels for 0% -> 7%
where the time goes in v2:
time: 199 us; the launch traced here: 197 us
  Pallas kernels  70.9 us (36%)
  starting transfers between devices  44.7 us (22%)
  waiting for transfers between devices  37.4 us (19%)
  blocking collectives  23.4 us (12%)
  other arithmetic  10.4 us (5%)
  local copies, waits for them, and re-layouts  8.81 us (4%)
    all_to_all x5, starting transfers between devices, exchange(): lax.all_to_all(value, 'facet', split_axis=0, concat_axis=0, tiled=True)  25.6 us
    all_to_all x5, waiting for transfers between devices, exchange(): lax.all_to_all(value, 'facet', split_axis=0, concat_axis=0, tiled=True)  20.6 us
    all_to_all x2, starting transfers between devices, to_facets(): lax.all_to_all(copies, ('facet', 'sub'), split_axis=0, concat_axis=0, til...  19.2 us
    all_to_all x2, waiting for transfers between devices, to_facets(): lax.all_to_all(copies, ('facet', 'sub'), split_axis=0, concat_axis=0, til...  16.8 us
    pallas_call x1, Pallas kernels, update(): pl.pallas_call(update_kernel, grid=(HIGH5 // PAIR5,), out_shape=jax.Shape...  14.8 us
    pallas_call x2, Pallas kernels, visibilities(): pl.pallas_call(visibility_kernel, grid=(VCAP // VBLOCK,), out_shape=(jax....  13.3 us
    all_to_all x1, blocking collectives, exchange(): lax.all_to_all(value, 'facet', split_axis=0, concat_axis=0, tiled=True)  12.4 us
    unnamed x1, blocking collectives  11 us
  transfers between devices with their start and end apart: 7, of which 6 were waited for; matrix products, arithmetic and copies ran while one was open for 7% of the time, Pallas kernels for 7%

profile of v2, /device:TPU:1, one launch (start us, length us, event | category | flops | bytes accessed | tf_op | source)
XLA Modules:
  0.0 197.1 jit_solution(4807485487890991013)
XLA Ops:
  1.3 5.3 %section.1.first_ref = bf16[16,32,128]{2,1,0:T(8,128)(2,1)} custom-call(s32[1]{0:T(128)S(6)} %copy.18.column_ref, s32[2,16]{1,0:T(2,128)} %offsets_ref.5, f32[128,8192]{1,0:T(8,128)} %bitcast.15), custom_call_target="tpu_custom_call" | custom-call | tf_op jit(solution)/shard_map/section/pallas_call | solution.py:113
  6.6 7.6 %all-to-all-start = ((bf16[16,32,128]{2,1,0:T(8,128)(2,1)}), bf16[16,32,128]{2,1,0:T(8,128)(2,1)S(1)}, u32[]{:S(2)}, u32[]{:S(2)}) async-start(bf16[16,32,128]{2,1,0:T(8,128)(2,1)} %section.1.first_ref), calls=%async_computation | async-start | bytes 262144 | tf_op jit(solution)/shard_map/all_to_all | solution.py:446
  14.2 8.4 %row_tables.1 = (bf16[4096,512]{1,0:T(8,128)(2,1)}, f32[16,16,128]{2,1,0:T(8,128)}, f32[16,16,128]{2,1,0:T(8,128)}) custom-call(s32[2,16]{1,0:T(2,128)} %offsets_ref.5, s32[1,16]{1,0:T(1,128)} %rows_ref.1), custom_call_target="tpu_custom_call" | custom-call | tf_op jit(solution)/shard_map/row_tables/pallas_call | solution.py:150
  23.2 4.9 %grids.2 = bf16[16,32,256]{2,1,0:T(8,128)(2,1)} custom-call(bf16[16,32,128]{2,1,0:T(8,128)(2,1)} %copy-done.5, f32[16,16,128]{2,1,0:T(8,128)} %get-tuple-element.10.c_ref, f32[16,16,128]{2,1,0:T(8,128)} %get-tuple-element.11.s_ref, bf16[4096,512]{1,0:T(8,128)(2,1)} %get-tuple-element.12.table_ref), custom_call_target="tpu_custom_call" | custom-call | tf_op jit(solution)/shard_map/grids/pallas_call | solution.py:198
  28.1 6.7 %all-to-all-start.1 = ((bf16[16,32,256]{2,1,0:T(8,128)(2,1)}), bf16[16,32,256]{2,1,0:T(8,128)(2,1)S(1)}, u32[]{:S(2)}, u32[]{:S(2)}) async-start(bf16[16,32,256]{2,1,0:T(8,128)(2,1)} %grids.2), calls=%async_computation.1 | async-start | bytes 524288 | tf_op jit(solution)/shard_map/all_to_all | solution.py:446
  35.4 5.0 %vis_tables.1 = (bf16[256,4096]{1,0:T(8,128)(2,1)}, bf16[256,4096]{1,0:T(8,128)(2,1)}) custom-call(s32[2,4096]{1,0:T(2,128)} %bitcast.21), custom_call_target="tpu_custom_call" | custom-call | tf_op jit(solution)/shard_map/vis_tables/pallas_call | solution.py:271
  40.4 1.7 all-to-all-done.1.in_ref
  42.8 6.7 %visibilities.2 = (bf16[16,32,256]{2,1,0:T(8,128)(2,1)}, f32[2,4096]{1,0:T(2,128)}) custom-call(s32[1,16]{1,0:T(1,128)} %counts_ref.3, bf16[2,4096]{1,0:T(2,128)(2,1)} %bitcast.22, bf16[1,4096]{1,0:T(2,128)(2,1)} %bitcast.24, bf16[16,32,256]{2,1,0:T(8,128)(2,1)} %copy-done.3, bf16[256,4096]{1,0:T(8,128)(2,1)} %get-tuple-element.13.ku_ref, ...), custom_call_target="tpu_custom_call" | custom-call | tf_op jit(solution)/shard_map/visibilities/pallas_call | solution.py:323
  49.5 12.4 %all_to_all.40.in_ref = bf16[16,32,256]{2,1,0:T(8,128)(2,1)} all-to-all(bf16[16,32,256]{2,1,0:T(8,128)(2,1)} %get-tuple-element.15), channel_id=1, replica_groups=mesh['facet'=16,'sub'=8] {'facet'}, dimensions={0} | all-to-all | bytes 524288 | tf_op jit(solution)/shard_map/all_to_all | solution.py:446
  61.9 5.1 %adjoint.2 = bf16[16,8,16,256]{3,2,1,0:T(8,128)(2,1)} custom-call(bf16[16,32,256]{2,1,0:T(8,128)(2,1)} %all_to_all.40.in_ref, f32[16,16,128]{2,1,0:T(8,128)} %get-tuple-element.10.c_ref, f32[16,16,128]{2,1,0:T(8,128)} %get-tuple-element.11.s_ref, bf16[4096,512]{1,0:T(8,128)(2,1)} %get-tuple-element.12.table_ref), custom_call_target="tpu_custom_call" | custom-call | tf_op jit(solution)/shard_map/adjoint/pallas_call | solution.py:243
  67.0 9.8 %all-to-all-start.3 = ((bf16[128,16,256]{2,1,0:T(8,128)(2,1)}), bf16[128,16,256]{2,1,0:T(8,128)(2,1)S(1)}, u32[]{:S(2)}, u32[]{:S(2)}) async-start(bf16[128,16,256]{2,1,0:T(8,128)(2,1)} %bitcast.19), calls=%async_computation.3 | async-start | bytes 2097152 | tf_op jit(solution)/shard_map/all_to_all | solution.py:451
  77.4 0.8 dynamic-update-slice
  78.2 11.0 %all-reduce = s32[8]{0:T(128)S(1)} all-reduce(s32[8]{0:T(128)S(1)} %dynamic-update-slice), channel_id=3, replica_groups=mesh['facet'=16,'sub'=8] {'sub'}, use_global_device_ids=true, to_apply=%add | all-reduce | flops 8 | bytes 64
  90.5 5.6 %all-to-all-done.3.adj0_ref = bf16[128,16,256]{2,1,0:T(8,128)(2,1)S(1)} async-done(((bf16[128,16,256]{2,1,0:T(8,128)(2,1)}), bf16[128,16,256]{2,1,0:T(8,128)(2,1)S(1)}, u32[]{:S(2)}, u32[]{:S(2)}) %all-to-all-start.3) | async-done | bytes 1048608 | tf_op jit(solution)/shard_map/all_to_all | solution.py:451
  96.1 1.0 copy-done
  97.1 4.3 %gram.1 = bf16[16,32,128]{2,1,0:T(8,128)(2,1)} custom-call(f32[2]{0:T(128)} %step_ref.3, s32[8]{0:T(128)} %reduce.starts_ref, s32[1]{0:T(128)S(6)} %copy.18.column_ref, s32[2,16]{1,0:T(2,128)} %offsets_ref.5, bf16[16,8,16,256]{3,2,1,0:T(8,128)(2,1)} %bitcast.17, bf16[16,32,128]{2,1,0:T(8,128)(2,1)} %section.1.first_ref), custom_call_target="tpu_custom_call" | custom-call | tf_op jit(solution)/shard_map/gram/pallas_call | solution.py:379
  101.4 4.1 %all-to-all-start.4 = ((bf16[16,32,128]{2,1,0:T(8,128)(2,1)}), bf16[16,32,128]{2,1,0:T(8,128)(2,1)S(1)}, u32[]{:S(2)}, u32[]{:S(2)}) async-start(bf16[16,32,128]{2,1,0:T(8,128)(2,1)} %gram.1), calls=%async_computation.4 | async-start | bytes 262144 | tf_op jit(solution)/shard_map/all_to_all | solution.py:446
  105.5 0.7 broadcast_add_fusion
  106.2 6.0 %all-to-all-done.4.in_ref = bf16[16,32,128]{2,1,0:T(8,128)(2,1)S(1)} async-done(((bf16[16,32,128]{2,1,0:T(8,128)(2,1)}), bf16[16,32,128]{2,1,0:T(8,128)(2,1)S(1)}, u32[]{:S(2)}, u32[]{:S(2)}) %all-to-all-start.4) | async-done | bytes 131104 | tf_op jit(solution)/shard_map/all_to_all | solution.py:446
  112.8 4.9 %grids.3 = bf16[16,32,256]{2,1,0:T(8,128)(2,1)} custom-call(bf16[16,32,128]{2,1,0:T(8,128)(2,1)} %copy-done.6, f32[16,16,128]{2,1,0:T(8,128)} %get-tuple-element.10.c_ref, f32[16,16,128]{2,1,0:T(8,128)} %get-tuple-element.11.s_ref, bf16[4096,512]{1,0:T(8,128)(2,1)} %get-tuple-element.12.table_ref), custom_call_target="tpu_custom_call" | custom-call | tf_op jit(solution)/shard_map/grids/pallas_call | solution.py:198
  117.7 3.6 %all-to-all-start.5 = ((bf16[16,32,256]{2,1,0:T(8,128)(2,1)}), bf16[16,32,256]{2,1,0:T(8,128)(2,1)S(1)}, u32[]{:S(2)}, u32[]{:S(2)}) async-start(bf16[16,32,256]{2,1,0:T(8,128)(2,1)} %grids.3), calls=%async_computation.5 | async-start | bytes 524288 | tf_op jit(solution)/shard_map/all_to_all | solution.py:446
  122.1 6.6 %all-to-all-done.5.in_ref = bf16[16,32,256]{2,1,0:T(8,128)(2,1)S(1)} async-done(((bf16[16,32,256]{2,1,0:T(8,128)(2,1)}), bf16[16,32,256]{2,1,0:T(8,128)(2,1)S(1)}, u32[]{:S(2)}, u32[]{:S(2)}) %all-to-all-start.5) | async-done | bytes 262176 | tf_op jit(solution)/shard_map/all_to_all | solution.py:446
  129.4 6.7 %visibilities.3 = (bf16[16,32,256]{2,1,0:T(8,128)(2,1)}, f32[2,4096]{1,0:T(2,128)}) custom-call(s32[1,16]{1,0:T(1,128)} %counts_ref.3, bf16[2,4096]{1,0:T(2,128)(2,1)} %bitcast.23, bf16[1,4096]{1,0:T(2,128)(2,1)} %bitcast.25, bf16[16,32,256]{2,1,0:T(8,128)(2,1)} %copy-done.2, bf16[256,4096]{1,0:T(8,128)(2,1)} %get-tuple-element.13.ku_ref, ...), custom_call_target="tpu_custom_call" | custom-call | tf_op jit(solution)/shard_map/visibilities/pallas_call | solution.py:323
  136.0 3.7 %all-to-all-start.6 = ((bf16[16,32,256]{2,1,0:T(8,128)(2,1)}), bf16[16,32,256]{2,1,0:T(8,128)(2,1)S(1)}, u32[]{:S(2)}, u32[]{:S(2)}) async-start(bf16[16,32,256]{2,1,0:T(8,128)(2,1)} %get-tuple-element.16), calls=%async_computation.6 | async-start | bytes 524288 | tf_op jit(solution)/shard_map/all_to_all | solution.py:446
  139.7 0.9 negate_select_fusion.2
  140.6 6.4 %all-to-all-done.6.in_ref = bf16[16,32,256]{2,1,0:T(8,128)(2,1)S(1)} async-done(((bf16[16,32,256]{2,1,0:T(8,128)(2,1)}), bf16[16,32,256]{2,1,0:T(8,128)(2,1)S(1)}, u32[]{:S(2)}, u32[]{:S(2)}) %all-to-all-start.6) | async-done | bytes 262176 | tf_op jit(solution)/shard_map/all_to_all | solution.py:446
  147.7 5.0 %adjoint.3 = bf16[16,8,16,256]{3,2,1,0:T(8,128)(2,1)} custom-call(bf16[16,32,256]{2,1,0:T(8,128)(2,1)} %copy-done.4, f32[16,16,128]{2,1,0:T(8,128)} %get-tuple-element.10.c_ref, f32[16,16,128]{2,1,0:T(8,128)} %get-tuple-element.11.s_ref, bf16[4096,512]{1,0:T(8,128)(2,1)} %get-tuple-element.12.table_ref), custom_call_target="tpu_custom_call" | custom-call | tf_op jit(solution)/shard_map/adjoint/pallas_call | solution.py:243
  152.7 9.4 %all-to-all-start.7 = ((bf16[128,16,256]{2,1,0:T(8,128)(2,1)}), bf16[128,16,256]{2,1,0:T(8,128)(2,1)S(1)}, u32[]{:S(2)}, u32[]{:S(2)}) async-start(bf16[128,16,256]{2,1,0:T(8,128)(2,1)} %bitcast.20), calls=%async_computation.7 | async-start | bytes 2097152 | tf_op jit(solution)/shard_map/all_to_all | solution.py:451
  162.1 7.5 %fusion.2 = (bf16[2048,512]{1,0:T(8,128)(2,1)}, bf16[2048,512]{1,0:T(8,128)(2,1)}) fusion(s32[2048]{0:T(1024)S(1)} %add.164), kind=kLoop, calls=%fused_computation.4 | loop fusion | flops 44040192 | bytes 4202496 | tf_op jit(solution)/shard_map/convert_element_type | solution.py:442
  170.2 11.2 %all-to-all-done.7.adj1_ref = bf16[128,16,256]{2,1,0:T(8,128)(2,1)S(1)} async-done(((bf16[128,16,256]{2,1,0:T(8,128)(2,1)}), bf16[128,16,256]{2,1,0:T(8,128)(2,1)S(1)}, u32[]{:S(2)}, u32[]{:S(2)}) %all-to-all-start.7) | async-done | bytes 1048608 | tf_op jit(solution)/shard_map/all_to_all | solution.py:451
  181.4 1.0 copy-done.1
  182.4 14.8 %update.1 = f32[128,8192]{1,0:T(8,128)} custom-call(f32[2]{0:T(128)} %step_ref.3, bf16[128,16,256]{2,1,0:T(8,128)(2,1)} %copy-done, bf16[128,16,256]{2,1,0:T(8,128)(2,1)} %copy-done.1, bf16[2048,512]{1,0:T(8,128)(2,1)} %get-tuple-element.27.tc_ref, bf16[2048,512]{1,0:T(8,128)(2,1)} %get-tuple-element.26.ts_ref, f32[16,2048]{1,0:T(8,128)} %get-tuple-element.25.pc_ref, ...), custom_call_target="tpu_custom_call" | custom-call | tf_op jit(solution)/shard_map/update/pallas_call | solution.py:422
  (33 shorter events, 7.4 us)
Async XLA Ops:
  1.3 33.5 %copy-start.7 = (s32[2,1,1,4096]{3,2,1,0:T(1,128)S(1)}, s32[2,1,1,4096]{3,2,1,0:T(1,128)}, u32[]{:S(2)}) copy-start(s32[2,1,1,4096]{3,2,1,0:T(1,128)} %param.15) | copy-start | bytes 98308
  6.6 16.0 %all-to-all-start = ((bf16[16,32,128]{2,1,0:T(8,128)(2,1)}), bf16[16,32,128]{2,1,0:T(8,128)(2,1)S(1)}, u32[]{:S(2)}, u32[]{:S(2)}) async-start(bf16[16,32,128]{2,1,0:T(8,128)(2,1)} %section.1.first_ref), calls=%async_computation | async-start | bytes 262144 | tf_op jit(solution)/shard_map/all_to_all | solution.py:446
  22.6 0.7 copy-start.5
  28.1 14.0 %all-to-all-start.1 = ((bf16[16,32,256]{2,1,0:T(8,128)(2,1)}), bf16[16,32,256]{2,1,0:T(8,128)(2,1)S(1)}, u32[]{:S(2)}, u32[]{:S(2)}) async-start(bf16[16,32,256]{2,1,0:T(8,128)(2,1)} %grids.2), calls=%async_computation.1 | async-start | bytes 524288 | tf_op jit(solution)/shard_map/all_to_all | solution.py:446
  42.1 0.7 copy-start.3
  49.5 27.3 %copy-start.10 = (u32[128]{0:T(128)S(1)}, u32[128]{0:T(128)}, u32[]{:S(2)}) copy-start(u32[128]{0:T(128)} %constant.16) | copy-start | bytes 1540
  49.5 40.4 %copy-start.9 = (s32[2,16]{1,0:T(2,128)S(1)}, s32[2,16]{1,0:T(2,128)}, u32[]{:S(2)}) copy-start(s32[2,16]{1,0:T(2,128)} %offsets_ref.5) | copy-start | bytes 388
  67.0 29.1 %all-to-all-start.3 = ((bf16[128,16,256]{2,1,0:T(8,128)(2,1)}), bf16[128,16,256]{2,1,0:T(8,128)(2,1)S(1)}, u32[]{:S(2)}, u32[]{:S(2)}) async-start(bf16[128,16,256]{2,1,0:T(8,128)(2,1)} %bitcast.19), calls=%async_computation.3 | async-start | bytes 2097152 | tf_op jit(solution)/shard_map/all_to_all | solution.py:451
  96.1 1.0 copy-start
  101.4 10.8 %all-to-all-start.4 = ((bf16[16,32,128]{2,1,0:T(8,128)(2,1)}), bf16[16,32,128]{2,1,0:T(8,128)(2,1)S(1)}, u32[]{:S(2)}, u32[]{:S(2)}) async-start(bf16[16,32,128]{2,1,0:T(8,128)(2,1)} %gram.1), calls=%async_computation.4 | async-start | bytes 262144 | tf_op jit(solution)/shard_map/all_to_all | solution.py:446
  112.2 0.7 copy-start.6
  117.7 11.0 %all-to-all-start.5 = ((bf16[16,32,256]{2,1,0:T(8,128)(2,1)}), bf16[16,32,256]{2,1,0:T(8,128)(2,1)S(1)}, u32[]{:S(2)}, u32[]{:S(2)}) async-start(bf16[16,32,256]{2,1,0:T(8,128)(2,1)} %grids.3), calls=%async_computation.5 | async-start | bytes 524288 | tf_op jit(solution)/shard_map/all_to_all | solution.py:446
  128.7 0.7 copy-start.2
  136.0 11.0 %all-to-all-start.6 = ((bf16[16,32,256]{2,1,0:T(8,128)(2,1)}), bf16[16,32,256]{2,1,0:T(8,128)(2,1)S(1)}, u32[]{:S(2)}, u32[]{:S(2)}) async-start(bf16[16,32,256]{2,1,0:T(8,128)(2,1)} %get-tuple-element.16), calls=%async_computation.6 | async-start | bytes 524288 | tf_op jit(solution)/shard_map/all_to_all | solution.py:446
  147.0 0.7 copy-start.4
  152.7 16.8 %copy-start.8 = (f32[2,4096]{1,0:T(2,128)S(1)}, f32[2,4096]{1,0:T(2,128)}, u32[]{:S(2)}) copy-start(f32[2,4096]{1,0:T(2,128)} %get-tuple-element.17) | copy-start | bytes 98308
  152.7 28.6 %all-to-all-start.7 = ((bf16[128,16,256]{2,1,0:T(8,128)(2,1)}), bf16[128,16,256]{2,1,0:T(8,128)(2,1)S(1)}, u32[]{:S(2)}, u32[]{:S(2)}) async-start(bf16[128,16,256]{2,1,0:T(8,128)(2,1)} %bitcast.20), calls=%async_computation.7 | async-start | bytes 2097152 | tf_op jit(solution)/shard_map/all_to_all | solution.py:451
  181.4 1.0 copy-start.1

commit v3 on v2

v3 whole, which is shorter than its diff:
```python
import math

import jax
import jax.numpy as jnp
from jax import lax
from jax.experimental import pallas as pl
from jax.experimental.pallas import tpu as pltpu
from jax.sharding import PartitionSpec as P

NIMG = 65536
FW = 8192
FROWS = 128
SGW = 256
VCAP = 4096
OS = 8
KSUP = 4
FACETS = 16
NCOL = 8
NROWSG = 16
SLICE = SGW // FACETS
COLUMNS = NCOL * SGW

STEP1 = 256
HIGH1 = FW // STEP1
PARTS1 = 2
STEP5 = 512
HIGH5 = FW // STEP5
PAIR5 = 2
VBLOCK = 1024
CHUNK = 4
UNROLL4 = 2

BF = jnp.bfloat16
F32 = jnp.float32
I32 = jnp.int32
NORM = 1.0 / math.sqrt(FACETS * FROWS * FW)
PARAMS = pltpu.CompilerParams(vmem_limit_bytes=16 << 20)
WIDE_PARAMS = pltpu.CompilerParams(vmem_limit_bytes=24 << 20)
SMEM_SPEC = pl.BlockSpec(memory_space=pltpu.SMEM)
VMEM_SPEC = pl.BlockSpec(memory_space=pltpu.VMEM)
HBM_SPEC = pl.BlockSpec(memory_space=pltpu.HBM)


def cos_sin(index, bits=16):
    quadrant = (index + (1 << (bits - 3))) >> (bits - 2)
    angle = (index - (quadrant << (bits - 2))).astype(F32) * (2.0 * math.pi / (1 << bits))
    square = angle * angle
    sine = angle * (1.0 + square * (-1.0 / 6 + square * (1.0 / 120 + square * (-1.0 / 5040 + square / 362880))))
    cosine = 1.0 + square * (-0.5 + square * (1.0 / 24 + square * (-1.0 / 720 + square / 40320)))
    swapped = (quadrant & 1) != 0
    c = jnp.where(swapped, sine, cosine)
    s = jnp.where(swapped, cosine, sine)
    c = jnp.where(((quadrant + 1) & 2) != 0, -c, c)
    s = jnp.where((quadrant & 2) != 0, -s, s)
    return c, s


def phase(frequency, pixel):
    return cos_sin((frequency * pixel) & (NIMG - 1))


def on_chip(value):
    return pltpu.with_memory_space_constraint(value, pltpu.VMEM)


def off_chip(value):
    return pltpu.with_memory_space_constraint(value, pltpu.HBM)


def write_out(pairs):
    copies = [pltpu.make_async_copy(source, target, sem) for source, target, sem in pairs]
    for copy in copies:
        copy.start()
    for copy in copies:
        copy.wait()


def iota(shape, dim):
    return lax.broadcasted_iota(I32, shape, dim)


def column_of(ref, count, lanes):
    row = iota((count, lanes), 0)
    value = jnp.zeros((count, lanes), I32)
    for i in range(count):
        value = jnp.where(row == i, ref[i], value)
    return value


def section_kernel(column_ref, offsets_ref, model_ref, out_hbm, table_ref, pc_ref, ps_ref, re_ref, im_ref, out_ref, sem):
    part = pl.program_id(0)
    highs = HIGH1 // PARTS1

    @pl.when(part == 0)
    def _():
        column_start = column_ref[0]
        pixel_start = offsets_ref[1, lax.axis_index("facet")]
        freq = column_start + iota((STEP1, SGW), 1)
        c, s = phase(freq, iota((STEP1, SGW), 0))
        table_ref[:, :SGW] = c.astype(BF)
        table_ref[:, SGW:] = (-s).astype(BF)
        freq = column_start + iota((HIGH1, SGW), 1)
        c, s = phase(freq, pixel_start + STEP1 * iota((HIGH1, SGW), 0))
        pc_ref[...] = c
        ps_ref[...] = s
        re_ref[...] = jnp.zeros((FROWS, SGW), F32)
        im_ref[...] = jnp.zeros((FROWS, SGW), F32)

    acc_re = re_ref[...]
    acc_im = im_ref[...]
    for high in range(highs):
        block = model_ref[:, high * STEP1 : (high + 1) * STEP1].astype(BF)
        product = jnp.dot(block, table_ref[...], preferred_element_type=F32)
        re = product[:, :SGW]
        im = product[:, SGW:]
        pc = pc_ref[pl.ds(part * highs + high, 1), :]
        ps = ps_ref[pl.ds(part * highs + high, 1), :]
        acc_re = acc_re + (re * pc + im * ps)
        acc_im = acc_im + (im * pc - re * ps)
    re_ref[...] = acc_re
    im_ref[...] = acc_im

    @pl.when(part == PARTS1 - 1)
    def _():
        re = re_ref[...].T.astype(BF)
        im = im_ref[...].T.astype(BF)
        out_ref[:, :SLICE, :] = re.reshape(FACETS, SLICE, FROWS)
        out_ref[:, SLICE:, :] = im.reshape(FACETS, SLICE, FROWS)
        write_out([(out_ref, out_hbm, sem)])


def section(column_start, offsets, model):
    return pl.pallas_call(
        section_kernel,
        grid=(PARTS1,),
        out_shape=jax.ShapeDtypeStruct((FACETS, 2 * SLICE, FROWS), BF),
        in_specs=[SMEM_SPEC, SMEM_SPEC, pl.BlockSpec((FROWS, FW // PARTS1), lambda i: (0, i))],
        out_specs=HBM_SPEC,
        scratch_shapes=[
            pltpu.VMEM((STEP1, 2 * SGW), BF),
            pltpu.VMEM((HIGH1, SGW), F32),
            pltpu.VMEM((HIGH1, SGW), F32),
            pltpu.VMEM((FROWS, SGW), F32),
            pltpu.VMEM((FROWS, SGW), F32),
            pltpu.VMEM((FACETS, 2 * SLICE, FROWS), BF),
            pltpu.SemaphoreType.DMA,
        ],
        compiler_params=PARAMS,
        name="section",
    )(column_start, offsets, off_chip(model))


def row_table_kernel(offsets_ref, rows_ref, table_ref, c_ref, s_ref, base_ref, turn_ref):
    c, s = phase(iota((FROWS, SGW), 1), iota((FROWS, SGW), 0))
    base_ref[0] = c
    base_ref[1] = s
    row = iota((FACETS, SGW), 0)
    start = jnp.zeros((FACETS, SGW), I32)
    for f in range(FACETS):
        start = jnp.where(row == f, offsets_ref[0, f], start)
    c, s = phase(iota((FACETS, SGW), 1), start)
    turn_ref[0] = c
    turn_ref[1] = s
    row = iota((NROWSG, FROWS), 0)
    freq = jnp.zeros((NROWSG, FROWS), I32)
    for r in range(NROWSG):
        freq = jnp.where(row == r, rows_ref[0, r], freq)

    def one(f, carry):
        cf = turn_ref[0, pl.ds(f, 1), :]
        sf = turn_ref[1, pl.ds(f, 1), :]
        c = (base_ref[0] * cf - base_ref[1] * sf).astype(BF)
        s = (base_ref[1] * cf + base_ref[0] * sf).astype(BF)
        top = pl.ds(pl.multiple_of(f * 2 * FROWS, 2 * FROWS), FROWS)
        low = pl.ds(pl.multiple_of(f * 2 * FROWS + FROWS, FROWS), FROWS)
        table_ref[top, :SGW] = c
        table_ref[top, SGW:] = -s
        table_ref[low, :SGW] = s
        table_ref[low, SGW:] = c
        c, s = phase(freq, offsets_ref[0, f] + iota((NROWSG, FROWS), 1))
        c_ref[f] = c
        s_ref[f] = s
        return carry

    lax.fori_loop(0, FACETS, one, 0)


def row_tables(offsets, rows):
    return pl.pallas_call(
        row_table_kernel,
        out_shape=(
            pltpu.VMEM((FACETS * 2 * FROWS, 2 * SGW), BF),
            pltpu.VMEM((FACETS, NROWSG, FROWS), F32),
            pltpu.VMEM((FACETS, NROWSG, FROWS), F32),
        ),
        in_specs=[SMEM_SPEC, SMEM_SPEC],
        out_specs=(VMEM_SPEC, VMEM_SPEC, VMEM_SPEC),
        scratch_shapes=[
            pltpu.VMEM((2, FROWS, SGW), F32),
            pltpu.VMEM((2, FACETS, SGW), F32),
        ],
        compiler_params=PARAMS,
        name="row_tables",
    )(offsets, rows)


def grid_kernel(in_ref, c_ref, s_ref, table_ref, out_hbm, turned_ref, out_ref, sem):
    for f in range(FACETS):
        re = in_ref[f, :SLICE, :].astype(F32)
        im = in_ref[f, SLICE:, :].astype(F32)
        left = f * 2 * FROWS
        for r in range(NROWSG):
            c = c_ref[f, r : r + 1, :]
            s = s_ref[f, r : r + 1, :]
            lines = slice(r * SLICE, (r + 1) * SLICE)
            turned_ref[lines, left : left + FROWS] = (re * c + im * s).astype(BF)
            turned_ref[lines, left + FROWS : left + 2 * FROWS] = (im * c - re * s).astype(BF)
    product = jnp.dot(turned_ref[...], table_ref[...], preferred_element_type=F32)
    total = (NORM * product).astype(BF)
    out_ref[:, :SLICE, :] = total[:, :SGW].reshape(NROWSG, SLICE, SGW)
    out_ref[:, SLICE:, :] = total[:, SGW:].reshape(NROWSG, SLICE, SGW)
    write_out([(out_ref, out_hbm, sem)])


def grids(sections, tables):
    table, c, s = tables
    return pl.pallas_call(
        grid_kernel,
        out_shape=jax.ShapeDtypeStruct((NROWSG, 2 * SLICE, SGW), BF),
        in_specs=[VMEM_SPEC] * 4,
        out_specs=HBM_SPEC,
        scratch_shapes=[
            pltpu.VMEM((NROWSG * SLICE, FACETS * 2 * FROWS), BF),
            pltpu.VMEM((NROWSG, 2 * SLICE, SGW), BF),
            pltpu.SemaphoreType.DMA,
        ],
        compiler_params=PARAMS,
        name="grids",
    )(on_chip(sections), on_chip(c), on_chip(s), on_chip(table))


def adjoint_kernel(in_ref, c_ref, s_ref, table_ref, out_hbm, lines_ref, out_ref, sems):
    lines_ref[:, :SGW] = in_ref[:, :SLICE, :].reshape(NROWSG * SLICE, SGW)
    lines_ref[:, SGW:] = in_ref[:, SLICE:, :].reshape(NROWSG * SLICE, SGW)

    def one(f, carry):
        table = table_ref[pl.ds(pl.multiple_of(f * 2 * FROWS, 2 * FROWS), 2 * FROWS), :]
        product = lax.dot_general(
            lines_ref[...], table, (((1,), (1,)), ((), ())), preferred_element_type=F32
        )
        acc_re = jnp.zeros((SLICE, FROWS), F32)
        acc_im = jnp.zeros((SLICE, FROWS), F32)
        for r in range(NROWSG):
            re = product[r * SLICE : (r + 1) * SLICE, :FROWS]
            im = product[r * SLICE : (r + 1) * SLICE, FROWS:]
            c = c_ref[f, r : r + 1, :]
            s = s_ref[f, r : r + 1, :]
            acc_re = acc_re + (re * c - im * s)
            acc_im = acc_im + (im * c + re * s)
        out_ref[f] = jnp.concatenate([acc_re, acc_im], axis=1).astype(BF)
        return carry

    lax.fori_loop(0, FACETS, one, 0, unroll=UNROLL4)
    write_out([(out_ref, out_hbm.at[:, copy], sems.at[copy]) for copy in range(NCOL)])


def adjoint(gridded, tables):
    table, c, s = tables
    return pl.pallas_call(
        adjoint_kernel,
        out_shape=jax.ShapeDtypeStruct((FACETS, NCOL, SLICE, 2 * FROWS), BF),
        in_specs=[VMEM_SPEC] * 4,
        out_specs=HBM_SPEC,
        scratch_shapes=[
            pltpu.VMEM((NROWSG * SLICE, 2 * SGW), BF),
            pltpu.VMEM((FACETS, SLICE, 2 * FROWS), BF),
            pltpu.SemaphoreType.DMA((NCOL,)),
        ],
        compiler_params=PARAMS,
        name="adjoint",
    )(on_chip(gridded), on_chip(c), on_chip(s), on_chip(table))


def kernel_columns(position):
    cells = iota((SGW, position.shape[1]), 0) * OS + OS // 2
    offset = cells - position
    distance = offset.astype(F32) * (1.0 / OS)
    inside = jnp.abs(offset) <= KSUP * OS
    return jnp.where(inside, jnp.exp(-0.5 * distance * distance), 0.0).astype(BF)


def vis_table_kernel(uv_ref, ku_ref, kv_ref):
    def one(part, carry):
        cut = pl.ds(pl.multiple_of(part * 256, 256), 256)
        ku_ref[:, cut] = kernel_columns(uv_ref[0:1, cut])
        kv_ref[:, cut] = kernel_columns(uv_ref[1:2, cut])
        return carry

    lax.fori_loop(0, VCAP // 256, one, 0)


def vis_tables(uv):
    shape = pltpu.VMEM((SGW, VCAP), BF)
    return pl.pallas_call(
        vis_table_kernel,
        out_shape=(shape, shape),
        in_specs=[VMEM_SPEC],
        out_specs=(VMEM_SPEC, VMEM_SPEC),
        compiler_params=PARAMS,
        name="vis_tables",
    )(uv)


def visibility_kernel(counts_ref, obs_ref, weight_ref, in_ref, ku_ref, kv_ref, gridded_hbm, res_ref, acc_ref, gridded_ref, sem):
    count = counts_ref[0, lax.axis_index("facet")]
    grid = [in_ref[:, half * SLICE : (half + 1) * SLICE, :].reshape(SGW, SGW) for half in range(2)]
    for part in range(VCAP // VBLOCK):
        cut = slice(part * VBLOCK, (part + 1) * VBLOCK)
        live = part * VBLOCK + iota((1, VBLOCK), 1) < count
        weight = weight_ref[:, cut].astype(F32)
        for half in range(2):
            sampled = jnp.dot(grid[half], ku_ref[:, cut], preferred_element_type=F32)
            predicted = jnp.sum(sampled * kv_ref[:, cut].astype(F32), axis=0, keepdims=True)
            observed = obs_ref[half : half + 1, cut].astype(F32)
            residual = jnp.where(live, weight * (observed - predicted), 0.0)
            res_ref[half : half + 1, cut] = residual
            weighted = (residual * kv_ref[:, cut].astype(F32)).astype(BF)
            total = lax.dot_general(
                weighted, ku_ref[:, cut], (((1,), (1,)), ((), ())), preferred_element_type=F32
            )
            if part:
                total = total + acc_ref[half]
            if part + 1 < VCAP // VBLOCK:
                acc_ref[half] = total
            else:
                lines = total.astype(BF).reshape(FACETS, SLICE, SGW)
                gridded_ref[:, half * SLICE : (half + 1) * SLICE, :] = lines
    write_out([(gridded_ref, gridded_hbm, sem)])


def visibilities(counts, obs, weight, grid, tables):
    return pl.pallas_call(
        visibility_kernel,
        out_shape=(
            jax.ShapeDtypeStruct((FACETS, 2 * SLICE, SGW), BF),
            jax.ShapeDtypeStruct((2, VCAP), F32),
        ),
        in_specs=[SMEM_SPEC] + [VMEM_SPEC] * 5,
        out_specs=(HBM_SPEC, VMEM_SPEC),
        scratch_shapes=[
            pltpu.VMEM((2, SGW, SGW), F32),
            pltpu.VMEM((FACETS, 2 * SLICE, SGW), BF),
            pltpu.SemaphoreType.DMA,
        ],
        compiler_params=PARAMS,
        name="visibilities",
    )(counts, obs, weight, on_chip(grid), *map(on_chip, tables))


def dirichlet(distance, pixel_start):
    distance = ((distance & (NIMG - 1)) ^ (NIMG // 2)) - NIMG // 2
    top = cos_sin((distance * (NIMG // (NIMG // FW * 2))) & (NIMG - 1))[1]
    bottom = cos_sin(distance, 17)[1]
    ratio = jnp.where(distance == 0, float(FW), top / jnp.where(distance == 0, 1.0, bottom))
    c, s = cos_sin((distance * (2 * pixel_start + FW - 1)) & (2 * NIMG - 1), 17)
    return c * ratio, s * ratio


def gram_kernel(step_ref, starts_ref, column_ref, offsets_ref, adj_ref, first_ref, out_hbm, flip_ref, v_ref, out_ref, sem):
    wide = 2 * SGW
    pixel_start = offsets_ref[1, lax.axis_index("facet")]
    own = column_ref[0]
    row = iota((NCOL, wide), 0)
    starts = jnp.zeros((NCOL, wide), I32)
    for c in range(NCOL):
        starts = jnp.where(row == c, starts_ref[c], starts)
    lane = iota((NCOL, wide), 1)
    v_ref[0], v_ref[1] = dirichlet(starts - own + (lane - (SGW - 1)), pixel_start)
    v_ref[2], v_ref[3] = dirichlet(starts + own + (2 * (SGW - 1) - lane), pixel_start)
    anti = (iota((SGW, SGW), 0) + iota((SGW, SGW), 1)) == SGW - 1
    flip_ref[...] = jnp.where(anti, 1.0, 0.0).astype(BF)
    totals = [None] * 4
    for c in range(NCOL):
        lines = adj_ref[:, c].reshape(SGW, 2 * FROWS)
        turned = jnp.dot(flip_ref[...], lines, preferred_element_type=F32).astype(BF)
        for k in range(4):
            spread = jnp.broadcast_to(v_ref[k, c : c + 1, :], (SGW, wide))
            band = pltpu.roll(spread, SGW + 1, 1, stride=1, stride_axis=0)[:, :SGW].astype(BF)
            term = jnp.dot(band, lines if k < 2 else turned, preferred_element_type=F32)
            totals[k] = term if c == 0 else totals[k] + term
    scale = step_ref[0] * (0.5 * NORM)
    p1, p2, p3, p4 = totals
    re = p1[:, :FROWS] - p2[:, FROWS:] + p3[:, :FROWS] - p4[:, FROWS:]
    im = p2[:, :FROWS] + p1[:, FROWS:] - p4[:, :FROWS] - p3[:, FROWS:]
    first = first_ref[...].astype(F32)
    out_ref[:, :SLICE, :] = (first[:, :SLICE] + (scale * re).reshape(FACETS, SLICE, FROWS)).astype(BF)
    out_ref[:, SLICE:, :] = (first[:, SLICE:] + (scale * im).reshape(FACETS, SLICE, FROWS)).astype(BF)
    write_out([(out_ref, out_hbm, sem)])


def gram(steps, column_starts, column_start, offsets, adj, first):
    return pl.pallas_call(
        gram_kernel,
        out_shape=jax.ShapeDtypeStruct((FACETS, 2 * SLICE, FROWS), BF),
        in_specs=[SMEM_SPEC] * 4 + [VMEM_SPEC] * 2,
        out_specs=HBM_SPEC,
        scratch_shapes=[
            pltpu.VMEM((SGW, SGW), BF),
            pltpu.VMEM((4, NCOL, 2 * SGW), F32),
            pltpu.VMEM((FACETS, 2 * SLICE, FROWS), BF),
            pltpu.SemaphoreType.DMA,
        ],
        compiler_params=PARAMS,
        name="gram",
    )(steps, column_starts, column_start, offsets, on_chip(adj.reshape(FACETS, NCOL, SLICE, 2 * FROWS)), first)


def update_kernel(step_ref, adj0_ref, adj1_ref, table_ref, pc_ref, ps_ref, model_ref, out_ref, both_ref, even_ref, odd_ref):
    part = pl.program_id(0)

    def turn(pair, target_ref):
        re = both_ref[:FROWS, :]
        im = both_ref[FROWS:, :]
        for p in range(PAIR5):
            pc = pc_ref[pl.ds(pair * PAIR5 + p, 1), :]
            ps = ps_ref[pl.ds(pair * PAIR5 + p, 1), :]
            lines = slice(p * FROWS, (p + 1) * FROWS)
            target_ref[lines, :COLUMNS] = (re * pc - im * ps).astype(BF)
            target_ref[lines, COLUMNS:] = (im * pc + re * ps).astype(BF)

    def add(place, source_ref):
        gradient = jnp.dot(source_ref[...], table_ref[...], preferred_element_type=F32)
        for p in range(PAIR5):
            left = (place * PAIR5 + p) * STEP5
            lines = gradient[p * FROWS : (p + 1) * FROWS]
            out_ref[:, left : left + STEP5] = model_ref[:, left : left + STEP5] + lines

    @pl.when(part == 0)
    def _():
        first = step_ref[0] * NORM
        second = step_ref[1] * NORM
        for j in range(FACETS):
            lines0 = adj0_ref[j * NCOL : (j + 1) * NCOL].reshape(NCOL * SLICE, 2 * FROWS).astype(F32)
            lines1 = adj1_ref[j * NCOL : (j + 1) * NCOL].reshape(NCOL * SLICE, 2 * FROWS).astype(F32)
            both = first * lines0 + second * lines1
            both_ref[:, j * NCOL * SLICE : (j + 1) * NCOL * SLICE] = both.T
        turn(0, even_ref)

    turn(2 * part + 1, odd_ref)
    add(0, even_ref)
    turn(jnp.minimum(2 * part + 2, HIGH5 // PAIR5 - 2), even_ref)
    add(1, odd_ref)


def update(steps, adj0, adj1, tables, model):
    wide = pl.BlockSpec((FROWS, 2 * PAIR5 * STEP5), lambda i: (0, i))
    return pl.pallas_call(
        update_kernel,
        grid=(HIGH5 // PAIR5 // 2,),
        out_shape=jax.ShapeDtypeStruct((FROWS, FW), F32),
        in_specs=[SMEM_SPEC] + [VMEM_SPEC] * 5 + [wide],
        out_specs=wide,
        scratch_shapes=[
            pltpu.VMEM((2 * FROWS, COLUMNS), F32),
            pltpu.VMEM((PAIR5 * FROWS, 2 * COLUMNS), BF),
            pltpu.VMEM((PAIR5 * FROWS, 2 * COLUMNS), BF),
        ],
        compiler_params=WIDE_PARAMS,
        name="update",
    )(steps, on_chip(adj0), on_chip(adj1), *map(on_chip, tables), off_chip(model))


def update_table_kernel(starts_ref, offsets_ref, table_ref, pc_ref, ps_ref, base_ref, turn_ref):
    group = NCOL * SLICE
    line = iota((group, STEP5), 0)
    freq = line & (SLICE - 1)
    for c in range(NCOL):
        freq = freq + jnp.where((line >> 4) == c, starts_ref[c], 0)
    base_ref[0], base_ref[1] = phase(freq, iota((group, STEP5), 1))
    turn_ref[0], turn_ref[1] = phase(SLICE * iota((FACETS, STEP5), 0), iota((FACETS, STEP5), 1))

    def one(j, carry):
        c = turn_ref[0, pl.ds(j, 1), :]
        s = turn_ref[1, pl.ds(j, 1), :]
        cut = pl.ds(pl.multiple_of(j * group, group), group)
        table_ref[cut, :] = (base_ref[0] * c - base_ref[1] * s).astype(BF)
        cut = pl.ds(pl.multiple_of(COLUMNS + j * group, group), group)
        table_ref[cut, :] = (-(base_ref[1] * c + base_ref[0] * s)).astype(BF)
        return carry

    lax.fori_loop(0, FACETS, one, 0)
    lane = iota((HIGH5, COLUMNS), 1)
    freq = SLICE * (lane >> 7) + (lane & (SLICE - 1))
    for c in range(NCOL):
        freq = freq + jnp.where(((lane >> 4) & (NCOL - 1)) == c, starts_ref[c], 0)
    pixel_start = offsets_ref[1, lax.axis_index("facet")]
    pc_ref[...], ps_ref[...] = phase(freq, pixel_start + STEP5 * iota((HIGH5, COLUMNS), 0))


def update_tables(column_starts, offsets):
    return pl.pallas_call(
        update_table_kernel,
        out_shape=(
            pltpu.VMEM((2 * COLUMNS, STEP5), BF),
            pltpu.VMEM((HIGH5, COLUMNS), F32),
            pltpu.VMEM((HIGH5, COLUMNS), F32),
        ),
        in_specs=[SMEM_SPEC, SMEM_SPEC],
        out_specs=(VMEM_SPEC, VMEM_SPEC, VMEM_SPEC),
        scratch_shapes=[
            pltpu.VMEM((2, NCOL * SLICE, STEP5), F32),
            pltpu.VMEM((2, FACETS, STEP5), F32),
        ],
        compiler_params=PARAMS,
        name="update_tables",
    )(column_starts, offsets)


def exchange(value):
    return lax.all_to_all(value, "facet", split_axis=0, concat_axis=0, tiled=True)


def to_facets(value):
    copies = value.reshape(FACETS * NCOL, *value.shape[2:])
    return lax.all_to_all(copies, ("facet", "sub"), split_axis=0, concat_axis=0, tiled=True)


def local(
    model_image,
    step_sizes,
    facet_offsets,
    col_offsets,
    row_offsets,
    counts,
    vis_uv,
    vis_obs,
    vis_weight,
):
    lines = lax.optimization_barrier(jnp.broadcast_to(col_offsets[:, None], (8, 128)))
    column_starts = lax.optimization_barrier(lax.all_gather(lines, "sub", axis=0, tiled=True))[::8, 0]
    uv = vis_uv.reshape(2, VCAP)
    obs = vis_obs.reshape(2, VCAP)
    weight = vis_weight.reshape(1, VCAP)
    model = model_image[0]
    first = section(col_offsets, facet_offsets, model)
    rows = row_tables(facet_offsets, row_offsets)
    kernels = vis_tables(uv)
    grid = exchange(grids(exchange(first), rows))
    gridded, residual = visibilities(counts, obs, weight, grid, kernels)
    adj0 = to_facets(adjoint(exchange(gridded), rows))
    tables = update_tables(column_starts, facet_offsets)
    second = gram(step_sizes, column_starts, col_offsets, facet_offsets, adj0, first)
    grid = exchange(grids(exchange(second), rows))
    gridded, residual = visibilities(counts, obs, weight, grid, kernels)
    adj1 = to_facets(adjoint(exchange(gridded), rows))
    model = update(step_sizes, adj0, adj1, tables, model)
    return model[None], residual.reshape(2, 1, 1, VCAP)


def solution(mesh):
    in_specs = (
        P("facet", None, None),
        P(),
        P(),
        P("sub"),
        P("sub", None),
        P("sub", None),
        P(None, "sub", "facet", None),
        P(None, "sub", "facet", None),
        P("sub", "facet", None),
    )
    out_specs = (P("facet", None, None), P(None, "sub", "facet", None))
    return jax.shard_map(local, mesh=mesh, in_specs=in_specs, out_specs=out_specs, check_vma=False)
```

time: 199 us -> 183 us (0.920)
  blocking collectives: 23.4 us -> 62.9 us
  Pallas kernels: 70.9 us -> 45.9 us
  waiting for transfers between devices: 37.4 us -> 23.2 us
  starting transfers between devices: 44.7 us -> 30.7 us
  other arithmetic: 10.4 us -> 0.12 us
  local copies, waits for them, and re-layouts: 8.81 us -> 17.6 us
    all_to_all x1 -> x4, blocking collectives: 12.4 us -> 47.6 us  [exchange(): lax.all_to_all(value, 'facet', split_axis=0, concat_axis=0, tiled=True)]
    pallas_call x9 -> x10, Pallas kernels: 61.3 us -> 37.8 us  [the longest x1 12.6 us: update(): pl.pallas_call(update_kernel, grid=(HIGH5 // PAIR5 // 2,), out_shape=jax....]
    all_gather x0 -> x1, blocking collectives: none -> 15.4 us  [local(): lax.all_gather(lines, 'sub', axis=0, tiled=True)]
    all_to_all x5 -> x2, waiting for transfers between devices: 20.6 us -> 5.38 us  [exchange(): lax.all_to_all(value, 'facet', split_axis=0, concat_axis=0, tiled=True)]
    all_to_all x5 -> x2, starting transfers between devices: 25.6 us -> 11.2 us  [exchange(): lax.all_to_all(value, 'facet', split_axis=0, concat_axis=0, tiled=True)]
    unnamed x1 -> x0, blocking collectives: 11 us -> none
    unnamed x28 -> x40, local copies, waits for them, and re-layouts: 8.14 us -> 17.6 us
    convert_element_type x1 -> x0, other arithmetic: 7.45 us -> none  [update_tables(): return (c.astype(BF), (-s).astype(BF), pc, ps)]
  transfers between devices with their start and end apart: 7 -> 4, of which waited for: 6 -> 4; matrix products, arithmetic and copies ran while one was open for 7% -> 0% of each run, Pallas kernels for 7% -> 4%
where the time goes in v3:
time: 183 us; the launch traced here: 182 us
  blocking collectives  62.9 us (34%)
  Pallas kernels  45.9 us (25%)
  starting transfers between devices  30.7 us (17%)
  waiting for transfers between devices  23.2 us (13%)
  local copies, waits for them, and re-layouts  17.6 us (10%)
    all_to_all x4, blocking collectives, exchange(): lax.all_to_all(value, 'facet', split_axis=0, concat_axis=0, tiled=True)  47.6 us
    all_to_all x2, starting transfers between devices, to_facets(): lax.all_to_all(copies, ('facet', 'sub'), split_axis=0, concat_axis=0, til...  19.5 us
    all_to_all x2, waiting for transfers between devices, to_facets(): lax.all_to_all(copies, ('facet', 'sub'), split_axis=0, concat_axis=0, til...  17.8 us
    unnamed x40, local copies, waits for them, and re-layouts  17.6 us
    all_gather x1, blocking collectives, local(): lax.all_gather(lines, 'sub', axis=0, tiled=True)  15.4 us
    pallas_call x1, Pallas kernels, update(): pl.pallas_call(update_kernel, grid=(HIGH5 // PAIR5 // 2,), out_shape=jax....  12.6 us
    all_to_all x2, starting transfers between devices, exchange(): lax.all_to_all(value, 'facet', split_axis=0, concat_axis=0, tiled=True)  11.2 us
    pallas_call x2, Pallas kernels, visibilities(): pl.pallas_call(visibility_kernel, out_shape=(jax.ShapeDtypeStruct((FACETS...  7.19 us
  transfers between devices with their start and end apart: 4, of which 4 were waited for; matrix products, arithmetic and copies ran while one was open for 0% of the time, Pallas kernels for 4%

profile of v3, /device:TPU:1, one launch (start us, length us, event | category | flops | bytes accessed | tf_op | source)
XLA Modules:
  0.0 182.0 jit_solution(3920613985312284361)
XLA Ops:
  2.0 4.6 %section.1.first_ref = bf16[16,32,128]{2,1,0:T(8,128)(2,1)} custom-call(s32[1]{0:T(128)} %copy.17.column_ref, s32[2,16]{1,0:T(2,128)S(1)} %copy-done.13, f32[128,8192]{1,0:T(8,128)} %bitcast.21), custom_call_target="tpu_custom_call" | custom-call | tf_op jit(solution)/shard_map/section/pallas_call | solution.py:133
  6.6 7.6 %all-to-all-start = ((bf16[16,32,128]{2,1,0:T(8,128)(2,1)}), bf16[16,32,128]{2,1,0:T(8,128)(2,1)S(1)}, u32[]{:S(2)}, u32[]{:S(2)}) async-start(bf16[16,32,128]{2,1,0:T(8,128)(2,1)} %section.1.first_ref), calls=%async_computation | async-start | bytes 262144 | tf_op jit(solution)/shard_map/all_to_all | solution.py:520
  14.3 1.8 row_tables.1
  16.1 2.0 %copy-done = bf16[4096,512]{1,0:T(8,128)(2,1)} copy-done((bf16[4096,512]{1,0:T(8,128)(2,1)}, bf16[4096,512]{1,0:T(8,128)(2,1)S(1)}, u32[]{:S(2)}) %copy-start) | copy-done | bytes 4194328
  18.1 3.0 %all-to-all-done.in_ref = bf16[16,32,128]{2,1,0:T(8,128)(2,1)S(1)} async-done(((bf16[16,32,128]{2,1,0:T(8,128)(2,1)}), bf16[16,32,128]{2,1,0:T(8,128)(2,1)S(1)}, u32[]{:S(2)}, u32[]{:S(2)}) %all-to-all-start) | async-done | bytes 131104 | tf_op jit(solution)/shard_map/all_to_all | solution.py:520
  21.1 2.2 %copy-done.1 = bf16[4096,512]{1,0:T(8,128)(2,1)S(1)} copy-done((bf16[4096,512]{1,0:T(8,128)(2,1)S(1)}, bf16[4096,512]{1,0:T(8,128)(2,1)}, u32[]{:S(2)}) %copy-start.1) | copy-done | bytes 4194328
  23.3 2.0 %grids.2 = bf16[16,32,256]{2,1,0:T(8,128)(2,1)} custom-call(bf16[16,32,128]{2,1,0:T(8,128)(2,1)S(1)} %all-to-all-done.in_ref, f32[16,16,128]{2,1,0:T(8,128)S(1)} %get-tuple-element.13.c_ref, f32[16,16,128]{2,1,0:T(8,128)S(1)} %get-tuple-element.14.s_ref, bf16[4096,512]{1,0:T(8,128)(2,1)S(1)} %copy-done.1), custom_call_target="tpu_custom_call" | custom-call | tf_op jit(solution)/shard_map/grids/pallas_call | solution.py:227
  25.3 3.6 %all-to-all-start.1 = ((bf16[16,32,256]{2,1,0:T(8,128)(2,1)}), bf16[16,32,256]{2,1,0:T(8,128)(2,1)S(1)}, u32[]{:S(2)}, u32[]{:S(2)}) async-start(bf16[16,32,256]{2,1,0:T(8,128)(2,1)} %grids.2), calls=%async_computation.1 | async-start | bytes 524288 | tf_op jit(solution)/shard_map/all_to_all | solution.py:520
  29.0 3.6 %vis_tables.1 = (bf16[256,4096]{1,0:T(8,128)(2,1)S(1)}, bf16[256,4096]{1,0:T(8,128)(2,1)S(1)}) custom-call(s32[2,4096]{1,0:T(2,128)S(1)} %bitcast.15), custom_call_target="tpu_custom_call" | custom-call | tf_op jit(solution)/shard_map/vis_tables/pallas_call | solution.py:304
  32.6 1.3 copy-done.5
  33.9 2.4 %all-to-all-done.1.in_ref = bf16[16,32,256]{2,1,0:T(8,128)(2,1)S(1)} async-done(((bf16[16,32,256]{2,1,0:T(8,128)(2,1)}), bf16[16,32,256]{2,1,0:T(8,128)(2,1)S(1)}, u32[]{:S(2)}, u32[]{:S(2)}) %all-to-all-start.1) | async-done | bytes 262176 | tf_op jit(solution)/shard_map/all_to_all | solution.py:520
  36.3 1.7 copy-done.6
  38.0 3.9 %visibilities.2 = (bf16[16,32,256]{2,1,0:T(8,128)(2,1)S(1)}, f32[2,4096]{1,0:T(2,128)}) custom-call(s32[1,16]{1,0:T(1,128)S(1)} %copy-done.15, bf16[2,4096]{1,0:T(2,128)(2,1)S(1)} %bitcast.16, bf16[1,4096]{1,0:T(2,128)(2,1)S(1)} %bitcast.18, bf16[16,32,256]{2,1,0:T(8,128)(2,1)S(1)} %all-to-all-done.1.in_ref, bf16[256,4096]{1,0:T(8,128)(2,1)S(1)} %get-tuple-element.16.ku_ref, ...), custom_call_target="tpu_custom_call" | custom-call | tf_op jit(solution)/shard_map/visibilities/pallas_call | solution.py:342
  41.9 11.6 %all_to_all.40.in_ref = bf16[16,32,256]{2,1,0:T(8,128)(2,1)S(1)} all-to-all(bf16[16,32,256]{2,1,0:T(8,128)(2,1)S(1)} %get-tuple-element.18), channel_id=1, replica_groups=mesh['facet'=16,'sub'=8] {'facet'}, dimensions={0} | all-to-all | bytes 524288 | tf_op jit(solution)/shard_map/all_to_all | solution.py:520
  53.5 2.9 %adjoint.2 = bf16[16,8,16,256]{3,2,1,0:T(8,128)(2,1)S(1)} custom-call(bf16[16,32,256]{2,1,0:T(8,128)(2,1)S(1)} %all_to_all.40.in_ref, f32[16,16,128]{2,1,0:T(8,128)S(1)} %get-tuple-element.13.c_ref, f32[16,16,128]{2,1,0:T(8,128)S(1)} %get-tuple-element.14.s_ref, bf16[4096,512]{1,0:T(8,128)(2,1)S(1)} %copy-done.2), custom_call_target="tpu_custom_call" | custom-call | tf_op jit(solution)/shard_map/adjoint/pallas_call | solution.py:269
  57.5 10.1 %all-to-all-start.3 = ((bf16[128,16,256]{2,1,0:T(8,128)(2,1)}), bf16[128,16,256]{2,1,0:T(8,128)(2,1)S(1)}, u32[]{:S(2)}, u32[]{:S(2)}) async-start(bf16[128,16,256]{2,1,0:T(8,128)(2,1)} %bitcast.14), calls=%async_computation.3 | async-start | bytes 2097152 | tf_op jit(solution)/shard_map/all_to_all | solution.py:525
  67.5 15.4 %all_gather.3 = s32[64,128]{1,0:T(8,128)S(1)} all-gather(s32[8,128]{1,0:T(8,128)S(1)} %broadcast_in_dim.12), channel_id=1, replica_groups=mesh['facet'=16,'sub'=8] {'sub'}, dimensions={0}, use_global_device_ids=true | all-gather | bytes 36864 | tf_op jit(solution)/shard_map/all_gather | solution.py:540
  83.0 3.8 %all-to-all-done.3.adj0_ref = bf16[128,16,256]{2,1,0:T(8,128)(2,1)S(1)} async-done(((bf16[128,16,256]{2,1,0:T(8,128)(2,1)}), bf16[128,16,256]{2,1,0:T(8,128)(2,1)S(1)}, u32[]{:S(2)}, u32[]{:S(2)}) %all-to-all-start.3) | async-done | bytes 1048608 | tf_op jit(solution)/shard_map/all_to_all | solution.py:525
  86.8 3.5 %gram.1 = bf16[16,32,128]{2,1,0:T(8,128)(2,1)S(1)} custom-call(f32[2]{0:T(128)S(1)} %copy-done.16, s32[8]{0:T(128)S(1)} %reduce.starts_ref, s32[1]{0:T(128)} %copy.17.column_ref, s32[2,16]{1,0:T(2,128)S(1)} %copy-done.14, bf16[16,8,16,256]{3,2,1,0:T(8,128)(2,1)S(1)} %bitcast.13, bf16[16,32,128]{2,1,0:T(8,128)(2,1)} %section.1.first_ref), custom_call_target="tpu_custom_call" | custom-call | tf_op jit(solution)/shard_map/gram/pallas_call | solution.py:402
  90.3 14.4 %all_to_all.41.in_ref = bf16[16,32,128]{2,1,0:T(8,128)(2,1)S(1)} all-to-all(bf16[16,32,128]{2,1,0:T(8,128)(2,1)S(1)} %gram.1), channel_id=1, replica_groups=mesh['facet'=16,'sub'=8] {'facet'}, dimensions={0} | all-to-all | bytes 262144 | tf_op jit(solution)/shard_map/all_to_all | solution.py:520
  104.7 2.2 %copy-done.3 = bf16[4096,512]{1,0:T(8,128)(2,1)S(1)} copy-done((bf16[4096,512]{1,0:T(8,128)(2,1)S(1)}, bf16[4096,512]{1,0:T(8,128)(2,1)}, u32[]{:S(2)}) %copy-start.3) | copy-done | bytes 4194328
  108.2 10.7 %all_to_all.42.in_ref = bf16[16,32,256]{2,1,0:T(8,128)(2,1)S(1)} all-to-all(bf16[16,32,256]{2,1,0:T(8,128)(2,1)S(1)} %grids.3), channel_id=1, replica_groups=mesh['facet'=16,'sub'=8] {'facet'}, dimensions={0} | all-to-all | bytes 524288 | tf_op jit(solution)/shard_map/all_to_all | solution.py:520
  118.9 1.6 copy-done.7
  120.5 3.3 %visibilities.3 = (bf16[16,32,256]{2,1,0:T(8,128)(2,1)S(1)}, f32[2,4096]{1,0:T(2,128)S(1)}) custom-call(s32[1,16]{1,0:T(1,128)S(1)} %copy-done.15, bf16[2,4096]{1,0:T(2,128)(2,1)S(1)} %bitcast.17, bf16[1,4096]{1,0:T(2,128)(2,1)S(1)} %bitcast.19, bf16[16,32,256]{2,1,0:T(8,128)(2,1)S(1)} %all_to_all.42.in_ref, bf16[256,4096]{1,0:T(8,128)(2,1)S(1)} %get-tuple-element.16.ku_ref, ...), custom_call_target="tpu_custom_call" | custom-call | tf_op jit(solution)/shard_map/visibilities/pallas_call | solution.py:342
  123.8 10.9 %all_to_all.43.in_ref = bf16[16,32,256]{2,1,0:T(8,128)(2,1)S(1)} all-to-all(bf16[16,32,256]{2,1,0:T(8,128)(2,1)S(1)} %get-tuple-element.19), channel_id=1, replica_groups=mesh['facet'=16,'sub'=8] {'facet'}, dimensions={0} | all-to-all | bytes 524288 | tf_op jit(solution)/shard_map/all_to_all | solution.py:520
  134.7 3.8 %adjoint.3 = bf16[16,8,16,256]{3,2,1,0:T(8,128)(2,1)} custom-call(bf16[16,32,256]{2,1,0:T(8,128)(2,1)S(1)} %all_to_all.43.in_ref, f32[16,16,128]{2,1,0:T(8,128)S(1)} %get-tuple-element.13.c_ref, f32[16,16,128]{2,1,0:T(8,128)S(1)} %get-tuple-element.14.s_ref, bf16[4096,512]{1,0:T(8,128)(2,1)S(1)} %copy-done.4), custom_call_target="tpu_custom_call" | custom-call | tf_op jit(solution)/shard_map/adjoint/pallas_call | solution.py:269
  138.5 9.4 %all-to-all-start.7 = ((bf16[128,16,256]{2,1,0:T(8,128)(2,1)}), bf16[128,16,256]{2,1,0:T(8,128)(2,1)S(1)}, u32[]{:S(2)}, u32[]{:S(2)}) async-start(bf16[128,16,256]{2,1,0:T(8,128)(2,1)} %bitcast.6), calls=%async_computation.7 | async-start | bytes 2097152 | tf_op jit(solution)/shard_map/all_to_all | solution.py:525
  147.9 2.6 %update_tables.1 = (bf16[4096,512]{1,0:T(8,128)(2,1)S(1)}, f32[16,2048]{1,0:T(8,128)S(1)}, f32[16,2048]{1,0:T(8,128)S(1)}) custom-call(s32[8]{0:T(128)S(1)} %reduce.starts_ref, s32[2,16]{1,0:T(2,128)S(1)} %copy-done.14), custom_call_target="tpu_custom_call" | custom-call | tf_op jit(solution)/shard_map/update_tables/pallas_call | solution.py:501
  150.5 2.0 %copy-done.8 = bf16[4096,512]{1,0:T(8,128)(2,1)} copy-done((bf16[4096,512]{1,0:T(8,128)(2,1)}, bf16[4096,512]{1,0:T(8,128)(2,1)S(1)}, u32[]{:S(2)}) %copy-start.8) | copy-done | bytes 4194328
  153.2 14.0 %all-to-all-done.7.adj1_ref = bf16[128,16,256]{2,1,0:T(8,128)(2,1)S(1)} async-done(((bf16[128,16,256]{2,1,0:T(8,128)(2,1)}), bf16[128,16,256]{2,1,0:T(8,128)(2,1)S(1)}, u32[]{:S(2)}, u32[]{:S(2)}) %all-to-all-start.7) | async-done | bytes 1048608 | tf_op jit(solution)/shard_map/all_to_all | solution.py:525
  167.2 2.2 %copy-done.9 = bf16[4096,512]{1,0:T(8,128)(2,1)S(1)} copy-done((bf16[4096,512]{1,0:T(8,128)(2,1)S(1)}, bf16[4096,512]{1,0:T(8,128)(2,1)}, u32[]{:S(2)}) %copy-start.9) | copy-done | bytes 4194328
  169.4 12.6 %update.1 = f32[128,8192]{1,0:T(8,128)} custom-call(f32[2]{0:T(128)S(1)} %copy-done.16, bf16[128,16,256]{2,1,0:T(8,128)(2,1)S(1)} %all-to-all-done.3.adj0_ref, bf16[128,16,256]{2,1,0:T(8,128)(2,1)S(1)} %all-to-all-done.7.adj1_ref, bf16[4096,512]{1,0:T(8,128)(2,1)S(1)} %copy-done.9, f32[16,2048]{1,0:T(8,128)S(1)} %get-tuple-element.21.pc_ref, ...), custom_call_target="tpu_custom_call" | custom-call | tf_op jit(solution)/shard_map/update/pallas_call | solution.py:457
  (36 shorter events, 3.8 us)
Async XLA Ops:
  0.6 13.6 %copy-start.14 = (s32[2,16]{1,0:T(2,128)S(1)}, s32[2,16]{1,0:T(2,128)}, u32[]{:S(2)}) copy-start(s32[2,16]{1,0:T(2,128)} %offsets_ref.7) | copy-start | bytes 388
  0.6 13.6 %copy-start.17 = (s32[1,16]{1,0:T(1,128)S(1)}, s32[1,16]{1,0:T(1,128)}, u32[]{:S(2)}) copy-start(s32[1,16]{1,0:T(1,128)} %rows_ref.1) | copy-start | bytes 196
  1.3 0.7 copy-start.13
  2.0 26.9 %copy-start.18 = (s32[2,1,1,4096]{3,2,1,0:T(1,128)S(1)}, s32[2,1,1,4096]{3,2,1,0:T(1,128)}, u32[]{:S(2)}) copy-start(s32[2,1,1,4096]{3,2,1,0:T(1,128)} %param.15) | copy-start | bytes 98308
  2.0 34.2 %copy-start.11 = (bf16[2,1,1,4096]{3,0,2,1:T(2,128)(2,1)S(1)}, bf16[2,1,1,4096]{3,0,2,1:T(2,128)(2,1)}, u32[]{:S(2)}) copy-start(bf16[2,1,1,4096]{3,0,2,1:T(2,128)(2,1)} %param.16) | copy-start | bytes 49156
  2.0 34.3 %copy-start.12 = (bf16[1,1,4096]{2,1,0:T(2,128)(2,1)S(1)}, bf16[1,1,4096]{2,1,0:T(2,128)(2,1)}, u32[]{:S(2)}) copy-start(bf16[1,1,4096]{2,1,0:T(2,128)(2,1)} %param.17) | copy-start | bytes 24580
  2.0 34.3 %copy-start.15 = (s32[1,16]{1,0:T(1,128)S(1)}, s32[1,16]{1,0:T(1,128)}, u32[]{:S(2)}) copy-start(s32[1,16]{1,0:T(1,128)} %counts_ref.3) | copy-start | bytes 196
  6.6 14.5 %all-to-all-start = ((bf16[16,32,128]{2,1,0:T(8,128)(2,1)}), bf16[16,32,128]{2,1,0:T(8,128)(2,1)S(1)}, u32[]{:S(2)}, u32[]{:S(2)}) async-start(bf16[16,32,128]{2,1,0:T(8,128)(2,1)} %section.1.first_ref), calls=%async_computation | async-start | bytes 262144 | tf_op jit(solution)/shard_map/all_to_all | solution.py:520
  16.1 2.0 %copy-start = (bf16[4096,512]{1,0:T(8,128)(2,1)}, bf16[4096,512]{1,0:T(8,128)(2,1)S(1)}, u32[]{:S(2)}) copy-start(bf16[4096,512]{1,0:T(8,128)(2,1)S(1)} %get-tuple-element.15.table_ref) | copy-start | bytes 12582916
  21.1 2.2 %copy-start.1 = (bf16[4096,512]{1,0:T(8,128)(2,1)S(1)}, bf16[4096,512]{1,0:T(8,128)(2,1)}, u32[]{:S(2)}) copy-start(bf16[4096,512]{1,0:T(8,128)(2,1)} %copy-done) | copy-start | bytes 12582916
  25.3 11.0 %all-to-all-start.1 = ((bf16[16,32,256]{2,1,0:T(8,128)(2,1)}), bf16[16,32,256]{2,1,0:T(8,128)(2,1)S(1)}, u32[]{:S(2)}, u32[]{:S(2)}) async-start(bf16[16,32,256]{2,1,0:T(8,128)(2,1)} %grids.2), calls=%async_computation.1 | async-start | bytes 524288 | tf_op jit(solution)/shard_map/all_to_all | solution.py:520
  32.6 1.3 copy-start.5
  36.2 17.3 %copy-start.2 = (bf16[4096,512]{1,0:T(8,128)(2,1)S(1)}, bf16[4096,512]{1,0:T(8,128)(2,1)}, u32[]{:S(2)}) copy-start(bf16[4096,512]{1,0:T(8,128)(2,1)} %copy-done) | copy-start | bytes 12582916
  36.3 1.7 copy-start.6
  41.9 44.9 %copy-start.16 = (f32[2]{0:T(128)S(1)}, f32[2]{0:T(128)}, u32[]{:S(2)}) copy-start(f32[2]{0:T(128)} %step_ref.3) | copy-start | bytes 28
  56.5 1.0 copy-start.10
  57.5 29.4 %all-to-all-start.3 = ((bf16[128,16,256]{2,1,0:T(8,128)(2,1)}), bf16[128,16,256]{2,1,0:T(8,128)(2,1)S(1)}, u32[]{:S(2)}, u32[]{:S(2)}) async-start(bf16[128,16,256]{2,1,0:T(8,128)(2,1)} %bitcast.14), calls=%async_computation.3 | async-start | bytes 2097152 | tf_op jit(solution)/shard_map/all_to_all | solution.py:525
  104.7 2.2 %copy-start.3 = (bf16[4096,512]{1,0:T(8,128)(2,1)S(1)}, bf16[4096,512]{1,0:T(8,128)(2,1)}, u32[]{:S(2)}) copy-start(bf16[4096,512]{1,0:T(8,128)(2,1)} %copy-done) | copy-start | bytes 12582916
  106.9 27.8 %copy-start.4 = (bf16[4096,512]{1,0:T(8,128)(2,1)S(1)}, bf16[4096,512]{1,0:T(8,128)(2,1)}, u32[]{:S(2)}) copy-start(bf16[4096,512]{1,0:T(8,128)(2,1)} %copy-done) | copy-start | bytes 12582916
  118.9 1.6 copy-start.7
  138.5 28.7 %all-to-all-start.7 = ((bf16[128,16,256]{2,1,0:T(8,128)(2,1)}), bf16[128,16,256]{2,1,0:T(8,128)(2,1)S(1)}, u32[]{:S(2)}, u32[]{:S(2)}) async-start(bf16[128,16,256]{2,1,0:T(8,128)(2,1)} %bitcast.6), calls=%async_computation.7 | async-start | bytes 2097152 | tf_op jit(solution)/shard_map/all_to_all | solution.py:525
  150.5 2.0 %copy-start.8 = (bf16[4096,512]{1,0:T(8,128)(2,1)}, bf16[4096,512]{1,0:T(8,128)(2,1)S(1)}, u32[]{:S(2)}) copy-start(bf16[4096,512]{1,0:T(8,128)(2,1)S(1)} %get-tuple-element.20.table_ref) | copy-start | bytes 12582916
  167.2 2.2 %copy-start.9 = (bf16[4096,512]{1,0:T(8,128)(2,1)S(1)}, bf16[4096,512]{1,0:T(8,128)(2,1)}, u32[]{:S(2)}) copy-start(bf16[4096,512]{1,0:T(8,128)(2,1)} %copy-done.8) | copy-start | bytes 12582916

commit v4 on v3

--- a/solution.py
+++ b/solution.py
@@ -22,13 +22,13 @@
 
 STEP1 = 256
 HIGH1 = FW // STEP1
-PARTS1 = 2
+PARTS1 = 4
 STEP5 = 512
 HIGH5 = FW // STEP5
 PAIR5 = 2
 VBLOCK = 1024
 CHUNK = 4
-UNROLL4 = 2
+UNROLL4 = 8
 
 BF = jnp.bfloat16
 F32 = jnp.float32
@@ -87,198 +87,57 @@
     return value
 
 
-def section_kernel(column_ref, offsets_ref, model_ref, out_hbm, table_ref, pc_ref, ps_ref, re_ref, im_ref, out_ref, sem):
-    part = pl.program_id(0)
-    highs = HIGH1 // PARTS1
-
-    @pl.when(part == 0)
-    def _():
-        column_start = column_ref[0]
-        pixel_start = offsets_ref[1, lax.axis_index("facet")]
-        freq = column_start + iota((STEP1, SGW), 1)
-        c, s = phase(freq, iota((STEP1, SGW), 0))
-        table_ref[:, :SGW] = c.astype(BF)
-        table_ref[:, SGW:] = (-s).astype(BF)
-        freq = column_start + iota((HIGH1, SGW), 1)
-        c, s = phase(freq, pixel_start + STEP1 * iota((HIGH1, SGW), 0))
-        pc_ref[...] = c
-        ps_ref[...] = s
-        re_ref[...] = jnp.zeros((FROWS, SGW), F32)
-        im_ref[...] = jnp.zeros((FROWS, SGW), F32)
-
-    acc_re = re_ref[...]
-    acc_im = im_ref[...]
-    for high in range(highs):
+def section_kernel(column_ref, offsets_ref, model_hbm, out_hbm, model_ref, table_ref, pc_ref, ps_ref, out_ref, sems, sem):
+    wide = FW // PARTS1
+    fetches = []
+    for part in range(PARTS1):
+        cut = pl.ds(part * wide, wide)
+        fetches.append(pltpu.make_async_copy(model_hbm.at[:, cut], model_ref.at[:, cut], sems.at[part]))
+        fetches[-1].start()
+    column_start = column_ref[0]
+    pixel_start = offsets_ref[1, lax.axis_index("facet")]
+    freq = column_start + iota((STEP1, SGW), 1)
+    c, s = phase(freq, iota((STEP1, SGW), 0))
+    table_ref[:, :SGW] = c.astype(BF)
+    table_ref[:, SGW:] = (-s).astype(BF)
+    freq = column_start + iota((HIGH1, SGW), 1)
+    pc_ref[...], ps_ref[...] = phase(freq, pixel_start + STEP1 * iota((HIGH1, SGW), 0))
+    acc_re = jnp.zeros((FROWS, SGW), F32)
+    acc_im = jnp.zeros((FROWS, SGW), F32)
+    for high in range(HIGH1):
+        if high % (HIGH1 // PARTS1) == 0:
+            fetches[high // (HIGH1 // PARTS1)].wait()
         block = model_ref[:, high * STEP1 : (high + 1) * STEP1].astype(BF)
         product = jnp.dot(block, table_ref[...], preferred_element_type=F32)
         re = product[:, :SGW]
         im = product[:, SGW:]
-        pc = pc_ref[pl.ds(part * highs + high, 1), :]
-        ps = ps_ref[pl.ds(part * highs + high, 1), :]
+        pc = pc_ref[high : high + 1, :]
+        ps = ps_ref[high : high + 1, :]
         acc_re = acc_re + (re * pc + im * ps)
         acc_im = acc_im + (im * pc - re * ps)
-    re_ref[...] = acc_re
-    im_ref[...] = acc_im
-
-    @pl.when(part == PARTS1 - 1)
-    def _():
-        re = re_ref[...].T.astype(BF)
-        im = im_ref[...].T.astype(BF)
-        out_ref[:, :SLICE, :] = re.reshape(FACETS, SLICE, FROWS)
-        out_ref[:, SLICE:, :] = im.reshape(FACETS, SLICE, FROWS)
-        write_out([(out_ref, out_hbm, sem)])
+    out_ref[:, :SLICE, :] = acc_re.T.astype(BF).reshape(FACETS, SLICE, FROWS)
+    out_ref[:, SLICE:, :] = acc_im.T.astype(BF).reshape(FACETS, SLICE, FROWS)
+    write_out([(out_ref, out_hbm, sem)])
 
 
 def section(column_start, offsets, model):
     return pl.pallas_call(
         section_kernel,
-        grid=(PARTS1,),
         out_shape=jax.ShapeDtypeStruct((FACETS, 2 * SLICE, FROWS), BF),
-        in_specs=[SMEM_SPEC, SMEM_SPEC, pl.BlockSpec((FROWS, FW // PARTS1), lambda i: (0, i))],
+        in_specs=[SMEM_SPEC, SMEM_SPEC, HBM_SPEC],
         out_specs=HBM_SPEC,
         scratch_shapes=[
+            pltpu.VMEM((FROWS, FW), F32),
             pltpu.VMEM((STEP1, 2 * SGW), BF),
             pltpu.VMEM((HIGH1, SGW), F32),
             pltpu.VMEM((HIGH1, SGW), F32),
-            pltpu.VMEM((FROWS, SGW), F32),
-            pltpu.VMEM((FROWS, SGW), F32),
             pltpu.VMEM((FACETS, 2 * SLICE, FROWS), BF),
+            pltpu.SemaphoreType.DMA((PARTS1,)),
             pltpu.SemaphoreType.DMA,
         ],
         compiler_params=PARAMS,
         name="section",
     )(column_start, offsets, off_chip(model))
-
-
-def row_table_kernel(offsets_ref, rows_ref, table_ref, c_ref, s_ref, base_ref, turn_ref):
-    c, s = phase(iota((FROWS, SGW), 1), iota((FROWS, SGW), 0))
-    base_ref[0] = c
-    base_ref[1] = s
-    row = iota((FACETS, SGW), 0)
-    start = jnp.zeros((FACETS, SGW), I32)
-    for f in range(FACETS):
-        start = jnp.where(row == f, offsets_ref[0, f], start)
-    c, s = phase(iota((FACETS, SGW), 1), start)
-    turn_ref[0] = c
-    turn_ref[1] = s
-    row = iota((NROWSG, FROWS), 0)
-    freq = jnp.zeros((NROWSG, FROWS), I32)
-    for r in range(NROWSG):
-        freq = jnp.where(row == r, rows_ref[0, r], freq)
-
-    def one(f, carry):
-        cf = turn_ref[0, pl.ds(f, 1), :]
-        sf = turn_ref[1, pl.ds(f, 1), :]
-        c = (base_ref[0] * cf - base_ref[1] * sf).astype(BF)
-        s = (base_ref[1] * cf + base_ref[0] * sf).astype(BF)
-        top = pl.ds(pl.multiple_of(f * 2 * FROWS, 2 * FROWS), FROWS)
-        low = pl.ds(pl.multiple_of(f * 2 * FROWS + FROWS, FROWS), FROWS)
-        table_ref[top, :SGW] = c
-        table_ref[top, SGW:] = -s
-        table_ref[low, :SGW] = s
-        table_ref[low, SGW:] = c
-        c, s = phase(freq, offsets_ref[0, f] + iota((NROWSG, FROWS), 1))
-        c_ref[f] = c
-        s_ref[f] = s
-        return carry
-
-    lax.fori_loop(0, FACETS, one, 0)
-
-
-def row_tables(offsets, rows):
-    return pl.pallas_call(
-        row_table_kernel,
-        out_shape=(
-            pltpu.VMEM((FACETS * 2 * FROWS, 2 * SGW), BF),
-            pltpu.VMEM((FACETS, NROWSG, FROWS), F32),
-            pltpu.VMEM((FACETS, NROWSG, FROWS), F32),
-        ),
-        in_specs=[SMEM_SPEC, SMEM_SPEC],
-        out_specs=(VMEM_SPEC, VMEM_SPEC, VMEM_SPEC),
-        scratch_shapes=[
-            pltpu.VMEM((2, FROWS, SGW), F32),
-            pltpu.VMEM((2, FACETS, SGW), F32),
-        ],
-        compiler_params=PARAMS,
-        name="row_tables",
-    )(offsets, rows)
-
-
-def grid_kernel(in_ref, c_ref, s_ref, table_ref, out_hbm, turned_ref, out_ref, sem):
-    for f in range(FACETS):
-        re = in_ref[f, :SLICE, :].astype(F32)
-        im = in_ref[f, SLICE:, :].astype(F32)
-        left = f * 2 * FROWS
-        for r in range(NROWSG):
-            c = c_ref[f, r : r + 1, :]
-            s = s_ref[f, r : r + 1, :]
-            lines = slice(r * SLICE, (r + 1) * SLICE)
-            turned_ref[lines, left : left + FROWS] = (re * c + im * s).astype(BF)
-            turned_ref[lines, left + FROWS : left + 2 * FROWS] = (im * c - re * s).astype(BF)
-    product = jnp.dot(turned_ref[...], table_ref[...], preferred_element_type=F32)
-    total = (NORM * product).astype(BF)
-    out_ref[:, :SLICE, :] = total[:, :SGW].reshape(NROWSG, SLICE, SGW)
-    out_ref[:, SLICE:, :] = total[:, SGW:].reshape(NROWSG, SLICE, SGW)
-    write_out([(out_ref, out_hbm, sem)])
-
-
-def grids(sections, tables):
-    table, c, s = tables
-    return pl.pallas_call(
-        grid_kernel,
-        out_shape=jax.ShapeDtypeStruct((NROWSG, 2 * SLICE, SGW), BF),
-        in_specs=[VMEM_SPEC] * 4,
-        out_specs=HBM_SPEC,
-        scratch_shapes=[
-            pltpu.VMEM((NROWSG * SLICE, FACETS * 2 * FROWS), BF),
-            pltpu.VMEM((NROWSG, 2 * SLICE, SGW), BF),
-            pltpu.SemaphoreType.DMA,
-        ],
-        compiler_params=PARAMS,
-        name="grids",
-    )(on_chip(sections), on_chip(c), on_chip(s), on_chip(table))
-
-
-def adjoint_kernel(in_ref, c_ref, s_ref, table_ref, out_hbm, lines_ref, out_ref, sems):
-    lines_ref[:, :SGW] = in_ref[:, :SLICE, :].reshape(NROWSG * SLICE, SGW)
-    lines_ref[:, SGW:] = in_ref[:, SLICE:, :].reshape(NROWSG * SLICE, SGW)
-
-    def one(f, carry):
-        table = table_ref[pl.ds(pl.multiple_of(f * 2 * FROWS, 2 * FROWS), 2 * FROWS), :]
-        product = lax.dot_general(
-            lines_ref[...], table, (((1,), (1,)), ((), ())), preferred_element_type=F32
-        )
-        acc_re = jnp.zeros((SLICE, FROWS), F32)
-        acc_im = jnp.zeros((SLICE, FROWS), F32)
-        for r in range(NROWSG):
-            re = product[r * SLICE : (r + 1) * SLICE, :FROWS]
-            im = product[r * SLICE : (r + 1) * SLICE, FROWS:]
-            c = c_ref[f, r : r + 1, :]
-            s = s_ref[f, r : r + 1, :]
-            acc_re = acc_re + (re * c - im * s)
-            acc_im = acc_im + (im * c + re * s)
-        out_ref[f] = jnp.concatenate([acc_re, acc_im], axis=1).astype(BF)
-        return carry
-
-    lax.fori_loop(0, FACETS, one, 0, unroll=UNROLL4)
-    write_out([(out_ref, out_hbm.at[:, copy], sems.at[copy]) for copy in range(NCOL)])
-
-
-def adjoint(gridded, tables):
-    table, c, s = tables
-    return pl.pallas_call(
-        adjoint_kernel,
-        out_shape=jax.ShapeDtypeStruct((FACETS, NCOL, SLICE, 2 * FROWS), BF),
-        in_specs=[VMEM_SPEC] * 4,
-        out_specs=HBM_SPEC,
-        scratch_shapes=[
-            pltpu.VMEM((NROWSG * SLICE, 2 * SGW), BF),
-            pltpu.VMEM((FACETS, SLICE, 2 * FROWS), BF),
-            pltpu.SemaphoreType.DMA((NCOL,)),
-        ],
-        compiler_params=PARAMS,
-        name="adjoint",
-    )(on_chip(gridded), on_chip(c), on_chip(s), on_chip(table))
 
 
 def kernel_columns(position):
@@ -289,26 +148,137 @@
     return jnp.where(inside, jnp.exp(-0.5 * distance * distance), 0.0).astype(BF)
 
 
-def vis_table_kernel(uv_ref, ku_ref, kv_ref):
-    def one(part, carry):
-        cut = pl.ds(pl.multiple_of(part * 256, 256), 256)
+def table_kernel(offsets_ref, rows_ref, uv_ref, table_ref, c_ref, s_ref, ku_ref, kv_ref, base_ref, turn_ref):
+    base_ref[0], base_ref[1] = phase(iota((FROWS, SGW), 1), iota((FROWS, SGW), 0))
+    row = iota((FACETS, SGW), 0)
+    start = jnp.zeros((FACETS, SGW), I32)
+    for f in range(FACETS):
+        start = jnp.where(row == f, offsets_ref[0, f], start)
+    turn_ref[0], turn_ref[1] = phase(iota((FACETS, SGW), 1), start)
+    row = iota((NROWSG, FROWS), 0)
+    freq = jnp.zeros((NROWSG, FROWS), I32)
+    for r in range(NROWSG):
+        freq = jnp.where(row == r, rows_ref[0, r], freq)
+
+    def one(f, carry):
+        cf = turn_ref[0, pl.ds(f, 1), :]
+        sf = turn_ref[1, pl.ds(f, 1), :]
+        lines = pl.ds(pl.multiple_of(f * FROWS, FROWS), FROWS)
+        table_ref[0, lines, :] = (base_ref[0] * cf - base_ref[1] * sf).astype(BF)
+        table_ref[1, lines, :] = (base_ref[1] * cf + base_ref[0] * sf).astype(BF)
+        c_ref[f], s_ref[f] = phase(freq, offsets_ref[0, f] + iota((NROWSG, FROWS), 1))
+        cut = pl.ds(pl.multiple_of(f * SGW, SGW), SGW)
         ku_ref[:, cut] = kernel_columns(uv_ref[0:1, cut])
         kv_ref[:, cut] = kernel_columns(uv_ref[1:2, cut])
         return carry
 
-    lax.fori_loop(0, VCAP // 256, one, 0)
-
-
-def vis_tables(uv):
-    shape = pltpu.VMEM((SGW, VCAP), BF)
-    return pl.pallas_call(
-        vis_table_kernel,
-        out_shape=(shape, shape),
-        in_specs=[VMEM_SPEC],
-        out_specs=(VMEM_SPEC, VMEM_SPEC),
-        compiler_params=PARAMS,
-        name="vis_tables",
-    )(uv)
+    lax.fori_loop(0, FACETS, one, 0)
+
+
+def cycle_tables(offsets, rows, uv):
+    return pl.pallas_call(
+        table_kernel,
+        out_shape=(
+            pltpu.VMEM((2, FACETS * FROWS, SGW), BF),
+            pltpu.VMEM((FACETS, NROWSG, FROWS), F32),
+            pltpu.VMEM((FACETS, NROWSG, FROWS), F32),
+            pltpu.VMEM((SGW, VCAP), BF),
+            pltpu.VMEM((SGW, VCAP), BF),
+        ),
+        in_specs=[SMEM_SPEC, SMEM_SPEC, VMEM_SPEC],
+        out_specs=(VMEM_SPEC,) * 5,
+        scratch_shapes=[
+            pltpu.VMEM((2, FROWS, SGW), F32),
+            pltpu.VMEM((2, FACETS, SGW), F32),
+        ],
+        compiler_params=PARAMS,
+        name="cycle_tables",
+    )(offsets, rows, uv)
+
+
+def grid_kernel(in_ref, c_ref, s_ref, table_ref, out_hbm, turned_ref, out_ref, sem):
+    half = NROWSG * SLICE
+    for f in range(FACETS):
+        re = in_ref[f, :SLICE, :].astype(F32)
+        im = in_ref[f, SLICE:, :].astype(F32)
+        cut = slice(f * FROWS, (f + 1) * FROWS)
+        for r in range(NROWSG):
+            c = c_ref[f, r : r + 1, :]
+            s = s_ref[f, r : r + 1, :]
+            turned_ref[r * SLICE : (r + 1) * SLICE, cut] = (re * c + im * s).astype(BF)
+            turned_ref[half + r * SLICE : half + (r + 1) * SLICE, cut] = (im * c - re * s).astype(BF)
+    by_c = jnp.dot(turned_ref[...], table_ref[0], preferred_element_type=F32)
+    by_s = jnp.dot(turned_ref[...], table_ref[1], preferred_element_type=F32)
+    re = (NORM * (by_c[:half] + by_s[half:])).astype(BF)
+    im = (NORM * (by_c[half:] - by_s[:half])).astype(BF)
+    out_ref[:, :SLICE, :] = re.reshape(NROWSG, SLICE, SGW)
+    out_ref[:, SLICE:, :] = im.reshape(NROWSG, SLICE, SGW)
+    write_out([(out_ref, out_hbm, sem)])
+
+
+def grids(sections, tables):
+    table, c, s = tables
+    return pl.pallas_call(
+        grid_kernel,
+        out_shape=jax.ShapeDtypeStruct((NROWSG, 2 * SLICE, SGW), BF),
+        in_specs=[VMEM_SPEC] * 4,
+        out_specs=HBM_SPEC,
+        scratch_shapes=[
+            pltpu.VMEM((2 * NROWSG * SLICE, FACETS * FROWS), BF),
+            pltpu.VMEM((NROWSG, 2 * SLICE, SGW), BF),
+            pltpu.SemaphoreType.DMA,
+        ],
+        compiler_params=PARAMS,
+        name="grids",
+    )(on_chip(sections), on_chip(c), on_chip(s), on_chip(table))
+
+
+def adjoint_kernel(in_ref, c_ref, s_ref, table_ref, out_hbm, lines_ref, out_ref, sems):
+    half = NROWSG * SLICE
+    lines_ref[:half] = in_ref[:, :SLICE, :].reshape(half, SGW)
+    lines_ref[half:] = in_ref[:, SLICE:, :].reshape(half, SGW)
+
+    def one(pair, carry):
+        cut = pl.ds(pl.multiple_of(pair * 2 * FROWS, 2 * FROWS), 2 * FROWS)
+        dims = (((1,), (1,)), ((), ()))
+        by_c = lax.dot_general(lines_ref[...], table_ref[0, cut, :], dims, preferred_element_type=F32)
+        by_s = lax.dot_general(lines_ref[...], table_ref[1, cut, :], dims, preferred_element_type=F32)
+        for k in range(2):
+            f = 2 * pair + k
+            lanes = slice(k * FROWS, (k + 1) * FROWS)
+            acc_re = jnp.zeros((SLICE, FROWS), F32)
+            acc_im = jnp.zeros((SLICE, FROWS), F32)
+            for r in range(NROWSG):
+                top = slice(r * SLICE, (r + 1) * SLICE)
+                low = slice(half + r * SLICE, half + (r + 1) * SLICE)
+                re = by_c[top, lanes] - by_s[low, lanes]
+                im = by_c[low, lanes] + by_s[top, lanes]
+                c = c_ref[f, r : r + 1, :]
+                s = s_ref[f, r : r + 1, :]
+                acc_re = acc_re + (re * c - im * s)
+                acc_im = acc_im + (im * c + re * s)
+            out_ref[f] = jnp.concatenate([acc_re, acc_im], axis=1).astype(BF)
+        return carry
+
+    lax.fori_loop(0, FACETS // 2, one, 0, unroll=UNROLL4)
+    write_out([(out_ref, out_hbm.at[:, copy], sems.at[copy]) for copy in range(NCOL)])
+
+
+def adjoint(gridded, tables):
+    table, c, s = tables
+    return pl.pallas_call(
+        adjoint_kernel,
+        out_shape=jax.ShapeDtypeStruct((FACETS, NCOL, SLICE, 2 * FROWS), BF),
+        in_specs=[VMEM_SPEC] * 4,
+        out_specs=HBM_SPEC,
+        scratch_shapes=[
+            pltpu.VMEM((2 * NROWSG * SLICE, SGW), BF),
+            pltpu.VMEM((FACETS, SLICE, 2 * FROWS), BF),
+            pltpu.SemaphoreType.DMA((NCOL,)),
+        ],
+        compiler_params=PARAMS,
+        name="adjoint",
+    )(on_chip(gridded), on_chip(c), on_chip(s), on_chip(table))
 
 
 def visibility_kernel(counts_ref, obs_ref, weight_ref, in_ref, ku_ref, kv_ref, gridded_hbm, res_ref, acc_ref, gridded_ref, sem):
@@ -415,8 +385,9 @@
     )(steps, column_starts, column_start, offsets, on_chip(adj.reshape(FACETS, NCOL, SLICE, 2 * FROWS)), first)
 
 
-def update_kernel(step_ref, adj0_ref, adj1_ref, table_ref, pc_ref, ps_ref, model_ref, out_ref, both_ref, even_ref, odd_ref):
+def update_kernel(step_ref, adj0_ref, adj1_ref, table_hbm, pc_ref, ps_ref, model_ref, out_ref, table_ref, both_ref, even_ref, odd_ref, sem):
     part = pl.program_id(0)
+    fetch = pltpu.make_async_copy(table_hbm, table_ref, sem)
 
     def turn(pair, target_ref):
         re = both_ref[:FROWS, :]
@@ -437,6 +408,7 @@
 
     @pl.when(part == 0)
     def _():
+        fetch.start()
         first = step_ref[0] * NORM
         second = step_ref[1] * NORM
         for j in range(FACETS):
@@ -445,6 +417,7 @@
             both = first * lines0 + second * lines1
             both_ref[:, j * NCOL * SLICE : (j + 1) * NCOL * SLICE] = both.T
         turn(0, even_ref)
+        fetch.wait()
 
     turn(2 * part + 1, odd_ref)
     add(0, even_ref)
@@ -453,24 +426,27 @@
 
 
 def update(steps, adj0, adj1, tables, model):
+    table, pc, ps = tables
     wide = pl.BlockSpec((FROWS, 2 * PAIR5 * STEP5), lambda i: (0, i))
     return pl.pallas_call(
         update_kernel,
         grid=(HIGH5 // PAIR5 // 2,),
         out_shape=jax.ShapeDtypeStruct((FROWS, FW), F32),
-        in_specs=[SMEM_SPEC] + [VMEM_SPEC] * 5 + [wide],
+        in_specs=[SMEM_SPEC, VMEM_SPEC, VMEM_SPEC, HBM_SPEC, VMEM_SPEC, VMEM_SPEC, wide],
         out_specs=wide,
         scratch_shapes=[
+            pltpu.VMEM((2 * COLUMNS, STEP5), BF),
             pltpu.VMEM((2 * FROWS, COLUMNS), F32),
             pltpu.VMEM((PAIR5 * FROWS, 2 * COLUMNS), BF),
             pltpu.VMEM((PAIR5 * FROWS, 2 * COLUMNS), BF),
+            pltpu.SemaphoreType.DMA,
         ],
         compiler_params=WIDE_PARAMS,
         name="update",
-    )(steps, on_chip(adj0), on_chip(adj1), *map(on_chip, tables), off_chip(model))
-
-
-def update_table_kernel(starts_ref, offsets_ref, table_ref, pc_ref, ps_ref, base_ref, turn_ref):
+    )(steps, on_chip(adj0), on_chip(adj1), off_chip(table), on_chip(pc), on_chip(ps), off_chip(model))
+
+
+def update_table_kernel(starts_ref, offsets_ref, table_hbm, pc_ref, ps_ref, table_ref, base_ref, turn_ref, sem):
     group = NCOL * SLICE
     line = iota((group, STEP5), 0)
     freq = line & (SLICE - 1)
@@ -495,21 +471,24 @@
         freq = freq + jnp.where(((lane >> 4) & (NCOL - 1)) == c, starts_ref[c], 0)
     pixel_start = offsets_ref[1, lax.axis_index("facet")]
     pc_ref[...], ps_ref[...] = phase(freq, pixel_start + STEP5 * iota((HIGH5, COLUMNS), 0))
+    write_out([(table_ref, table_hbm, sem)])
 
 
 def update_tables(column_starts, offsets):
     return pl.pallas_call(
         update_table_kernel,
         out_shape=(
-            pltpu.VMEM((2 * COLUMNS, STEP5), BF),
+            pltpu.HBM((2 * COLUMNS, STEP5), BF),
             pltpu.VMEM((HIGH5, COLUMNS), F32),
             pltpu.VMEM((HIGH5, COLUMNS), F32),
         ),
         in_specs=[SMEM_SPEC, SMEM_SPEC],
-        out_specs=(VMEM_SPEC, VMEM_SPEC, VMEM_SPEC),
-        scratch_shapes=[
+        out_specs=(HBM_SPEC, VMEM_SPEC, VMEM_SPEC),
+        scratch_shapes=[
+            pltpu.VMEM((2 * COLUMNS, STEP5), BF),
             pltpu.VMEM((2, NCOL * SLICE, STEP5), F32),
             pltpu.VMEM((2, FACETS, STEP5), F32),
+            pltpu.SemaphoreType.DMA,
         ],
         compiler_params=PARAMS,
         name="update_tables",
@@ -536,17 +515,18 @@
     vis_obs,
     vis_weight,
 ):
-    lines = lax.optimization_barrier(jnp.broadcast_to(col_offsets[:, None], (8, 128)))
-    column_starts = lax.optimization_barrier(lax.all_gather(lines, "sub", axis=0, tiled=True))[::8, 0]
+    lines = lax.optimization_barrier(jnp.broadcast_to(col_offsets[:, None].astype(F32), (256, 128)))
+    column_starts = lax.optimization_barrier(lax.all_gather(lines, "sub", axis=0, tiled=True))[::256, 0].astype(I32)
     uv = vis_uv.reshape(2, VCAP)
     obs = vis_obs.reshape(2, VCAP)
     weight = vis_weight.reshape(1, VCAP)
     model = model_image[0]
     first = section(col_offsets, facet_offsets, model)
-    rows = row_tables(facet_offsets, row_offsets)
-    kernels = vis_tables(uv)
+    tables = cycle_tables(facet_offsets, row_offsets, uv)
+    rows, kernels = tables[:3], tables[3:]
     grid = exchange(grids(exchange(first), rows))
     gridded, residual = visibilities(counts, obs, weight, grid, kernels)
+    gridded, column_starts = lax.optimization_barrier((gridded, column_starts))
     adj0 = to_facets(adjoint(exchange(gridded), rows))
     tables = update_tables(column_starts, facet_offsets)
     second = gram(step_sizes, column_starts, col_offsets, facet_offsets, adj0, first)

time: 183 us -> 185 us (1.011)
  blocking collectives: 62.9 us -> 84.9 us
  starting transfers between devices: 30.7 us -> 16.4 us
  between operations: 1.55 us -> 14.9 us
  local copies, waits for them, and re-layouts: 17.6 us -> 8.17 us
  waiting for transfers between devices: 23.2 us -> 14.5 us
    all_to_all x0 -> x1, blocking collectives: none -> 29.5 us  [to_facets(): lax.all_to_all(copies, ('facet', 'sub'), split_axis=0, concat_axis=0, til...]
    all_gather x1 -> x0, blocking collectives: 15.4 us -> none  [local(): lax.all_gather(lines, 'sub', axis=0, tiled=True)]
    unnamed x40 -> x32, local copies, waits for them, and re-layouts: 17.6 us -> 6.59 us
    all_to_all x2 -> x1, starting transfers between devices: 19.5 us -> 8.79 us  [to_facets(): lax.all_to_all(copies, ('facet', 'sub'), split_axis=0, concat_axis=0, til...]
    all_to_all x4 -> x5, blocking collectives: 47.6 us -> 55.4 us  [exchange(): lax.all_to_all(value, 'facet', split_axis=0, concat_axis=0, tiled=True)]
    all_to_all x2 -> x1, waiting for transfers between devices: 5.38 us -> 0.01 us  [exchange(): lax.all_to_all(value, 'facet', split_axis=0, concat_axis=0, tiled=True)]
    all_to_all x2 -> x1, starting transfers between devices: 11.2 us -> 7.6 us  [exchange(): lax.all_to_all(value, 'facet', split_axis=0, concat_axis=0, tiled=True)]
    all_to_all x2 -> x1, waiting for transfers between devices: 17.8 us -> 14.4 us  [to_facets(): lax.all_to_all(copies, ('facet', 'sub'), split_axis=0, concat_axis=0, til...]
  transfers between devices with their start and end apart: 4 -> 3, of which waited for: 4 -> 1; matrix products, arithmetic and copies ran while one was open for 0% -> 0% of each run, Pallas kernels for 4% -> 10%
where the time goes in v4:
time: 185 us; the launch traced here: 184 us
  blocking collectives  84.9 us (46%)
  Pallas kernels  45.1 us (24%)
  starting transfers between devices  16.4 us (9%)
  between operations  14.9 us (8%)
  waiting for transfers between devices  14.5 us (8%)
  local copies, waits for them, and re-layouts  8.17 us (4%)
    all_to_all x5, blocking collectives, exchange(): lax.all_to_all(value, 'facet', split_axis=0, concat_axis=0, tiled=True)  55.4 us
    all_to_all x1, blocking collectives, to_facets(): lax.all_to_all(copies, ('facet', 'sub'), split_axis=0, concat_axis=0, til...  29.5 us
    all_to_all x1, waiting for transfers between devices, to_facets(): lax.all_to_all(copies, ('facet', 'sub'), split_axis=0, concat_axis=0, til...  14.4 us
    pallas_call x1, Pallas kernels, update(): pl.pallas_call(update_kernel, grid=(HIGH5 // PAIR5 // 2,), out_shape=jax....  14 us
    all_to_all x1, starting transfers between devices, to_facets(): lax.all_to_all(copies, ('facet', 'sub'), split_axis=0, concat_axis=0, til...  8.79 us
    all_to_all x1, starting transfers between devices, exchange(): lax.all_to_all(value, 'facet', split_axis=0, concat_axis=0, tiled=True)  7.6 us
    pallas_call x2, Pallas kernels, visibilities(): pl.pallas_call(visibility_kernel, out_shape=(jax.ShapeDtypeStruct((FACETS...  7.21 us
    unnamed x32, local copies, waits for them, and re-layouts  6.59 us
  transfers between devices with their start and end apart: 3, of which 1 were waited for; matrix products, arithmetic and copies ran while one was open for 0% of the time, Pallas kernels for 10%

profile of v4, /device:TPU:1, one launch (start us, length us, event | category | flops | bytes accessed | tf_op | source)
XLA Modules:
  0.0 184.1 jit_solution(10535755509025029373)
XLA Ops:
  7.2 0.0 copy-start.10
  7.2 0.0 all-gather.2.cloned.1.call-start
  7.9 0.7 broadcast_in_dim.12
  8.6 0.0 all-gather.2.cloned.1.call-update
  8.6 0.7 copy-done.9
  9.3 4.7 %section.1.first_ref = bf16[16,32,128]{2,1,0:T(8,128)(2,1)} custom-call(s32[1]{0:T(128)S(6)} %copy.15.column_ref, s32[2,16]{1,0:T(2,128)S(1)} %copy-done.9, f32[128,8192]{1,0:T(8,128)} %bitcast.23), custom_call_target="tpu_custom_call" | custom-call | tf_op jit(solution)/shard_map/section/pallas_call | solution.py:124
  14.0 7.6 %all-to-all-start = ((bf16[16,32,128]{2,1,0:T(8,128)(2,1)}), bf16[16,32,128]{2,1,0:T(8,128)(2,1)S(1)}, u32[]{:S(2)}, u32[]{:S(2)}) async-start(bf16[16,32,128]{2,1,0:T(8,128)(2,1)} %section.1.first_ref), calls=%async_computation | async-start | bytes 262144 | tf_op jit(solution)/shard_map/all_to_all | solution.py:499
  21.7 5.1 %cycle_tables.1 = (bf16[2,2048,256]{2,1,0:T(8,128)(2,1)S(1)}, f32[16,16,128]{2,1,0:T(8,128)S(1)}, f32[16,16,128]{2,1,0:T(8,128)S(1)}, bf16[256,4096]{1,0:T(8,128)(2,1)S(1)}, bf16[256,4096]{1,0:T(8,128)(2,1)S(1)}) custom-call(s32[2,16]{1,0:T(2,128)S(1)} %copy-done.10, s32[1,16]{1,0:T(1,128)S(1)} %copy-done.13, s32[2,4096]{1,0:T(2,128)S(1)} %bitcast.17), custom_call_target="tpu_custom_call" | custom-call | tf_op jit(solution)/shard_map/cycle_tables/pallas_call | solution.py:179
  26.7 1.3 copy-done
  28.1 1.3 copy-done.3
  29.4 1.3 grids.2
  30.7 13.8 %all_to_all.40.in_ref = bf16[16,32,256]{2,1,0:T(8,128)(2,1)S(1)} all-to-all(bf16[16,32,256]{2,1,0:T(8,128)(2,1)S(1)} %grids.2), channel_id=1, replica_groups=mesh['facet'=16,'sub'=8] {'facet'}, dimensions={0} | all-to-all | bytes 524288 | tf_op jit(solution)/shard_map/all_to_all | solution.py:499
  44.5 1.6 copy-done.4
  46.1 3.9 %visibilities.2 = (bf16[16,32,256]{2,1,0:T(8,128)(2,1)S(1)}, f32[2,4096]{1,0:T(2,128)}) custom-call(s32[1,16]{1,0:T(1,128)S(1)} %copy-done.11, bf16[2,4096]{1,0:T(2,128)(2,1)S(1)} %bitcast.18, bf16[1,4096]{1,0:T(2,128)(2,1)S(1)} %bitcast.20, bf16[16,32,256]{2,1,0:T(8,128)(2,1)S(1)} %all_to_all.40.in_ref, bf16[256,4096]{1,0:T(8,128)(2,1)S(1)} %copy-done.1, ...), custom_call_target="tpu_custom_call" | custom-call | tf_op jit(solution)/shard_map/visibilities/pallas_call | solution.py:312
  50.0 0.0 all-gather.2.cloned.1.call-done
  50.1 0.9 slice.3
  51.0 10.8 %all_to_all.41.in_ref = bf16[16,32,256]{2,1,0:T(8,128)(2,1)S(1)} all-to-all(bf16[16,32,256]{2,1,0:T(8,128)(2,1)S(1)} %get-tuple-element.21), channel_id=1, replica_groups=mesh['facet'=16,'sub'=8] {'facet'}, dimensions={0} | all-to-all | bytes 524288 | tf_op jit(solution)/shard_map/all_to_all | solution.py:499
  61.8 1.9 %adjoint.2 = bf16[16,8,16,256]{3,2,1,0:T(8,128)(2,1)S(1)} custom-call(bf16[16,32,256]{2,1,0:T(8,128)(2,1)S(1)} %all_to_all.41.in_ref, f32[16,16,128]{2,1,0:T(8,128)S(1)} %get-tuple-element.15.c_ref, f32[16,16,128]{2,1,0:T(8,128)S(1)} %get-tuple-element.16.s_ref, bf16[2,2048,256]{2,1,0:T(8,128)(2,1)S(1)} %get-tuple-element.17.table_ref), custom_call_target="tpu_custom_call" | custom-call | tf_op jit(solution)/shard_map/adjoint/pallas_call | solution.py:269
  63.7 29.5 %all_to_all.42.adj0_ref = bf16[128,16,256]{2,1,0:T(8,128)(2,1)S(1)} all-to-all(bf16[128,16,256]{2,1,0:T(8,128)(2,1)S(1)} %bitcast.16), channel_id=1, replica_groups=mesh['facet'=16,'sub'=8] {'facet','sub'}, dimensions={0} | all-to-all | bytes 2097152 | tf_op jit(solution)/shard_map/all_to_all | solution.py:504
  93.3 3.5 %gram.1 = bf16[16,32,128]{2,1,0:T(8,128)(2,1)S(1)} custom-call(f32[2]{0:T(128)S(1)} %copy-done.12, s32[8]{0:T(128)S(1)} %convert_bitcast_fusion.starts_ref, s32[1]{0:T(128)S(6)} %copy.15.column_ref, s32[2,16]{1,0:T(2,128)S(1)} %copy-done.10, bf16[16,8,16,256]{3,2,1,0:T(8,128)(2,1)S(1)} %bitcast.14, bf16[16,32,128]{2,1,0:T(8,128)(2,1)} %section.1.first_ref), custom_call_target="tpu_custom_call" | custom-call | tf_op jit(solution)/shard_map/gram/pallas_call | solution.py:372
  96.7 9.3 %all_to_all.43.in_ref = bf16[16,32,128]{2,1,0:T(8,128)(2,1)S(1)} all-to-all(bf16[16,32,128]{2,1,0:T(8,128)(2,1)S(1)} %gram.1), channel_id=1, replica_groups=mesh['facet'=16,'sub'=8] {'facet'}, dimensions={0} | all-to-all | bytes 262144 | tf_op jit(solution)/shard_map/all_to_all | solution.py:499
  106.0 1.3 grids.3
  107.3 10.8 %all_to_all.44.in_ref = bf16[16,32,256]{2,1,0:T(8,128)(2,1)S(1)} all-to-all(bf16[16,32,256]{2,1,0:T(8,128)(2,1)S(1)} %grids.3), channel_id=1, replica_groups=mesh['facet'=16,'sub'=8] {'facet'}, dimensions={0} | all-to-all | bytes 524288 | tf_op jit(solution)/shard_map/all_to_all | solution.py:499
  118.2 3.3 %visibilities.3 = (bf16[16,32,256]{2,1,0:T(8,128)(2,1)S(1)}, f32[2,4096]{1,0:T(2,128)S(1)}) custom-call(s32[1,16]{1,0:T(1,128)S(1)} %copy-done.11, bf16[2,4096]{1,0:T(2,128)(2,1)S(1)} %bitcast.19, bf16[1,4096]{1,0:T(2,128)(2,1)S(1)} %bitcast.21, bf16[16,32,256]{2,1,0:T(8,128)(2,1)S(1)} %all_to_all.44.in_ref, bf16[256,4096]{1,0:T(8,128)(2,1)S(1)} %copy-done.2, ...), custom_call_target="tpu_custom_call" | custom-call | tf_op jit(solution)/shard_map/visibilities/pallas_call | solution.py:312
  121.5 10.7 %all_to_all.45.in_ref = bf16[16,32,256]{2,1,0:T(8,128)(2,1)S(1)} all-to-all(bf16[16,32,256]{2,1,0:T(8,128)(2,1)S(1)} %get-tuple-element.23), channel_id=1, replica_groups=mesh['facet'=16,'sub'=8] {'facet'}, dimensions={0} | all-to-all | bytes 524288 | tf_op jit(solution)/shard_map/all_to_all | solution.py:499
  132.2 1.9 %adjoint.3 = bf16[16,8,16,256]{3,2,1,0:T(8,128)(2,1)S(1)} custom-call(bf16[16,32,256]{2,1,0:T(8,128)(2,1)S(1)} %all_to_all.45.in_ref, f32[16,16,128]{2,1,0:T(8,128)S(1)} %get-tuple-element.15.c_ref, f32[16,16,128]{2,1,0:T(8,128)S(1)} %get-tuple-element.16.s_ref, bf16[2,2048,256]{2,1,0:T(8,128)(2,1)S(1)} %get-tuple-element.17.table_ref), custom_call_target="tpu_custom_call" | custom-call | tf_op jit(solution)/shard_map/adjoint/pallas_call | solution.py:269
  134.2 1.0 copy-done.6
  135.1 8.8 %all-to-all-start.7 = ((bf16[128,16,256]{2,1,0:T(8,128)(2,1)}), bf16[128,16,256]{2,1,0:T(8,128)(2,1)S(1)}, u32[]{:S(2)}, u32[]{:S(2)}) async-start(bf16[128,16,256]{2,1,0:T(8,128)(2,1)} %bitcast.15), calls=%async_computation.7 | async-start | bytes 2097152 | tf_op jit(solution)/shard_map/all_to_all | solution.py:504
  143.9 4.2 %update_tables.1 = (bf16[4096,512]{1,0:T(8,128)(2,1)}, f32[16,2048]{1,0:T(8,128)S(1)}, f32[16,2048]{1,0:T(8,128)S(1)}) custom-call(s32[8]{0:T(128)S(1)} %convert_bitcast_fusion.starts_ref, s32[2,16]{1,0:T(2,128)S(1)} %copy-done.10), custom_call_target="tpu_custom_call" | custom-call | tf_op jit(solution)/shard_map/update_tables/pallas_call | solution.py:478
  148.1 0.6 copy.11
  148.8 14.4 %all-to-all-done.7.adj1_ref = bf16[128,16,256]{2,1,0:T(8,128)(2,1)S(1)} async-done(((bf16[128,16,256]{2,1,0:T(8,128)(2,1)}), bf16[128,16,256]{2,1,0:T(8,128)(2,1)S(1)}, u32[]{:S(2)}, u32[]{:S(2)}) %all-to-all-start.7) | async-done | bytes 1048608 | tf_op jit(solution)/shard_map/all_to_all | solution.py:504
  163.2 14.0 %update.1 = f32[128,8192]{1,0:T(8,128)} custom-call(f32[2]{0:T(128)S(1)} %copy-done.12, bf16[128,16,256]{2,1,0:T(8,128)(2,1)S(1)} %all_to_all.42.adj0_ref, bf16[128,16,256]{2,1,0:T(8,128)(2,1)S(1)} %all-to-all-done.7.adj1_ref, bf16[4096,512]{1,0:T(8,128)(2,1)} %get-tuple-element.24.table_hbm, f32[16,2048]{1,0:T(8,128)S(1)} %get-tuple-element.25.pc_ref, ...), custom_call_target="tpu_custom_call" | custom-call | tf_op jit(solution)/shard_map/update/pallas_call | solution.py:431
  (27 shorter events, 0.1 us)
Async XLA Ops:
  7.2 14.5 %copy-start.10 = (s32[2,16]{1,0:T(2,128)S(1)}, s32[2,16]{1,0:T(2,128)}, u32[]{:S(2)}) copy-start(s32[2,16]{1,0:T(2,128)} %offsets_ref.7) | copy-start | bytes 388
  7.2 14.4 %copy-start.14 = (s32[2,1,1,4096]{3,2,1,0:T(1,128)S(1)}, s32[2,1,1,4096]{3,2,1,0:T(1,128)}, u32[]{:S(2)}) copy-start(s32[2,1,1,4096]{3,2,1,0:T(1,128)} %param.15) | copy-start | bytes 98308
  7.2 14.5 %copy-start.13 = (s32[1,16]{1,0:T(1,128)S(1)}, s32[1,16]{1,0:T(1,128)}, u32[]{:S(2)}) copy-start(s32[1,16]{1,0:T(1,128)} %rows_ref.1) | copy-start | bytes 196
  7.2 37.3 %copy-start.11 = (s32[1,16]{1,0:T(1,128)S(1)}, s32[1,16]{1,0:T(1,128)}, u32[]{:S(2)}) copy-start(s32[1,16]{1,0:T(1,128)} %counts_ref.3) | copy-start | bytes 196
  7.2 37.3 %copy-start.8 = (bf16[1,1,4096]{2,1,0:T(2,128)(2,1)S(1)}, bf16[1,1,4096]{2,1,0:T(2,128)(2,1)}, u32[]{:S(2)}) copy-start(bf16[1,1,4096]{2,1,0:T(2,128)(2,1)} %param.17) | copy-start | bytes 24580
  7.2 37.3 %copy-start.7 = (bf16[2,1,1,4096]{3,0,2,1:T(2,128)(2,1)S(1)}, bf16[2,1,1,4096]{3,0,2,1:T(2,128)(2,1)}, u32[]{:S(2)}) copy-start(bf16[2,1,1,4096]{3,0,2,1:T(2,128)(2,1)} %param.16) | copy-start | bytes 49156
  7.2 42.8 %all-gather.2.cloned.1.call-start = ((), (), s32[]{:S(2)}) async-start(), calls=%async_computation.8 | async-start | bytes 1179648 | tf_op jit(solution)/shard_map/all_gather | solution.py:519
  8.6 0.7 copy-start.9
  14.0 15.4 %all-to-all-start = ((bf16[16,32,128]{2,1,0:T(8,128)(2,1)}), bf16[16,32,128]{2,1,0:T(8,128)(2,1)S(1)}, u32[]{:S(2)}, u32[]{:S(2)}) async-start(bf16[16,32,128]{2,1,0:T(8,128)(2,1)} %section.1.first_ref), calls=%async_computation | async-start | bytes 262144 | tf_op jit(solution)/shard_map/all_to_all | solution.py:499
  26.7 1.3 copy-start
  28.1 1.3 copy-start.3
  29.4 15.1 %copy-start.1 = (bf16[256,4096]{1,0:T(8,128)(2,1)S(1)}, bf16[256,4096]{1,0:T(8,128)(2,1)}, u32[]{:S(2)}) copy-start(bf16[256,4096]{1,0:T(8,128)(2,1)} %copy-done) | copy-start | bytes 6291460
  44.5 1.6 copy-start.4
  50.0 43.2 %copy-start.12 = (f32[2]{0:T(128)S(1)}, f32[2]{0:T(128)}, u32[]{:S(2)}) copy-start(f32[2]{0:T(128)} %step_ref.3) | copy-start | bytes 28
  63.7 54.5 %copy-start.2 = (bf16[256,4096]{1,0:T(8,128)(2,1)S(1)}, bf16[256,4096]{1,0:T(8,128)(2,1)}, u32[]{:S(2)}) copy-start(bf16[256,4096]{1,0:T(8,128)(2,1)} %copy-done) | copy-start | bytes 6291460
  63.7 54.4 %copy-start.5 = (bf16[256,4096]{1,0:T(8,128)(2,1)S(1)}, bf16[256,4096]{1,0:T(8,128)(2,1)}, u32[]{:S(2)}) copy-start(bf16[256,4096]{1,0:T(8,128)(2,1)} %copy-done.3) | copy-start | bytes 6291460
  134.2 1.0 copy-start.6
  135.1 28.1 %all-to-all-start.7 = ((bf16[128,16,256]{2,1,0:T(8,128)(2,1)}), bf16[128,16,256]{2,1,0:T(8,128)(2,1)S(1)}, u32[]{:S(2)}, u32[]{:S(2)}) async-start(bf16[128,16,256]{2,1,0:T(8,128)(2,1)} %bitcast.15), calls=%async_computation.7 | async-start | bytes 2097152 | tf_op jit(solution)/shard_map/all_to_all | solution.py:504
Sparse Core Ops, SparseCore 0:
  9.8 27.2 all-gather.1

commit v5 on v4

--- a/solution.py
+++ b/solution.py
@@ -515,8 +515,8 @@
     vis_obs,
     vis_weight,
 ):
-    lines = lax.optimization_barrier(jnp.broadcast_to(col_offsets[:, None].astype(F32), (256, 128)))
-    column_starts = lax.optimization_barrier(lax.all_gather(lines, "sub", axis=0, tiled=True))[::256, 0].astype(I32)
+    lines = lax.optimization_barrier(jnp.broadcast_to(col_offsets[:, None], (8, 128)))
+    column_starts = lax.optimization_barrier(lax.all_gather(lines, "sub", axis=0, tiled=True))[::8, 0]
     uv = vis_uv.reshape(2, VCAP)
     obs = vis_obs.reshape(2, VCAP)
     weight = vis_weight.reshape(1, VCAP)
@@ -526,7 +526,6 @@
     rows, kernels = tables[:3], tables[3:]
     grid = exchange(grids(exchange(first), rows))
     gridded, residual = visibilities(counts, obs, weight, grid, kernels)
-    gridded, column_starts = lax.optimization_barrier((gridded, column_starts))
     adj0 = to_facets(adjoint(exchange(gridded), rows))
     tables = update_tables(column_starts, facet_offsets)
     second = gram(step_sizes, column_starts, col_offsets, facet_offsets, adj0, first)

time: 185 us -> 177 us (0.957)
  between operations: 14.9 us -> 1.71 us
  starting transfers between devices: 16.4 us -> 27.5 us
  blocking collectives: 84.9 us -> 75.9 us
  waiting for transfers between devices: 14.5 us -> 18.2 us
    all_to_all x1 -> x0, blocking collectives: 29.5 us -> none  [to_facets(): lax.all_to_all(copies, ('facet', 'sub'), split_axis=0, concat_axis=0, til...]
    all_gather x0 -> x1, blocking collectives: none -> 15.4 us  [local(): lax.all_gather(lines, 'sub', axis=0, tiled=True)]
    all_to_all x1 -> x2, starting transfers between devices: 8.79 us -> 19.9 us  [to_facets(): lax.all_to_all(copies, ('facet', 'sub'), split_axis=0, concat_axis=0, til...]
    all_to_all x5, blocking collectives: 55.4 us -> 60.5 us  [exchange(): lax.all_to_all(value, 'facet', split_axis=0, concat_axis=0, tiled=True)]
    all_to_all x1 -> x2, waiting for transfers between devices: 14.4 us -> 18.2 us  [to_facets(): lax.all_to_all(copies, ('facet', 'sub'), split_axis=0, concat_axis=0, til...]
    unnamed x32 -> x34, local copies, waits for them, and re-layouts: 6.59 us -> 7.55 us
  transfers between devices with their start and end apart: 3 -> 3, of which waited for: 1 -> 2; matrix products, arithmetic and copies ran while one was open for 0% -> 0% of each run, Pallas kernels for 10% -> 5%
where the time goes in v5:
time: 177 us; the launch traced here: 176 us
  blocking collectives  75.9 us (43%)
  Pallas kernels  44.9 us (25%)
  starting transfers between devices  27.5 us (16%)
  waiting for transfers between devices  18.2 us (10%)
  local copies, waits for them, and re-layouts  7.57 us (4%)
    all_to_all x5, blocking collectives, exchange(): lax.all_to_all(value, 'facet', split_axis=0, concat_axis=0, tiled=True)  60.5 us
    all_to_all x2, starting transfers between devices, to_facets(): lax.all_to_all(copies, ('facet', 'sub'), split_axis=0, concat_axis=0, til...  19.9 us
    all_to_all x2, waiting for transfers between devices, to_facets(): lax.all_to_all(copies, ('facet', 'sub'), split_axis=0, concat_axis=0, til...  18.2 us
    all_gather x1, blocking collectives, local(): lax.all_gather(lines, 'sub', axis=0, tiled=True)  15.4 us
    pallas_call x1, Pallas kernels, update(): pl.pallas_call(update_kernel, grid=(HIGH5 // PAIR5 // 2,), out_shape=jax....  14 us
    all_to_all x1, starting transfers between devices, exchange(): lax.all_to_all(value, 'facet', split_axis=0, concat_axis=0, tiled=True)  7.6 us
    unnamed x34, local copies, waits for them, and re-layouts  7.55 us
    pallas_call x2, Pallas kernels, visibilities(): pl.pallas_call(visibility_kernel, out_shape=(jax.ShapeDtypeStruct((FACETS...  7.2 us
  transfers between devices with their start and end apart: 3, of which 2 were waited for; matrix products, arithmetic and copies ran while one was open for 0% of the time, Pallas kernels for 5%

profile of v5, /device:TPU:1, one launch (start us, length us, event | category | flops | bytes accessed | tf_op | source)
XLA Modules:
  0.0 175.9 jit_solution(15623591064759301128)
XLA Ops:
  1.3 0.7 copy-done.10
  2.0 4.7 %section.1.first_ref = bf16[16,32,128]{2,1,0:T(8,128)(2,1)} custom-call(s32[1]{0:T(128)} %copy.17.column_ref, s32[2,16]{1,0:T(2,128)S(1)} %copy-done.10, f32[128,8192]{1,0:T(8,128)} %bitcast.22), custom_call_target="tpu_custom_call" | custom-call | tf_op jit(solution)/shard_map/section/pallas_call | solution.py:124
  6.7 7.6 %all-to-all-start = ((bf16[16,32,128]{2,1,0:T(8,128)(2,1)}), bf16[16,32,128]{2,1,0:T(8,128)(2,1)S(1)}, u32[]{:S(2)}, u32[]{:S(2)}) async-start(bf16[16,32,128]{2,1,0:T(8,128)(2,1)} %section.1.first_ref), calls=%async_computation | async-start | bytes 262144 | tf_op jit(solution)/shard_map/all_to_all | solution.py:499
  14.4 5.1 %cycle_tables.1 = (bf16[2,2048,256]{2,1,0:T(8,128)(2,1)S(1)}, f32[16,16,128]{2,1,0:T(8,128)S(1)}, f32[16,16,128]{2,1,0:T(8,128)S(1)}, bf16[256,4096]{1,0:T(8,128)(2,1)S(1)}, bf16[256,4096]{1,0:T(8,128)(2,1)S(1)}) custom-call(s32[2,16]{1,0:T(2,128)S(1)} %copy-done.11, s32[1,16]{1,0:T(1,128)S(1)} %copy-done.14, s32[2,4096]{1,0:T(2,128)S(1)} %bitcast.16), custom_call_target="tpu_custom_call" | custom-call | tf_op jit(solution)/shard_map/cycle_tables/pallas_call | solution.py:179
  19.5 0.0 copy-start
  19.5 1.3 copy-done
  20.8 1.3 copy-done.3
  22.1 1.3 grids.2
  23.4 13.8 %all_to_all.40.in_ref = bf16[16,32,256]{2,1,0:T(8,128)(2,1)S(1)} all-to-all(bf16[16,32,256]{2,1,0:T(8,128)(2,1)S(1)} %grids.2), channel_id=1, replica_groups=mesh['facet'=16,'sub'=8] {'facet'}, dimensions={0} | all-to-all | bytes 524288 | tf_op jit(solution)/shard_map/all_to_all | solution.py:499
  37.2 1.6 copy-done.4
  38.8 3.9 %visibilities.2 = (bf16[16,32,256]{2,1,0:T(8,128)(2,1)S(1)}, f32[2,4096]{1,0:T(2,128)}) custom-call(s32[1,16]{1,0:T(1,128)S(1)} %copy-done.12, bf16[2,4096]{1,0:T(2,128)(2,1)S(1)} %bitcast.17, bf16[1,4096]{1,0:T(2,128)(2,1)S(1)} %bitcast.19, bf16[16,32,256]{2,1,0:T(8,128)(2,1)S(1)} %all_to_all.40.in_ref, bf16[256,4096]{1,0:T(8,128)(2,1)S(1)} %copy-done.1, ...), custom_call_target="tpu_custom_call" | custom-call | tf_op jit(solution)/shard_map/visibilities/pallas_call | solution.py:312
  42.7 0.0 copy-start.13
  42.8 10.8 %all_to_all.41.in_ref = bf16[16,32,256]{2,1,0:T(8,128)(2,1)S(1)} all-to-all(bf16[16,32,256]{2,1,0:T(8,128)(2,1)S(1)} %get-tuple-element.18), channel_id=1, replica_groups=mesh['facet'=16,'sub'=8] {'facet'}, dimensions={0} | all-to-all | bytes 524288 | tf_op jit(solution)/shard_map/all_to_all | solution.py:499
  53.5 1.8 adjoint.2
  55.3 1.0 copy-done.7
  56.3 10.5 %all-to-all-start.3 = ((bf16[128,16,256]{2,1,0:T(8,128)(2,1)}), bf16[128,16,256]{2,1,0:T(8,128)(2,1)S(1)}, u32[]{:S(2)}, u32[]{:S(2)}) async-start(bf16[128,16,256]{2,1,0:T(8,128)(2,1)} %bitcast.15), calls=%async_computation.3 | async-start | bytes 2097152 | tf_op jit(solution)/shard_map/all_to_all | solution.py:504
  66.7 15.4 %all_gather.3 = s32[64,128]{1,0:T(8,128)S(1)} all-gather(s32[8,128]{1,0:T(8,128)S(1)} %broadcast_in_dim.12), channel_id=1, replica_groups=mesh['facet'=16,'sub'=8] {'sub'}, dimensions={0}, use_global_device_ids=true | all-gather | bytes 36864 | tf_op jit(solution)/shard_map/all_gather | solution.py:519
  82.1 0.1 reduce.starts_ref
  82.2 3.8 %all-to-all-done.3.adj0_ref = bf16[128,16,256]{2,1,0:T(8,128)(2,1)S(1)} async-done(((bf16[128,16,256]{2,1,0:T(8,128)(2,1)}), bf16[128,16,256]{2,1,0:T(8,128)(2,1)S(1)}, u32[]{:S(2)}, u32[]{:S(2)}) %all-to-all-start.3) | async-done | bytes 1048608 | tf_op jit(solution)/shard_map/all_to_all | solution.py:504
  86.0 3.6 %gram.1 = bf16[16,32,128]{2,1,0:T(8,128)(2,1)S(1)} custom-call(f32[2]{0:T(128)S(1)} %copy-done.13, s32[8]{0:T(128)S(1)} %reduce.starts_ref, s32[1]{0:T(128)} %copy.17.column_ref, s32[2,16]{1,0:T(2,128)S(1)} %copy-done.11, bf16[16,8,16,256]{3,2,1,0:T(8,128)(2,1)S(1)} %bitcast.13, bf16[16,32,128]{2,1,0:T(8,128)(2,1)} %section.1.first_ref), custom_call_target="tpu_custom_call" | custom-call | tf_op jit(solution)/shard_map/gram/pallas_call | solution.py:372
  89.7 14.4 %all_to_all.42.in_ref = bf16[16,32,128]{2,1,0:T(8,128)(2,1)S(1)} all-to-all(bf16[16,32,128]{2,1,0:T(8,128)(2,1)S(1)} %gram.1), channel_id=1, replica_groups=mesh['facet'=16,'sub'=8] {'facet'}, dimensions={0} | all-to-all | bytes 262144 | tf_op jit(solution)/shard_map/all_to_all | solution.py:499
  104.1 1.3 grids.3
  105.4 10.7 %all_to_all.43.in_ref = bf16[16,32,256]{2,1,0:T(8,128)(2,1)S(1)} all-to-all(bf16[16,32,256]{2,1,0:T(8,128)(2,1)S(1)} %grids.3), channel_id=1, replica_groups=mesh['facet'=16,'sub'=8] {'facet'}, dimensions={0} | all-to-all | bytes 524288 | tf_op jit(solution)/shard_map/all_to_all | solution.py:499
  116.1 3.3 %visibilities.3 = (bf16[16,32,256]{2,1,0:T(8,128)(2,1)S(1)}, f32[2,4096]{1,0:T(2,128)S(1)}) custom-call(s32[1,16]{1,0:T(1,128)S(1)} %copy-done.12, bf16[2,4096]{1,0:T(2,128)(2,1)S(1)} %bitcast.18, bf16[1,4096]{1,0:T(2,128)(2,1)S(1)} %bitcast.20, bf16[16,32,256]{2,1,0:T(8,128)(2,1)S(1)} %all_to_all.43.in_ref, bf16[256,4096]{1,0:T(8,128)(2,1)S(1)} %copy-done.2, ...), custom_call_target="tpu_custom_call" | custom-call | tf_op jit(solution)/shard_map/visibilities/pallas_call | solution.py:312
  119.4 10.9 %all_to_all.44.in_ref = bf16[16,32,256]{2,1,0:T(8,128)(2,1)S(1)} all-to-all(bf16[16,32,256]{2,1,0:T(8,128)(2,1)S(1)} %get-tuple-element.19), channel_id=1, replica_groups=mesh['facet'=16,'sub'=8] {'facet'}, dimensions={0} | all-to-all | bytes 524288 | tf_op jit(solution)/shard_map/all_to_all | solution.py:499
  130.3 1.8 adjoint.3
  132.0 1.0 copy-done.6
  133.0 9.4 %all-to-all-start.7 = ((bf16[128,16,256]{2,1,0:T(8,128)(2,1)}), bf16[128,16,256]{2,1,0:T(8,128)(2,1)S(1)}, u32[]{:S(2)}, u32[]{:S(2)}) async-start(bf16[128,16,256]{2,1,0:T(8,128)(2,1)} %bitcast.14), calls=%async_computation.7 | async-start | bytes 2097152 | tf_op jit(solution)/shard_map/all_to_all | solution.py:504
  142.4 4.2 %update_tables.1 = (bf16[4096,512]{1,0:T(8,128)(2,1)}, f32[16,2048]{1,0:T(8,128)S(1)}, f32[16,2048]{1,0:T(8,128)S(1)}) custom-call(s32[8]{0:T(128)S(1)} %reduce.starts_ref, s32[2,16]{1,0:T(2,128)S(1)} %copy-done.11), custom_call_target="tpu_custom_call" | custom-call | tf_op jit(solution)/shard_map/update_tables/pallas_call | solution.py:478
  146.6 0.6 copy.13
  147.3 14.4 %all-to-all-done.7.adj1_ref = bf16[128,16,256]{2,1,0:T(8,128)(2,1)S(1)} async-done(((bf16[128,16,256]{2,1,0:T(8,128)(2,1)}), bf16[128,16,256]{2,1,0:T(8,128)(2,1)S(1)}, u32[]{:S(2)}, u32[]{:S(2)}) %all-to-all-start.7) | async-done | bytes 1048608 | tf_op jit(solution)/shard_map/all_to_all | solution.py:504
  161.7 14.0 %update.1 = f32[128,8192]{1,0:T(8,128)} custom-call(f32[2]{0:T(128)S(1)} %copy-done.13, bf16[128,16,256]{2,1,0:T(8,128)(2,1)S(1)} %all-to-all-done.3.adj0_ref, bf16[128,16,256]{2,1,0:T(8,128)(2,1)S(1)} %all-to-all-done.7.adj1_ref, bf16[4096,512]{1,0:T(8,128)(2,1)} %get-tuple-element.20.table_hbm, f32[16,2048]{1,0:T(8,128)S(1)} %get-tuple-element.21.pc_ref, ...), custom_call_target="tpu_custom_call" | custom-call | tf_op jit(solution)/shard_map/update/pallas_call | solution.py:431
  (28 shorter events, 0.1 us)
Async XLA Ops:
  0.6 36.6 %copy-start.8 = (bf16[2,1,1,4096]{3,0,2,1:T(2,128)(2,1)S(1)}, bf16[2,1,1,4096]{3,0,2,1:T(2,128)(2,1)}, u32[]{:S(2)}) copy-start(bf16[2,1,1,4096]{3,0,2,1:T(2,128)(2,1)} %param.16) | copy-start | bytes 49156
  0.6 36.6 %copy-start.9 = (bf16[1,1,4096]{2,1,0:T(2,128)(2,1)S(1)}, bf16[1,1,4096]{2,1,0:T(2,128)(2,1)}, u32[]{:S(2)}) copy-start(bf16[1,1,4096]{2,1,0:T(2,128)(2,1)} %param.17) | copy-start | bytes 24580
  1.3 0.7 copy-start.10
  2.0 12.4 %copy-start.15 = (s32[2,1,1,4096]{3,2,1,0:T(1,128)S(1)}, s32[2,1,1,4096]{3,2,1,0:T(1,128)}, u32[]{:S(2)}) copy-start(s32[2,1,1,4096]{3,2,1,0:T(1,128)} %param.15) | copy-start | bytes 98308
  2.0 12.4 %copy-start.11 = (s32[2,16]{1,0:T(2,128)S(1)}, s32[2,16]{1,0:T(2,128)}, u32[]{:S(2)}) copy-start(s32[2,16]{1,0:T(2,128)} %offsets_ref.7) | copy-start | bytes 388
  2.0 12.4 %copy-start.14 = (s32[1,16]{1,0:T(1,128)S(1)}, s32[1,16]{1,0:T(1,128)}, u32[]{:S(2)}) copy-start(s32[1,16]{1,0:T(1,128)} %rows_ref.1) | copy-start | bytes 196
  2.0 35.2 %copy-start.12 = (s32[1,16]{1,0:T(1,128)S(1)}, s32[1,16]{1,0:T(1,128)}, u32[]{:S(2)}) copy-start(s32[1,16]{1,0:T(1,128)} %counts_ref.3) | copy-start | bytes 196
  6.7 15.4 %all-to-all-start = ((bf16[16,32,128]{2,1,0:T(8,128)(2,1)}), bf16[16,32,128]{2,1,0:T(8,128)(2,1)S(1)}, u32[]{:S(2)}, u32[]{:S(2)}) async-start(bf16[16,32,128]{2,1,0:T(8,128)(2,1)} %section.1.first_ref), calls=%async_computation | async-start | bytes 262144 | tf_op jit(solution)/shard_map/all_to_all | solution.py:499
  19.5 1.3 copy-start
  20.8 1.3 copy-start.3
  22.1 15.1 %copy-start.1 = (bf16[256,4096]{1,0:T(8,128)(2,1)S(1)}, bf16[256,4096]{1,0:T(8,128)(2,1)}, u32[]{:S(2)}) copy-start(bf16[256,4096]{1,0:T(8,128)(2,1)} %copy-done) | copy-start | bytes 6291460
  37.2 1.6 copy-start.4
  42.7 43.3 %copy-start.13 = (f32[2]{0:T(128)S(1)}, f32[2]{0:T(128)}, u32[]{:S(2)}) copy-start(f32[2]{0:T(128)} %step_ref.3) | copy-start | bytes 28
  55.3 1.0 copy-start.7
  56.3 29.7 %all-to-all-start.3 = ((bf16[128,16,256]{2,1,0:T(8,128)(2,1)}), bf16[128,16,256]{2,1,0:T(8,128)(2,1)S(1)}, u32[]{:S(2)}, u32[]{:S(2)}) async-start(bf16[128,16,256]{2,1,0:T(8,128)(2,1)} %bitcast.15), calls=%async_computation.3 | async-start | bytes 2097152 | tf_op jit(solution)/shard_map/all_to_all | solution.py:504
  86.0 30.1 %copy-start.2 = (bf16[256,4096]{1,0:T(8,128)(2,1)S(1)}, bf16[256,4096]{1,0:T(8,128)(2,1)}, u32[]{:S(2)}) copy-start(bf16[256,4096]{1,0:T(8,128)(2,1)} %copy-done) | copy-start | bytes 6291460
  86.0 30.1 %copy-start.5 = (bf16[256,4096]{1,0:T(8,128)(2,1)S(1)}, bf16[256,4096]{1,0:T(8,128)(2,1)}, u32[]{:S(2)}) copy-start(bf16[256,4096]{1,0:T(8,128)(2,1)} %copy-done.3) | copy-start | bytes 6291460
  132.0 1.0 copy-start.6
  133.0 28.7 %all-to-all-start.7 = ((bf16[128,16,256]{2,1,0:T(8,128)(2,1)}), bf16[128,16,256]{2,1,0:T(8,128)(2,1)S(1)}, u32[]{:S(2)}, u32[]{:S(2)}) async-start(bf16[128,16,256]{2,1,0:T(8,128)(2,1)} %bitcast.14), calls=%async_computation.7 | async-start | bytes 2097152 | tf_op jit(solution)/shard_map/all_to_all | solution.py:504

commit v6 on v5

--- a/solution.py
+++ b/solution.py
@@ -25,7 +25,9 @@
 PARTS1 = 4
 STEP5 = 512
 HIGH5 = FW // STEP5
-PAIR5 = 2
+PAIR5 = 4
+HALF = FROWS // 2
+PARTS7 = 2
 VBLOCK = 1024
 CHUNK = 4
 UNROLL4 = 8
@@ -257,23 +259,25 @@
                 s = s_ref[f, r : r + 1, :]
                 acc_re = acc_re + (re * c - im * s)
                 acc_im = acc_im + (im * c + re * s)
-            out_ref[f] = jnp.concatenate([acc_re, acc_im], axis=1).astype(BF)
+            lower = iota((SLICE, FROWS), 1) < HALF
+            out_ref[0, f] = jnp.where(lower, acc_re, pltpu.roll(acc_im, HALF, 1)).astype(BF)
+            out_ref[1, f] = jnp.where(lower, pltpu.roll(acc_re, HALF, 1), acc_im).astype(BF)
         return carry
 
     lax.fori_loop(0, FACETS // 2, one, 0, unroll=UNROLL4)
-    write_out([(out_ref, out_hbm.at[:, copy], sems.at[copy]) for copy in range(NCOL)])
+    write_out([(out_ref.at[copy % 2], out_hbm.at[:, copy], sems.at[copy]) for copy in range(NCOL)])
 
 
 def adjoint(gridded, tables):
     table, c, s = tables
     return pl.pallas_call(
         adjoint_kernel,
-        out_shape=jax.ShapeDtypeStruct((FACETS, NCOL, SLICE, 2 * FROWS), BF),
+        out_shape=jax.ShapeDtypeStruct((FACETS, NCOL, SLICE, FROWS), BF),
         in_specs=[VMEM_SPEC] * 4,
         out_specs=HBM_SPEC,
         scratch_shapes=[
             pltpu.VMEM((2 * NROWSG * SLICE, SGW), BF),
-            pltpu.VMEM((FACETS, SLICE, 2 * FROWS), BF),
+            pltpu.VMEM((2, FACETS, SLICE, FROWS), BF),
             pltpu.SemaphoreType.DMA((NCOL,)),
         ],
         compiler_params=PARAMS,
@@ -336,7 +340,7 @@
     return c * ratio, s * ratio
 
 
-def gram_kernel(step_ref, starts_ref, column_ref, offsets_ref, adj_ref, first_ref, out_hbm, flip_ref, v_ref, out_ref, sem):
+def gram_kernel(step_ref, starts_ref, column_ref, offsets_ref, mine_ref, theirs_ref, first_ref, out_hbm, flip_ref, v_ref, out_ref, sem):
     wide = 2 * SGW
     pixel_start = offsets_ref[1, lax.axis_index("facet")]
     own = column_ref[0]
@@ -351,7 +355,8 @@
     flip_ref[...] = jnp.where(anti, 1.0, 0.0).astype(BF)
     totals = [None] * 4
     for c in range(NCOL):
-        lines = adj_ref[:, c].reshape(SGW, 2 * FROWS)
+        lines = [half_ref[:, c].reshape(SGW, FROWS) for half_ref in (mine_ref, theirs_ref)]
+        lines = jnp.concatenate(lines, axis=1)
         turned = jnp.dot(flip_ref[...], lines, preferred_element_type=F32).astype(BF)
         for k in range(4):
             spread = jnp.broadcast_to(v_ref[k, c : c + 1, :], (SGW, wide))
@@ -360,19 +365,32 @@
             totals[k] = term if c == 0 else totals[k] + term
     scale = step_ref[0] * (0.5 * NORM)
     p1, p2, p3, p4 = totals
-    re = p1[:, :FROWS] - p2[:, FROWS:] + p3[:, :FROWS] - p4[:, FROWS:]
-    im = p2[:, :FROWS] + p1[:, FROWS:] - p4[:, :FROWS] - p3[:, FROWS:]
+    upper = (lax.axis_index("sub") & 1) == 1
+    left = iota((SGW, FROWS), 1) < HALF
+
+    def joined(straight, crossed):
+        mine, theirs = [
+            straight[:, k * FROWS : (k + 1) * FROWS] + pltpu.roll(crossed[:, k * FROWS : (k + 1) * FROWS], HALF, 1)
+            for k in range(2)
+        ]
+        low = jnp.where(upper, theirs, mine)
+        high = jnp.where(upper, mine, theirs)
+        return jnp.where(left, low, pltpu.roll(high, HALF, 1))
+
+    re = joined(p1 + p3, -(p2 + p4))
+    im = joined(p2 - p4, p1 - p3)
     first = first_ref[...].astype(F32)
     out_ref[:, :SLICE, :] = (first[:, :SLICE] + (scale * re).reshape(FACETS, SLICE, FROWS)).astype(BF)
     out_ref[:, SLICE:, :] = (first[:, SLICE:] + (scale * im).reshape(FACETS, SLICE, FROWS)).astype(BF)
     write_out([(out_ref, out_hbm, sem)])
 
 
-def gram(steps, column_starts, column_start, offsets, adj, first):
+def gram(steps, column_starts, column_start, offsets, mine, theirs, first):
+    shape = (FACETS, NCOL, SLICE, FROWS)
     return pl.pallas_call(
         gram_kernel,
         out_shape=jax.ShapeDtypeStruct((FACETS, 2 * SLICE, FROWS), BF),
-        in_specs=[SMEM_SPEC] * 4 + [VMEM_SPEC] * 2,
+        in_specs=[SMEM_SPEC] * 4 + [VMEM_SPEC] * 3,
         out_specs=HBM_SPEC,
         scratch_shapes=[
             pltpu.VMEM((SGW, SGW), BF),
@@ -382,68 +400,88 @@
         ],
         compiler_params=PARAMS,
         name="gram",
-    )(steps, column_starts, column_start, offsets, on_chip(adj.reshape(FACETS, NCOL, SLICE, 2 * FROWS)), first)
-
-
-def update_kernel(step_ref, adj0_ref, adj1_ref, table_hbm, pc_ref, ps_ref, model_ref, out_ref, table_ref, both_ref, even_ref, odd_ref, sem):
+    )(steps, column_starts, column_start, offsets, on_chip(mine.reshape(shape)), on_chip(theirs.reshape(shape)), first)
+
+
+def update_kernel(step_ref, adj0_ref, adj1_ref, table_hbm, pc_ref, ps_ref, out_ref, table_ref, both_ref, even_ref, odd_ref, sem):
     part = pl.program_id(0)
     fetch = pltpu.make_async_copy(table_hbm, table_ref, sem)
 
-    def turn(pair, target_ref):
-        re = both_ref[:FROWS, :]
-        im = both_ref[FROWS:, :]
+    def turn(group, target_ref):
+        re = both_ref[:HALF, :]
+        im = both_ref[HALF:, :]
         for p in range(PAIR5):
-            pc = pc_ref[pl.ds(pair * PAIR5 + p, 1), :]
-            ps = ps_ref[pl.ds(pair * PAIR5 + p, 1), :]
-            lines = slice(p * FROWS, (p + 1) * FROWS)
+            pc = pc_ref[pl.ds(group * PAIR5 + p, 1), :]
+            ps = ps_ref[pl.ds(group * PAIR5 + p, 1), :]
+            lines = slice(p * HALF, (p + 1) * HALF)
             target_ref[lines, :COLUMNS] = (re * pc - im * ps).astype(BF)
             target_ref[lines, COLUMNS:] = (im * pc + re * ps).astype(BF)
 
-    def add(place, source_ref):
-        gradient = jnp.dot(source_ref[...], table_ref[...], preferred_element_type=F32)
+    def put(place, source_ref):
+        gradient = jnp.dot(source_ref[...], table_ref[...], preferred_element_type=F32).astype(BF)
         for p in range(PAIR5):
             left = (place * PAIR5 + p) * STEP5
-            lines = gradient[p * FROWS : (p + 1) * FROWS]
-            out_ref[:, left : left + STEP5] = model_ref[:, left : left + STEP5] + lines
+            out_ref[:, left : left + STEP5] = gradient[p * HALF : (p + 1) * HALF]
 
     @pl.when(part == 0)
     def _():
         fetch.start()
         first = step_ref[0] * NORM
         second = step_ref[1] * NORM
+        group = NCOL * SLICE
         for j in range(FACETS):
-            lines0 = adj0_ref[j * NCOL : (j + 1) * NCOL].reshape(NCOL * SLICE, 2 * FROWS).astype(F32)
-            lines1 = adj1_ref[j * NCOL : (j + 1) * NCOL].reshape(NCOL * SLICE, 2 * FROWS).astype(F32)
-            both = first * lines0 + second * lines1
-            both_ref[:, j * NCOL * SLICE : (j + 1) * NCOL * SLICE] = both.T
+            lines0 = adj0_ref[j * NCOL : (j + 1) * NCOL].reshape(group, FROWS).astype(F32)
+            lines1 = adj1_ref[j * NCOL : (j + 1) * NCOL].reshape(group, FROWS).astype(F32)
+            both_ref[:, j * group : (j + 1) * group] = (first * lines0 + second * lines1).T
         turn(0, even_ref)
         fetch.wait()
 
     turn(2 * part + 1, odd_ref)
-    add(0, even_ref)
+    put(0, even_ref)
     turn(jnp.minimum(2 * part + 2, HIGH5 // PAIR5 - 2), even_ref)
-    add(1, odd_ref)
-
-
-def update(steps, adj0, adj1, tables, model):
+    put(1, odd_ref)
+
+
+def update(steps, adj0, adj1, tables):
     table, pc, ps = tables
-    wide = pl.BlockSpec((FROWS, 2 * PAIR5 * STEP5), lambda i: (0, i))
     return pl.pallas_call(
         update_kernel,
         grid=(HIGH5 // PAIR5 // 2,),
-        out_shape=jax.ShapeDtypeStruct((FROWS, FW), F32),
-        in_specs=[SMEM_SPEC, VMEM_SPEC, VMEM_SPEC, HBM_SPEC, VMEM_SPEC, VMEM_SPEC, wide],
-        out_specs=wide,
+        out_shape=jax.ShapeDtypeStruct((HALF, FW), BF),
+        in_specs=[SMEM_SPEC, VMEM_SPEC, VMEM_SPEC, HBM_SPEC, VMEM_SPEC, VMEM_SPEC],
+        out_specs=pl.BlockSpec((HALF, 2 * PAIR5 * STEP5), lambda i: (0, i)),
         scratch_shapes=[
             pltpu.VMEM((2 * COLUMNS, STEP5), BF),
-            pltpu.VMEM((2 * FROWS, COLUMNS), F32),
-            pltpu.VMEM((PAIR5 * FROWS, 2 * COLUMNS), BF),
-            pltpu.VMEM((PAIR5 * FROWS, 2 * COLUMNS), BF),
+            pltpu.VMEM((FROWS, COLUMNS), F32),
+            pltpu.VMEM((PAIR5 * HALF, 2 * COLUMNS), BF),
+            pltpu.VMEM((PAIR5 * HALF, 2 * COLUMNS), BF),
             pltpu.SemaphoreType.DMA,
         ],
         compiler_params=WIDE_PARAMS,
         name="update",
-    )(steps, on_chip(adj0), on_chip(adj1), off_chip(table), on_chip(pc), on_chip(ps), off_chip(model))
+    )(steps, on_chip(adj0), on_chip(adj1), off_chip(table), on_chip(pc), on_chip(ps))
+
+
+def step_kernel(mine_ref, theirs_ref, model_ref, out_ref):
+    upper = (lax.axis_index("sub") & 1) == 1
+    mine = mine_ref[...].astype(F32)
+    theirs = theirs_ref[...].astype(F32)
+    out_ref[:HALF] = model_ref[:HALF] + jnp.where(upper, theirs, mine)
+    out_ref[HALF:] = model_ref[HALF:] + jnp.where(upper, mine, theirs)
+
+
+def take_step(mine, theirs, model):
+    part = pl.BlockSpec((HALF, FW // PARTS7), lambda i: (0, i))
+    wide = pl.BlockSpec((FROWS, FW // PARTS7), lambda i: (0, i))
+    return pl.pallas_call(
+        step_kernel,
+        grid=(PARTS7,),
+        out_shape=jax.ShapeDtypeStruct((FROWS, FW), F32),
+        in_specs=[part, part, wide],
+        out_specs=wide,
+        compiler_params=PARAMS,
+        name="take_step",
+    )(mine, theirs, off_chip(model))
 
 
 def update_table_kernel(starts_ref, offsets_ref, table_hbm, pc_ref, ps_ref, table_ref, base_ref, turn_ref, sem):
@@ -497,6 +535,10 @@
 
 def exchange(value):
     return lax.all_to_all(value, "facet", split_axis=0, concat_axis=0, tiled=True)
+
+
+def other_core(value):
+    return lax.ppermute(value, "sub", [(i, i ^ 1) for i in range(NCOL)])
 
 
 def to_facets(value):
@@ -527,12 +569,14 @@
     grid = exchange(grids(exchange(first), rows))
     gridded, residual = visibilities(counts, obs, weight, grid, kernels)
     adj0 = to_facets(adjoint(exchange(gridded), rows))
-    tables = update_tables(column_starts, facet_offsets)
-    second = gram(step_sizes, column_starts, col_offsets, facet_offsets, adj0, first)
+    adj0, column_starts = lax.optimization_barrier((adj0, column_starts))
+    second = gram(step_sizes, column_starts, col_offsets, facet_offsets, adj0, other_core(adj0), first)
     grid = exchange(grids(exchange(second), rows))
     gridded, residual = visibilities(counts, obs, weight, grid, kernels)
     adj1 = to_facets(adjoint(exchange(gridded), rows))
-    model = update(step_sizes, adj0, adj1, tables, model)
+    tables = update_tables(column_starts, facet_offsets)
+    step = update(step_sizes, adj0, adj1, tables)
+    model = take_step(step, other_core(step), model)
     return model[None], residual.reshape(2, 1, 1, VCAP)
 
 

time: 177 us -> 169 us (0.955)
  waiting for transfers between devices: 18.2 us -> 12.6 us
  local copies, waits for them, and re-layouts: 7.57 us -> 5.63 us
    all_to_all x2, waiting for transfers between devices: 18.2 us -> 9.42 us  [to_facets(): lax.all_to_all(copies, ('facet', 'sub'), split_axis=0, concat_axis=0, til...]
    pallas_call x1, Pallas kernels: 14 us -> 7.52 us  [update(): pl.pallas_call(update_kernel, grid=(HIGH5 // PAIR5 // 2,), out_shape=jax....]
    pallas_call x0 -> x1, Pallas kernels: none -> 3.95 us  [take_step(): pl.pallas_call(step_kernel, grid=(PARTS7,), out_shape=jax.ShapeDtypeStruc...]
    ppermute x0 -> x2, waiting for transfers between devices: none -> 3.17 us  [other_core(): return lax.ppermute(value, 'sub', [(i, i ^ 1) for i in range(NCOL)])]
    ppermute x0 -> x2, starting transfers between devices: none -> 1.97 us  [other_core(): return lax.ppermute(value, 'sub', [(i, i ^ 1) for i in range(NCOL)])]
    unnamed x34 -> x30, local copies, waits for them, and re-layouts: 7.55 us -> 5.61 us
  transfers between devices with their start and end apart: 3 -> 5, of which waited for: 2 -> 3; matrix products, arithmetic and copies ran while one was open for 0% -> 0% of each run, Pallas kernels for 5% -> 6%
where the time goes in v6:
time: 169 us; the launch traced here: 168 us
  blocking collectives  76 us (45%)
  Pallas kernels  44.1 us (26%)
  starting transfers between devices  27.9 us (17%)
  waiting for transfers between devices  12.6 us (7%)
  local copies, waits for them, and re-layouts  5.63 us (3%)
    all_to_all x5, blocking collectives, exchange(): lax.all_to_all(value, 'facet', split_axis=0, concat_axis=0, tiled=True)  62.1 us
    all_to_all x2, starting transfers between devices, to_facets(): lax.all_to_all(copies, ('facet', 'sub'), split_axis=0, concat_axis=0, til...  18.3 us
    all_gather x1, blocking collectives, local(): lax.all_gather(lines, 'sub', axis=0, tiled=True)  13.9 us
    all_to_all x2, waiting for transfers between devices, to_facets(): lax.all_to_all(copies, ('facet', 'sub'), split_axis=0, concat_axis=0, til...  9.42 us
    all_to_all x1, starting transfers between devices, exchange(): lax.all_to_all(value, 'facet', split_axis=0, concat_axis=0, tiled=True)  7.6 us
    pallas_call x1, Pallas kernels, update(): pl.pallas_call(update_kernel, grid=(HIGH5 // PAIR5 // 2,), out_shape=jax....  7.52 us
    pallas_call x2, Pallas kernels, visibilities(): pl.pallas_call(visibility_kernel, out_shape=(jax.ShapeDtypeStruct((FACETS...  7.29 us
    unnamed x30, local copies, waits for them, and re-layouts  5.61 us
  transfers between devices with their start and end apart: 5, of which 3 were waited for; matrix products, arithmetic and copies ran while one was open for 0% of the time, Pallas kernels for 6%

profile of v6, /device:TPU:1, one launch (start us, length us, event | category | flops | bytes accessed | tf_op | source)
XLA Modules:
  0.0 168.0 jit_solution(3591047628858225789)
XLA Ops:
  1.3 0.7 copy-done.8
  2.0 4.7 %section.1.first_ref = bf16[16,32,128]{2,1,0:T(8,128)(2,1)} custom-call(s32[1]{0:T(128)} %copy.17.column_ref, s32[2,16]{1,0:T(2,128)S(1)} %copy-done.8, f32[128,8192]{1,0:T(8,128)} %bitcast.22), custom_call_target="tpu_custom_call" | custom-call | tf_op jit(solution)/shard_map/section/pallas_call | solution.py:126
  6.7 7.6 %all-to-all-start = ((bf16[16,32,128]{2,1,0:T(8,128)(2,1)}), bf16[16,32,128]{2,1,0:T(8,128)(2,1)S(1)}, u32[]{:S(2)}, u32[]{:S(2)}) async-start(bf16[16,32,128]{2,1,0:T(8,128)(2,1)} %section.1.first_ref), calls=%async_computation | async-start | bytes 262144 | tf_op jit(solution)/shard_map/all_to_all | solution.py:537
  14.4 5.1 %cycle_tables.1 = (bf16[2,2048,256]{2,1,0:T(8,128)(2,1)S(1)}, f32[16,16,128]{2,1,0:T(8,128)S(1)}, f32[16,16,128]{2,1,0:T(8,128)S(1)}, bf16[256,4096]{1,0:T(8,128)(2,1)S(1)}, bf16[256,4096]{1,0:T(8,128)(2,1)S(1)}) custom-call(s32[2,16]{1,0:T(2,128)S(1)} %copy-done.9, s32[1,16]{1,0:T(1,128)S(1)} %copy-done.12, s32[2,4096]{1,0:T(2,128)S(1)} %bitcast.16), custom_call_target="tpu_custom_call" | custom-call | tf_op jit(solution)/shard_map/cycle_tables/pallas_call | solution.py:181
  19.5 1.3 copy-done
  20.8 1.3 copy-done.3
  22.1 1.3 grids.2
  23.4 13.8 %all_to_all.40.in_ref = bf16[16,32,256]{2,1,0:T(8,128)(2,1)S(1)} all-to-all(bf16[16,32,256]{2,1,0:T(8,128)(2,1)S(1)} %grids.2), channel_id=1, replica_groups=mesh['facet'=16,'sub'=8] {'facet'}, dimensions={0} | all-to-all | bytes 524288 | tf_op jit(solution)/shard_map/all_to_all | solution.py:537
  37.3 1.6 copy-done.4
  38.8 4.0 %visibilities.2 = (bf16[16,32,256]{2,1,0:T(8,128)(2,1)S(1)}, f32[2,4096]{1,0:T(2,128)}) custom-call(s32[1,16]{1,0:T(1,128)S(1)} %copy-done.10, bf16[2,4096]{1,0:T(2,128)(2,1)S(1)} %bitcast.17, bf16[1,4096]{1,0:T(2,128)(2,1)S(1)} %bitcast.19, bf16[16,32,256]{2,1,0:T(8,128)(2,1)S(1)} %all_to_all.40.in_ref, bf16[256,4096]{1,0:T(8,128)(2,1)S(1)} %copy-done.1, ...), custom_call_target="tpu_custom_call" | custom-call | tf_op jit(solution)/shard_map/visibilities/pallas_call | solution.py:316
  42.8 10.8 %all_to_all.41.in_ref = bf16[16,32,256]{2,1,0:T(8,128)(2,1)S(1)} all-to-all(bf16[16,32,256]{2,1,0:T(8,128)(2,1)S(1)} %get-tuple-element.20), channel_id=1, replica_groups=mesh['facet'=16,'sub'=8] {'facet'}, dimensions={0} | all-to-all | bytes 524288 | tf_op jit(solution)/shard_map/all_to_all | solution.py:537
  53.6 2.5 %adjoint.2 = bf16[16,8,16,128]{3,2,1,0:T(8,128)(2,1)} custom-call(bf16[16,32,256]{2,1,0:T(8,128)(2,1)S(1)} %all_to_all.41.in_ref, f32[16,16,128]{2,1,0:T(8,128)S(1)} %get-tuple-element.15.c_ref, f32[16,16,128]{2,1,0:T(8,128)S(1)} %get-tuple-element.16.s_ref, bf16[2,2048,256]{2,1,0:T(8,128)(2,1)S(1)} %get-tuple-element.17.table_ref), custom_call_target="tpu_custom_call" | custom-call | tf_op jit(solution)/shard_map/adjoint/pallas_call | solution.py:273
  56.1 10.4 %all-to-all-start.3 = ((bf16[128,16,128]{2,1,0:T(8,128)(2,1)}), bf16[128,16,128]{2,1,0:T(8,128)(2,1)S(1)}, u32[]{:S(2)}, u32[]{:S(2)}) async-start(bf16[128,16,128]{2,1,0:T(8,128)(2,1)} %bitcast.3), calls=%async_computation.3 | async-start | bytes 1048576 | tf_op jit(solution)/shard_map/all_to_all | solution.py:546
  66.6 13.9 %all_gather.3 = s32[64,128]{1,0:T(8,128)S(1)} all-gather(s32[8,128]{1,0:T(8,128)S(1)} %broadcast_in_dim.12), channel_id=1, replica_groups=mesh['facet'=16,'sub'=8] {'sub'}, dimensions={0}, use_global_device_ids=true | all-gather | bytes 36864 | tf_op jit(solution)/shard_map/all_gather | solution.py:561
  80.5 0.1 reduce.starts_ref
  80.7 0.8 collective-permute-start
  81.4 1.5 collective-permute-done
  83.0 3.7 %gram.1 = bf16[16,32,128]{2,1,0:T(8,128)(2,1)S(1)} custom-call(f32[2]{0:T(128)S(1)} %copy-done.11, s32[8]{0:T(128)S(1)} %reduce.starts_ref, s32[1]{0:T(128)} %copy.17.column_ref, s32[2,16]{1,0:T(2,128)S(1)} %copy-done.9, bf16[16,8,16,128]{3,2,1,0:T(8,128)(2,1)S(1)} %bitcast.14, bf16[16,8,16,128]{3,2,1,0:T(8,128)(2,1)S(1)} %bitcast.15, ...), custom_call_target="tpu_custom_call" | custom-call | tf_op jit(solution)/shard_map/gram/pallas_call | solution.py:390
  86.7 16.0 %all_to_all.42.in_ref = bf16[16,32,128]{2,1,0:T(8,128)(2,1)S(1)} all-to-all(bf16[16,32,128]{2,1,0:T(8,128)(2,1)S(1)} %gram.1), channel_id=1, replica_groups=mesh['facet'=16,'sub'=8] {'facet'}, dimensions={0} | all-to-all | bytes 262144 | tf_op jit(solution)/shard_map/all_to_all | solution.py:537
  102.7 1.3 grids.3
  104.0 10.7 %all_to_all.43.in_ref = bf16[16,32,256]{2,1,0:T(8,128)(2,1)S(1)} all-to-all(bf16[16,32,256]{2,1,0:T(8,128)(2,1)S(1)} %grids.3), channel_id=1, replica_groups=mesh['facet'=16,'sub'=8] {'facet'}, dimensions={0} | all-to-all | bytes 524288 | tf_op jit(solution)/shard_map/all_to_all | solution.py:537
  114.7 3.3 %visibilities.3 = (bf16[16,32,256]{2,1,0:T(8,128)(2,1)S(1)}, f32[2,4096]{1,0:T(2,128)S(1)}) custom-call(s32[1,16]{1,0:T(1,128)S(1)} %copy-done.10, bf16[2,4096]{1,0:T(2,128)(2,1)S(1)} %bitcast.18, bf16[1,4096]{1,0:T(2,128)(2,1)S(1)} %bitcast.20, bf16[16,32,256]{2,1,0:T(8,128)(2,1)S(1)} %all_to_all.43.in_ref, bf16[256,4096]{1,0:T(8,128)(2,1)S(1)} %copy-done.2, ...), custom_call_target="tpu_custom_call" | custom-call | tf_op jit(solution)/shard_map/visibilities/pallas_call | solution.py:316
  118.0 10.9 %all_to_all.44.in_ref = bf16[16,32,256]{2,1,0:T(8,128)(2,1)S(1)} all-to-all(bf16[16,32,256]{2,1,0:T(8,128)(2,1)S(1)} %get-tuple-element.23), channel_id=1, replica_groups=mesh['facet'=16,'sub'=8] {'facet'}, dimensions={0} | all-to-all | bytes 524288 | tf_op jit(solution)/shard_map/all_to_all | solution.py:537
  128.9 2.5 %adjoint.3 = bf16[16,8,16,128]{3,2,1,0:T(8,128)(2,1)} custom-call(bf16[16,32,256]{2,1,0:T(8,128)(2,1)S(1)} %all_to_all.44.in_ref, f32[16,16,128]{2,1,0:T(8,128)S(1)} %get-tuple-element.15.c_ref, f32[16,16,128]{2,1,0:T(8,128)S(1)} %get-tuple-element.16.s_ref, bf16[2,2048,256]{2,1,0:T(8,128)(2,1)S(1)} %get-tuple-element.17.table_ref), custom_call_target="tpu_custom_call" | custom-call | tf_op jit(solution)/shard_map/adjoint/pallas_call | solution.py:273
  131.4 7.9 %all-to-all-start.7 = ((bf16[128,16,128]{2,1,0:T(8,128)(2,1)}), bf16[128,16,128]{2,1,0:T(8,128)(2,1)S(1)}, u32[]{:S(2)}, u32[]{:S(2)}) async-start(bf16[128,16,128]{2,1,0:T(8,128)(2,1)} %bitcast.7), calls=%async_computation.7 | async-start | bytes 1048576 | tf_op jit(solution)/shard_map/all_to_all | solution.py:546
  139.3 4.2 %update_tables.1 = (bf16[4096,512]{1,0:T(8,128)(2,1)}, f32[16,2048]{1,0:T(8,128)S(1)}, f32[16,2048]{1,0:T(8,128)S(1)}) custom-call(s32[8]{0:T(128)S(1)} %reduce.starts_ref, s32[2,16]{1,0:T(2,128)S(1)} %copy-done.9), custom_call_target="tpu_custom_call" | custom-call | tf_op jit(solution)/shard_map/update_tables/pallas_call | solution.py:516
  143.6 9.4 %all-to-all-done.7.adj1_ref = bf16[128,16,128]{2,1,0:T(8,128)(2,1)S(1)} async-done(((bf16[128,16,128]{2,1,0:T(8,128)(2,1)}), bf16[128,16,128]{2,1,0:T(8,128)(2,1)S(1)}, u32[]{:S(2)}, u32[]{:S(2)}) %all-to-all-start.7) | async-done | bytes 524320 | tf_op jit(solution)/shard_map/all_to_all | solution.py:546
  153.0 7.5 %update.1.mine_ref = bf16[64,8192]{1,0:T(8,128)(2,1)S(1)} custom-call(f32[2]{0:T(128)S(1)} %copy-done.11, bf16[128,16,128]{2,1,0:T(8,128)(2,1)S(1)} %all-to-all-done.3.adj0_ref, bf16[128,16,128]{2,1,0:T(8,128)(2,1)S(1)} %all-to-all-done.7.adj1_ref, bf16[4096,512]{1,0:T(8,128)(2,1)} %get-tuple-element.24.table_hbm, f32[16,2048]{1,0:T(8,128)S(1)} %get-tuple-element.25.pc_ref, ...), custom_call_target="tpu_custom_call" | custom-call | tf_op jit(solution)/shard_map/update/pallas_call | solution.py:447
  160.5 1.2 collective-permute-start.1
  161.7 0.6 copy.13
  162.4 1.6 collective-permute-done.1.theirs_ref
  164.0 4.0 %take_step.1 = f32[128,8192]{1,0:T(8,128)} custom-call(bf16[64,8192]{1,0:T(8,128)(2,1)S(1)} %update.1.mine_ref, bf16[64,8192]{1,0:T(8,128)(2,1)S(1)} %collective-permute-done.1.theirs_ref, f32[128,8192]{1,0:T(8,128)} %bitcast.23), custom_call_target="tpu_custom_call" | custom-call | tf_op jit(solution)/shard_map/take_step/pallas_call | solution.py:476
  (29 shorter events, 0.1 us)
Async XLA Ops:
  0.6 36.6 %copy-start.7 = (bf16[1,1,4096]{2,1,0:T(2,128)(2,1)S(1)}, bf16[1,1,4096]{2,1,0:T(2,128)(2,1)}, u32[]{:S(2)}) copy-start(bf16[1,1,4096]{2,1,0:T(2,128)(2,1)} %param.17) | copy-start | bytes 24580
  0.6 36.6 %copy-start.6 = (bf16[2,1,1,4096]{3,0,2,1:T(2,128)(2,1)S(1)}, bf16[2,1,1,4096]{3,0,2,1:T(2,128)(2,1)}, u32[]{:S(2)}) copy-start(bf16[2,1,1,4096]{3,0,2,1:T(2,128)(2,1)} %param.16) | copy-start | bytes 49156
  1.3 0.7 copy-start.8
  2.0 12.4 %copy-start.13 = (s32[2,1,1,4096]{3,2,1,0:T(1,128)S(1)}, s32[2,1,1,4096]{3,2,1,0:T(1,128)}, u32[]{:S(2)}) copy-start(s32[2,1,1,4096]{3,2,1,0:T(1,128)} %param.15) | copy-start | bytes 98308
  2.0 12.4 %copy-start.9 = (s32[2,16]{1,0:T(2,128)S(1)}, s32[2,16]{1,0:T(2,128)}, u32[]{:S(2)}) copy-start(s32[2,16]{1,0:T(2,128)} %offsets_ref.7) | copy-start | bytes 388
  2.0 12.4 %copy-start.12 = (s32[1,16]{1,0:T(1,128)S(1)}, s32[1,16]{1,0:T(1,128)}, u32[]{:S(2)}) copy-start(s32[1,16]{1,0:T(1,128)} %rows_ref.1) | copy-start | bytes 196
  2.0 35.2 %copy-start.10 = (s32[1,16]{1,0:T(1,128)S(1)}, s32[1,16]{1,0:T(1,128)}, u32[]{:S(2)}) copy-start(s32[1,16]{1,0:T(1,128)} %counts_ref.3) | copy-start | bytes 196
  6.7 15.4 %all-to-all-start = ((bf16[16,32,128]{2,1,0:T(8,128)(2,1)}), bf16[16,32,128]{2,1,0:T(8,128)(2,1)S(1)}, u32[]{:S(2)}, u32[]{:S(2)}) async-start(bf16[16,32,128]{2,1,0:T(8,128)(2,1)} %section.1.first_ref), calls=%async_computation | async-start | bytes 262144 | tf_op jit(solution)/shard_map/all_to_all | solution.py:537
  19.5 1.3 copy-start
  20.8 1.3 copy-start.3
  22.1 15.1 %copy-start.1 = (bf16[256,4096]{1,0:T(8,128)(2,1)S(1)}, bf16[256,4096]{1,0:T(8,128)(2,1)}, u32[]{:S(2)}) copy-start(bf16[256,4096]{1,0:T(8,128)(2,1)} %copy-done) | copy-start | bytes 6291460
  37.2 1.6 copy-start.4
  38.8 44.1 %copy-start.11 = (f32[2]{0:T(128)S(1)}, f32[2]{0:T(128)}, u32[]{:S(2)}) copy-start(f32[2]{0:T(128)} %step_ref.3) | copy-start | bytes 28
  56.1 24.5 %all-to-all-start.3 = ((bf16[128,16,128]{2,1,0:T(8,128)(2,1)}), bf16[128,16,128]{2,1,0:T(8,128)(2,1)S(1)}, u32[]{:S(2)}, u32[]{:S(2)}) async-start(bf16[128,16,128]{2,1,0:T(8,128)(2,1)} %bitcast.3), calls=%async_computation.3 | async-start | bytes 1048576 | tf_op jit(solution)/shard_map/all_to_all | solution.py:546
  80.7 34.0 %copy-start.2 = (bf16[256,4096]{1,0:T(8,128)(2,1)S(1)}, bf16[256,4096]{1,0:T(8,128)(2,1)}, u32[]{:S(2)}) copy-start(bf16[256,4096]{1,0:T(8,128)(2,1)} %copy-done) | copy-start | bytes 6291460
  80.7 34.0 %copy-start.5 = (bf16[256,4096]{1,0:T(8,128)(2,1)S(1)}, bf16[256,4096]{1,0:T(8,128)(2,1)}, u32[]{:S(2)}) copy-start(bf16[256,4096]{1,0:T(8,128)(2,1)} %copy-done.3) | copy-start | bytes 6291460
  80.7 2.3 %collective-permute-start = (bf16[128,16,128]{2,1,0:T(8,128)(2,1)S(1)}, bf16[128,16,128]{2,1,0:T(8,128)(2,1)S(1)}, u32[]{:S(2)}, u32[]{:S(2)}) collective-permute-start(bf16[128,16,128]{2,1,0:T(8,128)(2,1)S(1)} %all-to-all-done.3.adj0_ref), channel_id=1, source_target_pairs={{0,1},{1,0},{2,3},{3,2},{4,5},{5,4},{6,7},{7,6},{8,9},{9,8},{10,11... | collective-permute-start | bytes 1572872 | tf_op jit(solution)/shard_map/ppermute | solution.py:541
  131.4 21.6 %all-to-all-start.7 = ((bf16[128,16,128]{2,1,0:T(8,128)(2,1)}), bf16[128,16,128]{2,1,0:T(8,128)(2,1)S(1)}, u32[]{:S(2)}, u32[]{:S(2)}) async-start(bf16[128,16,128]{2,1,0:T(8,128)(2,1)} %bitcast.7), calls=%async_computation.7 | async-start | bytes 1048576 | tf_op jit(solution)/shard_map/all_to_all | solution.py:546
  160.5 3.5 %collective-permute-start.1 = (bf16[64,8192]{1,0:T(8,128)(2,1)S(1)}, bf16[64,8192]{1,0:T(8,128)(2,1)S(1)}, u32[]{:S(2)}, u32[]{:S(2)}) collective-permute-start(bf16[64,8192]{1,0:T(8,128)(2,1)S(1)} %update.1.mine_ref), channel_id=1, source_target_pairs={{0,1},{1,0},{2,3},{3,2},{4,5},{5,4},{6,7},{7,6},{8,9},{9,8},{10,11... | collective-permute-start | bytes 3145736 | tf_op jit(solution)/shard_map/ppermute | solution.py:541

commit v7 on v6

--- a/solution.py
+++ b/solution.py
@@ -23,6 +23,8 @@
 STEP1 = 256
 HIGH1 = FW // STEP1
 PARTS1 = 4
+GROUP1 = 4
+ROWS1 = 32
 STEP5 = 512
 HIGH5 = FW // STEP5
 PAIR5 = 4
@@ -89,7 +91,7 @@
     return value
 
 
-def section_kernel(column_ref, offsets_ref, model_hbm, out_hbm, model_ref, table_ref, pc_ref, ps_ref, out_ref, sems, sem):
+def section_kernel(column_ref, offsets_ref, model_hbm, out_hbm, model_ref, table_ref, pc_ref, ps_ref, block_ref, acc_ref, out_ref, sems, sem):
     wide = FW // PARTS1
     fetches = []
     for part in range(PARTS1):
@@ -104,21 +106,28 @@
     table_ref[:, SGW:] = (-s).astype(BF)
     freq = column_start + iota((HIGH1, SGW), 1)
     pc_ref[...], ps_ref[...] = phase(freq, pixel_start + STEP1 * iota((HIGH1, SGW), 0))
-    acc_re = jnp.zeros((FROWS, SGW), F32)
-    acc_im = jnp.zeros((FROWS, SGW), F32)
-    for high in range(HIGH1):
-        if high % (HIGH1 // PARTS1) == 0:
-            fetches[high // (HIGH1 // PARTS1)].wait()
-        block = model_ref[:, high * STEP1 : (high + 1) * STEP1].astype(BF)
-        product = jnp.dot(block, table_ref[...], preferred_element_type=F32)
-        re = product[:, :SGW]
-        im = product[:, SGW:]
-        pc = pc_ref[high : high + 1, :]
-        ps = ps_ref[high : high + 1, :]
-        acc_re = acc_re + (re * pc + im * ps)
-        acc_im = acc_im + (im * pc - re * ps)
-    out_ref[:, :SLICE, :] = acc_re.T.astype(BF).reshape(FACETS, SLICE, FROWS)
-    out_ref[:, SLICE:, :] = acc_im.T.astype(BF).reshape(FACETS, SLICE, FROWS)
+    for first in range(0, HIGH1, GROUP1):
+        if first % (HIGH1 // PARTS1) == 0:
+            fetches[first // (HIGH1 // PARTS1)].wait()
+        for k in range(GROUP1):
+            cut = slice((first + k) * STEP1, (first + k + 1) * STEP1)
+            block_ref[k * FROWS : (k + 1) * FROWS] = model_ref[:, cut].astype(BF)
+        product = jnp.dot(block_ref[...], table_ref[...], preferred_element_type=F32)
+        for row in range(0, FROWS, ROWS1):
+            lines = slice(row, row + ROWS1)
+            acc_re = acc_ref[0, lines, :] if first else 0.0
+            acc_im = acc_ref[1, lines, :] if first else 0.0
+            for k in range(GROUP1):
+                re = product[k * FROWS + row : k * FROWS + row + ROWS1, :SGW]
+                im = product[k * FROWS + row : k * FROWS + row + ROWS1, SGW:]
+                pc = pc_ref[first + k : first + k + 1, :]
+                ps = ps_ref[first + k : first + k + 1, :]
+                acc_re = acc_re + (re * pc + im * ps)
+                acc_im = acc_im + (im * pc - re * ps)
+            acc_ref[0, lines, :] = acc_re
+            acc_ref[1, lines, :] = acc_im
+    out_ref[:, :SLICE, :] = acc_ref[0].T.astype(BF).reshape(FACETS, SLICE, FROWS)
+    out_ref[:, SLICE:, :] = acc_ref[1].T.astype(BF).reshape(FACETS, SLICE, FROWS)
     write_out([(out_ref, out_hbm, sem)])
 
 
@@ -133,6 +142,8 @@
             pltpu.VMEM((STEP1, 2 * SGW), BF),
             pltpu.VMEM((HIGH1, SGW), F32),
             pltpu.VMEM((HIGH1, SGW), F32),
+            pltpu.VMEM((GROUP1 * FROWS, STEP1), BF),
+            pltpu.VMEM((2, FROWS, SGW), F32),
             pltpu.VMEM((FACETS, 2 * SLICE, FROWS), BF),
             pltpu.SemaphoreType.DMA((PARTS1,)),
             pltpu.SemaphoreType.DMA,
@@ -150,7 +161,7 @@
     return jnp.where(inside, jnp.exp(-0.5 * distance * distance), 0.0).astype(BF)
 
 
-def table_kernel(offsets_ref, rows_ref, uv_ref, table_ref, c_ref, s_ref, ku_ref, kv_ref, base_ref, turn_ref):
+def row_table_kernel(offsets_ref, rows_ref, table_ref, c_ref, s_ref, base_ref, turn_ref):
     base_ref[0], base_ref[1] = phase(iota((FROWS, SGW), 1), iota((FROWS, SGW), 0))
     row = iota((FACETS, SGW), 0)
     start = jnp.zeros((FACETS, SGW), I32)
@@ -169,33 +180,28 @@
         table_ref[0, lines, :] = (base_ref[0] * cf - base_ref[1] * sf).astype(BF)
         table_ref[1, lines, :] = (base_ref[1] * cf + base_ref[0] * sf).astype(BF)
         c_ref[f], s_ref[f] = phase(freq, offsets_ref[0, f] + iota((NROWSG, FROWS), 1))
-        cut = pl.ds(pl.multiple_of(f * SGW, SGW), SGW)
-        ku_ref[:, cut] = kernel_columns(uv_ref[0:1, cut])
-        kv_ref[:, cut] = kernel_columns(uv_ref[1:2, cut])
         return carry
 
     lax.fori_loop(0, FACETS, one, 0)
 
 
-def cycle_tables(offsets, rows, uv):
-    return pl.pallas_call(
-        table_kernel,
+def row_tables(offsets, rows):
+    return pl.pallas_call(
+        row_table_kernel,
         out_shape=(
             pltpu.VMEM((2, FACETS * FROWS, SGW), BF),
             pltpu.VMEM((FACETS, NROWSG, FROWS), F32),
             pltpu.VMEM((FACETS, NROWSG, FROWS), F32),
-            pltpu.VMEM((SGW, VCAP), BF),
-            pltpu.VMEM((SGW, VCAP), BF),
         ),
-        in_specs=[SMEM_SPEC, SMEM_SPEC, VMEM_SPEC],
-        out_specs=(VMEM_SPEC,) * 5,
+        in_specs=[SMEM_SPEC, SMEM_SPEC],
+        out_specs=(VMEM_SPEC,) * 3,
         scratch_shapes=[
             pltpu.VMEM((2, FROWS, SGW), F32),
             pltpu.VMEM((2, FACETS, SGW), F32),
         ],
         compiler_params=PARAMS,
-        name="cycle_tables",
-    )(offsets, rows, uv)
+        name="row_tables",
+    )(offsets, rows)
 
 
 def grid_kernel(in_ref, c_ref, s_ref, table_ref, out_hbm, turned_ref, out_ref, sem):
@@ -285,22 +291,24 @@
     )(on_chip(gridded), on_chip(c), on_chip(s), on_chip(table))
 
 
-def visibility_kernel(counts_ref, obs_ref, weight_ref, in_ref, ku_ref, kv_ref, gridded_hbm, res_ref, acc_ref, gridded_ref, sem):
+def visibility_pass(counts_ref, obs_ref, weight_ref, in_ref, kernels, gridded_hbm, res_ref, acc_ref, gridded_ref, sem):
     count = counts_ref[0, lax.axis_index("facet")]
     grid = [in_ref[:, half * SLICE : (half + 1) * SLICE, :].reshape(SGW, SGW) for half in range(2)]
     for part in range(VCAP // VBLOCK):
         cut = slice(part * VBLOCK, (part + 1) * VBLOCK)
+        ku, kv = kernels(cut)
         live = part * VBLOCK + iota((1, VBLOCK), 1) < count
         weight = weight_ref[:, cut].astype(F32)
         for half in range(2):
-            sampled = jnp.dot(grid[half], ku_ref[:, cut], preferred_element_type=F32)
-            predicted = jnp.sum(sampled * kv_ref[:, cut].astype(F32), axis=0, keepdims=True)
+            sampled = jnp.dot(grid[half], ku, preferred_element_type=F32)
+            predicted = jnp.sum(sampled * kv.astype(F32), axis=0, keepdims=True)
             observed = obs_ref[half : half + 1, cut].astype(F32)
             residual = jnp.where(live, weight * (observed - predicted), 0.0)
-            res_ref[half : half + 1, cut] = residual
-            weighted = (residual * kv_ref[:, cut].astype(F32)).astype(BF)
+            if res_ref is not None:
+                res_ref[half : half + 1, cut] = residual
+            weighted = (residual * kv.astype(F32)).astype(BF)
             total = lax.dot_general(
-                weighted, ku_ref[:, cut], (((1,), (1,)), ((), ())), preferred_element_type=F32
+                weighted, ku, (((1,), (1,)), ((), ())), preferred_element_type=F32
             )
             if part:
                 total = total + acc_ref[half]
@@ -312,23 +320,63 @@
     write_out([(gridded_ref, gridded_hbm, sem)])
 
 
-def visibilities(counts, obs, weight, grid, tables):
-    return pl.pallas_call(
-        visibility_kernel,
+def first_kernel(counts_ref, obs_ref, weight_ref, in_ref, uv_ref, gridded_hbm, ku_ref, kv_ref, acc_ref, gridded_ref, sem):
+    def kernels(cut):
+        ku_ref[:, cut] = kernel_columns(uv_ref[0:1, cut])
+        kv_ref[:, cut] = kernel_columns(uv_ref[1:2, cut])
+        return ku_ref[:, cut], kv_ref[:, cut]
+
+    visibility_pass(counts_ref, obs_ref, weight_ref, in_ref, kernels, gridded_hbm, None, acc_ref, gridded_ref, sem)
+
+
+def last_kernel(counts_ref, obs_ref, weight_ref, in_ref, ku_ref, kv_ref, gridded_hbm, res_ref, acc_ref, gridded_ref, sem):
+    def kernels(cut):
+        return ku_ref[:, cut], kv_ref[:, cut]
+
+    visibility_pass(counts_ref, obs_ref, weight_ref, in_ref, kernels, gridded_hbm, res_ref, acc_ref, gridded_ref, sem)
+
+
+VIS_SCRATCH = [
+    pltpu.VMEM((2, SGW, SGW), F32),
+    pltpu.VMEM((FACETS, 2 * SLICE, SGW), BF),
+    pltpu.SemaphoreType.DMA,
+]
+
+
+def first_visibilities(counts, obs, weight, grid, uv):
+    return pl.pallas_call(
+        first_kernel,
+        out_shape=(
+            jax.ShapeDtypeStruct((FACETS, 2 * SLICE, SGW), BF),
+            pltpu.VMEM((SGW, VCAP), BF),
+            pltpu.VMEM((SGW, VCAP), BF),
+        ),
+        in_specs=[SMEM_SPEC] + [VMEM_SPEC] * 4,
+        out_specs=(HBM_SPEC, VMEM_SPEC, VMEM_SPEC),
+        scratch_shapes=VIS_SCRATCH,
+        compiler_params=PARAMS,
+        name="first_visibilities",
+    )(counts, obs, weight, on_chip(grid), uv)
+
+
+def last_visibilities(counts, obs, weight, grid, ku, kv):
+    return pl.pallas_call(
+        last_kernel,
         out_shape=(
             jax.ShapeDtypeStruct((FACETS, 2 * SLICE, SGW), BF),
             jax.ShapeDtypeStruct((2, VCAP), F32),
         ),
         in_specs=[SMEM_SPEC] + [VMEM_SPEC] * 5,
         out_specs=(HBM_SPEC, VMEM_SPEC),
-        scratch_shapes=[
-            pltpu.VMEM((2, SGW, SGW), F32),
-            pltpu.VMEM((FACETS, 2 * SLICE, SGW), BF),
-            pltpu.SemaphoreType.DMA,
-        ],
-        compiler_params=PARAMS,
-        name="visibilities",
-    )(counts, obs, weight, on_chip(grid), *map(on_chip, tables))
+        scratch_shapes=VIS_SCRATCH,
+        compiler_params=PARAMS,
+        name="last_visibilities",
+    )(counts, obs, weight, on_chip(grid), on_chip(ku), on_chip(kv))
+
+
+def start_of(starts_ref, column):
+    own = lax.axis_index("sub")
+    return starts_ref[2 * (((own >> 1) - (column >> 1)) & (NCOL // 2 - 1)) + ((own ^ column) & 1)]
 
 
 def dirichlet(distance, pixel_start):
@@ -347,7 +395,7 @@
     row = iota((NCOL, wide), 0)
     starts = jnp.zeros((NCOL, wide), I32)
     for c in range(NCOL):
-        starts = jnp.where(row == c, starts_ref[c], starts)
+        starts = jnp.where(row == c, start_of(starts_ref, c), starts)
     lane = iota((NCOL, wide), 1)
     v_ref[0], v_ref[1] = dirichlet(starts - own + (lane - (SGW - 1)), pixel_start)
     v_ref[2], v_ref[3] = dirichlet(starts + own + (2 * (SGW - 1) - lane), pixel_start)
@@ -489,7 +537,7 @@
     line = iota((group, STEP5), 0)
     freq = line & (SLICE - 1)
     for c in range(NCOL):
-        freq = freq + jnp.where((line >> 4) == c, starts_ref[c], 0)
+        freq = freq + jnp.where((line >> 4) == c, start_of(starts_ref, c), 0)
     base_ref[0], base_ref[1] = phase(freq, iota((group, STEP5), 1))
     turn_ref[0], turn_ref[1] = phase(SLICE * iota((FACETS, STEP5), 0), iota((FACETS, STEP5), 1))
 
@@ -506,7 +554,7 @@
     lane = iota((HIGH5, COLUMNS), 1)
     freq = SLICE * (lane >> 7) + (lane & (SLICE - 1))
     for c in range(NCOL):
-        freq = freq + jnp.where(((lane >> 4) & (NCOL - 1)) == c, starts_ref[c], 0)
+        freq = freq + jnp.where(((lane >> 4) & (NCOL - 1)) == c, start_of(starts_ref, c), 0)
     pixel_start = offsets_ref[1, lax.axis_index("facet")]
     pc_ref[...], ps_ref[...] = phase(freq, pixel_start + STEP5 * iota((HIGH5, COLUMNS), 0))
     write_out([(table_ref, table_hbm, sem)])
@@ -541,6 +589,15 @@
     return lax.ppermute(value, "sub", [(i, i ^ 1) for i in range(NCOL)])
 
 
+def all_starts(own):
+    lines = lax.optimization_barrier(jnp.broadcast_to(own[:, None], (8, 128)))
+    pair = jnp.concatenate([lines, other_core(lines)], axis=0)
+    chips = [pair]
+    for away in range(2, NCOL, 2):
+        chips.append(lax.ppermute(pair, "sub", [(i, (i + away) % NCOL) for i in range(NCOL)]))
+    return jnp.concatenate([chip[::8, 0] for chip in chips])
+
+
 def to_facets(value):
     copies = value.reshape(FACETS * NCOL, *value.shape[2:])
     return lax.all_to_all(copies, ("facet", "sub"), split_axis=0, concat_axis=0, tiled=True)
@@ -557,22 +614,20 @@
     vis_obs,
     vis_weight,
 ):
-    lines = lax.optimization_barrier(jnp.broadcast_to(col_offsets[:, None], (8, 128)))
-    column_starts = lax.optimization_barrier(lax.all_gather(lines, "sub", axis=0, tiled=True))[::8, 0]
+    column_starts = all_starts(col_offsets)
     uv = vis_uv.reshape(2, VCAP)
     obs = vis_obs.reshape(2, VCAP)
     weight = vis_weight.reshape(1, VCAP)
     model = model_image[0]
     first = section(col_offsets, facet_offsets, model)
-    tables = cycle_tables(facet_offsets, row_offsets, uv)
-    rows, kernels = tables[:3], tables[3:]
+    rows = row_tables(facet_offsets, row_offsets)
     grid = exchange(grids(exchange(first), rows))
-    gridded, residual = visibilities(counts, obs, weight, grid, kernels)
+    gridded, ku, kv = first_visibilities(counts, obs, weight, grid, uv)
+    gridded, column_starts = lax.optimization_barrier((gridded, column_starts))
     adj0 = to_facets(adjoint(exchange(gridded), rows))
-    adj0, column_starts = lax.optimization_barrier((adj0, column_starts))
     second = gram(step_sizes, column_starts, col_offsets, facet_offsets, adj0, other_core(adj0), first)
     grid = exchange(grids(exchange(second), rows))
-    gridded, residual = visibilities(counts, obs, weight, grid, kernels)
+    gridded, residual = last_visibilities(counts, obs, weight, grid, ku, kv)
     adj1 = to_facets(adjoint(exchange(gridded), rows))
     tables = update_tables(column_starts, facet_offsets)
     step = update(step_sizes, adj0, adj1, tables)

time: 169 us -> 163 us (0.964)
  blocking collectives: 76 us -> 66 us
  waiting for transfers between devices: 12.6 us -> 21.5 us
  local copies, waits for them, and re-layouts: 5.63 us -> 1.46 us
    all_to_all x0 -> x1, blocking collectives: none -> 21.1 us  [to_facets(): lax.all_to_all(copies, ('facet', 'sub'), split_axis=0, concat_axis=0, til...]
    all_to_all x5 -> x4, blocking collectives: 62.1 us -> 44.9 us  [exchange(): lax.all_to_all(value, 'facet', split_axis=0, concat_axis=0, tiled=True)]
    all_gather x1 -> x0, blocking collectives: 13.9 us -> none  [local(): lax.all_gather(lines, 'sub', axis=0, tiled=True)]
    all_to_all x2 -> x1, starting transfers between devices: 18.3 us -> 8.16 us  [to_facets(): lax.all_to_all(copies, ('facet', 'sub'), split_axis=0, concat_axis=0, til...]
    all_to_all x1 -> x2, waiting for transfers between devices: 0.01 us -> 5.13 us  [exchange(): lax.all_to_all(value, 'facet', split_axis=0, concat_axis=0, tiled=True)]
    ppermute x0 -> x3, starting transfers between devices: none -> 4.47 us  [all_starts(): lax.ppermute(pair, 'sub', [(i, (i + away) % NCOL) for i in range(NCOL)])]
    unnamed x30 -> x18, local copies, waits for them, and re-layouts: 5.61 us -> 1.37 us
    all_to_all x1 -> x2, starting transfers between devices: 7.6 us -> 11.1 us  [exchange(): lax.all_to_all(value, 'facet', split_axis=0, concat_axis=0, tiled=True)]
  transfers between devices with their start and end apart: 5 -> 9, of which waited for: 3 -> 6; matrix products, arithmetic and copies ran while one was open for 0% -> 1% of each run, Pallas kernels for 6% -> 4%
where the time goes in v7:
time: 163 us; the launch traced here: 162 us
  blocking collectives  66 us (40%)
  Pallas kernels  43 us (26%)
  starting transfers between devices  28.2 us (17%)
  waiting for transfers between devices  21.5 us (13%)
    all_to_all x4, blocking collectives, exchange(): lax.all_to_all(value, 'facet', split_axis=0, concat_axis=0, tiled=True)  44.9 us
    all_to_all x1, blocking collectives, to_facets(): lax.all_to_all(copies, ('facet', 'sub'), split_axis=0, concat_axis=0, til...  21.1 us
    all_to_all x2, starting transfers between devices, exchange(): lax.all_to_all(value, 'facet', split_axis=0, concat_axis=0, tiled=True)  11.1 us
    all_to_all x1, waiting for transfers between devices, to_facets(): lax.all_to_all(copies, ('facet', 'sub'), split_axis=0, concat_axis=0, til...  9.41 us
    all_to_all x1, starting transfers between devices, to_facets(): lax.all_to_all(copies, ('facet', 'sub'), split_axis=0, concat_axis=0, til...  8.16 us
    pallas_call x1, Pallas kernels, update(): pl.pallas_call(update_kernel, grid=(HIGH5 // PAIR5 // 2,), out_shape=jax....  7.52 us
    pallas_call x1, Pallas kernels, first_visibilities(): pl.pallas_call(first_kernel, out_shape=(jax.ShapeDtypeStruct((FACETS, 2 *...  6.12 us
    all_to_all x2, waiting for transfers between devices, exchange(): lax.all_to_all(value, 'facet', split_axis=0, concat_axis=0, tiled=True)  5.13 us
  transfers between devices with their start and end apart: 9, of which 6 were waited for; matrix products, arithmetic and copies ran while one was open for 1% of the time, Pallas kernels for 4%

profile of v7, /device:TPU:1, one launch (start us, length us, event | category | flops | bytes accessed | tf_op | source)
XLA Modules:
  0.0 162.2 jit_solution(7360280244096918403)
XLA Ops:
  1.3 0.7 copy-done.2
  2.0 4.7 %section.1.first_ref = bf16[16,32,128]{2,1,0:T(8,128)(2,1)} custom-call(s32[1]{0:T(128)} %copy.17.column_ref, s32[2,16]{1,0:T(2,128)S(1)} %copy-done.2, f32[128,8192]{1,0:T(8,128)} %bitcast.23), custom_call_target="tpu_custom_call" | custom-call | tf_op jit(solution)/shard_map/section/pallas_call | solution.py:135
  6.7 7.6 %all-to-all-start = ((bf16[16,32,128]{2,1,0:T(8,128)(2,1)}), bf16[16,32,128]{2,1,0:T(8,128)(2,1)S(1)}, u32[]{:S(2)}, u32[]{:S(2)}) async-start(bf16[16,32,128]{2,1,0:T(8,128)(2,1)} %section.1.first_ref), calls=%async_computation | async-start | bytes 262144 | tf_op jit(solution)/shard_map/all_to_all | solution.py:585
  14.3 1.7 %row_tables.1 = (bf16[2,2048,256]{2,1,0:T(8,128)(2,1)S(1)}, f32[16,16,128]{2,1,0:T(8,128)S(1)}, f32[16,16,128]{2,1,0:T(8,128)S(1)}) custom-call(s32[2,16]{1,0:T(2,128)S(1)} %copy-done.3, s32[1,16]{1,0:T(1,128)S(1)} %copy-done.6), custom_call_target="tpu_custom_call" | custom-call | tf_op jit(solution)/shard_map/row_tables/pallas_call | solution.py:189
  16.0 5.1 %all-to-all-done.in_ref = bf16[16,32,128]{2,1,0:T(8,128)(2,1)S(1)} async-done(((bf16[16,32,128]{2,1,0:T(8,128)(2,1)}), bf16[16,32,128]{2,1,0:T(8,128)(2,1)S(1)}, u32[]{:S(2)}, u32[]{:S(2)}) %all-to-all-start) | async-done | bytes 131104 | tf_op jit(solution)/shard_map/all_to_all | solution.py:585
  21.1 2.0 %grids.2 = bf16[16,32,256]{2,1,0:T(8,128)(2,1)} custom-call(bf16[16,32,128]{2,1,0:T(8,128)(2,1)S(1)} %all-to-all-done.in_ref, f32[16,16,128]{2,1,0:T(8,128)S(1)} %get-tuple-element.15.c_ref, f32[16,16,128]{2,1,0:T(8,128)S(1)} %get-tuple-element.16.s_ref, bf16[2,2048,256]{2,1,0:T(8,128)(2,1)S(1)} %get-tuple-element.17.table_ref), custom_call_target="tpu_custom_call" | custom-call | tf_op jit(solution)/shard_map/grids/pallas_call | solution.py:229
  23.1 3.5 %all-to-all-start.1 = ((bf16[16,32,256]{2,1,0:T(8,128)(2,1)}), bf16[16,32,256]{2,1,0:T(8,128)(2,1)S(1)}, u32[]{:S(2)}, u32[]{:S(2)}) async-start(bf16[16,32,256]{2,1,0:T(8,128)(2,1)} %grids.2), calls=%async_computation.1 | async-start | bytes 524288 | tf_op jit(solution)/shard_map/all_to_all | solution.py:585
  26.7 2.1 %collective-permute-start = (s32[8,128]{1,0:T(8,128)S(1)}, s32[8,128]{1,0:T(8,128)S(1)}, u32[]{:S(2)}, u32[]{:S(2)}) collective-permute-start(s32[8,128]{1,0:T(8,128)S(1)} %broadcast_in_dim.12), channel_id=1, source_target_pairs={{0,1},{1,0},{2,3},{3,2},{4,5},{5,4},{6,7},{7,6},{8,9},{9,8},{10,11... | collective-permute-start | bytes 12296 | tf_op jit(solution)/shard_map/ppermute | solution.py:589
  28.8 0.8 collective-permute-done
  29.6 3.8 %collective-permute-start.3 = (s32[16,128]{1,0:T(8,128)S(1)}, s32[16,128]{1,0:T(8,128)S(1)}, u32[]{:S(2)}, u32[]{:S(2)}) collective-permute-start(s32[16,128]{1,0:T(8,128)S(1)} %pad_add_fusion), channel_id=1, source_target_pairs={{0,6},{1,7},{2,0},{3,1},{4,2},{5,3},{6,4},{7,5},{8,14},{9,15},{10,... | collective-permute-start | bytes 24584 | tf_op jit(solution)/shard_map/ppermute | solution.py:597
  33.4 0.7 collective-permute-start.1
  34.4 3.0 %collective-permute-done.2 = s32[16,128]{1,0:T(8,128)S(1)} collective-permute-done((s32[16,128]{1,0:T(8,128)S(1)}, s32[16,128]{1,0:T(8,128)S(1)}, u32[]{:S(2)}, u32[]{:S(2)}) %collective-permute-start.2) | collective-permute-done | bytes 8224 | tf_op jit(solution)/shard_map/ppermute | solution.py:597
  37.8 6.1 %first_visibilities.1 = (bf16[16,32,256]{2,1,0:T(8,128)(2,1)S(1)}, bf16[256,4096]{1,0:T(8,128)(2,1)S(1)}, bf16[256,4096]{1,0:T(8,128)(2,1)S(1)}) custom-call(s32[1,16]{1,0:T(1,128)S(1)} %copy-done.4, bf16[2,4096]{1,0:T(2,128)(2,1)S(1)} %bitcast.18, bf16[1,4096]{1,0:T(2,128)(2,1)S(1)} %bitcast.20, bf16[16,32,256]{2,1,0:T(8,128)(2,1)S(1)} %all-to-all-done.1.in_ref, ...), custom_call_target="tpu_custom_call" | custom-call | tf_op jit(solution)/shard_map/first_visibilities/pallas_call | solution.py:347
  43.9 14.1 %all_to_all.40.in_ref = bf16[16,32,256]{2,1,0:T(8,128)(2,1)S(1)} all-to-all(bf16[16,32,256]{2,1,0:T(8,128)(2,1)S(1)} %get-tuple-element.19), channel_id=1, replica_groups=mesh['facet'=16,'sub'=8] {'facet'}, dimensions={0} | all-to-all | bytes 524288 | tf_op jit(solution)/shard_map/all_to_all | solution.py:585
  58.0 1.8 %adjoint.2 = bf16[16,8,16,128]{3,2,1,0:T(8,128)(2,1)S(1)} custom-call(bf16[16,32,256]{2,1,0:T(8,128)(2,1)S(1)} %all_to_all.40.in_ref, f32[16,16,128]{2,1,0:T(8,128)S(1)} %get-tuple-element.15.c_ref, f32[16,16,128]{2,1,0:T(8,128)S(1)} %get-tuple-element.16.s_ref, bf16[2,2048,256]{2,1,0:T(8,128)(2,1)S(1)} %get-tuple-element.17.table_ref), custom_call_target="tpu_custom_call" | custom-call | tf_op jit(solution)/shard_map/adjoint/pallas_call | solution.py:279
  59.8 21.1 %all_to_all.41.adj0_ref = bf16[128,16,128]{2,1,0:T(8,128)(2,1)S(1)} all-to-all(bf16[128,16,128]{2,1,0:T(8,128)(2,1)S(1)} %bitcast.15), channel_id=1, replica_groups=mesh['facet'=16,'sub'=8] {'facet','sub'}, dimensions={0} | all-to-all | bytes 1048576 | tf_op jit(solution)/shard_map/all_to_all | solution.py:603
  80.9 1.1 collective-permute-start.4
  82.0 1.5 collective-permute-done.4
  83.6 3.7 %gram.1 = bf16[16,32,128]{2,1,0:T(8,128)(2,1)S(1)} custom-call(f32[2]{0:T(128)S(1)} %copy-done.5, s32[8]{0:T(128)S(1)} %pad_add_fusion.1.starts_ref, s32[1]{0:T(128)} %copy.17.column_ref, s32[2,16]{1,0:T(2,128)S(1)} %copy-done.3, bf16[16,8,16,128]{3,2,1,0:T(8,128)(2,1)S(1)} %bitcast.14, bf16[16,8,16,128]{3,2,1,0:T(8,128)(2,1)S(1)} %bitcast.16, ...), custom_call_target="tpu_custom_call" | custom-call | tf_op jit(solution)/shard_map/gram/pallas_call | solution.py:438
  87.3 9.3 %all_to_all.42.in_ref = bf16[16,32,128]{2,1,0:T(8,128)(2,1)S(1)} all-to-all(bf16[16,32,128]{2,1,0:T(8,128)(2,1)S(1)} %gram.1), channel_id=1, replica_groups=mesh['facet'=16,'sub'=8] {'facet'}, dimensions={0} | all-to-all | bytes 262144 | tf_op jit(solution)/shard_map/all_to_all | solution.py:585
  96.6 1.3 grids.3
  98.0 10.7 %all_to_all.43.in_ref = bf16[16,32,256]{2,1,0:T(8,128)(2,1)S(1)} all-to-all(bf16[16,32,256]{2,1,0:T(8,128)(2,1)S(1)} %grids.3), channel_id=1, replica_groups=mesh['facet'=16,'sub'=8] {'facet'}, dimensions={0} | all-to-all | bytes 524288 | tf_op jit(solution)/shard_map/all_to_all | solution.py:585
  108.6 3.4 %last_visibilities.1 = (bf16[16,32,256]{2,1,0:T(8,128)(2,1)S(1)}, f32[2,4096]{1,0:T(2,128)S(1)}) custom-call(s32[1,16]{1,0:T(1,128)S(1)} %copy-done.4, bf16[2,4096]{1,0:T(2,128)(2,1)S(1)} %bitcast.19, bf16[1,4096]{1,0:T(2,128)(2,1)S(1)} %bitcast.21, bf16[16,32,256]{2,1,0:T(8,128)(2,1)S(1)} %all_to_all.43.in_ref, ...), custom_call_target="tpu_custom_call" | custom-call | tf_op jit(solution)/shard_map/last_visibilities/pallas_call | solution.py:363
  112.0 10.8 %all_to_all.44.in_ref = bf16[16,32,256]{2,1,0:T(8,128)(2,1)S(1)} all-to-all(bf16[16,32,256]{2,1,0:T(8,128)(2,1)S(1)} %get-tuple-element.23), channel_id=1, replica_groups=mesh['facet'=16,'sub'=8] {'facet'}, dimensions={0} | all-to-all | bytes 524288 | tf_op jit(solution)/shard_map/all_to_all | solution.py:585
  122.8 2.5 %adjoint.3 = bf16[16,8,16,128]{3,2,1,0:T(8,128)(2,1)} custom-call(bf16[16,32,256]{2,1,0:T(8,128)(2,1)S(1)} %all_to_all.44.in_ref, f32[16,16,128]{2,1,0:T(8,128)S(1)} %get-tuple-element.15.c_ref, f32[16,16,128]{2,1,0:T(8,128)S(1)} %get-tuple-element.16.s_ref, bf16[2,2048,256]{2,1,0:T(8,128)(2,1)S(1)} %get-tuple-element.17.table_ref), custom_call_target="tpu_custom_call" | custom-call | tf_op jit(solution)/shard_map/adjoint/pallas_call | solution.py:279
  125.4 8.2 %all-to-all-start.7 = ((bf16[128,16,128]{2,1,0:T(8,128)(2,1)}), bf16[128,16,128]{2,1,0:T(8,128)(2,1)S(1)}, u32[]{:S(2)}, u32[]{:S(2)}) async-start(bf16[128,16,128]{2,1,0:T(8,128)(2,1)} %bitcast.7), calls=%async_computation.7 | async-start | bytes 1048576 | tf_op jit(solution)/shard_map/all_to_all | solution.py:603
  133.5 4.3 %update_tables.1 = (bf16[4096,512]{1,0:T(8,128)(2,1)}, f32[16,2048]{1,0:T(8,128)S(1)}, f32[16,2048]{1,0:T(8,128)S(1)}) custom-call(s32[8]{0:T(128)S(1)} %pad_add_fusion.1.starts_ref, s32[2,16]{1,0:T(2,128)S(1)} %copy-done.3), custom_call_target="tpu_custom_call" | custom-call | tf_op jit(solution)/shard_map/update_tables/pallas_call | solution.py:564
  137.8 9.4 %all-to-all-done.7.adj1_ref = bf16[128,16,128]{2,1,0:T(8,128)(2,1)S(1)} async-done(((bf16[128,16,128]{2,1,0:T(8,128)(2,1)}), bf16[128,16,128]{2,1,0:T(8,128)(2,1)S(1)}, u32[]{:S(2)}, u32[]{:S(2)}) %all-to-all-start.7) | async-done | bytes 524320 | tf_op jit(solution)/shard_map/all_to_all | solution.py:603
  147.2 7.5 %update.1.mine_ref = bf16[64,8192]{1,0:T(8,128)(2,1)S(1)} custom-call(f32[2]{0:T(128)S(1)} %copy-done.5, bf16[128,16,128]{2,1,0:T(8,128)(2,1)S(1)} %all_to_all.41.adj0_ref, bf16[128,16,128]{2,1,0:T(8,128)(2,1)S(1)} %all-to-all-done.7.adj1_ref, bf16[4096,512]{1,0:T(8,128)(2,1)} %get-tuple-element.24.table_hbm, f32[16,2048]{1,0:T(8,128)S(1)} %get-tuple-element.25.pc_ref, ...), custom_call_target="tpu_custom_call" | custom-call | tf_op jit(solution)/shard_map/update/pallas_call | solution.py:495
  154.7 1.2 collective-permute-start.5
  156.6 1.6 %collective-permute-done.5.theirs_ref = bf16[64,8192]{1,0:T(8,128)(2,1)S(1)} collective-permute-done((bf16[64,8192]{1,0:T(8,128)(2,1)S(1)}, bf16[64,8192]{1,0:T(8,128)(2,1)S(1)}, u32[]{:S(2)}, u32[]{:S(2)}) %collective-permute-start.5) | collective-permute-done | bytes 1048608 | tf_op jit(solution)/shard_map/ppermute | solution.py:589
  158.3 4.0 %take_step.1 = f32[128,8192]{1,0:T(8,128)} custom-call(bf16[64,8192]{1,0:T(8,128)(2,1)S(1)} %update.1.mine_ref, bf16[64,8192]{1,0:T(8,128)(2,1)S(1)} %collective-permute-done.5.theirs_ref, f32[128,8192]{1,0:T(8,128)} %bitcast.24), custom_call_target="tpu_custom_call" | custom-call | tf_op jit(solution)/shard_map/take_step/pallas_call | solution.py:524
  (32 shorter events, 1.4 us)
Async XLA Ops:
  0.6 37.1 %copy-start.1 = (bf16[1,1,4096]{2,1,0:T(2,128)(2,1)S(1)}, bf16[1,1,4096]{2,1,0:T(2,128)(2,1)}, u32[]{:S(2)}) copy-start(bf16[1,1,4096]{2,1,0:T(2,128)(2,1)} %param.17) | copy-start | bytes 24580
  0.6 37.1 %copy-start = (bf16[2,1,1,4096]{3,0,2,1:T(2,128)(2,1)S(1)}, bf16[2,1,1,4096]{3,0,2,1:T(2,128)(2,1)}, u32[]{:S(2)}) copy-start(bf16[2,1,1,4096]{3,0,2,1:T(2,128)(2,1)} %param.16) | copy-start | bytes 49156
  1.3 0.7 copy-start.2
  2.0 12.3 %copy-start.3 = (s32[2,16]{1,0:T(2,128)S(1)}, s32[2,16]{1,0:T(2,128)}, u32[]{:S(2)}) copy-start(s32[2,16]{1,0:T(2,128)} %offsets_ref.7) | copy-start | bytes 388
  2.0 12.3 %copy-start.6 = (s32[1,16]{1,0:T(1,128)S(1)}, s32[1,16]{1,0:T(1,128)}, u32[]{:S(2)}) copy-start(s32[1,16]{1,0:T(1,128)} %rows_ref.1) | copy-start | bytes 196
  2.0 32.1 %copy-start.7 = (s32[2,1,1,4096]{3,2,1,0:T(1,128)S(1)}, s32[2,1,1,4096]{3,2,1,0:T(1,128)}, u32[]{:S(2)}) copy-start(s32[2,1,1,4096]{3,2,1,0:T(1,128)} %param.15) | copy-start | bytes 98308
  2.0 35.8 %copy-start.4 = (s32[1,16]{1,0:T(1,128)S(1)}, s32[1,16]{1,0:T(1,128)}, u32[]{:S(2)}) copy-start(s32[1,16]{1,0:T(1,128)} %counts_ref.3) | copy-start | bytes 196
  6.7 14.5 %all-to-all-start = ((bf16[16,32,128]{2,1,0:T(8,128)(2,1)}), bf16[16,32,128]{2,1,0:T(8,128)(2,1)S(1)}, u32[]{:S(2)}, u32[]{:S(2)}) async-start(bf16[16,32,128]{2,1,0:T(8,128)(2,1)} %section.1.first_ref), calls=%async_computation | async-start | bytes 262144 | tf_op jit(solution)/shard_map/all_to_all | solution.py:585
  21.1 62.4 %copy-start.5 = (f32[2]{0:T(128)S(1)}, f32[2]{0:T(128)}, u32[]{:S(2)}) copy-start(f32[2]{0:T(128)} %step_ref.3) | copy-start | bytes 28
  23.1 14.6 %all-to-all-start.1 = ((bf16[16,32,256]{2,1,0:T(8,128)(2,1)}), bf16[16,32,256]{2,1,0:T(8,128)(2,1)S(1)}, u32[]{:S(2)}, u32[]{:S(2)}) async-start(bf16[16,32,256]{2,1,0:T(8,128)(2,1)} %grids.2), calls=%async_computation.1 | async-start | bytes 524288 | tf_op jit(solution)/shard_map/all_to_all | solution.py:585
  26.7 2.9 %collective-permute-start = (s32[8,128]{1,0:T(8,128)S(1)}, s32[8,128]{1,0:T(8,128)S(1)}, u32[]{:S(2)}, u32[]{:S(2)}) collective-permute-start(s32[8,128]{1,0:T(8,128)S(1)} %broadcast_in_dim.12), channel_id=1, source_target_pairs={{0,1},{1,0},{2,3},{3,2},{4,5},{5,4},{6,7},{7,6},{8,9},{9,8},{10,11... | collective-permute-start | bytes 12296 | tf_op jit(solution)/shard_map/ppermute | solution.py:589
  29.6 4.6 %collective-permute-start.3 = (s32[16,128]{1,0:T(8,128)S(1)}, s32[16,128]{1,0:T(8,128)S(1)}, u32[]{:S(2)}, u32[]{:S(2)}) collective-permute-start(s32[16,128]{1,0:T(8,128)S(1)} %pad_add_fusion), channel_id=1, source_target_pairs={{0,6},{1,7},{2,0},{3,1},{4,2},{5,3},{6,4},{7,5},{8,14},{9,15},{10,... | collective-permute-start | bytes 24584 | tf_op jit(solution)/shard_map/ppermute | solution.py:597
  33.4 4.0 %collective-permute-start.2 = (s32[16,128]{1,0:T(8,128)S(1)}, s32[16,128]{1,0:T(8,128)S(1)}, u32[]{:S(2)}, u32[]{:S(2)}) collective-permute-start(s32[16,128]{1,0:T(8,128)S(1)} %pad_add_fusion), channel_id=1, source_target_pairs={{0,4},{1,5},{2,6},{3,7},{4,0},{5,1},{6,2},{7,3},{8,12},{9,13},{10,... | collective-permute-start | bytes 24584 | tf_op jit(solution)/shard_map/ppermute | solution.py:597
  33.4 4.1 %collective-permute-start.1 = (s32[16,128]{1,0:T(8,128)S(1)}, s32[16,128]{1,0:T(8,128)S(1)}, u32[]{:S(2)}, u32[]{:S(2)}) collective-permute-start(s32[16,128]{1,0:T(8,128)S(1)} %pad_add_fusion), channel_id=1, source_target_pairs={{0,2},{1,3},{2,4},{3,5},{4,6},{5,7},{6,0},{7,1},{8,10},{9,11},{10,... | collective-permute-start | bytes 24584 | tf_op jit(solution)/shard_map/ppermute | solution.py:597
  80.9 2.7 %collective-permute-start.4 = (bf16[128,16,128]{2,1,0:T(8,128)(2,1)S(1)}, bf16[128,16,128]{2,1,0:T(8,128)(2,1)S(1)}, u32[]{:S(2)}, u32[]{:S(2)}) collective-permute-start(bf16[128,16,128]{2,1,0:T(8,128)(2,1)S(1)} %all_to_all.41.adj0_ref), channel_id=1, source_target_pairs={{0,1},{1,0},{2,3},{3,2},{4,5},{5,4},{6,7},{7,6},{8,9},{9,8},{10,11... | collective-permute-start | bytes 1572872 | tf_op jit(solution)/shard_map/ppermute | solution.py:589
  125.4 21.8 %all-to-all-start.7 = ((bf16[128,16,128]{2,1,0:T(8,128)(2,1)}), bf16[128,16,128]{2,1,0:T(8,128)(2,1)S(1)}, u32[]{:S(2)}, u32[]{:S(2)}) async-start(bf16[128,16,128]{2,1,0:T(8,128)(2,1)} %bitcast.7), calls=%async_computation.7 | async-start | bytes 1048576 | tf_op jit(solution)/shard_map/all_to_all | solution.py:603
  154.7 3.5 %collective-permute-start.5 = (bf16[64,8192]{1,0:T(8,128)(2,1)S(1)}, bf16[64,8192]{1,0:T(8,128)(2,1)S(1)}, u32[]{:S(2)}, u32[]{:S(2)}) collective-permute-start(bf16[64,8192]{1,0:T(8,128)(2,1)S(1)} %update.1.mine_ref), channel_id=1, source_target_pairs={{0,1},{1,0},{2,3},{3,2},{4,5},{5,4},{6,7},{7,6},{8,9},{9,8},{10,11... | collective-permute-start | bytes 3145736 | tf_op jit(solution)/shard_map/ppermute | solution.py:589

commit v8 on v7

--- a/solution.py
+++ b/solution.py
@@ -29,7 +29,7 @@
 HIGH5 = FW // STEP5
 PAIR5 = 4
 HALF = FROWS // 2
-PARTS7 = 2
+PARTS7 = 4
 VBLOCK = 1024
 CHUNK = 4
 UNROLL4 = 8
@@ -154,11 +154,11 @@
 
 
 def kernel_columns(position):
-    cells = iota((SGW, position.shape[1]), 0) * OS + OS // 2
-    offset = cells - position
-    distance = offset.astype(F32) * (1.0 / OS)
-    inside = jnp.abs(offset) <= KSUP * OS
-    return jnp.where(inside, jnp.exp(-0.5 * distance * distance), 0.0).astype(BF)
+    cells = (iota((SGW, position.shape[1]), 0) * OS + OS // 2).astype(F32)
+    offset = cells - position.astype(F32)
+    square = offset * offset
+    value = jnp.exp2(square * (-0.5 / (OS * OS) / math.log(2.0)))
+    return jnp.where(square <= float((KSUP * OS) ** 2), value, 0.0).astype(BF)
 
 
 def row_table_kernel(offsets_ref, rows_ref, table_ref, c_ref, s_ref, base_ref, turn_ref):
@@ -510,26 +510,33 @@
     )(steps, on_chip(adj0), on_chip(adj1), off_chip(table), on_chip(pc), on_chip(ps))
 
 
-def step_kernel(mine_ref, theirs_ref, model_ref, out_ref):
+def step_kernel(mine_ref, theirs_ref, model_ref, out_hbm, out_ref, sems):
     upper = (lax.axis_index("sub") & 1) == 1
-    mine = mine_ref[...].astype(F32)
-    theirs = theirs_ref[...].astype(F32)
-    out_ref[:HALF] = model_ref[:HALF] + jnp.where(upper, theirs, mine)
-    out_ref[HALF:] = model_ref[HALF:] + jnp.where(upper, mine, theirs)
+    wide = FW // PARTS7
+    sent = []
+    for part in range(PARTS7):
+        cut = slice(part * wide, (part + 1) * wide)
+        mine = mine_ref[:, cut].astype(F32)
+        theirs = theirs_ref[:, cut].astype(F32)
+        out_ref[:HALF, cut] = model_ref[:HALF, cut] + jnp.where(upper, theirs, mine)
+        out_ref[HALF:, cut] = model_ref[HALF:, cut] + jnp.where(upper, mine, theirs)
+        lanes = pl.ds(part * wide, wide)
+        sent.append(pltpu.make_async_copy(out_ref.at[:, lanes], out_hbm.at[:, lanes], sems.at[part]))
+        sent[-1].start()
+    for copy in sent:
+        copy.wait()
 
 
 def take_step(mine, theirs, model):
-    part = pl.BlockSpec((HALF, FW // PARTS7), lambda i: (0, i))
-    wide = pl.BlockSpec((FROWS, FW // PARTS7), lambda i: (0, i))
     return pl.pallas_call(
         step_kernel,
-        grid=(PARTS7,),
         out_shape=jax.ShapeDtypeStruct((FROWS, FW), F32),
-        in_specs=[part, part, wide],
-        out_specs=wide,
+        in_specs=[VMEM_SPEC] * 3,
+        out_specs=HBM_SPEC,
+        scratch_shapes=[pltpu.VMEM((FROWS, FW), F32), pltpu.SemaphoreType.DMA((PARTS7,))],
         compiler_params=PARAMS,
         name="take_step",
-    )(mine, theirs, off_chip(model))
+    )(on_chip(mine), on_chip(theirs), on_chip(model))
 
 
 def update_table_kernel(starts_ref, offsets_ref, table_hbm, pc_ref, ps_ref, table_ref, base_ref, turn_ref, sem):

time: 163 us -> 160 us (0.982)
  Pallas kernels: 43 us -> 40 us
    pallas_call x1, Pallas kernels: 3.95 us -> 2.2 us  [take_step(): pl.pallas_call(step_kernel, out_shape=jax.ShapeDtypeStruct((FROWS, FW), F...]
where the time goes in v8:
time: 160 us; the launch traced here: 159 us
  blocking collectives  66 us (41%)
  Pallas kernels  40 us (25%)
  starting transfers between devices  28.2 us (18%)
  waiting for transfers between devices  21.5 us (13%)
  between operations  1.67 us (1%)
    all_to_all x4, blocking collectives, exchange(): lax.all_to_all(value, 'facet', split_axis=0, concat_axis=0, tiled=True)  44.9 us
    all_to_all x1, blocking collectives, to_facets(): lax.all_to_all(copies, ('facet', 'sub'), split_axis=0, concat_axis=0, til...  21.1 us
    all_to_all x2, starting transfers between devices, exchange(): lax.all_to_all(value, 'facet', split_axis=0, concat_axis=0, tiled=True)  11.1 us
    all_to_all x1, waiting for transfers between devices, to_facets(): lax.all_to_all(copies, ('facet', 'sub'), split_axis=0, concat_axis=0, til...  9.41 us
    all_to_all x1, starting transfers between devices, to_facets(): lax.all_to_all(copies, ('facet', 'sub'), split_axis=0, concat_axis=0, til...  8.17 us
    pallas_call x1, Pallas kernels, update(): pl.pallas_call(update_kernel, grid=(HIGH5 // PAIR5 // 2,), out_shape=jax....  7.79 us
    all_to_all x2, waiting for transfers between devices, exchange(): lax.all_to_all(value, 'facet', split_axis=0, concat_axis=0, tiled=True)  5.13 us
    pallas_call x1, Pallas kernels, section(): pl.pallas_call(section_kernel, out_shape=jax.ShapeDtypeStruct((FACETS, 2...  4.67 us
  transfers between devices with their start and end apart: 9, of which 6 were waited for; matrix products, arithmetic and copies ran while one was open for 1% of the time, Pallas kernels for 4%

profile of v8, /device:TPU:1, one launch (start us, length us, event | category | flops | bytes accessed | tf_op | source)
XLA Modules:
  0.0 159.4 jit_solution(293862500497568362)
XLA Ops:
  1.3 0.7 copy-done.3
  2.0 4.7 %section.1.first_ref = bf16[16,32,128]{2,1,0:T(8,128)(2,1)} custom-call(s32[1]{0:T(128)} %copy.17.column_ref, s32[2,16]{1,0:T(2,128)S(1)} %copy-done.3, f32[128,8192]{1,0:T(8,128)} %bitcast.14), custom_call_target="tpu_custom_call" | custom-call | tf_op jit(solution)/shard_map/section/pallas_call | solution.py:135
  6.7 7.6 %all-to-all-start = ((bf16[16,32,128]{2,1,0:T(8,128)(2,1)}), bf16[16,32,128]{2,1,0:T(8,128)(2,1)S(1)}, u32[]{:S(2)}, u32[]{:S(2)}) async-start(bf16[16,32,128]{2,1,0:T(8,128)(2,1)} %section.1.first_ref), calls=%async_computation | async-start | bytes 262144 | tf_op jit(solution)/shard_map/all_to_all | solution.py:592
  14.3 1.7 %row_tables.1 = (bf16[2,2048,256]{2,1,0:T(8,128)(2,1)S(1)}, f32[16,16,128]{2,1,0:T(8,128)S(1)}, f32[16,16,128]{2,1,0:T(8,128)S(1)}) custom-call(s32[2,16]{1,0:T(2,128)S(1)} %copy-done.4, s32[1,16]{1,0:T(1,128)S(1)} %copy-done.7), custom_call_target="tpu_custom_call" | custom-call | tf_op jit(solution)/shard_map/row_tables/pallas_call | solution.py:189
  16.0 5.1 %all-to-all-done.in_ref = bf16[16,32,128]{2,1,0:T(8,128)(2,1)S(1)} async-done(((bf16[16,32,128]{2,1,0:T(8,128)(2,1)}), bf16[16,32,128]{2,1,0:T(8,128)(2,1)S(1)}, u32[]{:S(2)}, u32[]{:S(2)}) %all-to-all-start) | async-done | bytes 131104 | tf_op jit(solution)/shard_map/all_to_all | solution.py:592
  21.1 2.0 %grids.2 = bf16[16,32,256]{2,1,0:T(8,128)(2,1)} custom-call(bf16[16,32,128]{2,1,0:T(8,128)(2,1)S(1)} %all-to-all-done.in_ref, f32[16,16,128]{2,1,0:T(8,128)S(1)} %get-tuple-element.15.c_ref, f32[16,16,128]{2,1,0:T(8,128)S(1)} %get-tuple-element.16.s_ref, bf16[2,2048,256]{2,1,0:T(8,128)(2,1)S(1)} %get-tuple-element.17.table_ref), custom_call_target="tpu_custom_call" | custom-call | tf_op jit(solution)/shard_map/grids/pallas_call | solution.py:229
  23.1 3.5 %all-to-all-start.1 = ((bf16[16,32,256]{2,1,0:T(8,128)(2,1)}), bf16[16,32,256]{2,1,0:T(8,128)(2,1)S(1)}, u32[]{:S(2)}, u32[]{:S(2)}) async-start(bf16[16,32,256]{2,1,0:T(8,128)(2,1)} %grids.2), calls=%async_computation.1 | async-start | bytes 524288 | tf_op jit(solution)/shard_map/all_to_all | solution.py:592
  26.7 2.1 %collective-permute-start = (s32[8,128]{1,0:T(8,128)S(1)}, s32[8,128]{1,0:T(8,128)S(1)}, u32[]{:S(2)}, u32[]{:S(2)}) collective-permute-start(s32[8,128]{1,0:T(8,128)S(1)} %broadcast_in_dim.12), channel_id=1, source_target_pairs={{0,1},{1,0},{2,3},{3,2},{4,5},{5,4},{6,7},{7,6},{8,9},{9,8},{10,11... | collective-permute-start | bytes 12296 | tf_op jit(solution)/shard_map/ppermute | solution.py:596
  28.8 0.8 collective-permute-done
  29.6 3.8 %collective-permute-start.3 = (s32[16,128]{1,0:T(8,128)S(1)}, s32[16,128]{1,0:T(8,128)S(1)}, u32[]{:S(2)}, u32[]{:S(2)}) collective-permute-start(s32[16,128]{1,0:T(8,128)S(1)} %pad_add_fusion), channel_id=1, source_target_pairs={{0,6},{1,7},{2,0},{3,1},{4,2},{5,3},{6,4},{7,5},{8,14},{9,15},{10,... | collective-permute-start | bytes 24584 | tf_op jit(solution)/shard_map/ppermute | solution.py:604
  33.4 0.7 collective-permute-start.1
  34.4 3.0 %collective-permute-done.2 = s32[16,128]{1,0:T(8,128)S(1)} collective-permute-done((s32[16,128]{1,0:T(8,128)S(1)}, s32[16,128]{1,0:T(8,128)S(1)}, u32[]{:S(2)}, u32[]{:S(2)}) %collective-permute-start.2) | collective-permute-done | bytes 8224 | tf_op jit(solution)/shard_map/ppermute | solution.py:604
  37.8 4.6 %first_visibilities.1 = (bf16[16,32,256]{2,1,0:T(8,128)(2,1)S(1)}, bf16[256,4096]{1,0:T(8,128)(2,1)S(1)}, bf16[256,4096]{1,0:T(8,128)(2,1)S(1)}) custom-call(s32[1,16]{1,0:T(1,128)S(1)} %copy-done.5, bf16[2,4096]{1,0:T(2,128)(2,1)S(1)} %bitcast.20, bf16[1,4096]{1,0:T(2,128)(2,1)S(1)} %bitcast.22, bf16[16,32,256]{2,1,0:T(8,128)(2,1)S(1)} %all-to-all-done.1.in_ref, ...), custom_call_target="tpu_custom_call" | custom-call | tf_op jit(solution)/shard_map/first_visibilities/pallas_call | solution.py:347
  42.4 14.1 %all_to_all.40.in_ref = bf16[16,32,256]{2,1,0:T(8,128)(2,1)S(1)} all-to-all(bf16[16,32,256]{2,1,0:T(8,128)(2,1)S(1)} %get-tuple-element.19), channel_id=1, replica_groups=mesh['facet'=16,'sub'=8] {'facet'}, dimensions={0} | all-to-all | bytes 524288 | tf_op jit(solution)/shard_map/all_to_all | solution.py:592
  56.5 1.8 %adjoint.2 = bf16[16,8,16,128]{3,2,1,0:T(8,128)(2,1)S(1)} custom-call(bf16[16,32,256]{2,1,0:T(8,128)(2,1)S(1)} %all_to_all.40.in_ref, f32[16,16,128]{2,1,0:T(8,128)S(1)} %get-tuple-element.15.c_ref, f32[16,16,128]{2,1,0:T(8,128)S(1)} %get-tuple-element.16.s_ref, bf16[2,2048,256]{2,1,0:T(8,128)(2,1)S(1)} %get-tuple-element.17.table_ref), custom_call_target="tpu_custom_call" | custom-call | tf_op jit(solution)/shard_map/adjoint/pallas_call | solution.py:279
  58.3 21.1 %all_to_all.41.adj0_ref = bf16[128,16,128]{2,1,0:T(8,128)(2,1)S(1)} all-to-all(bf16[128,16,128]{2,1,0:T(8,128)(2,1)S(1)} %bitcast.17), channel_id=1, replica_groups=mesh['facet'=16,'sub'=8] {'facet','sub'}, dimensions={0} | all-to-all | bytes 1048576 | tf_op jit(solution)/shard_map/all_to_all | solution.py:610
  79.4 1.1 collective-permute-start.4
  80.5 1.5 collective-permute-done.4
  82.1 3.7 %gram.1 = bf16[16,32,128]{2,1,0:T(8,128)(2,1)S(1)} custom-call(f32[2]{0:T(128)S(1)} %copy-done.6, s32[8]{0:T(128)S(1)} %pad_add_fusion.1.starts_ref, s32[1]{0:T(128)} %copy.17.column_ref, s32[2,16]{1,0:T(2,128)S(1)} %copy-done.4, bf16[16,8,16,128]{3,2,1,0:T(8,128)(2,1)S(1)} %bitcast.16, bf16[16,8,16,128]{3,2,1,0:T(8,128)(2,1)S(1)} %bitcast.18, ...), custom_call_target="tpu_custom_call" | custom-call | tf_op jit(solution)/shard_map/gram/pallas_call | solution.py:438
  85.8 9.3 %all_to_all.42.in_ref = bf16[16,32,128]{2,1,0:T(8,128)(2,1)S(1)} all-to-all(bf16[16,32,128]{2,1,0:T(8,128)(2,1)S(1)} %gram.1), channel_id=1, replica_groups=mesh['facet'=16,'sub'=8] {'facet'}, dimensions={0} | all-to-all | bytes 262144 | tf_op jit(solution)/shard_map/all_to_all | solution.py:592
  95.1 1.3 grids.3
  96.4 10.7 %all_to_all.43.in_ref = bf16[16,32,256]{2,1,0:T(8,128)(2,1)S(1)} all-to-all(bf16[16,32,256]{2,1,0:T(8,128)(2,1)S(1)} %grids.3), channel_id=1, replica_groups=mesh['facet'=16,'sub'=8] {'facet'}, dimensions={0} | all-to-all | bytes 524288 | tf_op jit(solution)/shard_map/all_to_all | solution.py:592
  107.1 3.4 %last_visibilities.1 = (bf16[16,32,256]{2,1,0:T(8,128)(2,1)S(1)}, f32[2,4096]{1,0:T(2,128)S(1)}) custom-call(s32[1,16]{1,0:T(1,128)S(1)} %copy-done.5, bf16[2,4096]{1,0:T(2,128)(2,1)S(1)} %bitcast.21, bf16[1,4096]{1,0:T(2,128)(2,1)S(1)} %bitcast.23, bf16[16,32,256]{2,1,0:T(8,128)(2,1)S(1)} %all_to_all.43.in_ref, ...), custom_call_target="tpu_custom_call" | custom-call | tf_op jit(solution)/shard_map/last_visibilities/pallas_call | solution.py:363
  110.5 10.8 %all_to_all.44.in_ref = bf16[16,32,256]{2,1,0:T(8,128)(2,1)S(1)} all-to-all(bf16[16,32,256]{2,1,0:T(8,128)(2,1)S(1)} %get-tuple-element.23), channel_id=1, replica_groups=mesh['facet'=16,'sub'=8] {'facet'}, dimensions={0} | all-to-all | bytes 524288 | tf_op jit(solution)/shard_map/all_to_all | solution.py:592
  121.3 2.5 %adjoint.3 = bf16[16,8,16,128]{3,2,1,0:T(8,128)(2,1)} custom-call(bf16[16,32,256]{2,1,0:T(8,128)(2,1)S(1)} %all_to_all.44.in_ref, f32[16,16,128]{2,1,0:T(8,128)S(1)} %get-tuple-element.15.c_ref, f32[16,16,128]{2,1,0:T(8,128)S(1)} %get-tuple-element.16.s_ref, bf16[2,2048,256]{2,1,0:T(8,128)(2,1)S(1)} %get-tuple-element.17.table_ref), custom_call_target="tpu_custom_call" | custom-call | tf_op jit(solution)/shard_map/adjoint/pallas_call | solution.py:279
  123.9 8.2 %all-to-all-start.7 = ((bf16[128,16,128]{2,1,0:T(8,128)(2,1)}), bf16[128,16,128]{2,1,0:T(8,128)(2,1)S(1)}, u32[]{:S(2)}, u32[]{:S(2)}) async-start(bf16[128,16,128]{2,1,0:T(8,128)(2,1)} %bitcast.7), calls=%async_computation.7 | async-start | bytes 1048576 | tf_op jit(solution)/shard_map/all_to_all | solution.py:610
  132.0 4.3 %update_tables.1 = (bf16[4096,512]{1,0:T(8,128)(2,1)}, f32[16,2048]{1,0:T(8,128)S(1)}, f32[16,2048]{1,0:T(8,128)S(1)}) custom-call(s32[8]{0:T(128)S(1)} %pad_add_fusion.1.starts_ref, s32[2,16]{1,0:T(2,128)S(1)} %copy-done.4), custom_call_target="tpu_custom_call" | custom-call | tf_op jit(solution)/shard_map/update_tables/pallas_call | solution.py:571
  136.3 9.4 %all-to-all-done.7.adj1_ref = bf16[128,16,128]{2,1,0:T(8,128)(2,1)S(1)} async-done(((bf16[128,16,128]{2,1,0:T(8,128)(2,1)}), bf16[128,16,128]{2,1,0:T(8,128)(2,1)S(1)}, u32[]{:S(2)}, u32[]{:S(2)}) %all-to-all-start.7) | async-done | bytes 524320 | tf_op jit(solution)/shard_map/all_to_all | solution.py:610
  145.7 7.8 %update.1.mine_ref = bf16[64,8192]{1,0:T(8,128)(2,1)S(1)} custom-call(f32[2]{0:T(128)S(1)} %copy-done.6, bf16[128,16,128]{2,1,0:T(8,128)(2,1)S(1)} %all_to_all.41.adj0_ref, bf16[128,16,128]{2,1,0:T(8,128)(2,1)S(1)} %all-to-all-done.7.adj1_ref, bf16[4096,512]{1,0:T(8,128)(2,1)} %get-tuple-element.24.table_hbm, f32[16,2048]{1,0:T(8,128)S(1)} %get-tuple-element.25.pc_ref, ...), custom_call_target="tpu_custom_call" | custom-call | tf_op jit(solution)/shard_map/update/pallas_call | solution.py:495
  153.5 1.2 collective-permute-start.5
  155.4 1.6 %collective-permute-done.5.theirs_ref = bf16[64,8192]{1,0:T(8,128)(2,1)S(1)} collective-permute-done((bf16[64,8192]{1,0:T(8,128)(2,1)S(1)}, bf16[64,8192]{1,0:T(8,128)(2,1)S(1)}, u32[]{:S(2)}, u32[]{:S(2)}) %collective-permute-start.5) | collective-permute-done | bytes 1048608 | tf_op jit(solution)/shard_map/ppermute | solution.py:596
  157.0 2.2 %take_step.1 = f32[128,8192]{1,0:T(8,128)} custom-call(bf16[64,8192]{1,0:T(8,128)(2,1)S(1)} %update.1.mine_ref, bf16[64,8192]{1,0:T(8,128)(2,1)S(1)} %collective-permute-done.5.theirs_ref, f32[128,8192]{1,0:T(8,128)S(1)} %bitcast.15), custom_call_target="tpu_custom_call" | custom-call | tf_op jit(solution)/shard_map/take_step/pallas_call | solution.py:531
  (34 shorter events, 1.4 us)
Async XLA Ops:
  0.6 37.1 %copy-start.2 = (bf16[1,1,4096]{2,1,0:T(2,128)(2,1)S(1)}, bf16[1,1,4096]{2,1,0:T(2,128)(2,1)}, u32[]{:S(2)}) copy-start(bf16[1,1,4096]{2,1,0:T(2,128)(2,1)} %param.17) | copy-start | bytes 24580
  0.6 37.1 %copy-start.1 = (bf16[2,1,1,4096]{3,0,2,1:T(2,128)(2,1)S(1)}, bf16[2,1,1,4096]{3,0,2,1:T(2,128)(2,1)}, u32[]{:S(2)}) copy-start(bf16[2,1,1,4096]{3,0,2,1:T(2,128)(2,1)} %param.16) | copy-start | bytes 49156
  1.3 0.7 copy-start.3
  2.0 12.3 %copy-start.4 = (s32[2,16]{1,0:T(2,128)S(1)}, s32[2,16]{1,0:T(2,128)}, u32[]{:S(2)}) copy-start(s32[2,16]{1,0:T(2,128)} %offsets_ref.7) | copy-start | bytes 388
  2.0 12.3 %copy-start.7 = (s32[1,16]{1,0:T(1,128)S(1)}, s32[1,16]{1,0:T(1,128)}, u32[]{:S(2)}) copy-start(s32[1,16]{1,0:T(1,128)} %rows_ref.1) | copy-start | bytes 196
  2.0 32.1 %copy-start.8 = (s32[2,1,1,4096]{3,2,1,0:T(1,128)S(1)}, s32[2,1,1,4096]{3,2,1,0:T(1,128)}, u32[]{:S(2)}) copy-start(s32[2,1,1,4096]{3,2,1,0:T(1,128)} %param.15) | copy-start | bytes 98308
  2.0 35.8 %copy-start.5 = (s32[1,16]{1,0:T(1,128)S(1)}, s32[1,16]{1,0:T(1,128)}, u32[]{:S(2)}) copy-start(s32[1,16]{1,0:T(1,128)} %counts_ref.3) | copy-start | bytes 196
  6.7 14.5 %all-to-all-start = ((bf16[16,32,128]{2,1,0:T(8,128)(2,1)}), bf16[16,32,128]{2,1,0:T(8,128)(2,1)S(1)}, u32[]{:S(2)}, u32[]{:S(2)}) async-start(bf16[16,32,128]{2,1,0:T(8,128)(2,1)} %section.1.first_ref), calls=%async_computation | async-start | bytes 262144 | tf_op jit(solution)/shard_map/all_to_all | solution.py:592
  21.1 60.9 %copy-start.6 = (f32[2]{0:T(128)S(1)}, f32[2]{0:T(128)}, u32[]{:S(2)}) copy-start(f32[2]{0:T(128)} %step_ref.3) | copy-start | bytes 28
  23.1 14.6 %all-to-all-start.1 = ((bf16[16,32,256]{2,1,0:T(8,128)(2,1)}), bf16[16,32,256]{2,1,0:T(8,128)(2,1)S(1)}, u32[]{:S(2)}, u32[]{:S(2)}) async-start(bf16[16,32,256]{2,1,0:T(8,128)(2,1)} %grids.2), calls=%async_computation.1 | async-start | bytes 524288 | tf_op jit(solution)/shard_map/all_to_all | solution.py:592
  26.7 2.9 %collective-permute-start = (s32[8,128]{1,0:T(8,128)S(1)}, s32[8,128]{1,0:T(8,128)S(1)}, u32[]{:S(2)}, u32[]{:S(2)}) collective-permute-start(s32[8,128]{1,0:T(8,128)S(1)} %broadcast_in_dim.12), channel_id=1, source_target_pairs={{0,1},{1,0},{2,3},{3,2},{4,5},{5,4},{6,7},{7,6},{8,9},{9,8},{10,11... | collective-permute-start | bytes 12296 | tf_op jit(solution)/shard_map/ppermute | solution.py:596
  29.6 4.6 %collective-permute-start.3 = (s32[16,128]{1,0:T(8,128)S(1)}, s32[16,128]{1,0:T(8,128)S(1)}, u32[]{:S(2)}, u32[]{:S(2)}) collective-permute-start(s32[16,128]{1,0:T(8,128)S(1)} %pad_add_fusion), channel_id=1, source_target_pairs={{0,6},{1,7},{2,0},{3,1},{4,2},{5,3},{6,4},{7,5},{8,14},{9,15},{10,... | collective-permute-start | bytes 24584 | tf_op jit(solution)/shard_map/ppermute | solution.py:604
  33.4 4.0 %collective-permute-start.2 = (s32[16,128]{1,0:T(8,128)S(1)}, s32[16,128]{1,0:T(8,128)S(1)}, u32[]{:S(2)}, u32[]{:S(2)}) collective-permute-start(s32[16,128]{1,0:T(8,128)S(1)} %pad_add_fusion), channel_id=1, source_target_pairs={{0,4},{1,5},{2,6},{3,7},{4,0},{5,1},{6,2},{7,3},{8,12},{9,13},{10,... | collective-permute-start | bytes 24584 | tf_op jit(solution)/shard_map/ppermute | solution.py:604
  33.4 4.1 %collective-permute-start.1 = (s32[16,128]{1,0:T(8,128)S(1)}, s32[16,128]{1,0:T(8,128)S(1)}, u32[]{:S(2)}, u32[]{:S(2)}) collective-permute-start(s32[16,128]{1,0:T(8,128)S(1)} %pad_add_fusion), channel_id=1, source_target_pairs={{0,2},{1,3},{2,4},{3,5},{4,6},{5,7},{6,0},{7,1},{8,10},{9,11},{10,... | collective-permute-start | bytes 24584 | tf_op jit(solution)/shard_map/ppermute | solution.py:604
  79.4 2.7 %collective-permute-start.4 = (bf16[128,16,128]{2,1,0:T(8,128)(2,1)S(1)}, bf16[128,16,128]{2,1,0:T(8,128)(2,1)S(1)}, u32[]{:S(2)}, u32[]{:S(2)}) collective-permute-start(bf16[128,16,128]{2,1,0:T(8,128)(2,1)S(1)} %all_to_all.41.adj0_ref), channel_id=1, source_target_pairs={{0,1},{1,0},{2,3},{3,2},{4,5},{5,4},{6,7},{7,6},{8,9},{9,8},{10,11... | collective-permute-start | bytes 1572872 | tf_op jit(solution)/shard_map/ppermute | solution.py:596
  123.9 21.8 %all-to-all-start.7 = ((bf16[128,16,128]{2,1,0:T(8,128)(2,1)}), bf16[128,16,128]{2,1,0:T(8,128)(2,1)S(1)}, u32[]{:S(2)}, u32[]{:S(2)}) async-start(bf16[128,16,128]{2,1,0:T(8,128)(2,1)} %bitcast.7), calls=%async_computation.7 | async-start | bytes 1048576 | tf_op jit(solution)/shard_map/all_to_all | solution.py:610
  145.7 11.3 %copy-start = (f32[1,128,8192]{2,1,0:T(8,128)S(1)}, f32[1,128,8192]{2,1,0:T(8,128)}, u32[]{:S(2)}) copy-start(f32[1,128,8192]{2,1,0:T(8,128)} %param.9) | copy-start | bytes 12582916
  153.5 3.5 %collective-permute-start.5 = (bf16[64,8192]{1,0:T(8,128)(2,1)S(1)}, bf16[64,8192]{1,0:T(8,128)(2,1)S(1)}, u32[]{:S(2)}, u32[]{:S(2)}) collective-permute-start(bf16[64,8192]{1,0:T(8,128)(2,1)S(1)} %update.1.mine_ref), channel_id=1, source_target_pairs={{0,1},{1,0},{2,3},{3,2},{4,5},{5,4},{6,7},{7,6},{8,9},{9,8},{10,11... | collective-permute-start | bytes 3145736 | tf_op jit(solution)/shard_map/ppermute | solution.py:596

commit v9 on v8

--- a/solution.py
+++ b/solution.py
@@ -150,7 +150,7 @@
         ],
         compiler_params=PARAMS,
         name="section",
-    )(column_start, offsets, off_chip(model))
+    )(column_start, off_chip(offsets), off_chip(model))
 
 
 def kernel_columns(position):
@@ -374,11 +374,6 @@
     )(counts, obs, weight, on_chip(grid), on_chip(ku), on_chip(kv))
 
 
-def start_of(starts_ref, column):
-    own = lax.axis_index("sub")
-    return starts_ref[2 * (((own >> 1) - (column >> 1)) & (NCOL // 2 - 1)) + ((own ^ column) & 1)]
-
-
 def dirichlet(distance, pixel_start):
     distance = ((distance & (NIMG - 1)) ^ (NIMG // 2)) - NIMG // 2
     top = cos_sin((distance * (NIMG // (NIMG // FW * 2))) & (NIMG - 1))[1]
@@ -395,7 +390,7 @@
     row = iota((NCOL, wide), 0)
     starts = jnp.zeros((NCOL, wide), I32)
     for c in range(NCOL):
-        starts = jnp.where(row == c, start_of(starts_ref, c), starts)
+        starts = jnp.where(row == c, starts_ref[c], starts)
     lane = iota((NCOL, wide), 1)
     v_ref[0], v_ref[1] = dirichlet(starts - own + (lane - (SGW - 1)), pixel_start)
     v_ref[2], v_ref[3] = dirichlet(starts + own + (2 * (SGW - 1) - lane), pixel_start)
@@ -544,7 +539,7 @@
     line = iota((group, STEP5), 0)
     freq = line & (SLICE - 1)
     for c in range(NCOL):
-        freq = freq + jnp.where((line >> 4) == c, start_of(starts_ref, c), 0)
+        freq = freq + jnp.where((line >> 4) == c, starts_ref[c], 0)
     base_ref[0], base_ref[1] = phase(freq, iota((group, STEP5), 1))
     turn_ref[0], turn_ref[1] = phase(SLICE * iota((FACETS, STEP5), 0), iota((FACETS, STEP5), 1))
 
@@ -561,7 +556,7 @@
     lane = iota((HIGH5, COLUMNS), 1)
     freq = SLICE * (lane >> 7) + (lane & (SLICE - 1))
     for c in range(NCOL):
-        freq = freq + jnp.where(((lane >> 4) & (NCOL - 1)) == c, start_of(starts_ref, c), 0)
+        freq = freq + jnp.where(((lane >> 4) & (NCOL - 1)) == c, starts_ref[c], 0)
     pixel_start = offsets_ref[1, lax.axis_index("facet")]
     pc_ref[...], ps_ref[...] = phase(freq, pixel_start + STEP5 * iota((HIGH5, COLUMNS), 0))
     write_out([(table_ref, table_hbm, sem)])
@@ -592,17 +587,8 @@
     return lax.all_to_all(value, "facet", split_axis=0, concat_axis=0, tiled=True)
 
 
-def other_core(value):
-    return lax.ppermute(value, "sub", [(i, i ^ 1) for i in range(NCOL)])
-
-
-def all_starts(own):
-    lines = lax.optimization_barrier(jnp.broadcast_to(own[:, None], (8, 128)))
-    pair = jnp.concatenate([lines, other_core(lines)], axis=0)
-    chips = [pair]
-    for away in range(2, NCOL, 2):
-        chips.append(lax.ppermute(pair, "sub", [(i, (i + away) % NCOL) for i in range(NCOL)]))
-    return jnp.concatenate([chip[::8, 0] for chip in chips])
+def swapped(value, bit):
+    return lax.ppermute(value, "sub", [(i, i ^ bit) for i in range(NCOL)])
 
 
 def to_facets(value):
@@ -621,24 +607,29 @@
     vis_obs,
     vis_weight,
 ):
-    column_starts = all_starts(col_offsets)
+    mine = jnp.arange(NCOL, dtype=I32) == lax.axis_index("sub")
+    column_starts = jnp.where(mine, col_offsets[0], 0)
+    column_starts = column_starts + swapped(column_starts, 1)
     uv = vis_uv.reshape(2, VCAP)
     obs = vis_obs.reshape(2, VCAP)
     weight = vis_weight.reshape(1, VCAP)
     model = model_image[0]
     first = section(col_offsets, facet_offsets, model)
     rows = row_tables(facet_offsets, row_offsets)
-    grid = exchange(grids(exchange(first), rows))
+    sections, column_starts = lax.optimization_barrier((exchange(first), column_starts))
+    for bit in (2, 4):
+        column_starts = column_starts + swapped(column_starts, bit)
+    grid = exchange(grids(sections, rows))
     gridded, ku, kv = first_visibilities(counts, obs, weight, grid, uv)
     gridded, column_starts = lax.optimization_barrier((gridded, column_starts))
     adj0 = to_facets(adjoint(exchange(gridded), rows))
-    second = gram(step_sizes, column_starts, col_offsets, facet_offsets, adj0, other_core(adj0), first)
+    second = gram(step_sizes, column_starts, col_offsets, facet_offsets, adj0, swapped(adj0, 1), first)
     grid = exchange(grids(exchange(second), rows))
     gridded, residual = last_visibilities(counts, obs, weight, grid, ku, kv)
     adj1 = to_facets(adjoint(exchange(gridded), rows))
     tables = update_tables(column_starts, facet_offsets)
     step = update(step_sizes, adj0, adj1, tables)
-    model = take_step(step, other_core(step), model)
+    model = take_step(step, swapped(step, 1), model)
     return model[None], residual.reshape(2, 1, 1, VCAP)
 
 

time: 160 us -> 160 us (level)
  blocking collectives: 66 us -> 69.2 us
  waiting for transfers between devices: 21.5 us -> 19.7 us
    all_to_all x1, blocking collectives: 21.1 us -> 24.6 us  [to_facets(): lax.all_to_all(copies, ('facet', 'sub'), split_axis=0, concat_axis=0, til...]
    ppermute x6 -> x5, waiting for transfers between devices: 6.99 us -> 5.33 us  [swapped(): return lax.ppermute(value, 'sub', [(i, i ^ bit) for i in range(NCOL)])]
    ppermute x6 -> x5, starting transfers between devices: 8.91 us -> 9.01 us  [swapped(): return lax.ppermute(value, 'sub', [(i, i ^ bit) for i in range(NCOL)])]
  transfers between devices with their start and end apart: 9 -> 8, of which waited for: 6 -> 6; matrix products, arithmetic and copies ran while one was open for 1% -> 0% of each run, Pallas kernels for 4% -> 7%
where the time goes in v9:
time: 160 us; the launch traced here: 159 us
  blocking collectives  69.2 us (43%)
  Pallas kernels  40 us (25%)
  starting transfers between devices  27.6 us (17%)
  waiting for transfers between devices  19.7 us (12%)
  between operations  1.74 us (1%)
    all_to_all x4, blocking collectives, exchange(): lax.all_to_all(value, 'facet', split_axis=0, concat_axis=0, tiled=True)  44.6 us
    all_to_all x1, blocking collectives, to_facets(): lax.all_to_all(copies, ('facet', 'sub'), split_axis=0, concat_axis=0, til...  24.6 us
    all_to_all x2, starting transfers between devices, exchange(): lax.all_to_all(value, 'facet', split_axis=0, concat_axis=0, tiled=True)  10.4 us
    all_to_all x1, waiting for transfers between devices, to_facets(): lax.all_to_all(copies, ('facet', 'sub'), split_axis=0, concat_axis=0, til...  9.42 us
    ppermute x5, starting transfers between devices, swapped(): return lax.ppermute(value, 'sub', [(i, i ^ bit) for i in range(NCOL)])  9.01 us
    all_to_all x1, starting transfers between devices, to_facets(): lax.all_to_all(copies, ('facet', 'sub'), split_axis=0, concat_axis=0, til...  8.16 us
    pallas_call x1, Pallas kernels, update(): pl.pallas_call(update_kernel, grid=(HIGH5 // PAIR5 // 2,), out_shape=jax....  7.79 us
    ppermute x5, waiting for transfers between devices, swapped(): return lax.ppermute(value, 'sub', [(i, i ^ bit) for i in range(NCOL)])  5.33 us
  transfers between devices with their start and end apart: 8, of which 6 were waited for; matrix products, arithmetic and copies ran while one was open for 0% of the time, Pallas kernels for 7%

profile of v9, /device:TPU:1, one launch (start us, length us, event | category | flops | bytes accessed | tf_op | source)
XLA Modules:
  0.0 159.0 jit_solution(6705321072437580431)
XLA Ops:
  1.4 1.5 collective-permute-start
  2.9 4.8 %section.1.first_ref = bf16[16,32,128]{2,1,0:T(8,128)(2,1)} custom-call(s32[1]{0:T(128)} %copy.15.column_ref, s32[2,16]{1,0:T(2,128)} %offsets_ref.7, f32[128,8192]{1,0:T(8,128)} %bitcast.15), custom_call_target="tpu_custom_call" | custom-call | tf_op jit(solution)/shard_map/section/pallas_call | solution.py:135
  7.7 6.9 %all-to-all-start = ((bf16[16,32,128]{2,1,0:T(8,128)(2,1)}), bf16[16,32,128]{2,1,0:T(8,128)(2,1)S(1)}, u32[]{:S(2)}, u32[]{:S(2)}) async-start(bf16[16,32,128]{2,1,0:T(8,128)(2,1)} %section.1.first_ref), calls=%async_computation | async-start | bytes 262144 | tf_op jit(solution)/shard_map/all_to_all | solution.py:587
  14.6 1.7 %row_tables.1 = (bf16[2,2048,256]{2,1,0:T(8,128)(2,1)S(1)}, f32[16,16,128]{2,1,0:T(8,128)S(1)}, f32[16,16,128]{2,1,0:T(8,128)S(1)}) custom-call(s32[2,16]{1,0:T(2,128)S(1)} %copy-done.3, s32[1,16]{1,0:T(1,128)S(1)} %copy-done.6), custom_call_target="tpu_custom_call" | custom-call | tf_op jit(solution)/shard_map/row_tables/pallas_call | solution.py:189
  16.3 5.0 %all-to-all-done.in_ref = bf16[16,32,128]{2,1,0:T(8,128)(2,1)S(1)} async-done(((bf16[16,32,128]{2,1,0:T(8,128)(2,1)}), bf16[16,32,128]{2,1,0:T(8,128)(2,1)S(1)}, u32[]{:S(2)}, u32[]{:S(2)}) %all-to-all-start) | async-done | bytes 131104 | tf_op jit(solution)/shard_map/all_to_all | solution.py:587
  21.3 2.0 %grids.2 = bf16[16,32,256]{2,1,0:T(8,128)(2,1)} custom-call(bf16[16,32,128]{2,1,0:T(8,128)(2,1)S(1)} %all-to-all-done.in_ref, f32[16,16,128]{2,1,0:T(8,128)S(1)} %get-tuple-element.18.c_ref, f32[16,16,128]{2,1,0:T(8,128)S(1)} %get-tuple-element.19.s_ref, bf16[2,2048,256]{2,1,0:T(8,128)(2,1)S(1)} %get-tuple-element.20.table_ref), custom_call_target="tpu_custom_call" | custom-call | tf_op jit(solution)/shard_map/grids/pallas_call | solution.py:229
  23.3 3.6 %all-to-all-start.1 = ((bf16[16,32,256]{2,1,0:T(8,128)(2,1)}), bf16[16,32,256]{2,1,0:T(8,128)(2,1)S(1)}, u32[]{:S(2)}, u32[]{:S(2)}) async-start(bf16[16,32,256]{2,1,0:T(8,128)(2,1)} %grids.2), calls=%async_computation.1 | async-start | bytes 524288 | tf_op jit(solution)/shard_map/all_to_all | solution.py:587
  26.9 1.7 %collective-permute-start.1 = (s32[8]{0:T(128)S(1)}, s32[8]{0:T(128)S(1)}, u32[]{:S(2)}, u32[]{:S(2)}) collective-permute-start(s32[8]{0:T(128)S(1)} %fusion), channel_id=1, source_target_pairs={{0,2},{1,3},{2,0},{3,1},{4,6},{5,7},{6,4},{7,5},{8,10},{9,11},{10,... | collective-permute-start | bytes 104 | tf_op jit(solution)/shard_map/ppermute | solution.py:591
  28.6 0.9 collective-permute-done.1
  29.6 3.4 %collective-permute-start.2 = (s32[8]{0:T(128)S(1)}, s32[8]{0:T(128)S(1)}, u32[]{:S(2)}, u32[]{:S(2)}) collective-permute-start(s32[8]{0:T(128)S(1)} %add.10), channel_id=1, source_target_pairs={{0,4},{1,5},{2,6},{3,7},{4,0},{5,1},{6,2},{7,3},{8,12},{9,13},{10,... | collective-permute-start | bytes 104 | tf_op jit(solution)/shard_map/ppermute | solution.py:591
  33.0 1.2 collective-permute-done.2
  34.2 4.6 %first_visibilities.1 = (bf16[16,32,256]{2,1,0:T(8,128)(2,1)S(1)}, bf16[256,4096]{1,0:T(8,128)(2,1)S(1)}, bf16[256,4096]{1,0:T(8,128)(2,1)S(1)}) custom-call(s32[1,16]{1,0:T(1,128)S(1)} %copy-done.4, bf16[2,4096]{1,0:T(2,128)(2,1)S(1)} %bitcast.21, bf16[1,4096]{1,0:T(2,128)(2,1)S(1)} %bitcast.23, bf16[16,32,256]{2,1,0:T(8,128)(2,1)S(1)} %all-to-all-done.1.in_ref, ...), custom_call_target="tpu_custom_call" | custom-call | tf_op jit(solution)/shard_map/first_visibilities/pallas_call | solution.py:347
  38.8 13.8 %all_to_all.40.in_ref = bf16[16,32,256]{2,1,0:T(8,128)(2,1)S(1)} all-to-all(bf16[16,32,256]{2,1,0:T(8,128)(2,1)S(1)} %get-tuple-element.23), channel_id=1, replica_groups=mesh['facet'=16,'sub'=8] {'facet'}, dimensions={0} | all-to-all | bytes 524288 | tf_op jit(solution)/shard_map/all_to_all | solution.py:587
  52.6 1.8 %adjoint.2 = bf16[16,8,16,128]{3,2,1,0:T(8,128)(2,1)S(1)} custom-call(bf16[16,32,256]{2,1,0:T(8,128)(2,1)S(1)} %all_to_all.40.in_ref, f32[16,16,128]{2,1,0:T(8,128)S(1)} %get-tuple-element.18.c_ref, f32[16,16,128]{2,1,0:T(8,128)S(1)} %get-tuple-element.19.s_ref, bf16[2,2048,256]{2,1,0:T(8,128)(2,1)S(1)} %get-tuple-element.20.table_ref), custom_call_target="tpu_custom_call" | custom-call | tf_op jit(solution)/shard_map/adjoint/pallas_call | solution.py:279
  54.4 24.6 %all_to_all.41.adj0_ref = bf16[128,16,128]{2,1,0:T(8,128)(2,1)S(1)} all-to-all(bf16[128,16,128]{2,1,0:T(8,128)(2,1)S(1)} %bitcast.18), channel_id=1, replica_groups=mesh['facet'=16,'sub'=8] {'facet','sub'}, dimensions={0} | all-to-all | bytes 1048576 | tf_op jit(solution)/shard_map/all_to_all | solution.py:596
  79.1 1.1 collective-permute-start.3
  80.2 1.5 collective-permute-done.3
  81.7 3.7 %gram.1 = bf16[16,32,128]{2,1,0:T(8,128)(2,1)S(1)} custom-call(f32[2]{0:T(128)S(1)} %copy-done.5, s32[8]{0:T(128)S(1)} %add.11.starts_ref, s32[1]{0:T(128)} %copy.15.column_ref, s32[2,16]{1,0:T(2,128)S(1)} %copy-done.3, bf16[16,8,16,128]{3,2,1,0:T(8,128)(2,1)S(1)} %bitcast.17, bf16[16,8,16,128]{3,2,1,0:T(8,128)(2,1)S(1)} %bitcast.19, ...), custom_call_target="tpu_custom_call" | custom-call | tf_op jit(solution)/shard_map/gram/pallas_call | solution.py:433
  85.4 9.3 %all_to_all.42.in_ref = bf16[16,32,128]{2,1,0:T(8,128)(2,1)S(1)} all-to-all(bf16[16,32,128]{2,1,0:T(8,128)(2,1)S(1)} %gram.1), channel_id=1, replica_groups=mesh['facet'=16,'sub'=8] {'facet'}, dimensions={0} | all-to-all | bytes 262144 | tf_op jit(solution)/shard_map/all_to_all | solution.py:587
  94.8 1.3 grids.3
  96.1 10.7 %all_to_all.43.in_ref = bf16[16,32,256]{2,1,0:T(8,128)(2,1)S(1)} all-to-all(bf16[16,32,256]{2,1,0:T(8,128)(2,1)S(1)} %grids.3), channel_id=1, replica_groups=mesh['facet'=16,'sub'=8] {'facet'}, dimensions={0} | all-to-all | bytes 524288 | tf_op jit(solution)/shard_map/all_to_all | solution.py:587
  106.8 3.4 %last_visibilities.1 = (bf16[16,32,256]{2,1,0:T(8,128)(2,1)S(1)}, f32[2,4096]{1,0:T(2,128)S(1)}) custom-call(s32[1,16]{1,0:T(1,128)S(1)} %copy-done.4, bf16[2,4096]{1,0:T(2,128)(2,1)S(1)} %bitcast.22, bf16[1,4096]{1,0:T(2,128)(2,1)S(1)} %bitcast.24, bf16[16,32,256]{2,1,0:T(8,128)(2,1)S(1)} %all_to_all.43.in_ref, ...), custom_call_target="tpu_custom_call" | custom-call | tf_op jit(solution)/shard_map/last_visibilities/pallas_call | solution.py:363
  110.2 10.8 %all_to_all.44.in_ref = bf16[16,32,256]{2,1,0:T(8,128)(2,1)S(1)} all-to-all(bf16[16,32,256]{2,1,0:T(8,128)(2,1)S(1)} %get-tuple-element.27), channel_id=1, replica_groups=mesh['facet'=16,'sub'=8] {'facet'}, dimensions={0} | all-to-all | bytes 524288 | tf_op jit(solution)/shard_map/all_to_all | solution.py:587
  121.0 2.5 %adjoint.3 = bf16[16,8,16,128]{3,2,1,0:T(8,128)(2,1)} custom-call(bf16[16,32,256]{2,1,0:T(8,128)(2,1)S(1)} %all_to_all.44.in_ref, f32[16,16,128]{2,1,0:T(8,128)S(1)} %get-tuple-element.18.c_ref, f32[16,16,128]{2,1,0:T(8,128)S(1)} %get-tuple-element.19.s_ref, bf16[2,2048,256]{2,1,0:T(8,128)(2,1)S(1)} %get-tuple-element.20.table_ref), custom_call_target="tpu_custom_call" | custom-call | tf_op jit(solution)/shard_map/adjoint/pallas_call | solution.py:279
  123.5 8.2 %all-to-all-start.7 = ((bf16[128,16,128]{2,1,0:T(8,128)(2,1)}), bf16[128,16,128]{2,1,0:T(8,128)(2,1)S(1)}, u32[]{:S(2)}, u32[]{:S(2)}) async-start(bf16[128,16,128]{2,1,0:T(8,128)(2,1)} %bitcast.7), calls=%async_computation.7 | async-start | bytes 1048576 | tf_op jit(solution)/shard_map/all_to_all | solution.py:596
  131.7 4.2 %update_tables.1 = (bf16[4096,512]{1,0:T(8,128)(2,1)}, f32[16,2048]{1,0:T(8,128)S(1)}, f32[16,2048]{1,0:T(8,128)S(1)}) custom-call(s32[8]{0:T(128)S(1)} %add.11.starts_ref, s32[2,16]{1,0:T(2,128)S(1)} %copy-done.3), custom_call_target="tpu_custom_call" | custom-call | tf_op jit(solution)/shard_map/update_tables/pallas_call | solution.py:566
  135.9 9.4 %all-to-all-done.7.adj1_ref = bf16[128,16,128]{2,1,0:T(8,128)(2,1)S(1)} async-done(((bf16[128,16,128]{2,1,0:T(8,128)(2,1)}), bf16[128,16,128]{2,1,0:T(8,128)(2,1)S(1)}, u32[]{:S(2)}, u32[]{:S(2)}) %all-to-all-start.7) | async-done | bytes 524320 | tf_op jit(solution)/shard_map/all_to_all | solution.py:596
  145.3 7.8 %update.1.mine_ref = bf16[64,8192]{1,0:T(8,128)(2,1)S(1)} custom-call(f32[2]{0:T(128)S(1)} %copy-done.5, bf16[128,16,128]{2,1,0:T(8,128)(2,1)S(1)} %all_to_all.41.adj0_ref, bf16[128,16,128]{2,1,0:T(8,128)(2,1)S(1)} %all-to-all-done.7.adj1_ref, bf16[4096,512]{1,0:T(8,128)(2,1)} %get-tuple-element.28.table_hbm, f32[16,2048]{1,0:T(8,128)S(1)} %get-tuple-element.29.pc_ref, ...), custom_call_target="tpu_custom_call" | custom-call | tf_op jit(solution)/shard_map/update/pallas_call | solution.py:490
  153.1 1.2 collective-permute-start.4
  154.4 0.6 copy.11
  155.0 1.6 %collective-permute-done.4.theirs_ref = bf16[64,8192]{1,0:T(8,128)(2,1)S(1)} collective-permute-done((bf16[64,8192]{1,0:T(8,128)(2,1)S(1)}, bf16[64,8192]{1,0:T(8,128)(2,1)S(1)}, u32[]{:S(2)}, u32[]{:S(2)}) %collective-permute-start.4) | collective-permute-done | bytes 1048608 | tf_op jit(solution)/shard_map/ppermute | solution.py:591
  156.7 2.2 %take_step.1 = f32[128,8192]{1,0:T(8,128)} custom-call(bf16[64,8192]{1,0:T(8,128)(2,1)S(1)} %update.1.mine_ref, bf16[64,8192]{1,0:T(8,128)(2,1)S(1)} %collective-permute-done.4.theirs_ref, f32[128,8192]{1,0:T(8,128)S(1)} %bitcast.16), custom_call_target="tpu_custom_call" | custom-call | tf_op jit(solution)/shard_map/take_step/pallas_call | solution.py:526
  (23 shorter events, 0.1 us)
Async XLA Ops:
  0.6 13.9 %copy-start.3 = (s32[2,16]{1,0:T(2,128)S(1)}, s32[2,16]{1,0:T(2,128)}, u32[]{:S(2)}) copy-start(s32[2,16]{1,0:T(2,128)} %offsets_ref.7) | copy-start | bytes 388
  0.6 13.9 %copy-start.6 = (s32[1,16]{1,0:T(1,128)S(1)}, s32[1,16]{1,0:T(1,128)}, u32[]{:S(2)}) copy-start(s32[1,16]{1,0:T(1,128)} %rows_ref.1) | copy-start | bytes 196
  0.7 26.2 %copy-start.7 = (s32[2,1,1,4096]{3,2,1,0:T(1,128)S(1)}, s32[2,1,1,4096]{3,2,1,0:T(1,128)}, u32[]{:S(2)}) copy-start(s32[2,1,1,4096]{3,2,1,0:T(1,128)} %param.15) | copy-start | bytes 98308
  0.7 33.6 %copy-start.4 = (s32[1,16]{1,0:T(1,128)S(1)}, s32[1,16]{1,0:T(1,128)}, u32[]{:S(2)}) copy-start(s32[1,16]{1,0:T(1,128)} %counts_ref.3) | copy-start | bytes 196
  0.7 33.6 %copy-start.2 = (bf16[1,1,4096]{2,1,0:T(2,128)(2,1)S(1)}, bf16[1,1,4096]{2,1,0:T(2,128)(2,1)}, u32[]{:S(2)}) copy-start(bf16[1,1,4096]{2,1,0:T(2,128)(2,1)} %param.17) | copy-start | bytes 24580
  0.7 33.6 %copy-start.1 = (bf16[2,1,1,4096]{3,0,2,1:T(2,128)(2,1)S(1)}, bf16[2,1,1,4096]{3,0,2,1:T(2,128)(2,1)}, u32[]{:S(2)}) copy-start(bf16[2,1,1,4096]{3,0,2,1:T(2,128)(2,1)} %param.16) | copy-start | bytes 49156
  1.4 14.9 %collective-permute-start = (s32[8]{0:T(128)S(1)}, s32[8]{0:T(128)S(1)}, u32[]{:S(2)}, u32[]{:S(2)}) collective-permute-start(s32[8]{0:T(128)S(1)} %compare_select_fusion), channel_id=1, source_target_pairs={{0,1},{1,0},{2,3},{3,2},{4,5},{5,4},{6,7},{7,6},{8,9},{9,8},{10,11... | collective-permute-start | bytes 104 | tf_op jit(solution)/shard_map/ppermute | solution.py:591
  7.7 13.6 %all-to-all-start = ((bf16[16,32,128]{2,1,0:T(8,128)(2,1)}), bf16[16,32,128]{2,1,0:T(8,128)(2,1)S(1)}, u32[]{:S(2)}, u32[]{:S(2)}) async-start(bf16[16,32,128]{2,1,0:T(8,128)(2,1)} %section.1.first_ref), calls=%async_computation | async-start | bytes 262144 | tf_op jit(solution)/shard_map/all_to_all | solution.py:587
  21.3 60.4 %copy-start.5 = (f32[2]{0:T(128)S(1)}, f32[2]{0:T(128)}, u32[]{:S(2)}) copy-start(f32[2]{0:T(128)} %step_ref.3) | copy-start | bytes 28
  23.3 10.9 %all-to-all-start.1 = ((bf16[16,32,256]{2,1,0:T(8,128)(2,1)}), bf16[16,32,256]{2,1,0:T(8,128)(2,1)S(1)}, u32[]{:S(2)}, u32[]{:S(2)}) async-start(bf16[16,32,256]{2,1,0:T(8,128)(2,1)} %grids.2), calls=%async_computation.1 | async-start | bytes 524288 | tf_op jit(solution)/shard_map/all_to_all | solution.py:587
  26.9 2.6 %collective-permute-start.1 = (s32[8]{0:T(128)S(1)}, s32[8]{0:T(128)S(1)}, u32[]{:S(2)}, u32[]{:S(2)}) collective-permute-start(s32[8]{0:T(128)S(1)} %fusion), channel_id=1, source_target_pairs={{0,2},{1,3},{2,0},{3,1},{4,6},{5,7},{6,4},{7,5},{8,10},{9,11},{10,... | collective-permute-start | bytes 104 | tf_op jit(solution)/shard_map/ppermute | solution.py:591
  29.6 4.7 %collective-permute-start.2 = (s32[8]{0:T(128)S(1)}, s32[8]{0:T(128)S(1)}, u32[]{:S(2)}, u32[]{:S(2)}) collective-permute-start(s32[8]{0:T(128)S(1)} %add.10), channel_id=1, source_target_pairs={{0,4},{1,5},{2,6},{3,7},{4,0},{5,1},{6,2},{7,3},{8,12},{9,13},{10,... | collective-permute-start | bytes 104 | tf_op jit(solution)/shard_map/ppermute | solution.py:591
  79.1 2.7 %collective-permute-start.3 = (bf16[128,16,128]{2,1,0:T(8,128)(2,1)S(1)}, bf16[128,16,128]{2,1,0:T(8,128)(2,1)S(1)}, u32[]{:S(2)}, u32[]{:S(2)}) collective-permute-start(bf16[128,16,128]{2,1,0:T(8,128)(2,1)S(1)} %all_to_all.41.adj0_ref), channel_id=1, source_target_pairs={{0,1},{1,0},{2,3},{3,2},{4,5},{5,4},{6,7},{7,6},{8,9},{9,8},{10,11... | collective-permute-start | bytes 1572872 | tf_op jit(solution)/shard_map/ppermute | solution.py:591
  123.5 21.8 %all-to-all-start.7 = ((bf16[128,16,128]{2,1,0:T(8,128)(2,1)}), bf16[128,16,128]{2,1,0:T(8,128)(2,1)S(1)}, u32[]{:S(2)}, u32[]{:S(2)}) async-start(bf16[128,16,128]{2,1,0:T(8,128)(2,1)} %bitcast.7), calls=%async_computation.7 | async-start | bytes 1048576 | tf_op jit(solution)/shard_map/all_to_all | solution.py:596
  145.3 11.3 %copy-start = (f32[1,128,8192]{2,1,0:T(8,128)S(1)}, f32[1,128,8192]{2,1,0:T(8,128)}, u32[]{:S(2)}) copy-start(f32[1,128,8192]{2,1,0:T(8,128)} %param.9) | copy-start | bytes 12582916
  153.1 3.5 %collective-permute-start.4 = (bf16[64,8192]{1,0:T(8,128)(2,1)S(1)}, bf16[64,8192]{1,0:T(8,128)(2,1)S(1)}, u32[]{:S(2)}, u32[]{:S(2)}) collective-permute-start(bf16[64,8192]{1,0:T(8,128)(2,1)S(1)} %update.1.mine_ref), channel_id=1, source_target_pairs={{0,1},{1,0},{2,3},{3,2},{4,5},{5,4},{6,7},{7,6},{8,9},{9,8},{10,11... | collective-permute-start | bytes 3145736 | tf_op jit(solution)/shard_map/ppermute | solution.py:591

commit v10 on v9

--- a/solution.py
+++ b/solution.py
@@ -609,7 +609,8 @@
 ):
     mine = jnp.arange(NCOL, dtype=I32) == lax.axis_index("sub")
     column_starts = jnp.where(mine, col_offsets[0], 0)
-    column_starts = column_starts + swapped(column_starts, 1)
+    for bit in (1, 2):
+        column_starts = column_starts + swapped(column_starts, bit)
     uv = vis_uv.reshape(2, VCAP)
     obs = vis_obs.reshape(2, VCAP)
     weight = vis_weight.reshape(1, VCAP)
@@ -617,8 +618,7 @@
     first = section(col_offsets, facet_offsets, model)
     rows = row_tables(facet_offsets, row_offsets)
     sections, column_starts = lax.optimization_barrier((exchange(first), column_starts))
-    for bit in (2, 4):
-        column_starts = column_starts + swapped(column_starts, bit)
+    column_starts = column_starts + swapped(column_starts, 4)
     grid = exchange(grids(sections, rows))
     gridded, ku, kv = first_visibilities(counts, obs, weight, grid, uv)
     gridded, column_starts = lax.optimization_barrier((gridded, column_starts))

time: 160 us -> 157 us (0.981)
  blocking collectives: 69.2 us -> 66.1 us
    all_to_all x4, blocking collectives: 44.6 us -> 41.9 us  [exchange(): lax.all_to_all(value, 'facet', split_axis=0, concat_axis=0, tiled=True)]
  transfers between devices with their start and end apart: 8 -> 8, of which waited for: 6 -> 7; matrix products, arithmetic and copies ran while one was open for 0% -> 0% of each run, Pallas kernels for 7% -> 7%
where the time goes in v10:
time: 157 us
  blocking collectives  66.1 us (42%)
  Pallas kernels  40 us (25%)
  starting transfers between devices  28.6 us (18%)
  waiting for transfers between devices  19.5 us (12%)
  between operations  1.72 us (1%)
    all_to_all x4, blocking collectives, exchange(): lax.all_to_all(value, 'facet', split_axis=0, concat_axis=0, tiled=True)  41.9 us
    all_to_all x1, blocking collectives, to_facets(): lax.all_to_all(copies, ('facet', 'sub'), split_axis=0, concat_axis=0, til...  24.2 us
    all_to_all x2, starting transfers between devices, exchange(): lax.all_to_all(value, 'facet', split_axis=0, concat_axis=0, tiled=True)  11.2 us
    all_to_all x1, waiting for transfers between devices, to_facets(): lax.all_to_all(copies, ('facet', 'sub'), split_axis=0, concat_axis=0, til...  9.42 us
    ppermute x5, starting transfers between devices, swapped(): return lax.ppermute(value, 'sub', [(i, i ^ bit) for i in range(NCOL)])  9.24 us
    all_to_all x1, starting transfers between devices, to_facets(): lax.all_to_all(copies, ('facet', 'sub'), split_axis=0, concat_axis=0, til...  8.17 us
    pallas_call x1, Pallas kernels, update(): pl.pallas_call(update_kernel, grid=(HIGH5 // PAIR5 // 2,), out_shape=jax....  7.79 us
    ppermute x5, waiting for transfers between devices, swapped(): return lax.ppermute(value, 'sub', [(i, i ^ bit) for i in range(NCOL)])  5.33 us
  transfers between devices with their start and end apart: 8, of which 7 were waited for; matrix products, arithmetic and copies ran while one was open for 0% of the time, Pallas kernels for 7%

profile of v10, /device:TPU:1, one launch (start us, length us, event | category | flops | bytes accessed | tf_op | source)
XLA Modules:
  0.0 156.7 jit_solution(14172856978996302257)
XLA Ops:
  1.4 1.5 collective-permute-start
  2.9 4.8 %section.1.first_ref = bf16[16,32,128]{2,1,0:T(8,128)(2,1)} custom-call(s32[1]{0:T(128)} %copy.15.column_ref, s32[2,16]{1,0:T(2,128)} %offsets_ref.7, f32[128,8192]{1,0:T(8,128)} %bitcast.16), custom_call_target="tpu_custom_call" | custom-call | tf_op jit(solution)/shard_map/section/pallas_call | solution.py:135
  7.7 6.9 %all-to-all-start = ((bf16[16,32,128]{2,1,0:T(8,128)(2,1)}), bf16[16,32,128]{2,1,0:T(8,128)(2,1)S(1)}, u32[]{:S(2)}, u32[]{:S(2)}) async-start(bf16[16,32,128]{2,1,0:T(8,128)(2,1)} %section.1.first_ref), calls=%async_computation | async-start | bytes 262144 | tf_op jit(solution)/shard_map/all_to_all | solution.py:587
  14.6 1.7 %row_tables.1 = (bf16[2,2048,256]{2,1,0:T(8,128)(2,1)S(1)}, f32[16,16,128]{2,1,0:T(8,128)S(1)}, f32[16,16,128]{2,1,0:T(8,128)S(1)}) custom-call(s32[2,16]{1,0:T(2,128)S(1)} %copy-done.3, s32[1,16]{1,0:T(1,128)S(1)} %copy-done.6), custom_call_target="tpu_custom_call" | custom-call | tf_op jit(solution)/shard_map/row_tables/pallas_call | solution.py:189
  16.3 1.7 %collective-permute-start.1 = (s32[8]{0:T(128)S(1)}, s32[8]{0:T(128)S(1)}, u32[]{:S(2)}, u32[]{:S(2)}) collective-permute-start(s32[8]{0:T(128)S(1)} %fusion), channel_id=1, source_target_pairs={{0,2},{1,3},{2,0},{3,1},{4,6},{5,7},{6,4},{7,5},{8,10},{9,11},{10,... | collective-permute-start | bytes 104 | tf_op jit(solution)/shard_map/ppermute | solution.py:591
  18.0 1.2 collective-permute-done.1
  19.3 2.0 %all-to-all-done.in_ref = bf16[16,32,128]{2,1,0:T(8,128)(2,1)S(1)} async-done(((bf16[16,32,128]{2,1,0:T(8,128)(2,1)}), bf16[16,32,128]{2,1,0:T(8,128)(2,1)S(1)}, u32[]{:S(2)}, u32[]{:S(2)}) %all-to-all-start) | async-done | bytes 131104 | tf_op jit(solution)/shard_map/all_to_all | solution.py:587
  21.3 2.0 %grids.2 = bf16[16,32,256]{2,1,0:T(8,128)(2,1)} custom-call(bf16[16,32,128]{2,1,0:T(8,128)(2,1)S(1)} %all-to-all-done.in_ref, f32[16,16,128]{2,1,0:T(8,128)S(1)} %get-tuple-element.18.c_ref, f32[16,16,128]{2,1,0:T(8,128)S(1)} %get-tuple-element.19.s_ref, bf16[2,2048,256]{2,1,0:T(8,128)(2,1)S(1)} %get-tuple-element.20.table_ref), custom_call_target="tpu_custom_call" | custom-call | tf_op jit(solution)/shard_map/grids/pallas_call | solution.py:229
  23.3 4.4 %all-to-all-start.1 = ((bf16[16,32,256]{2,1,0:T(8,128)(2,1)}), bf16[16,32,256]{2,1,0:T(8,128)(2,1)S(1)}, u32[]{:S(2)}, u32[]{:S(2)}) async-start(bf16[16,32,256]{2,1,0:T(8,128)(2,1)} %grids.2), calls=%async_computation.1 | async-start | bytes 524288 | tf_op jit(solution)/shard_map/all_to_all | solution.py:587
  27.7 3.7 %collective-permute-start.2 = (s32[8]{0:T(128)S(1)}, s32[8]{0:T(128)S(1)}, u32[]{:S(2)}, u32[]{:S(2)}) collective-permute-start(s32[8]{0:T(128)S(1)} %fusion.1), channel_id=1, source_target_pairs={{0,4},{1,5},{2,6},{3,7},{4,0},{5,1},{6,2},{7,3},{8,12},{9,13},{10,... | collective-permute-start | bytes 104 | tf_op jit(solution)/shard_map/ppermute | solution.py:591
  31.4 0.9 collective-permute-done.2
  32.3 2.7 %all-to-all-done.1.in_ref = bf16[16,32,256]{2,1,0:T(8,128)(2,1)S(1)} async-done(((bf16[16,32,256]{2,1,0:T(8,128)(2,1)}), bf16[16,32,256]{2,1,0:T(8,128)(2,1)S(1)}, u32[]{:S(2)}, u32[]{:S(2)}) %all-to-all-start.1) | async-done | bytes 262176 | tf_op jit(solution)/shard_map/all_to_all | solution.py:587
  35.0 4.6 %first_visibilities.1 = (bf16[16,32,256]{2,1,0:T(8,128)(2,1)S(1)}, bf16[256,4096]{1,0:T(8,128)(2,1)S(1)}, bf16[256,4096]{1,0:T(8,128)(2,1)S(1)}) custom-call(s32[1,16]{1,0:T(1,128)S(1)} %copy-done.4, bf16[2,4096]{1,0:T(2,128)(2,1)S(1)} %bitcast.22, bf16[1,4096]{1,0:T(2,128)(2,1)S(1)} %bitcast.24, bf16[16,32,256]{2,1,0:T(8,128)(2,1)S(1)} %all-to-all-done.1.in_ref, ...), custom_call_target="tpu_custom_call" | custom-call | tf_op jit(solution)/shard_map/first_visibilities/pallas_call | solution.py:347
  39.6 11.1 %all_to_all.40.in_ref = bf16[16,32,256]{2,1,0:T(8,128)(2,1)S(1)} all-to-all(bf16[16,32,256]{2,1,0:T(8,128)(2,1)S(1)} %get-tuple-element.23), channel_id=1, replica_groups=mesh['facet'=16,'sub'=8] {'facet'}, dimensions={0} | all-to-all | bytes 524288 | tf_op jit(solution)/shard_map/all_to_all | solution.py:587
  50.7 1.8 %adjoint.2 = bf16[16,8,16,128]{3,2,1,0:T(8,128)(2,1)S(1)} custom-call(bf16[16,32,256]{2,1,0:T(8,128)(2,1)S(1)} %all_to_all.40.in_ref, f32[16,16,128]{2,1,0:T(8,128)S(1)} %get-tuple-element.18.c_ref, f32[16,16,128]{2,1,0:T(8,128)S(1)} %get-tuple-element.19.s_ref, bf16[2,2048,256]{2,1,0:T(8,128)(2,1)S(1)} %get-tuple-element.20.table_ref), custom_call_target="tpu_custom_call" | custom-call | tf_op jit(solution)/shard_map/adjoint/pallas_call | solution.py:279
  52.5 24.2 %all_to_all.41.adj0_ref = bf16[128,16,128]{2,1,0:T(8,128)(2,1)S(1)} all-to-all(bf16[128,16,128]{2,1,0:T(8,128)(2,1)S(1)} %bitcast.19), channel_id=1, replica_groups=mesh['facet'=16,'sub'=8] {'facet','sub'}, dimensions={0} | all-to-all | bytes 1048576 | tf_op jit(solution)/shard_map/all_to_all | solution.py:596
  76.7 1.1 collective-permute-start.3
  77.8 1.5 collective-permute-done.3
  79.4 3.7 %gram.1 = bf16[16,32,128]{2,1,0:T(8,128)(2,1)S(1)} custom-call(f32[2]{0:T(128)S(1)} %copy-done.5, s32[8]{0:T(128)S(1)} %add.11.starts_ref, s32[1]{0:T(128)} %copy.15.column_ref, s32[2,16]{1,0:T(2,128)S(1)} %copy-done.3, bf16[16,8,16,128]{3,2,1,0:T(8,128)(2,1)S(1)} %bitcast.18, bf16[16,8,16,128]{3,2,1,0:T(8,128)(2,1)S(1)} %bitcast.20, ...), custom_call_target="tpu_custom_call" | custom-call | tf_op jit(solution)/shard_map/gram/pallas_call | solution.py:433
  83.1 9.3 %all_to_all.42.in_ref = bf16[16,32,128]{2,1,0:T(8,128)(2,1)S(1)} all-to-all(bf16[16,32,128]{2,1,0:T(8,128)(2,1)S(1)} %gram.1), channel_id=1, replica_groups=mesh['facet'=16,'sub'=8] {'facet'}, dimensions={0} | all-to-all | bytes 262144 | tf_op jit(solution)/shard_map/all_to_all | solution.py:587
  92.4 1.3 grids.3
  93.7 10.7 %all_to_all.43.in_ref = bf16[16,32,256]{2,1,0:T(8,128)(2,1)S(1)} all-to-all(bf16[16,32,256]{2,1,0:T(8,128)(2,1)S(1)} %grids.3), channel_id=1, replica_groups=mesh['facet'=16,'sub'=8] {'facet'}, dimensions={0} | all-to-all | bytes 524288 | tf_op jit(solution)/shard_map/all_to_all | solution.py:587
  104.4 3.4 %last_visibilities.1 = (bf16[16,32,256]{2,1,0:T(8,128)(2,1)S(1)}, f32[2,4096]{1,0:T(2,128)S(1)}) custom-call(s32[1,16]{1,0:T(1,128)S(1)} %copy-done.4, bf16[2,4096]{1,0:T(2,128)(2,1)S(1)} %bitcast.23, bf16[1,4096]{1,0:T(2,128)(2,1)S(1)} %bitcast.25, bf16[16,32,256]{2,1,0:T(8,128)(2,1)S(1)} %all_to_all.43.in_ref, ...), custom_call_target="tpu_custom_call" | custom-call | tf_op jit(solution)/shard_map/last_visibilities/pallas_call | solution.py:363
  107.8 10.8 %all_to_all.44.in_ref = bf16[16,32,256]{2,1,0:T(8,128)(2,1)S(1)} all-to-all(bf16[16,32,256]{2,1,0:T(8,128)(2,1)S(1)} %get-tuple-element.27), channel_id=1, replica_groups=mesh['facet'=16,'sub'=8] {'facet'}, dimensions={0} | all-to-all | bytes 524288 | tf_op jit(solution)/shard_map/all_to_all | solution.py:587
  118.6 2.5 %adjoint.3 = bf16[16,8,16,128]{3,2,1,0:T(8,128)(2,1)} custom-call(bf16[16,32,256]{2,1,0:T(8,128)(2,1)S(1)} %all_to_all.44.in_ref, f32[16,16,128]{2,1,0:T(8,128)S(1)} %get-tuple-element.18.c_ref, f32[16,16,128]{2,1,0:T(8,128)S(1)} %get-tuple-element.19.s_ref, bf16[2,2048,256]{2,1,0:T(8,128)(2,1)S(1)} %get-tuple-element.20.table_ref), custom_call_target="tpu_custom_call" | custom-call | tf_op jit(solution)/shard_map/adjoint/pallas_call | solution.py:279
  121.1 8.2 %all-to-all-start.7 = ((bf16[128,16,128]{2,1,0:T(8,128)(2,1)}), bf16[128,16,128]{2,1,0:T(8,128)(2,1)S(1)}, u32[]{:S(2)}, u32[]{:S(2)}) async-start(bf16[128,16,128]{2,1,0:T(8,128)(2,1)} %bitcast.7), calls=%async_computation.7 | async-start | bytes 1048576 | tf_op jit(solution)/shard_map/all_to_all | solution.py:596
  129.3 4.2 %update_tables.1 = (bf16[4096,512]{1,0:T(8,128)(2,1)}, f32[16,2048]{1,0:T(8,128)S(1)}, f32[16,2048]{1,0:T(8,128)S(1)}) custom-call(s32[8]{0:T(128)S(1)} %add.11.starts_ref, s32[2,16]{1,0:T(2,128)S(1)} %copy-done.3), custom_call_target="tpu_custom_call" | custom-call | tf_op jit(solution)/shard_map/update_tables/pallas_call | solution.py:566
  133.6 9.4 %all-to-all-done.7.adj1_ref = bf16[128,16,128]{2,1,0:T(8,128)(2,1)S(1)} async-done(((bf16[128,16,128]{2,1,0:T(8,128)(2,1)}), bf16[128,16,128]{2,1,0:T(8,128)(2,1)S(1)}, u32[]{:S(2)}, u32[]{:S(2)}) %all-to-all-start.7) | async-done | bytes 524320 | tf_op jit(solution)/shard_map/all_to_all | solution.py:596
  143.0 7.8 %update.1.mine_ref = bf16[64,8192]{1,0:T(8,128)(2,1)S(1)} custom-call(f32[2]{0:T(128)S(1)} %copy-done.5, bf16[128,16,128]{2,1,0:T(8,128)(2,1)S(1)} %all_to_all.41.adj0_ref, bf16[128,16,128]{2,1,0:T(8,128)(2,1)S(1)} %all-to-all-done.7.adj1_ref, bf16[4096,512]{1,0:T(8,128)(2,1)} %get-tuple-element.28.table_hbm, f32[16,2048]{1,0:T(8,128)S(1)} %get-tuple-element.29.pc_ref, ...), custom_call_target="tpu_custom_call" | custom-call | tf_op jit(solution)/shard_map/update/pallas_call | solution.py:490
  150.8 1.2 collective-permute-start.4
  152.6 1.6 %collective-permute-done.4.theirs_ref = bf16[64,8192]{1,0:T(8,128)(2,1)S(1)} collective-permute-done((bf16[64,8192]{1,0:T(8,128)(2,1)S(1)}, bf16[64,8192]{1,0:T(8,128)(2,1)S(1)}, u32[]{:S(2)}, u32[]{:S(2)}) %collective-permute-start.4) | collective-permute-done | bytes 1048608 | tf_op jit(solution)/shard_map/ppermute | solution.py:591
  154.3 2.2 %take_step.1 = f32[128,8192]{1,0:T(8,128)} custom-call(bf16[64,8192]{1,0:T(8,128)(2,1)S(1)} %update.1.mine_ref, bf16[64,8192]{1,0:T(8,128)(2,1)S(1)} %collective-permute-done.4.theirs_ref, f32[128,8192]{1,0:T(8,128)S(1)} %bitcast.17), custom_call_target="tpu_custom_call" | custom-call | tf_op jit(solution)/shard_map/take_step/pallas_call | solution.py:526
  (23 shorter events, 0.7 us)
Async XLA Ops:
  0.6 13.9 %copy-start.3 = (s32[2,16]{1,0:T(2,128)S(1)}, s32[2,16]{1,0:T(2,128)}, u32[]{:S(2)}) copy-start(s32[2,16]{1,0:T(2,128)} %offsets_ref.7) | copy-start | bytes 388
  0.6 13.9 %copy-start.6 = (s32[1,16]{1,0:T(1,128)S(1)}, s32[1,16]{1,0:T(1,128)}, u32[]{:S(2)}) copy-start(s32[1,16]{1,0:T(1,128)} %rows_ref.1) | copy-start | bytes 196
  0.7 27.0 %copy-start.7 = (s32[2,1,1,4096]{3,2,1,0:T(1,128)S(1)}, s32[2,1,1,4096]{3,2,1,0:T(1,128)}, u32[]{:S(2)}) copy-start(s32[2,1,1,4096]{3,2,1,0:T(1,128)} %param.15) | copy-start | bytes 98308
  0.7 34.3 %copy-start.4 = (s32[1,16]{1,0:T(1,128)S(1)}, s32[1,16]{1,0:T(1,128)}, u32[]{:S(2)}) copy-start(s32[1,16]{1,0:T(1,128)} %counts_ref.3) | copy-start | bytes 196
  0.7 34.3 %copy-start.2 = (bf16[1,1,4096]{2,1,0:T(2,128)(2,1)S(1)}, bf16[1,1,4096]{2,1,0:T(2,128)(2,1)}, u32[]{:S(2)}) copy-start(bf16[1,1,4096]{2,1,0:T(2,128)(2,1)} %param.17) | copy-start | bytes 24580
  0.7 34.3 %copy-start.1 = (bf16[2,1,1,4096]{3,0,2,1:T(2,128)(2,1)S(1)}, bf16[2,1,1,4096]{3,0,2,1:T(2,128)(2,1)}, u32[]{:S(2)}) copy-start(bf16[2,1,1,4096]{3,0,2,1:T(2,128)(2,1)} %param.16) | copy-start | bytes 49156
  1.4 14.9 %collective-permute-start = (s32[8]{0:T(128)S(1)}, s32[8]{0:T(128)S(1)}, u32[]{:S(2)}, u32[]{:S(2)}) collective-permute-start(s32[8]{0:T(128)S(1)} %compare_select_fusion), channel_id=1, source_target_pairs={{0,1},{1,0},{2,3},{3,2},{4,5},{5,4},{6,7},{7,6},{8,9},{9,8},{10,11... | collective-permute-start | bytes 104 | tf_op jit(solution)/shard_map/ppermute | solution.py:591
  7.7 13.6 %all-to-all-start = ((bf16[16,32,128]{2,1,0:T(8,128)(2,1)}), bf16[16,32,128]{2,1,0:T(8,128)(2,1)S(1)}, u32[]{:S(2)}, u32[]{:S(2)}) async-start(bf16[16,32,128]{2,1,0:T(8,128)(2,1)} %section.1.first_ref), calls=%async_computation | async-start | bytes 262144 | tf_op jit(solution)/shard_map/all_to_all | solution.py:587
  16.3 2.9 %collective-permute-start.1 = (s32[8]{0:T(128)S(1)}, s32[8]{0:T(128)S(1)}, u32[]{:S(2)}, u32[]{:S(2)}) collective-permute-start(s32[8]{0:T(128)S(1)} %fusion), channel_id=1, source_target_pairs={{0,2},{1,3},{2,0},{3,1},{4,6},{5,7},{6,4},{7,5},{8,10},{9,11},{10,... | collective-permute-start | bytes 104 | tf_op jit(solution)/shard_map/ppermute | solution.py:591
  21.3 58.1 %copy-start.5 = (f32[2]{0:T(128)S(1)}, f32[2]{0:T(128)}, u32[]{:S(2)}) copy-start(f32[2]{0:T(128)} %step_ref.3) | copy-start | bytes 28
  23.3 11.7 %all-to-all-start.1 = ((bf16[16,32,256]{2,1,0:T(8,128)(2,1)}), bf16[16,32,256]{2,1,0:T(8,128)(2,1)S(1)}, u32[]{:S(2)}, u32[]{:S(2)}) async-start(bf16[16,32,256]{2,1,0:T(8,128)(2,1)} %grids.2), calls=%async_computation.1 | async-start | bytes 524288 | tf_op jit(solution)/shard_map/all_to_all | solution.py:587
  27.7 4.6 %collective-permute-start.2 = (s32[8]{0:T(128)S(1)}, s32[8]{0:T(128)S(1)}, u32[]{:S(2)}, u32[]{:S(2)}) collective-permute-start(s32[8]{0:T(128)S(1)} %fusion.1), channel_id=1, source_target_pairs={{0,4},{1,5},{2,6},{3,7},{4,0},{5,1},{6,2},{7,3},{8,12},{9,13},{10,... | collective-permute-start | bytes 104 | tf_op jit(solution)/shard_map/ppermute | solution.py:591
  76.7 2.7 %collective-permute-start.3 = (bf16[128,16,128]{2,1,0:T(8,128)(2,1)S(1)}, bf16[128,16,128]{2,1,0:T(8,128)(2,1)S(1)}, u32[]{:S(2)}, u32[]{:S(2)}) collective-permute-start(bf16[128,16,128]{2,1,0:T(8,128)(2,1)S(1)} %all_to_all.41.adj0_ref), channel_id=1, source_target_pairs={{0,1},{1,0},{2,3},{3,2},{4,5},{5,4},{6,7},{7,6},{8,9},{9,8},{10,11... | collective-permute-start | bytes 1572872 | tf_op jit(solution)/shard_map/ppermute | solution.py:591
  121.1 21.8 %all-to-all-start.7 = ((bf16[128,16,128]{2,1,0:T(8,128)(2,1)}), bf16[128,16,128]{2,1,0:T(8,128)(2,1)S(1)}, u32[]{:S(2)}, u32[]{:S(2)}) async-start(bf16[128,16,128]{2,1,0:T(8,128)(2,1)} %bitcast.7), calls=%async_computation.7 | async-start | bytes 1048576 | tf_op jit(solution)/shard_map/all_to_all | solution.py:596
  143.0 11.3 %copy-start = (f32[1,128,8192]{2,1,0:T(8,128)S(1)}, f32[1,128,8192]{2,1,0:T(8,128)}, u32[]{:S(2)}) copy-start(f32[1,128,8192]{2,1,0:T(8,128)} %param.9) | copy-start | bytes 12582916
  150.8 3.5 %collective-permute-start.4 = (bf16[64,8192]{1,0:T(8,128)(2,1)S(1)}, bf16[64,8192]{1,0:T(8,128)(2,1)S(1)}, u32[]{:S(2)}, u32[]{:S(2)}) collective-permute-start(bf16[64,8192]{1,0:T(8,128)(2,1)S(1)} %update.1.mine_ref), channel_id=1, source_target_pairs={{0,1},{1,0},{2,3},{3,2},{4,5},{5,4},{6,7},{7,6},{8,9},{9,8},{10,11... | collective-permute-start | bytes 3145736 | tf_op jit(solution)/shard_map/ppermute | solution.py:591

commit v11 on v10

--- a/solution.py
+++ b/solution.py
@@ -23,8 +23,8 @@
 STEP1 = 256
 HIGH1 = FW // STEP1
 PARTS1 = 4
-GROUP1 = 4
-ROWS1 = 32
+GROUP1 = 8
+ROWS1 = 64
 STEP5 = 512
 HIGH5 = FW // STEP5
 PAIR5 = 4

time: 157 us -> 157 us (level)
  no operation moved by 1% of the time
where the time goes in v11:
time: 157 us
  blocking collectives  66.1 us (42%)
  Pallas kernels  40 us (25%)
  starting transfers between devices  28.7 us (18%)
  waiting for transfers between devices  19.4 us (12%)
  between operations  1.72 us (1%)
    all_to_all x4, blocking collectives, exchange(): lax.all_to_all(value, 'facet', split_axis=0, concat_axis=0, tiled=True)  41.9 us
    all_to_all x1, blocking collectives, to_facets(): lax.all_to_all(copies, ('facet', 'sub'), split_axis=0, concat_axis=0, til...  24.2 us
    all_to_all x2, starting transfers between devices, exchange(): lax.all_to_all(value, 'facet', split_axis=0, concat_axis=0, tiled=True)  11.2 us
    all_to_all x1, waiting for transfers between devices, to_facets(): lax.all_to_all(copies, ('facet', 'sub'), split_axis=0, concat_axis=0, til...  9.42 us
    ppermute x5, starting transfers between devices, swapped(): return lax.ppermute(value, 'sub', [(i, i ^ bit) for i in range(NCOL)])  9.27 us
    all_to_all x1, starting transfers between devices, to_facets(): lax.all_to_all(copies, ('facet', 'sub'), split_axis=0, concat_axis=0, til...  8.17 us
    pallas_call x1, Pallas kernels, update(): pl.pallas_call(update_kernel, grid=(HIGH5 // PAIR5 // 2,), out_shape=jax....  7.79 us
    ppermute x5, waiting for transfers between devices, swapped(): return lax.ppermute(value, 'sub', [(i, i ^ bit) for i in range(NCOL)])  5.33 us
  transfers between devices with their start and end apart: 8, of which 7 were waited for; matrix products, arithmetic and copies ran while one was open for 0% of the time, Pallas kernels for 7%

profile of v11, /device:TPU:1, one launch (start us, length us, event | category | flops | bytes accessed | tf_op | source)
XLA Modules:
  0.0 156.6 jit_solution(8075047907960711206)
XLA Ops:
  1.4 1.5 collective-permute-start
  2.9 4.8 %section.1.first_ref = bf16[16,32,128]{2,1,0:T(8,128)(2,1)} custom-call(s32[1]{0:T(128)} %copy.15.column_ref, s32[2,16]{1,0:T(2,128)} %offsets_ref.7, f32[128,8192]{1,0:T(8,128)} %bitcast.16), custom_call_target="tpu_custom_call" | custom-call | tf_op jit(solution)/shard_map/section/pallas_call | solution.py:135
  7.7 6.8 %all-to-all-start = ((bf16[16,32,128]{2,1,0:T(8,128)(2,1)}), bf16[16,32,128]{2,1,0:T(8,128)(2,1)S(1)}, u32[]{:S(2)}, u32[]{:S(2)}) async-start(bf16[16,32,128]{2,1,0:T(8,128)(2,1)} %section.1.first_ref), calls=%async_computation | async-start | bytes 262144 | tf_op jit(solution)/shard_map/all_to_all | solution.py:587
  14.5 1.7 %row_tables.1 = (bf16[2,2048,256]{2,1,0:T(8,128)(2,1)S(1)}, f32[16,16,128]{2,1,0:T(8,128)S(1)}, f32[16,16,128]{2,1,0:T(8,128)S(1)}) custom-call(s32[2,16]{1,0:T(2,128)S(1)} %copy-done.3, s32[1,16]{1,0:T(1,128)S(1)} %copy-done.6), custom_call_target="tpu_custom_call" | custom-call | tf_op jit(solution)/shard_map/row_tables/pallas_call | solution.py:189
  16.3 1.7 %collective-permute-start.1 = (s32[8]{0:T(128)S(1)}, s32[8]{0:T(128)S(1)}, u32[]{:S(2)}, u32[]{:S(2)}) collective-permute-start(s32[8]{0:T(128)S(1)} %fusion), channel_id=1, source_target_pairs={{0,2},{1,3},{2,0},{3,1},{4,6},{5,7},{6,4},{7,5},{8,10},{9,11},{10,... | collective-permute-start | bytes 104 | tf_op jit(solution)/shard_map/ppermute | solution.py:591
  18.0 1.2 collective-permute-done.1
  19.2 2.0 %all-to-all-done.in_ref = bf16[16,32,128]{2,1,0:T(8,128)(2,1)S(1)} async-done(((bf16[16,32,128]{2,1,0:T(8,128)(2,1)}), bf16[16,32,128]{2,1,0:T(8,128)(2,1)S(1)}, u32[]{:S(2)}, u32[]{:S(2)}) %all-to-all-start) | async-done | bytes 131104 | tf_op jit(solution)/shard_map/all_to_all | solution.py:587
  21.3 2.0 %grids.2 = bf16[16,32,256]{2,1,0:T(8,128)(2,1)} custom-call(bf16[16,32,128]{2,1,0:T(8,128)(2,1)S(1)} %all-to-all-done.in_ref, f32[16,16,128]{2,1,0:T(8,128)S(1)} %get-tuple-element.18.c_ref, f32[16,16,128]{2,1,0:T(8,128)S(1)} %get-tuple-element.19.s_ref, bf16[2,2048,256]{2,1,0:T(8,128)(2,1)S(1)} %get-tuple-element.20.table_ref), custom_call_target="tpu_custom_call" | custom-call | tf_op jit(solution)/shard_map/grids/pallas_call | solution.py:229
  23.2 4.4 %all-to-all-start.1 = ((bf16[16,32,256]{2,1,0:T(8,128)(2,1)}), bf16[16,32,256]{2,1,0:T(8,128)(2,1)S(1)}, u32[]{:S(2)}, u32[]{:S(2)}) async-start(bf16[16,32,256]{2,1,0:T(8,128)(2,1)} %grids.2), calls=%async_computation.1 | async-start | bytes 524288 | tf_op jit(solution)/shard_map/all_to_all | solution.py:587
  27.7 3.7 %collective-permute-start.2 = (s32[8]{0:T(128)S(1)}, s32[8]{0:T(128)S(1)}, u32[]{:S(2)}, u32[]{:S(2)}) collective-permute-start(s32[8]{0:T(128)S(1)} %fusion.1), channel_id=1, source_target_pairs={{0,4},{1,5},{2,6},{3,7},{4,0},{5,1},{6,2},{7,3},{8,12},{9,13},{10,... | collective-permute-start | bytes 104 | tf_op jit(solution)/shard_map/ppermute | solution.py:591
  31.3 0.9 collective-permute-done.2
  32.3 2.7 %all-to-all-done.1.in_ref = bf16[16,32,256]{2,1,0:T(8,128)(2,1)S(1)} async-done(((bf16[16,32,256]{2,1,0:T(8,128)(2,1)}), bf16[16,32,256]{2,1,0:T(8,128)(2,1)S(1)}, u32[]{:S(2)}, u32[]{:S(2)}) %all-to-all-start.1) | async-done | bytes 262176 | tf_op jit(solution)/shard_map/all_to_all | solution.py:587
  35.0 4.6 %first_visibilities.1 = (bf16[16,32,256]{2,1,0:T(8,128)(2,1)S(1)}, bf16[256,4096]{1,0:T(8,128)(2,1)S(1)}, bf16[256,4096]{1,0:T(8,128)(2,1)S(1)}) custom-call(s32[1,16]{1,0:T(1,128)S(1)} %copy-done.4, bf16[2,4096]{1,0:T(2,128)(2,1)S(1)} %bitcast.22, bf16[1,4096]{1,0:T(2,128)(2,1)S(1)} %bitcast.24, bf16[16,32,256]{2,1,0:T(8,128)(2,1)S(1)} %all-to-all-done.1.in_ref, ...), custom_call_target="tpu_custom_call" | custom-call | tf_op jit(solution)/shard_map/first_visibilities/pallas_call | solution.py:347
  39.6 11.1 %all_to_all.40.in_ref = bf16[16,32,256]{2,1,0:T(8,128)(2,1)S(1)} all-to-all(bf16[16,32,256]{2,1,0:T(8,128)(2,1)S(1)} %get-tuple-element.23), channel_id=1, replica_groups=mesh['facet'=16,'sub'=8] {'facet'}, dimensions={0} | all-to-all | bytes 524288 | tf_op jit(solution)/shard_map/all_to_all | solution.py:587
  50.7 1.8 %adjoint.2 = bf16[16,8,16,128]{3,2,1,0:T(8,128)(2,1)S(1)} custom-call(bf16[16,32,256]{2,1,0:T(8,128)(2,1)S(1)} %all_to_all.40.in_ref, f32[16,16,128]{2,1,0:T(8,128)S(1)} %get-tuple-element.18.c_ref, f32[16,16,128]{2,1,0:T(8,128)S(1)} %get-tuple-element.19.s_ref, bf16[2,2048,256]{2,1,0:T(8,128)(2,1)S(1)} %get-tuple-element.20.table_ref), custom_call_target="tpu_custom_call" | custom-call | tf_op jit(solution)/shard_map/adjoint/pallas_call | solution.py:279
  52.5 24.2 %all_to_all.41.adj0_ref = bf16[128,16,128]{2,1,0:T(8,128)(2,1)S(1)} all-to-all(bf16[128,16,128]{2,1,0:T(8,128)(2,1)S(1)} %bitcast.19), channel_id=1, replica_groups=mesh['facet'=16,'sub'=8] {'facet','sub'}, dimensions={0} | all-to-all | bytes 1048576 | tf_op jit(solution)/shard_map/all_to_all | solution.py:596
  76.7 1.1 collective-permute-start.3
  77.8 1.5 collective-permute-done.3
  79.3 3.7 %gram.1 = bf16[16,32,128]{2,1,0:T(8,128)(2,1)S(1)} custom-call(f32[2]{0:T(128)S(1)} %copy-done.5, s32[8]{0:T(128)S(1)} %add.11.starts_ref, s32[1]{0:T(128)} %copy.15.column_ref, s32[2,16]{1,0:T(2,128)S(1)} %copy-done.3, bf16[16,8,16,128]{3,2,1,0:T(8,128)(2,1)S(1)} %bitcast.18, bf16[16,8,16,128]{3,2,1,0:T(8,128)(2,1)S(1)} %bitcast.20, ...), custom_call_target="tpu_custom_call" | custom-call | tf_op jit(solution)/shard_map/gram/pallas_call | solution.py:433
  83.0 9.3 %all_to_all.42.in_ref = bf16[16,32,128]{2,1,0:T(8,128)(2,1)S(1)} all-to-all(bf16[16,32,128]{2,1,0:T(8,128)(2,1)S(1)} %gram.1), channel_id=1, replica_groups=mesh['facet'=16,'sub'=8] {'facet'}, dimensions={0} | all-to-all | bytes 262144 | tf_op jit(solution)/shard_map/all_to_all | solution.py:587
  92.4 1.3 grids.3
  93.7 10.7 %all_to_all.43.in_ref = bf16[16,32,256]{2,1,0:T(8,128)(2,1)S(1)} all-to-all(bf16[16,32,256]{2,1,0:T(8,128)(2,1)S(1)} %grids.3), channel_id=1, replica_groups=mesh['facet'=16,'sub'=8] {'facet'}, dimensions={0} | all-to-all | bytes 524288 | tf_op jit(solution)/shard_map/all_to_all | solution.py:587
  104.4 3.4 %last_visibilities.1 = (bf16[16,32,256]{2,1,0:T(8,128)(2,1)S(1)}, f32[2,4096]{1,0:T(2,128)S(1)}) custom-call(s32[1,16]{1,0:T(1,128)S(1)} %copy-done.4, bf16[2,4096]{1,0:T(2,128)(2,1)S(1)} %bitcast.23, bf16[1,4096]{1,0:T(2,128)(2,1)S(1)} %bitcast.25, bf16[16,32,256]{2,1,0:T(8,128)(2,1)S(1)} %all_to_all.43.in_ref, ...), custom_call_target="tpu_custom_call" | custom-call | tf_op jit(solution)/shard_map/last_visibilities/pallas_call | solution.py:363
  107.8 10.8 %all_to_all.44.in_ref = bf16[16,32,256]{2,1,0:T(8,128)(2,1)S(1)} all-to-all(bf16[16,32,256]{2,1,0:T(8,128)(2,1)S(1)} %get-tuple-element.27), channel_id=1, replica_groups=mesh['facet'=16,'sub'=8] {'facet'}, dimensions={0} | all-to-all | bytes 524288 | tf_op jit(solution)/shard_map/all_to_all | solution.py:587
  118.6 2.5 %adjoint.3 = bf16[16,8,16,128]{3,2,1,0:T(8,128)(2,1)} custom-call(bf16[16,32,256]{2,1,0:T(8,128)(2,1)S(1)} %all_to_all.44.in_ref, f32[16,16,128]{2,1,0:T(8,128)S(1)} %get-tuple-element.18.c_ref, f32[16,16,128]{2,1,0:T(8,128)S(1)} %get-tuple-element.19.s_ref, bf16[2,2048,256]{2,1,0:T(8,128)(2,1)S(1)} %get-tuple-element.20.table_ref), custom_call_target="tpu_custom_call" | custom-call | tf_op jit(solution)/shard_map/adjoint/pallas_call | solution.py:279
  121.1 8.2 %all-to-all-start.7 = ((bf16[128,16,128]{2,1,0:T(8,128)(2,1)}), bf16[128,16,128]{2,1,0:T(8,128)(2,1)S(1)}, u32[]{:S(2)}, u32[]{:S(2)}) async-start(bf16[128,16,128]{2,1,0:T(8,128)(2,1)} %bitcast.7), calls=%async_computation.7 | async-start | bytes 1048576 | tf_op jit(solution)/shard_map/all_to_all | solution.py:596
  129.3 4.2 %update_tables.1 = (bf16[4096,512]{1,0:T(8,128)(2,1)}, f32[16,2048]{1,0:T(8,128)S(1)}, f32[16,2048]{1,0:T(8,128)S(1)}) custom-call(s32[8]{0:T(128)S(1)} %add.11.starts_ref, s32[2,16]{1,0:T(2,128)S(1)} %copy-done.3), custom_call_target="tpu_custom_call" | custom-call | tf_op jit(solution)/shard_map/update_tables/pallas_call | solution.py:566
  133.5 9.4 %all-to-all-done.7.adj1_ref = bf16[128,16,128]{2,1,0:T(8,128)(2,1)S(1)} async-done(((bf16[128,16,128]{2,1,0:T(8,128)(2,1)}), bf16[128,16,128]{2,1,0:T(8,128)(2,1)S(1)}, u32[]{:S(2)}, u32[]{:S(2)}) %all-to-all-start.7) | async-done | bytes 524320 | tf_op jit(solution)/shard_map/all_to_all | solution.py:596
  142.9 7.8 %update.1.mine_ref = bf16[64,8192]{1,0:T(8,128)(2,1)S(1)} custom-call(f32[2]{0:T(128)S(1)} %copy-done.5, bf16[128,16,128]{2,1,0:T(8,128)(2,1)S(1)} %all_to_all.41.adj0_ref, bf16[128,16,128]{2,1,0:T(8,128)(2,1)S(1)} %all-to-all-done.7.adj1_ref, bf16[4096,512]{1,0:T(8,128)(2,1)} %get-tuple-element.28.table_hbm, f32[16,2048]{1,0:T(8,128)S(1)} %get-tuple-element.29.pc_ref, ...), custom_call_target="tpu_custom_call" | custom-call | tf_op jit(solution)/shard_map/update/pallas_call | solution.py:490
  150.7 1.2 collective-permute-start.4
  152.6 1.6 %collective-permute-done.4.theirs_ref = bf16[64,8192]{1,0:T(8,128)(2,1)S(1)} collective-permute-done((bf16[64,8192]{1,0:T(8,128)(2,1)S(1)}, bf16[64,8192]{1,0:T(8,128)(2,1)S(1)}, u32[]{:S(2)}, u32[]{:S(2)}) %collective-permute-start.4) | collective-permute-done | bytes 1048608 | tf_op jit(solution)/shard_map/ppermute | solution.py:591
  154.3 2.2 %take_step.1 = f32[128,8192]{1,0:T(8,128)} custom-call(bf16[64,8192]{1,0:T(8,128)(2,1)S(1)} %update.1.mine_ref, bf16[64,8192]{1,0:T(8,128)(2,1)S(1)} %collective-permute-done.4.theirs_ref, f32[128,8192]{1,0:T(8,128)S(1)} %bitcast.17), custom_call_target="tpu_custom_call" | custom-call | tf_op jit(solution)/shard_map/take_step/pallas_call | solution.py:526
  (23 shorter events, 0.7 us)
Async XLA Ops:
  0.6 13.9 %copy-start.3 = (s32[2,16]{1,0:T(2,128)S(1)}, s32[2,16]{1,0:T(2,128)}, u32[]{:S(2)}) copy-start(s32[2,16]{1,0:T(2,128)} %offsets_ref.7) | copy-start | bytes 388
  0.6 13.9 %copy-start.6 = (s32[1,16]{1,0:T(1,128)S(1)}, s32[1,16]{1,0:T(1,128)}, u32[]{:S(2)}) copy-start(s32[1,16]{1,0:T(1,128)} %rows_ref.1) | copy-start | bytes 196
  0.7 27.0 %copy-start.7 = (s32[2,1,1,4096]{3,2,1,0:T(1,128)S(1)}, s32[2,1,1,4096]{3,2,1,0:T(1,128)}, u32[]{:S(2)}) copy-start(s32[2,1,1,4096]{3,2,1,0:T(1,128)} %param.15) | copy-start | bytes 98308
  0.7 34.3 %copy-start.4 = (s32[1,16]{1,0:T(1,128)S(1)}, s32[1,16]{1,0:T(1,128)}, u32[]{:S(2)}) copy-start(s32[1,16]{1,0:T(1,128)} %counts_ref.3) | copy-start | bytes 196
  0.7 34.3 %copy-start.2 = (bf16[1,1,4096]{2,1,0:T(2,128)(2,1)S(1)}, bf16[1,1,4096]{2,1,0:T(2,128)(2,1)}, u32[]{:S(2)}) copy-start(bf16[1,1,4096]{2,1,0:T(2,128)(2,1)} %param.17) | copy-start | bytes 24580
  0.7 34.3 %copy-start.1 = (bf16[2,1,1,4096]{3,0,2,1:T(2,128)(2,1)S(1)}, bf16[2,1,1,4096]{3,0,2,1:T(2,128)(2,1)}, u32[]{:S(2)}) copy-start(bf16[2,1,1,4096]{3,0,2,1:T(2,128)(2,1)} %param.16) | copy-start | bytes 49156
  1.4 14.9 %collective-permute-start = (s32[8]{0:T(128)S(1)}, s32[8]{0:T(128)S(1)}, u32[]{:S(2)}, u32[]{:S(2)}) collective-permute-start(s32[8]{0:T(128)S(1)} %compare_select_fusion), channel_id=1, source_target_pairs={{0,1},{1,0},{2,3},{3,2},{4,5},{5,4},{6,7},{7,6},{8,9},{9,8},{10,11... | collective-permute-start | bytes 104 | tf_op jit(solution)/shard_map/ppermute | solution.py:591
  7.7 13.6 %all-to-all-start = ((bf16[16,32,128]{2,1,0:T(8,128)(2,1)}), bf16[16,32,128]{2,1,0:T(8,128)(2,1)S(1)}, u32[]{:S(2)}, u32[]{:S(2)}) async-start(bf16[16,32,128]{2,1,0:T(8,128)(2,1)} %section.1.first_ref), calls=%async_computation | async-start | bytes 262144 | tf_op jit(solution)/shard_map/all_to_all | solution.py:587
  16.3 2.9 %collective-permute-start.1 = (s32[8]{0:T(128)S(1)}, s32[8]{0:T(128)S(1)}, u32[]{:S(2)}, u32[]{:S(2)}) collective-permute-start(s32[8]{0:T(128)S(1)} %fusion), channel_id=1, source_target_pairs={{0,2},{1,3},{2,0},{3,1},{4,6},{5,7},{6,4},{7,5},{8,10},{9,11},{10,... | collective-permute-start | bytes 104 | tf_op jit(solution)/shard_map/ppermute | solution.py:591
  21.3 58.1 %copy-start.5 = (f32[2]{0:T(128)S(1)}, f32[2]{0:T(128)}, u32[]{:S(2)}) copy-start(f32[2]{0:T(128)} %step_ref.3) | copy-start | bytes 28
  23.2 11.7 %all-to-all-start.1 = ((bf16[16,32,256]{2,1,0:T(8,128)(2,1)}), bf16[16,32,256]{2,1,0:T(8,128)(2,1)S(1)}, u32[]{:S(2)}, u32[]{:S(2)}) async-start(bf16[16,32,256]{2,1,0:T(8,128)(2,1)} %grids.2), calls=%async_computation.1 | async-start | bytes 524288 | tf_op jit(solution)/shard_map/all_to_all | solution.py:587
  27.7 4.6 %collective-permute-start.2 = (s32[8]{0:T(128)S(1)}, s32[8]{0:T(128)S(1)}, u32[]{:S(2)}, u32[]{:S(2)}) collective-permute-start(s32[8]{0:T(128)S(1)} %fusion.1), channel_id=1, source_target_pairs={{0,4},{1,5},{2,6},{3,7},{4,0},{5,1},{6,2},{7,3},{8,12},{9,13},{10,... | collective-permute-start | bytes 104 | tf_op jit(solution)/shard_map/ppermute | solution.py:591
  76.7 2.7 %collective-permute-start.3 = (bf16[128,16,128]{2,1,0:T(8,128)(2,1)S(1)}, bf16[128,16,128]{2,1,0:T(8,128)(2,1)S(1)}, u32[]{:S(2)}, u32[]{:S(2)}) collective-permute-start(bf16[128,16,128]{2,1,0:T(8,128)(2,1)S(1)} %all_to_all.41.adj0_ref), channel_id=1, source_target_pairs={{0,1},{1,0},{2,3},{3,2},{4,5},{5,4},{6,7},{7,6},{8,9},{9,8},{10,11... | collective-permute-start | bytes 1572872 | tf_op jit(solution)/shard_map/ppermute | solution.py:591
  121.1 21.8 %all-to-all-start.7 = ((bf16[128,16,128]{2,1,0:T(8,128)(2,1)}), bf16[128,16,128]{2,1,0:T(8,128)(2,1)S(1)}, u32[]{:S(2)}, u32[]{:S(2)}) async-start(bf16[128,16,128]{2,1,0:T(8,128)(2,1)} %bitcast.7), calls=%async_computation.7 | async-start | bytes 1048576 | tf_op jit(solution)/shard_map/all_to_all | solution.py:596
  142.9 11.3 %copy-start = (f32[1,128,8192]{2,1,0:T(8,128)S(1)}, f32[1,128,8192]{2,1,0:T(8,128)}, u32[]{:S(2)}) copy-start(f32[1,128,8192]{2,1,0:T(8,128)} %param.9) | copy-start | bytes 12582916
  150.7 3.5 %collective-permute-start.4 = (bf16[64,8192]{1,0:T(8,128)(2,1)S(1)}, bf16[64,8192]{1,0:T(8,128)(2,1)S(1)}, u32[]{:S(2)}, u32[]{:S(2)}) collective-permute-start(bf16[64,8192]{1,0:T(8,128)(2,1)S(1)} %update.1.mine_ref), channel_id=1, source_target_pairs={{0,1},{1,0},{2,3},{3,2},{4,5},{5,4},{6,7},{7,6},{8,9},{9,8},{10,11... | collective-permute-start | bytes 3145736 | tf_op jit(solution)/shard_map/ppermute | solution.py:591
